TPU v7x, 32 devices: a whole 2x2x4 slice. The times are simulated.
32 devices in a mesh: dp: 4 (over x, core), ctx: 8 (over z, y).
Axes of the slice: x: 2, y: 2, z: 4, core: 2. Of those that a mesh axis runs over, the one named last changes fastest.
Arguments:
- tokens: bfloat16 [4, 1024, 1024], P('dp', 'ctx'), may hold values from -6 to 6
- cotangent: bfloat16 [4, 1024, 1024], P('dp', 'ctx'), may hold values from -6 to 6
- domain_ids: int32 [4], P('dp'), may hold values from 0 to 7
- domain_weights: float32 [8], replicated, may hold values from 0.25 to 4
- stretch_offsets: int32 [4, 8], P('dp', 'ctx'), may hold values from 0 to 7, each once within a row
- gain_attn: bfloat16 [1024], P(('dp', 'ctx')), may hold values from 0.099609375 to 1.8984375
- gain_ffn: bfloat16 [1024], P(('dp', 'ctx')), may hold values from 0.099609375 to 1.8984375
- w_query: bfloat16 [1024, 1024], P(('dp', 'ctx')), may hold values from -0.1875 to 0.1875
- w_latent: bfloat16 [1024, 512], P(('dp', 'ctx')), may hold values from -0.1875 to 0.1875
- w_upkey: bfloat16 [512, 512], P(('dp', 'ctx')), may hold values from -0.375 to 0.375
- w_upvalue: bfloat16 [512, 512], P(('dp', 'ctx')), may hold values from -0.375 to 0.375
- w_out: bfloat16 [1024, 1024], P(('dp', 'ctx')), may hold values from -4 to 4
- w_gate: bfloat16 [1024, 2816], P(('dp', 'ctx')), may hold values from -0.1875 to 0.1875
- w_up: bfloat16 [1024, 2816], P(('dp', 'ctx')), may hold values from -0.1875 to 0.1875
- w_down: bfloat16 [2816, 1024], P(('dp', 'ctx')), may hold values from -0.109375 to 0.109375
Outputs:
- output: bfloat16 [4, 1024, 1024], P('dp', 'ctx')
- grad_tokens: bfloat16 [4, 1024, 1024], P('dp', 'ctx')
- grad_gain_attn: float32 [1024], P(('dp', 'ctx'))
- grad_gain_ffn: float32 [1024], P(('dp', 'ctx'))
- grad_query: float32 [1024, 1024], P(('dp', 'ctx'))
- grad_latent: float32 [1024, 512], P(('dp', 'ctx'))
- grad_upkey: float32 [512, 512], P(('dp', 'ctx'))
- grad_upvalue: float32 [512, 512], P(('dp', 'ctx'))
- grad_out: float32 [1024, 1024], P(('dp', 'ctx'))
- grad_gate: float32 [1024, 2816], P(('dp', 'ctx'))
- grad_up: float32 [1024, 2816], P(('dp', 'ctx'))
- grad_down: float32 [2816, 1024], P(('dp', 'ctx'))
Inputs may be any that keep to these rules, and one draw needn't show every extreme that they name: Each row stretch_offsets[s] is a permutation: the ctx indices hold the blocks of 128 positions of sequence s in this order.
All inputs are finite; a program needn't handle non-finite values.
Results may differ from a plain program's by a relative error of at most 0.02.
Values may be sent and summed in bfloat16 or wider, within the bound.
No kernel may reach another device: no remote copies, remote signals or barrier semaphores. Data moves between devices by JAX's collectives and lax.ppermute only.
A program may use at most 192 MiB of HBM per device.

v0:
```python
import jax
import jax.numpy as jnp
from jax import lax
from jax.sharding import PartitionSpec as P

HEADS = 16
HEAD = 64
LATENT = 256
DOMAINS = 8


EPS = 1e-06
SCALE = 0.125
heads_limit = 4


def norm_rows(values, gain):
    return values * lax.rsqrt(jnp.mean(values * values, -1, keepdims=True) + EPS) * gain


def product(left, right):
    return jnp.dot(left, right, preferred_element_type=jnp.float32)


def contract_rows(left, right):
    return lax.dot_general(
        left, right, (((0,), (0,)), ((), ())), preferred_element_type=jnp.float32
    )


def times_transposed(left, right):
    return lax.dot_general(
        left, right, (((1,), (1,)), ((), ())), preferred_element_type=jnp.float32
    )


def per_device(
    tokens,
    cotangent,
    domain_ids,
    domain_weights,
    stretch_offsets,
    gain_attn,
    gain_ffn,
    w_query,
    w_latent,
    w_upkey,
    w_upvalue,
    w_out,
    w_gate,
    w_up,
    w_down,
):
    seq_dev, span_rows, model_width = tokens.shape
    row_count = seq_dev * span_rows
    ctx_count = lax.axis_size("ctx")
    length = span_rows * ctx_count
    group_heads = HEADS // 2
    head_block = min(heads_limit, group_heads)
    per_group = group_heads // head_block
    block_count = seq_dev * 2 * per_group
    gathered = (
        lax.all_gather(gain_attn, ("dp", "ctx"), axis=0, tiled=True),
        lax.all_gather(gain_ffn, ("dp", "ctx"), axis=0, tiled=True),
        lax.all_gather(w_query, ("dp", "ctx"), axis=0, tiled=True),
        lax.all_gather(w_latent, ("dp", "ctx"), axis=0, tiled=True),
        lax.all_gather(w_upkey, ("dp", "ctx"), axis=0, tiled=True),
        lax.all_gather(w_upvalue, ("dp", "ctx"), axis=0, tiled=True),
        lax.all_gather(w_out, ("dp", "ctx"), axis=0, tiled=True),
        lax.all_gather(w_gate, ("dp", "ctx"), axis=0, tiled=True),
        lax.all_gather(w_up, ("dp", "ctx"), axis=0, tiled=True),
        lax.all_gather(w_down, ("dp", "ctx"), axis=0, tiled=True),
    )
    (
        gain_one,
        gain_two,
        query_full,
        latent_full,
        upkey_full,
        upvalue_full,
        out_full,
        gate_full,
        up_full,
        down_full,
    ) = gathered
    gain_one = gain_one.astype(jnp.float32)
    gain_two = gain_two.astype(jnp.float32)
    x_rows = tokens.reshape(row_count, model_width).astype(jnp.float32)
    normed_one = norm_rows(x_rows, gain_one)
    normed_low = normed_one.astype(jnp.bfloat16)
    query_rows = product(normed_low, query_full).astype(jnp.bfloat16)
    latent_rows = product(normed_low, latent_full).astype(jnp.bfloat16)
    query_five = query_rows.reshape(seq_dev, span_rows, 2, group_heads, HEAD)
    upkey_heads = upkey_full.reshape(2, LATENT, group_heads, HEAD)
    query_latent = jnp.einsum(
        "sqgje,glje->sgjql", query_five, upkey_heads, preferred_element_type=jnp.float32
    ).astype(jnp.bfloat16)
    query_blocks = query_latent.reshape(block_count, head_block, span_rows, LATENT)
    offset_low = stretch_offsets.astype(jnp.bfloat16)
    latent_local = latent_rows.reshape(seq_dev, span_rows, 2 * LATENT)
    keys_all, offsets_all = (
        lax.all_gather(latent_local, "ctx", axis=1, tiled=True),
        lax.all_gather(offset_low, "ctx", axis=1, tiled=True),
    )
    keys_four = keys_all.reshape(seq_dev, length, 2, LATENT)
    within = jnp.arange(span_rows, dtype=jnp.int32)
    query_pos = stretch_offsets * span_rows + within[None, :]
    key_pos = (
        offsets_all.astype(jnp.int32)[:, :, None] * span_rows + within[None, None, :]
    ).reshape(seq_dev, length)

    def block_keys(block_index):
        seq_index = block_index // (2 * per_group)
        group_index = block_index // per_group % 2
        keys_seq = lax.dynamic_index_in_dim(keys_four, seq_index, 0, keepdims=False)
        key_block = lax.dynamic_index_in_dim(keys_seq, group_index, 1, keepdims=False)
        query_row = lax.dynamic_index_in_dim(query_pos, seq_index, 0, keepdims=False)
        key_row = lax.dynamic_index_in_dim(key_pos, seq_index, 0, keepdims=False)
        allowed = query_row[:, None] >= key_row[None, :]
        return (key_block, allowed, seq_index, group_index)

    def scores_of(query_block, key_block, allowed):
        raw_scores = (
            jnp.einsum("hql,kl->hqk", query_block, key_block, preferred_element_type=jnp.float32)
            * SCALE
        )
        return jnp.where(allowed[None], raw_scores, -1e30)

    def forward_block(block_index):
        key_block, allowed, seq_index, group_index = block_keys(block_index)
        query_block = lax.dynamic_index_in_dim(query_blocks, block_index, 0, keepdims=False)
        scores = scores_of(query_block, key_block, allowed)
        row_max = jnp.max(scores, -1, keepdims=True)
        exp_terms = jnp.exp(scores - row_max)
        row_total = jnp.sum(exp_terms, -1, keepdims=True)
        probs_low = (exp_terms / row_total).astype(jnp.bfloat16)
        mixed_latent = jnp.einsum(
            "hqk,kl->hql", probs_low, key_block, preferred_element_type=jnp.float32
        )
        return (mixed_latent.astype(jnp.bfloat16), (row_max + jnp.log(row_total))[..., 0])

    mixed_blocks, log_totals = lax.map(forward_block, jnp.arange(block_count))
    mixed_five = mixed_blocks.reshape(seq_dev, 2, group_heads, span_rows, LATENT)
    upvalue_heads = upvalue_full.reshape(2, LATENT, group_heads, HEAD)
    value_rows = (
        jnp.einsum(
            "sgjql,glje->sqgje", mixed_five, upvalue_heads, preferred_element_type=jnp.float32
        )
        .astype(jnp.bfloat16)
        .reshape(row_count, HEADS * HEAD)
    )
    middle = x_rows + product(value_rows, out_full)
    normed_two = norm_rows(middle, gain_two)
    second_low = normed_two.astype(jnp.bfloat16)
    gate_pre = product(second_low, gate_full)
    up_pre = product(second_low, up_full)
    sigmoid_gate = jax.nn.sigmoid(gate_pre)
    silu_gate = gate_pre * sigmoid_gate
    hidden = (silu_gate * up_pre).astype(jnp.bfloat16)
    layer_rows = middle + product(hidden, down_full)
    output = layer_rows.astype(jnp.bfloat16).reshape(seq_dev, span_rows, model_width)
    regathered = (
        lax.all_gather(w_query, ("dp", "ctx"), axis=0, tiled=True),
        lax.all_gather(w_latent, ("dp", "ctx"), axis=0, tiled=True),
        lax.all_gather(w_upkey, ("dp", "ctx"), axis=0, tiled=True),
        lax.all_gather(w_upvalue, ("dp", "ctx"), axis=0, tiled=True),
        lax.all_gather(w_out, ("dp", "ctx"), axis=0, tiled=True),
        lax.all_gather(w_gate, ("dp", "ctx"), axis=0, tiled=True),
        lax.all_gather(w_up, ("dp", "ctx"), axis=0, tiled=True),
        lax.all_gather(w_down, ("dp", "ctx"), axis=0, tiled=True),
    )
    query_full, latent_full, upkey_full, upvalue_full, out_full, gate_full, up_full, down_full = (
        regathered
    )
    upkey_heads = upkey_full.reshape(2, LATENT, group_heads, HEAD)
    upvalue_heads = upvalue_full.reshape(2, LATENT, group_heads, HEAD)
    match = domain_ids[:, None] == jnp.arange(DOMAINS, dtype=jnp.int32)[None, :]
    seq_scale = jnp.sum(jnp.where(match, domain_weights[None, :], 0.0), -1)
    d_layer = (cotangent.astype(jnp.float32) * seq_scale[:, None, None]).reshape(
        row_count, model_width
    )
    d_layer_low = d_layer.astype(jnp.bfloat16)
    grad_down_part = contract_rows(hidden, d_layer_low)
    d_hidden = times_transposed(d_layer_low, down_full)
    d_gate = (d_hidden * up_pre * (sigmoid_gate * (1.0 + gate_pre * (1.0 - sigmoid_gate)))).astype(
        jnp.bfloat16
    )
    d_up = (d_hidden * silu_gate).astype(jnp.bfloat16)
    grad_gate_part = contract_rows(second_low, d_gate)
    grad_up_part = contract_rows(second_low, d_up)
    d_second = times_transposed(d_gate, gate_full) + times_transposed(d_up, up_full)
    norm_value, norm_pull = jax.vjp(norm_rows, middle, gain_two)
    d_middle_norm, grad_gain_two_part = norm_pull(d_second)
    d_middle = d_layer + d_middle_norm
    d_middle_low = d_middle.astype(jnp.bfloat16)
    grad_out_part = contract_rows(value_rows, d_middle_low)
    d_values = times_transposed(d_middle_low, out_full).astype(jnp.bfloat16)
    d_values_five = d_values.reshape(seq_dev, span_rows, 2, group_heads, HEAD)
    grad_upvalue_part = jnp.einsum(
        "sgjql,sqgje->glje", mixed_five, d_values_five, preferred_element_type=jnp.float32
    ).reshape(2 * LATENT, group_heads * HEAD)
    d_mixed = jnp.einsum(
        "sqgje,glje->sgjql", d_values_five, upvalue_heads, preferred_element_type=jnp.float32
    ).astype(jnp.bfloat16)
    d_mixed_blocks = d_mixed.reshape(block_count, head_block, span_rows, LATENT)

    def backward_block(key_grads, block_index):
        key_block, allowed, seq_index, group_index = block_keys(block_index)
        query_block = lax.dynamic_index_in_dim(query_blocks, block_index, 0, keepdims=False)
        d_block = lax.dynamic_index_in_dim(d_mixed_blocks, block_index, 0, keepdims=False)
        log_block = lax.dynamic_index_in_dim(log_totals, block_index, 0, keepdims=False)
        scores = scores_of(query_block, key_block, allowed)
        probs = jnp.exp(scores - log_block[..., None])
        probs_low = probs.astype(jnp.bfloat16)
        d_probs = jnp.einsum("hql,kl->hqk", d_block, key_block, preferred_element_type=jnp.float32)
        d_scores = probs * (d_probs - jnp.sum(probs * d_probs, -1, keepdims=True))
        d_scores_low = d_scores.astype(jnp.bfloat16) * jnp.bfloat16(SCALE)
        d_query = jnp.einsum(
            "hqk,kl->hql", d_scores_low, key_block, preferred_element_type=jnp.float32
        ).astype(jnp.bfloat16)
        d_keys = jnp.einsum(
            "hqk,hql->kl", d_scores_low, query_block, preferred_element_type=jnp.float32
        )
        d_keys = d_keys + jnp.einsum(
            "hqk,hql->kl", probs_low, d_block, preferred_element_type=jnp.float32
        )
        previous = lax.dynamic_slice(
            key_grads, (seq_index, 0, group_index, 0), (1, length, 1, LATENT)
        )
        key_grads = lax.dynamic_update_slice(
            key_grads, previous + d_keys[None, :, None, :], (seq_index, 0, group_index, 0)
        )
        return (key_grads, d_query)

    key_start = jnp.zeros((seq_dev, length, 2, LATENT), jnp.float32)
    key_grads, d_query_blocks = lax.scan(backward_block, key_start, jnp.arange(block_count))
    d_latent_local = lax.psum_scatter(
        key_grads.reshape(seq_dev, length, 2 * LATENT).astype(jnp.bfloat16),
        "ctx",
        scatter_dimension=1,
        tiled=True,
    )
    d_latent_low = d_latent_local.reshape(row_count, 2 * LATENT)
    d_query_five = d_query_blocks.reshape(seq_dev, 2, group_heads, span_rows, LATENT)
    grad_upkey_part = jnp.einsum(
        "sgjql,sqgje->glje", d_query_five, query_five, preferred_element_type=jnp.float32
    ).reshape(2 * LATENT, group_heads * HEAD)
    d_queries = (
        jnp.einsum(
            "sgjql,glje->sqgje", d_query_five, upkey_heads, preferred_element_type=jnp.float32
        )
        .astype(jnp.bfloat16)
        .reshape(row_count, HEADS * HEAD)
    )
    grad_query_part = contract_rows(normed_low, d_queries)
    grad_latent_part = contract_rows(normed_low, d_latent_low)
    d_first = times_transposed(d_queries, query_full) + times_transposed(d_latent_low, latent_full)
    first_value, first_pull = jax.vjp(norm_rows, x_rows, gain_one)
    d_x_norm, grad_gain_one_part = first_pull(d_first)
    grad_tokens = (
        (d_middle + d_x_norm).astype(jnp.bfloat16).reshape(seq_dev, span_rows, model_width)
    )
    partial_sums = (
        lax.psum_scatter(
            grad_gain_one_part.astype(jnp.bfloat16), "dp", scatter_dimension=0, tiled=True
        ).astype(jnp.float32),
        lax.psum_scatter(
            grad_gain_two_part.astype(jnp.bfloat16), "dp", scatter_dimension=0, tiled=True
        ).astype(jnp.float32),
        lax.psum_scatter(
            grad_query_part.astype(jnp.bfloat16), "dp", scatter_dimension=0, tiled=True
        ).astype(jnp.float32),
        lax.psum_scatter(
            grad_latent_part.astype(jnp.bfloat16), "dp", scatter_dimension=0, tiled=True
        ).astype(jnp.float32),
        lax.psum_scatter(
            grad_upkey_part.astype(jnp.bfloat16), "dp", scatter_dimension=0, tiled=True
        ).astype(jnp.float32),
        lax.psum_scatter(
            grad_upvalue_part.astype(jnp.bfloat16), "dp", scatter_dimension=0, tiled=True
        ).astype(jnp.float32),
        lax.psum_scatter(
            grad_out_part.astype(jnp.bfloat16), "dp", scatter_dimension=0, tiled=True
        ).astype(jnp.float32),
        lax.psum_scatter(
            grad_gate_part.astype(jnp.bfloat16), "dp", scatter_dimension=0, tiled=True
        ).astype(jnp.float32),
        lax.psum_scatter(
            grad_up_part.astype(jnp.bfloat16), "dp", scatter_dimension=0, tiled=True
        ).astype(jnp.float32),
        lax.psum_scatter(
            grad_down_part.astype(jnp.bfloat16), "dp", scatter_dimension=0, tiled=True
        ).astype(jnp.float32),
    )
    summed = (
        lax.psum_scatter(
            partial_sums[0].astype(jnp.bfloat16), "ctx", scatter_dimension=0, tiled=True
        ).astype(jnp.float32),
        lax.psum_scatter(
            partial_sums[1].astype(jnp.bfloat16), "ctx", scatter_dimension=0, tiled=True
        ).astype(jnp.float32),
        lax.psum_scatter(
            partial_sums[2].astype(jnp.bfloat16), "ctx", scatter_dimension=0, tiled=True
        ).astype(jnp.float32),
        lax.psum_scatter(
            partial_sums[3].astype(jnp.bfloat16), "ctx", scatter_dimension=0, tiled=True
        ).astype(jnp.float32),
        lax.psum_scatter(
            partial_sums[4].astype(jnp.bfloat16), "ctx", scatter_dimension=0, tiled=True
        ).astype(jnp.float32),
        lax.psum_scatter(
            partial_sums[5].astype(jnp.bfloat16), "ctx", scatter_dimension=0, tiled=True
        ).astype(jnp.float32),
        lax.psum_scatter(
            partial_sums[6].astype(jnp.bfloat16), "ctx", scatter_dimension=0, tiled=True
        ).astype(jnp.float32),
        lax.psum_scatter(
            partial_sums[7].astype(jnp.bfloat16), "ctx", scatter_dimension=0, tiled=True
        ).astype(jnp.float32),
        lax.psum_scatter(
            partial_sums[8].astype(jnp.bfloat16), "ctx", scatter_dimension=0, tiled=True
        ).astype(jnp.float32),
        lax.psum_scatter(
            partial_sums[9].astype(jnp.bfloat16), "ctx", scatter_dimension=0, tiled=True
        ).astype(jnp.float32),
    )
    return (
        output,
        grad_tokens,
        summed[0],
        summed[1],
        summed[2],
        summed[3],
        summed[4],
        summed[5],
        summed[6],
        summed[7],
        summed[8],
        summed[9],
    )


def solution(mesh):
    in_specs = (
        P("dp", "ctx", None),
        P("dp", "ctx", None),
        P("dp"),
        P(),
        P("dp", "ctx"),
        P(("dp", "ctx")),
        P(("dp", "ctx")),
        P(("dp", "ctx"), None),
        P(("dp", "ctx"), None),
        P(("dp", "ctx"), None),
        P(("dp", "ctx"), None),
        P(("dp", "ctx"), None),
        P(("dp", "ctx"), None),
        P(("dp", "ctx"), None),
        P(("dp", "ctx"), None),
    )
    out_specs = (
        P("dp", "ctx", None),
        P("dp", "ctx", None),
        P(("dp", "ctx")),
        P(("dp", "ctx")),
        P(("dp", "ctx"), None),
        P(("dp", "ctx"), None),
        P(("dp", "ctx"), None),
        P(("dp", "ctx"), None),
        P(("dp", "ctx"), None),
        P(("dp", "ctx"), None),
        P(("dp", "ctx"), None),
        P(("dp", "ctx"), None),
    )
    return jax.shard_map(
        per_device, mesh=mesh, in_specs=in_specs, out_specs=out_specs, check_vma=False
    )
```

profile of v0, /device:TPU:1, one launch (start us, length us, event | category | flops | bytes accessed | tf_op | source)
XLA Modules:
  0.0 1465.9 jit_solution(8777194372786977426)
XLA Ops:
  9.7 41.0 %all-reduce.7 = (bf16[1024]{0:T(1024)(128)(2,1)S(1)}, bf16[1024]{0:T(1024)(128)(2,1)S(1)}) all-reduce(bf16[1024]{0:T(1024)(128)(2,1)S(1)} %dynamic-update-slice.1, bf16[1024]{0:T(1024)(128)(2,1)S(1)} %dynamic-update-slice.2), channel_id=1, replica_groups=mesh['dp'=4,'ctx'=8] {'dp','ctx'}, use_global_device_ids=true, to_apply=%add.1 | all-reduce | flops 2048 | bytes 8192
  51.8 15.7 %all-gather.11.cloned.1.call-done = bf16[1024,512]{1,0:T(8,128)(2,1)} async-done(((bf16[32,512]{1,0:T(8,128)(2,1)}), bf16[1024,512]{1,0:T(8,128)(2,1)}) %all-gather.11.cloned.1.call-update) | async-done | bytes 1048592 | tf_op jit(solution)/shard_map/all_gather | solution.py:66
  67.5 2.3 convolution_convert_fusion.15
  75.1 16.5 %all-reduce = bf16[8]{0:T(256)(128)(2,1)S(1)} all-reduce(bf16[8]{0:T(256)(128)(2,1)S(1)} %dynamic-update-slice), channel_id=1, replica_groups=mesh['dp'=4,'ctx'=8] {'ctx'}, use_global_device_ids=true, to_apply=%add | all-reduce | flops 8 | bytes 32
  91.7 63.3 %all_gather.50 = bf16[512,512]{1,0:T(8,128)(2,1)S(1)} all-gather(bf16[16,512]{1,0:T(8,128)(2,1)S(1)} %copy-done.35), channel_id=1, replica_groups=mesh['dp'=4,'ctx'=8] {'dp','ctx'}, dimensions={0}, use_global_device_ids=true | all-gather | bytes 540672 | tf_op jit(solution)/shard_map/all_gather | solution.py:68
  156.2 68.7 %all_gather.47 = bf16[512,512]{1,0:T(8,128)(2,1)S(1)} all-gather(bf16[16,512]{1,0:T(8,128)(2,1)S(1)} %copy-done.36), channel_id=1, replica_groups=mesh['dp'=4,'ctx'=8] {'dp','ctx'}, dimensions={0}, use_global_device_ids=true | all-gather | bytes 540672 | tf_op jit(solution)/shard_map/all_gather | solution.py:67
  227.4 2.3 reshape.361
  231.1 2.1 convolution_convert_fusion.14
  235.0 30.8 %while.30 = (s32[]{:T(128)}, bf16[4,4,128,256]{3,2,1,0:T(8,128)(2,1)S(1)}, f32[4,4,128]{2,1,0:T(4,128)S(1)}, s32[4]{0:T(128)S(1)}, bf16[4,4,128,256]{3,2,1,0:T(8...) while((s32[]{:T(128)}, ...), condition=%wide.region_4.5_spmd.clone, body=%wide.region_1.4_spmd.clone.sunk | while | flops 543425152 | bytes 8422919 | solution.py:142
  266.8 2.1 multiply_reduce_fusion.3
  269.1 27.5 %all-gather.15.cloned.1.call-done = bf16[1024,2816]{1,0:T(8,128)(2,1)} async-done(((bf16[32,2816]{1,0:T(8,128)(2,1)}), bf16[1024,2816]{1,0:T(8,128)(2,1)}) %all-gather.15.cloned.1.call-update) | async-done | bytes 5767184 | tf_op jit(solution)/shard_map/all_gather | solution.py:70
  296.6 4.7 fusion.124
  301.3 64.3 %all-gather.17.cloned.1.call-done = bf16[1024,2816]{1,0:T(8,128)(2,1)} async-done(((bf16[32,2816]{1,0:T(8,128)(2,1)}), bf16[1024,2816]{1,0:T(8,128)(2,1)}) %all-gather.17.cloned.1.call-update) | async-done | bytes 5767184 | tf_op jit(solution)/shard_map/all_gather | solution.py:71
  365.6 4.8 fusion.125
  370.4 64.4 %all-gather.19.cloned.1.call-done = bf16[2816,1024]{1,0:T(8,128)(2,1)} async-done(((bf16[88,1024]{1,0:T(8,128)(2,1)}), bf16[2816,1024]{1,0:T(8,128)(2,1)}) %all-gather.19.cloned.1.call-update) | async-done | bytes 5767184 | tf_op jit(solution)/shard_map/all_gather | solution.py:72
  434.8 6.8 multiply_convert_fusion.1
  441.6 5.2 fusion.126
  446.8 2.1 multiply_reduce_fusion.1
  455.9 97.0 %while.31 = (s32[]{:T(128)}, f32[1,1024,2,256]{1,3,2,0:T(8,128)}, bf16[4,4,128,256]{3,2,1,0:T(8,128)(2,1)}, s32[4]{0:T(128)S(1)}, bf16[4,4,128,256]{3,2,1,0:T(8,...) while((s32[]{:T(128)}, f32[1,1024,2,256]{1,3,2,0:T(8,128)}, ...), condition=%wide.region_10.11_spmd.clone, body=%wide.region_8.10_spmd.clone.sunk | while | flops 1353453696 | bytes 43015752 | solution.py:236
  462.4 1.8 subtract_exponential_fusion.3
  464.2 2.5 convolution_bitcast_fusion.2
  466.6 2.8 fusion.193
  469.4 4.5 fusion.194
  476.6 3.7 fusion.195
  488.5 2.5 convolution_bitcast_fusion.2
  490.9 2.8 fusion.193
  493.7 4.5 fusion.194
  500.9 3.6 fusion.195
  510.9 1.8 subtract_exponential_fusion.3
  512.7 2.5 convolution_bitcast_fusion.2
  515.2 2.8 fusion.193
  518.0 4.5 fusion.194
  525.1 3.6 fusion.195
  536.9 2.5 convolution_bitcast_fusion.2
  539.4 2.8 fusion.193
  542.2 4.5 fusion.194
  549.3 3.6 fusion.195
  554.7 1.8 copy.71
  557.9 2.0 fusion.86
  566.5 51.9 %reduce-scatter.52.cloned.1.call-done = bf16[128,512]{1,0:T(8,128)(2,1)} async-done(((bf16[1024,512]{1,0:T(8,128)(2,1)}), bf16[128,512]{1,0:T(8,128)(2,1)}) %reduce-scatter.52.cloned.1.call-update) | async-done | bytes 131088
  621.7 2.2 convolution_convert_fusion.5
  624.1 2.0 convolution_convert_fusion.4
  626.2 4.2 convolution_convert_fusion.3
  631.5 4.2 convolution_convert_fusion.2
  636.8 4.8 convolution_convert_fusion.1
  643.3 24.0 %reduce-scatter.58.cloned.1.call-done = bf16[128,512]{1,0:T(8,128)(2,1)} async-done(((bf16[512,512]{1,0:T(8,128)(2,1)}), bf16[128,512]{1,0:T(8,128)(2,1)}) %reduce-scatter.58.cloned.1.call-update) | async-done | bytes 131088
  667.4 27.5 %reduce-scatter.32.cloned.1.call-done = bf16[256,512]{1,0:T(8,128)(2,1)} async-done(((bf16[1024,512]{1,0:T(8,128)(2,1)}), bf16[256,512]{1,0:T(8,128)(2,1)}) %reduce-scatter.32.cloned.1.call-update) | async-done | bytes 262160 | tf_op jit(solution)/shard_map/reduce_scatter | solution.py:273
  695.0 33.7 %reduce-scatter.28.cloned.1.call-done = bf16[256,1024]{1,0:T(8,128)(2,1)} async-done(((bf16[1024,1024]{1,0:T(8,128)(2,1)}), bf16[256,1024]{1,0:T(8,128)(2,1)}) %reduce-scatter.28.cloned.1.call-update) | async-done | bytes 524304 | tf_op jit(solution)/shard_map/reduce_scatter | solution.py:270
  728.8 34.1 %reduce-scatter.36.cloned.1.call-done = bf16[256,1024]{1,0:T(8,128)(2,1)} async-done(((bf16[1024,1024]{1,0:T(8,128)(2,1)}), bf16[256,1024]{1,0:T(8,128)(2,1)}) %reduce-scatter.36.cloned.1.call-update) | async-done | bytes 524304 | tf_op jit(solution)/shard_map/reduce_scatter | solution.py:282
  763.0 57.2 %reduce-scatter.40.cloned.1.call-done = bf16[256,2816]{1,0:T(8,128)(2,1)} async-done(((bf16[1024,2816]{1,0:T(8,128)(2,1)}), bf16[256,2816]{1,0:T(8,128)(2,1)}) %reduce-scatter.40.cloned.1.call-update) | async-done | bytes 1441808 | tf_op jit(solution)/shard_map/reduce_scatter | solution.py:285
  820.2 57.4 %reduce-scatter.44.cloned.1.call-done = bf16[256,2816]{1,0:T(8,128)(2,1)} async-done(((bf16[1024,2816]{1,0:T(8,128)(2,1)}), bf16[256,2816]{1,0:T(8,128)(2,1)}) %reduce-scatter.44.cloned.1.call-update) | async-done | bytes 1441808 | tf_op jit(solution)/shard_map/reduce_scatter | solution.py:288
  877.7 57.2 %reduce-scatter.48.cloned.1.call-done = bf16[704,1024]{1,0:T(8,128)(2,1)} async-done(((bf16[2816,1024]{1,0:T(8,128)(2,1)}), bf16[704,1024]{1,0:T(8,128)(2,1)}) %reduce-scatter.48.cloned.1.call-update) | async-done | bytes 1441808 | tf_op jit(solution)/shard_map/reduce_scatter | solution.py:291
  937.6 2.6 fusion.127
  940.2 4.4 fusion.89
  944.6 52.8 %reduce-scatter.56.cloned.1.call-done = bf16[16,512]{1,0:T(8,128)(2,1)} async-done(((bf16[128,512]{1,0:T(8,128)(2,1)}), bf16[16,512]{1,0:T(8,128)(2,1)}) %reduce-scatter.56.cloned.1.call-update) | async-done | bytes 16400
  999.0 61.9 %reduce-scatter.60.cloned.1.call-done = bf16[16,512]{1,0:T(8,128)(2,1)} async-done(((bf16[128,512]{1,0:T(8,128)(2,1)}), bf16[16,512]{1,0:T(8,128)(2,1)}) %reduce-scatter.60.cloned.1.call-update) | async-done | bytes 16400
  1063.0 7.6 all-reduce.9
  1070.8 15.8 %all-reduce.8 = (bf16[256]{0:T(256)(128)(2,1)S(1)}, bf16[256]{0:T(256)(128)(2,1)S(1)}) all-reduce(bf16[256]{0:T(256)(128)(2,1)S(1)} %dynamic-slice.10, bf16[256]{0:T(256)(128)(2,1)S(1)} %dynamic-slice.14), channel_id=5, replica_groups=mesh['dp'=4,'ctx'=8] {'ctx'}, use_global_device_ids=true, to_apply=%region_15.16.clone | all-reduce | flops 512 | bytes 2048
  1088.1 36.8 %reduce-scatter.34.cloned.1.call-done = bf16[32,512]{1,0:T(8,128)(2,1)} async-done(((bf16[256,512]{1,0:T(8,128)(2,1)}), bf16[32,512]{1,0:T(8,128)(2,1)}) %reduce-scatter.34.cloned.1.call-update) | async-done | bytes 32784 | tf_op jit(solution)/shard_map/reduce_scatter | solution.py:305
  1126.2 63.2 %reduce-scatter.30.cloned.1.call-done = bf16[32,1024]{1,0:T(8,128)(2,1)} async-done(((bf16[256,1024]{1,0:T(8,128)(2,1)}), bf16[32,1024]{1,0:T(8,128)(2,1)}) %reduce-scatter.30.cloned.1.call-update) | async-done | bytes 65552 | tf_op jit(solution)/shard_map/reduce_scatter | solution.py:302
  1190.9 62.8 %reduce-scatter.38.cloned.1.call-done = bf16[32,1024]{1,0:T(8,128)(2,1)} async-done(((bf16[256,1024]{1,0:T(8,128)(2,1)}), bf16[32,1024]{1,0:T(8,128)(2,1)}) %reduce-scatter.38.cloned.1.call-update) | async-done | bytes 65552 | tf_op jit(solution)/shard_map/reduce_scatter | solution.py:314
  1255.2 66.4 %reduce-scatter.42.cloned.1.call-done = bf16[32,2816]{1,0:T(8,128)(2,1)} async-done(((bf16[256,2816]{1,0:T(8,128)(2,1)}), bf16[32,2816]{1,0:T(8,128)(2,1)}) %reduce-scatter.42.cloned.1.call-update) | async-done | bytes 180240 | tf_op jit(solution)/shard_map/reduce_scatter | solution.py:317
  1323.4 66.4 %reduce-scatter.46.cloned.1.call-done = bf16[32,2816]{1,0:T(8,128)(2,1)} async-done(((bf16[256,2816]{1,0:T(8,128)(2,1)}), bf16[32,2816]{1,0:T(8,128)(2,1)}) %reduce-scatter.46.cloned.1.call-update) | async-done | bytes 180240 | tf_op jit(solution)/shard_map/reduce_scatter | solution.py:320
  1391.5 65.8 %reduce-scatter.50.cloned.1.call-done = bf16[88,1024]{1,0:T(8,128)(2,1)} async-done(((bf16[704,1024]{1,0:T(8,128)(2,1)}), bf16[88,1024]{1,0:T(8,128)(2,1)}) %reduce-scatter.50.cloned.1.call-update) | async-done | bytes 180240 | tf_op jit(solution)/shard_map/reduce_scatter | solution.py:323
  (276 shorter events, 94.3 us)
Async XLA Ops:
  7.2 66.6 %copy-start.37 = (u32[32]{0:T(128)S(1)}, u32[32]{0:T(128)}, u32[]{:S(2)}) copy-start(u32[32]{0:T(128)} %constant.233) | copy-start | bytes 388
  7.2 84.5 %copy-start.35 = (bf16[16,512]{1,0:T(8,128)(2,1)S(1)}, bf16[16,512]{1,0:T(8,128)(2,1)}, u32[]{:S(2)}) copy-start(bf16[16,512]{1,0:T(8,128)(2,1)} %param.29) | copy-start | bytes 49156
  7.2 60.3 %all-gather.11.cloned.1.call-start = ((), (), s32[]{:S(2)}) async-start(), calls=%async_computation.18 | async-start | bytes 1081344 | tf_op jit(solution)/shard_map/all_gather | solution.py:66
  7.9 219.4 %all-gather.21.cloned.1.call-start = ((), (), s32[]{:S(2)}) async-start(), calls=%async_computation.35 | async-start | bytes 1179648 | tf_op jit(solution)/shard_map/all_gather | solution.py:102
  69.8 161.2 %all-gather.9.cloned.1.call-start = ((), (), s32[]{:S(2)}) async-start(), calls=%async_computation.17 | async-start | bytes 2162688 | tf_op jit(solution)/shard_map/all_gather | solution.py:65
  70.6 195.8 %all-gather.13.cloned.1.call-start = ((), (), s32[]{:S(2)}) async-start(), calls=%async_computation.19 | async-start | bytes 2162688 | tf_op jit(solution)/shard_map/all_gather | solution.py:69
  71.1 85.0 %copy-start.36 = (bf16[16,512]{1,0:T(8,128)(2,1)S(1)}, bf16[16,512]{1,0:T(8,128)(2,1)}, u32[]{:S(2)}) copy-start(bf16[16,512]{1,0:T(8,128)(2,1)} %param.28) | copy-start | bytes 49156
  71.2 225.4 %all-gather.15.cloned.1.call-start = ((), (), s32[]{:S(2)}) async-start(), calls=%async_computation.20 | async-start | bytes 5947392 | tf_op jit(solution)/shard_map/all_gather | solution.py:70
  71.7 293.9 %all-gather.17.cloned.1.call-start = ((), (), s32[]{:S(2)}) async-start(), calls=%async_computation.21 | async-start | bytes 5947392 | tf_op jit(solution)/shard_map/all_gather | solution.py:71
  72.3 362.4 %all-gather.19.cloned.1.call-start = ((), (), s32[]{:S(2)}) async-start(), calls=%async_computation.22 | async-start | bytes 5947392 | tf_op jit(solution)/shard_map/all_gather | solution.py:72
  73.1 545.3 %reduce-scatter.52.cloned.1.call-start = ((), (), s32[]{:S(2)}) async-start(), calls=%async_computation.36 | async-start | bytes 1179648
  156.2 109.6 %copy-start.19 = (bf16[2,256,8,64]{1,3,2,0:T(8,128)(2,1)}, bf16[2,256,8,64]{1,3,2,0:T(8,128)(2,1)S(1)}, u32[]{:S(2)}) copy-start(bf16[2,256,8,64]{1,3,2,0:T(8,128)(2,1)S(1)} %copy.59) | copy-start | bytes 1572868
  156.2 70.6 %copy-start.38 = (f32[8]{0:T(128)S(1)}, f32[8]{0:T(128)}, u32[]{:S(2)}) copy-start(f32[8]{0:T(128)} %param.22) | copy-start | bytes 100
  226.1 7.3 copy-start.17
  227.4 3.7 copy-start.1
  233.3 1.6 copy-start.26
  265.8 3.1 copy-start.9
  266.3 35.0 %copy-start.29 = (bf16[2,8,128,64]{2,3,1,0:T(8,128)(2,1)}, bf16[2,8,128,64]{2,3,1,0:T(8,128)(2,1)S(1)}, u32[]{:S(2)}) copy-start(bf16[2,8,128,64]{2,3,1,0:T(8,128)(2,1)S(1)} %convolution_convert_fusion.13) | copy-start | bytes 786436
  268.9 180.0 %copy-start.4 = (f32[128,1024]{1,0:T(8,128)}, f32[128,1024]{1,0:T(8,128)S(1)}, u32[]{:S(2)}) copy-start(f32[128,1024]{1,0:T(8,128)S(1)} %get-tuple-element.428) | copy-start | bytes 1572868
  269.1 96.5 %copy-start.2 = (bf16[128,1024]{1,0:T(8,128)(2,1)}, bf16[128,1024]{1,0:T(8,128)(2,1)S(1)}, u32[]{:S(2)}) copy-start(bf16[128,1024]{1,0:T(8,128)(2,1)S(1)} %multiply_convert_fusion.4) | copy-start | bytes 786436
  365.6 69.2 %copy-start.32 = (f32[128,2816]{1,0:T(8,128)S(1)}, f32[128,2816]{1,0:T(8,128)}, u32[]{:S(2)}) copy-start(f32[128,2816]{1,0:T(8,128)} %fusion.124) | copy-start | bytes 4325380
  441.6 5.2 copy-start.24
  441.6 5.2 copy-start.22
  441.6 5.2 copy-start
  446.8 2.1 copy-start.33
  446.8 3.8 copy-start.12
  450.6 1.0 copy-start.20
  451.7 4.3 copy-start.27
  464.1 2.5 copy-start.7
  488.5 2.5 copy-start.7
  512.7 2.5 copy-start.7
  536.9 2.5 copy-start.7
  556.5 1.4 copy-start.8
  557.8 85.4 %reduce-scatter.54.cloned.1.call-start = ((), (), s32[]{:S(2)}) async-start(), calls=%async_computation.37 | async-start | bytes 655360
  559.9 3.2 copy-start.10
  563.1 104.2 %reduce-scatter.58.cloned.1.call-start = ((), (), s32[]{:S(2)}) async-start(), calls=%async_computation.39 | async-start | bytes 655360
  566.4 54.8 %copy-start.18 = (bf16[2,256,8,64]{1,3,2,0:T(8,128)(2,1)S(1)}, bf16[2,256,8,64]{1,3,2,0:T(8,128)(2,1)}, u32[]{:S(2)}) copy-start(bf16[2,256,8,64]{1,3,2,0:T(8,128)(2,1)} %copy-done.17) | copy-start | bytes 1572868
  566.4 128.5 %reduce-scatter.32.cloned.1.call-start = ((), (), s32[]{:S(2)}) async-start(), calls=%async_computation.25 | async-start | bytes 1310720 | tf_op jit(solution)/shard_map/reduce_scatter | solution.py:273
  621.2 107.5 %reduce-scatter.28.cloned.1.call-start = ((), (), s32[]{:S(2)}) async-start(), calls=%async_computation.23 | async-start | bytes 2621440 | tf_op jit(solution)/shard_map/reduce_scatter | solution.py:270
  621.7 2.3 copy-start.28
  621.7 2.3 copy-start.14
  621.7 2.3 copy-start.30
  624.0 2.2 copy-start.3
  624.0 2.2 copy-start.25
  624.0 138.9 %reduce-scatter.36.cloned.1.call-start = ((), (), s32[]{:S(2)}) async-start(), calls=%async_computation.27 | async-start | bytes 2621440 | tf_op jit(solution)/shard_map/reduce_scatter | solution.py:282
  626.1 194.0 %reduce-scatter.40.cloned.1.call-start = ((), (), s32[]{:S(2)}) async-start(), calls=%async_computation.29 | async-start | bytes 7208960 | tf_op jit(solution)/shard_map/reduce_scatter | solution.py:285
  630.4 1.1 copy-start.23
  630.4 247.2 %reduce-scatter.44.cloned.1.call-start = ((), (), s32[]{:S(2)}) async-start(), calls=%async_computation.31 | async-start | bytes 7208960 | tf_op jit(solution)/shard_map/reduce_scatter | solution.py:288
  635.7 1.1 copy-start.15
  635.7 1.2 copy-start.34
  635.7 299.2 %reduce-scatter.48.cloned.1.call-start = ((), (), s32[]{:S(2)}) async-start(), calls=%async_computation.33 | async-start | bytes 7208960 | tf_op jit(solution)/shard_map/reduce_scatter | solution.py:291
  641.7 355.7 %reduce-scatter.56.cloned.1.call-start = ((), (), s32[]{:S(2)}) async-start(), calls=%async_computation.38 | async-start | bytes 147456
  643.3 417.6 %reduce-scatter.60.cloned.1.call-start = ((), (), s32[]{:S(2)}) async-start(), calls=%async_computation.40 | async-start | bytes 147456
  667.3 457.5 %reduce-scatter.34.cloned.1.call-start = ((), (), s32[]{:S(2)}) async-start(), calls=%async_computation.26 | async-start | bytes 294912 | tf_op jit(solution)/shard_map/reduce_scatter | solution.py:305
  694.9 494.5 %reduce-scatter.30.cloned.1.call-start = ((), (), s32[]{:S(2)}) async-start(), calls=%async_computation.24 | async-start | bytes 589824 | tf_op jit(solution)/shard_map/reduce_scatter | solution.py:302
  728.7 525.0 %reduce-scatter.38.cloned.1.call-start = ((), (), s32[]{:S(2)}) async-start(), calls=%async_computation.28 | async-start | bytes 589824 | tf_op jit(solution)/shard_map/reduce_scatter | solution.py:314
  762.9 558.8 %reduce-scatter.42.cloned.1.call-start = ((), (), s32[]{:S(2)}) async-start(), calls=%async_computation.30 | async-start | bytes 1622016 | tf_op jit(solution)/shard_map/reduce_scatter | solution.py:317
  820.2 117.4 %copy-start.11 = (bf16[1024,1024]{1,0:T(8,128)(2,1)S(1)}, bf16[1024,1024]{1,0:T(8,128)(2,1)}, u32[]{:S(2)}) copy-start(bf16[1024,1024]{1,0:T(8,128)(2,1)} %all-gather.9.cloned.1.call-done) | copy-start | bytes 6291460
  820.2 569.6 %reduce-scatter.46.cloned.1.call-start = ((), (), s32[]{:S(2)}) async-start(), calls=%async_computation.32 | async-start | bytes 1622016 | tf_op jit(solution)/shard_map/reduce_scatter | solution.py:320
  877.7 579.7 %reduce-scatter.50.cloned.1.call-start = ((), (), s32[]{:S(2)}) async-start(), calls=%async_computation.34 | async-start | bytes 1622016 | tf_op jit(solution)/shard_map/reduce_scatter | solution.py:323
  934.9 5.3 copy-start.5
  937.6 2.7 copy-start.16
  940.2 122.2 %copy-start.21 = (bf16[1024,512]{1,0:T(8,128)(2,1)S(1)}, bf16[1024,512]{1,0:T(8,128)(2,1)}, u32[]{:S(2)}) copy-start(bf16[1024,512]{1,0:T(8,128)(2,1)} %all-gather.11.cloned.1.call-done) | copy-start | bytes 3145732
  940.2 122.2 %copy-start.31 = (f32[128,1024]{1,0:T(8,128)S(1)}, f32[128,1024]{1,0:T(8,128)}, u32[]{:S(2)}) copy-start(f32[128,1024]{1,0:T(8,128)} %fusion.127) | copy-start | bytes 1572868
  (2 other events, 1.8 us)
Sparse Core Ops, SparseCore 0:
  11.1 56.3 all-gather.10
  70.2 38.3 all-gather.20
  111.5 56.8 all-gather.8
  171.3 56.0 all-gather.12
  230.2 66.3 all-gather.14
  299.3 66.2 all-gather.16
  368.5 66.2 all-gather.18
  557.9 60.4 reduce-scatter.51
  621.0 22.1 reduce-scatter.53
  645.6 21.6 reduce-scatter.57
  670.0 24.8 reduce-scatter.31
  697.3 31.3 reduce-scatter.27
  731.4 31.4 reduce-scatter.35
  765.3 54.8 reduce-scatter.39
  822.7 54.8 reduce-scatter.43
  880.0 54.8 reduce-scatter.47
  938.4 58.9 reduce-scatter.55
  1000.9 59.9 reduce-scatter.59
  1064.6 60.2 reduce-scatter.33
  1128.4 60.9 reduce-scatter.29
  1192.8 60.9 reduce-scatter.37
  1257.5 64.1 reduce-scatter.41
  1325.5 64.2 reduce-scatter.45
  1393.5 63.8 reduce-scatter.49
where the time goes:
time: 1470 us
  waiting for transfers between devices  997 us (68%)
  blocking collectives  213 us (14%)
  matrix products  135 us (9%)
  local copies, waits for them, and re-layouts  51.3 us (3%)
  loops' own time  31.8 us (2%)
  other arithmetic  19.5 us (1%)
  between operations  17.6 us (1%)
    unnamed x29, waiting for transfers between devices  196 us
    unnamed x4, blocking collectives  80.9 us
    all_gather x1, blocking collectives, per_device(): lax.all_gather(w_upkey, ('dp', 'ctx'), axis=0, tiled=True)  68.7 us
    reduce_scatter x1, waiting for transfers between devices, per_device(): lax.psum_scatter(partial_sums[8].astype(jnp.bfloat16), 'ctx', scatter_dim...  66.4 us
    reduce_scatter x1, waiting for transfers between devices, per_device(): lax.psum_scatter(partial_sums[7].astype(jnp.bfloat16), 'ctx', scatter_dim...  66.4 us
    reduce_scatter x1, waiting for transfers between devices, per_device(): lax.psum_scatter(partial_sums[9].astype(jnp.bfloat16), 'ctx', scatter_dim...  65.8 us
    all_gather x1, waiting for transfers between devices, per_device(): lax.all_gather(w_down, ('dp', 'ctx'), axis=0, tiled=True)  64.4 us
    all_gather x1, waiting for transfers between devices, per_device(): lax.all_gather(w_up, ('dp', 'ctx'), axis=0, tiled=True)  64.3 us
  transfers between devices with their start and end apart: 24, of which 21 were waited for; matrix products, arithmetic and copies ran while one was open for 6% of the time, Pallas kernels for 0%

commit v1 on v0

v1 whole, which is shorter than its diff:
```python
import functools
import itertools

import jax
import jax.numpy as jnp
from jax import lax
from jax.experimental import pallas as pl
from jax.experimental.pallas import tpu as pltpu
from jax.sharding import PartitionSpec as P

HEADS = 16
HEAD = 64
LATENT = 256
DOMAINS = 8
EPS = 1e-06
SCALE = 0.125
MASKED = -1e30
AXES = ("dp", "ctx")
BF16 = jnp.bfloat16
F32 = jnp.float32
INFO = 8
VMEM_BYTES = 56 * 1024 * 1024


def product(left, right):
    return jnp.dot(left, right, preferred_element_type=F32)


def contract_rows(left, right):
    return lax.dot_general(left, right, (((0,), (0,)), ((), ())), preferred_element_type=F32)


def times_transposed(left, right):
    return lax.dot_general(left, right, (((1,), (1,)), ((), ())), preferred_element_type=F32)


def inverse_rms(rows):
    return lax.rsqrt(jnp.mean(rows * rows, -1, keepdims=True) + EPS)


def norm_back(rows, gain, grad):
    r = inverse_rms(rows)
    grad_gain = jnp.sum(grad * rows * r, 0)
    scaled = grad * gain
    mean = jnp.mean(scaled * rows, -1, keepdims=True)
    return r * scaled - rows * (r * r * r * mean), grad_gain


def groups_of(spots):
    groups = {}
    for n, (i, j, r, k) in enumerate(spots):
        groups.setdefault((i, r, k), []).append((j, n))
    return [(key, [n for _, n in sorted(found)]) for key, found in groups.items()]


def block_numbers(own):
    return jnp.arange(own.shape[0], dtype=own.dtype)


def permute_blocks(chosen, stack):
    out = product(chosen.astype(BF16), stack.reshape(stack.shape[0], -1)).astype(BF16)
    return out.reshape(-1, *stack.shape[1:])


def place_blocks(pieces, blocks, order, shapes):
    flat = [(o, *spot) for o, spots in enumerate(blocks) for spot in spots]
    if any(rows % 8 for rows, _ in shapes):
        made, at = [], 0
        for (rows, columns), spots in zip(shapes, blocks):
            groups = groups_of(spots)
            stack = jnp.concatenate([pieces[i][:, r : r + rows, k : k + columns] for (i, r, k), _ in groups])
            own = order[jnp.asarray([at + n for _, ns in groups for n in ns])]
            made.append(permute_blocks(own[None, :] == block_numbers(own)[:, None], stack).reshape(-1, columns))
            at += len(spots)
        return made

    def kernel(order_ref, *refs):
        sources, targets = refs[: len(pieces)], refs[len(pieces) :]
        for n, (o, i, j, r, k) in enumerate(flat):
            rows, columns = shapes[o]
            targets[o][order_ref[n]] = sources[i][j, r : r + rows, k : k + columns]

    made = pl.pallas_call(
        kernel,
        out_shape=[
            jax.ShapeDtypeStruct((len(spots), rows, columns), BF16)
            for (rows, columns), spots in zip(shapes, blocks)
        ],
        in_specs=[pl.BlockSpec(memory_space=pltpu.SMEM)]
        + [pl.BlockSpec(memory_space=pltpu.VMEM)] * len(pieces),
        out_specs=[pl.BlockSpec(memory_space=pltpu.VMEM)] * len(shapes),
        compiler_params=pltpu.CompilerParams(vmem_limit_bytes=VMEM_BYTES),
        name="place_blocks",
    )(order, *pieces)
    return [whole.reshape(-1, whole.shape[-1]) for whole in made]


def cut_blocks(matrices, blocks, order, shapes, piece_shapes):
    flat = [(o, *spot) for o, spots in enumerate(blocks) for spot in spots]
    if any(rows % 8 for rows, _ in shapes):
        bands, at = [{} for _ in piece_shapes], 0
        for (rows, columns), spots, matrix in zip(shapes, blocks, matrices):
            grid = matrix.reshape(len(spots), rows, columns)
            for (i, r, k), ns in groups_of(spots):
                own = order[jnp.asarray([at + n for n in ns])]
                chosen = own[:, None] == jnp.arange(len(spots), dtype=own.dtype)[None, :]
                bands[i].setdefault(r, {})[k] = permute_blocks(chosen, grid)
            at += len(spots)
        return [
            jnp.concatenate(
                [jnp.concatenate([row[k] for k in sorted(row)], 2) for _, row in sorted(band.items())], 1
            )
            for band in bands
        ]

    def kernel(order_ref, *refs):
        sources, targets = refs[: len(matrices)], refs[len(matrices) :]
        for n, (o, i, j, r, k) in enumerate(flat):
            rows, columns = shapes[o]
            targets[i][j, r : r + rows, k : k + columns] = sources[o][order_ref[n]]

    grids = [matrix.reshape(-1, rows, columns) for matrix, (rows, columns) in zip(matrices, shapes)]
    return pl.pallas_call(
        kernel,
        out_shape=[jax.ShapeDtypeStruct(shape, BF16) for shape in piece_shapes],
        in_specs=[pl.BlockSpec(memory_space=pltpu.SMEM)]
        + [pl.BlockSpec(memory_space=pltpu.VMEM)] * len(matrices),
        out_specs=[pl.BlockSpec(memory_space=pltpu.VMEM)] * len(piece_shapes),
        compiler_params=pltpu.CompilerParams(vmem_limit_bytes=VMEM_BYTES),
        name="cut_blocks",
    )(order, *grids)


def pair_scores(query_latent, keys, query_pos, key_pos):
    scores = times_transposed(query_latent, keys) * SCALE
    both = jnp.concatenate([query_pos, query_pos], 0)
    return jnp.where(both >= key_pos, scores, MASKED)


def attend_kernel(q_ref, uk_ref, uv_ref, keys_ref, qpos_ref, kpos_ref, ql_ref, mixed_ref, lse_ref, values_ref):
    q, uk, uv, keys = q_ref[0], uk_ref[...], uv_ref[...], keys_ref[0]
    rows = q.shape[0]
    ql = jnp.concatenate(
        [times_transposed(q[:, k : k + HEAD], uk[:, k : k + HEAD]) for k in (0, HEAD)], 0
    ).astype(BF16)
    scores = pair_scores(ql, keys, qpos_ref[0], kpos_ref[0])
    top = jnp.max(scores, -1, keepdims=True)
    terms = jnp.exp(scores - top)
    total = jnp.sum(terms, -1, keepdims=True)
    probs = (terms * (1.0 / total)).astype(BF16)
    mixed = product(probs, keys).astype(BF16)
    ql_ref[0, 0] = ql
    mixed_ref[0, 0] = mixed
    lse_ref[0, 0] = top + jnp.log(total)
    values_ref[0] = jnp.concatenate(
        [product(mixed[:rows], uv[:, :HEAD]), product(mixed[rows:], uv[:, HEAD:])], 1
    ).astype(BF16)


def attend_back_kernel(
    q_ref, ql_ref, mixed_ref, lse_ref, dval_ref, uk_ref, uv_ref, keys_ref, qpos_ref, kpos_ref,
    dq_ref, guk_ref, guv_ref, *rest,
):
    dkeys_refs, (keys_acc, uk_acc, uv_acc) = rest[:-3], rest[-3:]
    seq, pair = pl.program_id(0), pl.program_id(1)
    q, ql, mixed, dval = q_ref[0], ql_ref[0, 0], mixed_ref[0, 0], dval_ref[0]
    uk, uv, keys = uk_ref[...], uv_ref[...], keys_ref[0]
    rows = q.shape[0]
    halves = (0, HEAD)
    scores = pair_scores(ql, keys, qpos_ref[0], kpos_ref[0])
    probs = jnp.exp(scores - lse_ref[0, 0])
    dmixed = jnp.concatenate(
        [times_transposed(dval[:, k : k + HEAD], uv[:, k : k + HEAD]) for k in halves], 0
    ).astype(BF16)
    dprobs = times_transposed(dmixed, keys)
    dscores = probs * (dprobs - jnp.sum(probs * dprobs, -1, keepdims=True))
    dscores = dscores.astype(BF16) * jnp.asarray(SCALE, BF16)
    dql = product(dscores, keys).astype(BF16)
    dkeys = contract_rows(dscores, ql) + contract_rows(probs.astype(BF16), dmixed)

    @pl.when(pair == 0)
    def _():
        keys_acc[...] = dkeys

    @pl.when(pair > 0)
    def _():
        keys_acc[...] += dkeys

    guk = jnp.concatenate(
        [contract_rows(dql[n * rows : (n + 1) * rows], q[:, k : k + HEAD]) for n, k in enumerate(halves)], 1
    )
    guv = jnp.concatenate(
        [contract_rows(mixed[n * rows : (n + 1) * rows], dval[:, k : k + HEAD]) for n, k in enumerate(halves)], 1
    )

    @pl.when(seq == 0)
    def _():
        uk_acc[pair] = guk
        uv_acc[pair] = guv

    @pl.when(seq > 0)
    def _():
        uk_acc[pair] += guk
        uv_acc[pair] += guv

    dq_ref[0] = jnp.concatenate(
        [product(dql[n * rows : (n + 1) * rows], uk[:, k : k + HEAD]) for n, k in enumerate(halves)], 1
    ).astype(BF16)
    last = pl.num_programs(1) - 1

    @pl.when(pair == last)
    def _():
        count = dkeys_refs[0].shape[0]
        for n, ref in enumerate(dkeys_refs):
            part = keys_acc[n * count * rows : (n + 1) * count * rows, :]
            ref[:, 0] = part.reshape(count, rows, LATENT).astype(BF16)

    @pl.when((pair == last) & (seq == pl.num_programs(0) - 1))
    def _():
        for n in range(uk_acc.shape[0]):
            guk_ref[:, 2 * n * HEAD : 2 * (n + 1) * HEAD] = uk_acc[n].astype(BF16)
            guv_ref[:, 2 * n * HEAD : 2 * (n + 1) * HEAD] = uv_acc[n].astype(BF16)


def attention_specs(length, rows):
    pair = pl.BlockSpec((1, rows, 2 * HEAD), lambda s, p: (s, 0, p))
    up = pl.BlockSpec((LATENT, 2 * HEAD), lambda s, p: (0, p))
    keys = pl.BlockSpec((1, length, LATENT), lambda s, p: (s, 0, 0))
    query_pos = pl.BlockSpec((1, rows, 1), lambda s, p: (s, 0, 0))
    key_pos = pl.BlockSpec((1, 1, length), lambda s, p: (s, 0, 0))
    wide = pl.BlockSpec((1, 1, 2 * rows, LATENT), lambda s, p: (s, p, 0, 0))
    thin = pl.BlockSpec((1, 1, 2 * rows, 1), lambda s, p: (s, p, 0, 0))
    return pair, up, keys, query_pos, key_pos, wide, thin


def attend(q, uk, uv, keys, query_pos, key_pos):
    seqs, length, _ = keys.shape
    rows, pairs = q.shape[1], q.shape[2] // (2 * HEAD)
    pair, up, key, qpos, kpos, wide, thin = attention_specs(length, rows)
    flops = seqs * pairs * 2 * rows * length * LATENT * 4
    return pl.pallas_call(
        attend_kernel,
        grid=(seqs, pairs),
        in_specs=[pair, up, up, key, qpos, kpos],
        out_specs=[wide, wide, thin, pair],
        out_shape=[
            jax.ShapeDtypeStruct((seqs, pairs, 2 * rows, LATENT), BF16),
            jax.ShapeDtypeStruct((seqs, pairs, 2 * rows, LATENT), BF16),
            jax.ShapeDtypeStruct((seqs, pairs, 2 * rows, 1), F32),
            jax.ShapeDtypeStruct(q.shape, BF16),
        ],
        compiler_params=pltpu.CompilerParams(vmem_limit_bytes=VMEM_BYTES),
        cost_estimate=pl.CostEstimate(flops=flops, bytes_accessed=6 << 20, transcendentals=seqs * pairs * 2 * rows * length),
        name="attend",
    )(q, uk, uv, keys, query_pos, key_pos)


def attend_back(q, ql, mixed, lse, dval, uk, uv, keys, query_pos, key_pos, parts):
    seqs, length, _ = keys.shape
    rows, pairs = q.shape[1], q.shape[2] // (2 * HEAD)
    pair, up, key, qpos, kpos, wide, thin = attention_specs(length, rows)
    whole = pl.BlockSpec(uk.shape, lambda s, p: (0, 0))
    count = length // rows // parts
    flops = seqs * pairs * 2 * rows * length * LATENT * 10
    return pl.pallas_call(
        attend_back_kernel,
        grid=(seqs, pairs),
        in_specs=[pair, wide, wide, thin, pair, up, up, key, qpos, kpos],
        out_specs=[pair, whole, whole]
        + [pl.BlockSpec((count, 1, rows, LATENT), lambda s, p: (0, s, 0, 0))] * parts,
        out_shape=[jax.ShapeDtypeStruct(q.shape, BF16)]
        + [jax.ShapeDtypeStruct(uk.shape, BF16)] * 2
        + [jax.ShapeDtypeStruct((count, seqs, rows, LATENT), BF16)] * parts,
        scratch_shapes=[
            pltpu.VMEM((length, LATENT), F32),
            pltpu.VMEM((pairs, LATENT, 2 * HEAD), F32),
            pltpu.VMEM((pairs, LATENT, 2 * HEAD), F32),
        ],
        compiler_params=pltpu.CompilerParams(vmem_limit_bytes=VMEM_BYTES),
        cost_estimate=pl.CostEstimate(flops=flops, bytes_accessed=8 << 20, transcendentals=seqs * pairs * 2 * rows * length),
        name="attend_back",
    )(q, ql, mixed, lse, dval, uk, uv, keys, query_pos, key_pos)


class Plan:
    def __init__(self, mesh):
        self.dp, self.ctx = mesh.shape["dp"], mesh.shape["ctx"]
        self.count = self.dp * self.ctx
        self.core = self.ctx
        self.cross = 2 * self.ctx
        top = self.count // 2
        bits = [1 << n for n in range(self.count.bit_length() - 1)]
        ctx_bits = [b for b in bits if b < self.ctx]
        self.half_bits = [b for b in bits if b != self.core]
        self.split_bits = [self.core, self.cross]
        self.quarter_bits = [b for b in bits if b not in self.split_bits]
        self.ctx_bits = ctx_bits
        self.top = top

    def swap(self, value, mask):
        return lax.ppermute(value, AXES, [(n, n ^ mask) for n in range(self.count)])

    def swap_bits(self, number, first, second):
        if first == second:
            return number
        one, two = (number // first) % 2, (number // second) % 2
        return number + (two - one) * first + (one - two) * second

    def deal(self, value, pairs):
        table = []
        for n in range(self.count):
            m = n
            for first, second in pairs:
                m = self.swap_bits(m, first, second)
            table.append((n, m))
        if all(a == b for a, b in table):
            return value
        return lax.ppermute(value, AXES, table)


def masks_of(bits):
    out = [0]
    for bit in bits:
        out = out + [m ^ bit for m in out]
    return out


def gather(plan, value, far, second, first, groups):
    done = [([m], value[None] if m == 0 else plan.swap(value, m)[None]) for m in masks_of(far)]
    for bit in (second, first):
        size = -(-len(done) // groups)
        sent = []
        for at in range(0, len(done), size):
            some = done[at : at + size]
            masks = [m for ms, _ in some for m in ms]
            stack = some[0][1] if len(some) == 1 else jnp.concatenate([a for _, a in some])
            sent.append(([m ^ bit for m in masks], plan.swap(stack, bit)))
        done = done + sent
    return done


def reduce_order(far, second, first):
    base = masks_of(far)
    return [[m ^ one ^ two for m in base] for one in (0, first) for two in (0, second)]


def reduce(plan, stacks, far, second, first):
    keep0, keep1, send0, send1 = stacks
    got1 = plan.swap(send1, first)
    got0 = plan.swap(send0, first)
    part1 = (keep1.astype(F32) + got1.astype(F32)).astype(BF16)
    got = plan.swap(part1, second)
    part = (keep0.astype(F32) + got0.astype(F32) + got.astype(F32)).astype(BF16)
    total = part[0].astype(F32)
    for n, mask in enumerate(masks_of(far)):
        if n:
            total = total + plan.swap(part[n], mask).astype(F32)
    return total


def per_device(plan, tokens, cotangent, domain_ids, domain_weights, stretch_offsets, gain_attn, gain_ffn,
               w_query, w_latent, w_upkey, w_upvalue, w_out, w_gate, w_up, w_down):
    _, rows, width = tokens.shape
    me = lax.axis_index("dp") * plan.ctx + lax.axis_index("ctx")
    core = (me // plan.core) % 2
    core_bit, cross_bit = plan.core, plan.cross
    count = plan.count
    shard = w_query.shape[0]
    up_shard = w_upkey.shape[0]
    down_shard = w_down.shape[0]
    half = w_query.shape[1] // 2
    latent_half = w_latent.shape[1] // 2
    quarter = w_gate.shape[1] // 4
    ctx_first, ctx_second, *ctx_far = plan.ctx_bits
    x_bit = plan.half_bits[-1]
    half_far = [b for b in plan.half_bits if b not in (x_bit, ctx_first)]
    quarter_far = [b for b in plan.quarter_bits if b not in (ctx_first, ctx_second)]

    def halves(value, size):
        low, high = value[:, :size], value[:, size:]
        return jnp.where(core == 0, low, high), jnp.where(core == 0, high, low)

    query_own, query_other = halves(w_query, half)
    latent_own, latent_other = halves(w_latent, latent_half)
    span = half + latent_half
    info = jnp.concatenate([gain_attn, gain_ffn, stretch_offsets[0].astype(BF16)])
    info = jnp.pad(info[None], ((0, INFO - 1), (0, span - info.shape[0])))
    mine = jnp.concatenate([jnp.concatenate([query_own, latent_own], 1), info])
    other = jnp.concatenate([jnp.concatenate([query_other, latent_other], 1), info])
    band = shard + INFO
    first_message = jnp.concatenate([mine, plan.swap(other, core_bit)])
    second_message = plan.deal(
        jnp.concatenate([jnp.concatenate([w_upkey, w_upvalue], 1).reshape(-1, width), w_out]),
        [(plan.top, core_bit)],
    )
    split_masks = masks_of(plan.split_bits)
    split = (me // core_bit) % 2 + 2 * ((me // cross_bit) % 2)
    columns = jnp.concatenate([w_gate, w_up]).reshape(2 * shard, 4, quarter).transpose(1, 0, 2)

    def quarter_of(mask_index):
        return lax.dynamic_index_in_dim(columns, split ^ mask_index, 0, keepdims=False)

    third_message = jnp.concatenate(
        [quarter_of(0)] + [plan.swap(quarter_of(n), m) for n, m in enumerate(split_masks) if n]
    )
    fourth_message = plan.deal(w_down, [(plan.top, cross_bit), (plan.top // 2, core_bit)])

    tokens_two = jnp.concatenate([tokens[0], plan.swap(tokens[0], core_bit)])
    x_two = tokens_two.astype(F32)

    half_stages = (half_far, ctx_first, x_bit)
    quarter_stages = (quarter_far, ctx_second, ctx_first)
    first_pieces = gather(plan, first_message, *half_stages, 4)
    second_pieces = gather(plan, second_message, *half_stages, 4)
    third_pieces = gather(plan, third_message, *quarter_stages, 4)
    fourth_pieces = gather(plan, fourth_message, *quarter_stages, 4)

    def spots(pieces):
        return [(i, j, m) for i, (masks, _) in enumerate(pieces) for j, m in enumerate(masks)]

    query_blocks, latent_blocks, order = [], [], []
    for i, j, m in spots(first_pieces):
        for b in (0, 1):
            query_blocks.append((i, j, b * band, 0))
            latent_blocks.append((i, j, b * band, half))
            order.append(me ^ (m ^ b * core_bit))
    query_full, latent_full = place_blocks(
        [a for _, a in first_pieces], [query_blocks, latent_blocks], jnp.stack(order + order),
        [(shard, half), (shard, latent_half)],
    )

    def owner_half(m):
        return plan.swap_bits(me ^ m, plan.top, core_bit) % (count // 2)

    up_rows = 2 * up_shard * w_upkey.shape[1] // width
    second_stacks = [a for _, a in second_pieces]
    out_blocks = [(i, j, up_rows, 0) for i, j, m in spots(second_pieces)]
    order_half = jnp.stack([owner_half(m) for _, _, m in spots(second_pieces)])
    pair_width = w_upkey.shape[1]
    upkey_blocks = [(i, j, 0, 0) for i, j, m in spots(second_pieces)]
    upvalue_blocks = [(i, j, 0, pair_width) for i, j, m in spots(second_pieces)]
    upkey_full, upvalue_full, out_full = place_blocks(
        second_stacks, [upkey_blocks, upvalue_blocks, out_blocks],
        jnp.concatenate([order_half] * 3),
        [(up_shard, pair_width), (up_shard, pair_width), (shard, width)],
    )

    gate_blocks, up_blocks, order = [], [], []
    for i, j, m in spots(third_pieces):
        for n, s in enumerate(split_masks):
            gate_blocks.append((i, j, n * 2 * shard, 0))
            up_blocks.append((i, j, n * 2 * shard + shard, 0))
            order.append(me ^ (m ^ s))
    order_columns = jnp.stack(order + order)
    gate_full, up_full = place_blocks(
        [a for _, a in third_pieces], [gate_blocks, up_blocks], order_columns, [(shard, quarter)] * 2
    )

    def owner_quarter(m):
        source = plan.swap_bits(me ^ m, plan.top // 2, core_bit)
        return plan.swap_bits(source, plan.top, cross_bit) % (count // 4)

    down_blocks = [(i, j, 0, 0) for i, j, m in spots(fourth_pieces)]
    order_down = jnp.stack([owner_quarter(m) for _, _, m in spots(fourth_pieces)])
    (down_full,) = place_blocks(
        [a for _, a in fourth_pieces], [down_blocks], order_down, [(down_shard, width)]
    )

    rows_info = jnp.concatenate(
        [a[:, shard :: band, : 2 * shard + 1] for _, a in first_pieces]
    )
    masks_info = [m for _, _, m in spots(first_pieces)]
    number = jnp.stack([jnp.stack([me ^ m, me ^ m ^ core_bit]) for m in masks_info]).reshape(-1)
    chosen = (number[:, None] == jnp.arange(count)[None, :]).astype(BF16)
    gains = contract_rows(chosen, rows_info[..., : 2 * shard].reshape(count, 2 * shard))
    gain_one = gains[:, :shard].reshape(width)
    gain_two = gains[:, shard:].reshape(width)
    ctx_masks = sum(reduce_order(ctx_far, ctx_second, ctx_first), [])
    offsets = jnp.stack(
        [rows_info[masks_info.index(m), :, 2 * shard] for m in ctx_masks], 1
    ).astype(jnp.int32)
    within = jnp.arange(rows, dtype=jnp.int32)
    key_pos = (offsets[:, :, None] * rows + within).reshape(2, 1, -1)
    query_pos = (offsets[:, :1] * rows + within)[:, :, None]

    normed_one = (x_two * inverse_rms(x_two) * gain_one).astype(BF16)
    latent = product(normed_one, latent_full).astype(BF16)
    latent_message = latent.reshape(2, rows, latent_half)
    key_pieces = gather(plan, latent_message, ctx_far, ctx_second, ctx_first, 4)
    key_of = {m: a[j] for masks, a in key_pieces for j, m in enumerate(masks)}
    keys = jnp.concatenate([key_of[m] for m in ctx_masks], 1)
    queries = product(normed_one, query_full).astype(BF16).reshape(2, rows, half)
    query_latent, mixed, lse, values = attend(queries, upkey_full, upvalue_full, keys, query_pos, key_pos)
    values = values.reshape(2 * rows, half)
    shares = product(values, out_full)
    x_own = x_two[:rows]
    middle = x_own + shares[:rows] + plan.swap(shares[rows:], core_bit)

    def spread(value):
        near = plan.swap(value, core_bit)
        across = plan.swap(value, cross_bit)
        return jnp.concatenate([value, near, across, plan.swap(across, core_bit)])

    def collect(shares):
        parts = shares.reshape(4, rows, width)
        got = plan.swap(jnp.stack([parts[1], parts[3]]), core_bit)
        across = plan.swap((parts[2] + got[1]).astype(BF16), cross_bit)
        return parts[0] + got[0] + across.astype(F32)

    match = domain_ids[:, None] == jnp.arange(DOMAINS, dtype=jnp.int32)[None, :]
    scale = jnp.sum(jnp.where(match, domain_weights[None, :], 0.0))
    dlayer = cotangent[0].astype(F32) * scale
    dy = spread(dlayer.astype(BF16))

    normed_two = spread((middle * inverse_rms(middle) * gain_two).astype(BF16))
    gate = product(normed_two, gate_full)
    up = product(normed_two, up_full)
    sigmoid = jax.nn.sigmoid(gate)
    silu = gate * sigmoid
    hidden = (silu * up).astype(BF16)
    dhidden = times_transposed(dy, down_full)
    dgate = (dhidden * up * (sigmoid * (1.0 + gate * (1.0 - sigmoid)))).astype(BF16)
    dup = (dhidden * silu).astype(BF16)
    dnormed_two = collect(times_transposed(dgate, gate_full) + times_transposed(dup, up_full))
    grad_gate = contract_rows(normed_two, dgate).astype(BF16)
    grad_up = contract_rows(normed_two, dup).astype(BF16)
    grad_down = contract_rows(hidden, dy).astype(BF16)
    output = (middle + collect(product(hidden, down_full))).astype(BF16)[None]

    quarter_order = reduce_order(*quarter_stages)
    blocks, order = [], []
    for i, masks in enumerate(quarter_order):
        for j, m in enumerate(masks):
            blocks.append((i, j, 0, 0))
            order.append(owner_quarter(m))
    down_stacks = cut_blocks(
        [grad_down], [blocks], jnp.stack(order), [(down_shard, width)],
        [(len(masks), down_shard, width) for masks in quarter_order],
    )
    down_sum = reduce(plan, down_stacks, *quarter_stages)
    grad_w_down = plan.deal(down_sum, [(plan.top // 2, core_bit), (plan.top, cross_bit)])

    gate_blocks, up_blocks, order = [], [], []
    for i, masks in enumerate(quarter_order):
        for j, m in enumerate(masks):
            for n, s in enumerate(split_masks):
                gate_blocks.append((i, j, n * 2 * shard, 0))
                up_blocks.append((i, j, n * 2 * shard + shard, 0))
                order.append(me ^ (m ^ s))
    column_stacks = cut_blocks(
        [grad_gate, grad_up], [gate_blocks, up_blocks], jnp.stack(order + order), [(shard, quarter)] * 2,
        [(len(masks), 8 * shard, quarter) for masks in quarter_order],
    )
    column_sum = reduce(plan, column_stacks, *quarter_stages).reshape(4, 2 * shard, quarter)
    got = [column_sum[0]] + [
        plan.swap(column_sum[n].astype(BF16), m).astype(F32) for n, m in enumerate(split_masks) if n
    ]
    got = jnp.stack(got)
    grad_columns = jnp.concatenate(
        [lax.dynamic_index_in_dim(got, split ^ n, 0, keepdims=False) for n in range(4)], 1
    )
    grad_w_gate, grad_w_up = grad_columns[:shard], grad_columns[shard:]

    dmiddle_norm, grad_gain_two = norm_back(middle, gain_two, dnormed_two)
    dmiddle = dlayer + dmiddle_norm
    dm = dmiddle.astype(BF16)
    dm_two = jnp.concatenate([dm, plan.swap(dm, core_bit)])
    grad_out = contract_rows(values, dm_two).astype(BF16)
    dvalues = times_transposed(dm_two, out_full).astype(BF16).reshape(2, rows, half)
    dqueries, grad_upkey, grad_upvalue, *dkeys = attend_back(
        queries, query_latent, mixed, lse, dvalues, upkey_full, upvalue_full, keys, query_pos, key_pos, 4
    )
    dlatent = reduce(plan, dkeys, ctx_far, ctx_second, ctx_first).astype(BF16).reshape(2 * rows, latent_half)
    dqueries = dqueries.reshape(2 * rows, half)
    shares = times_transposed(dqueries, query_full) + times_transposed(dlatent, latent_full)
    dnormed_one = shares[:rows] + plan.swap(shares[rows:], core_bit)
    dx_norm, grad_gain_one = norm_back(x_own, gain_one, dnormed_one)
    grad_tokens = (dmiddle + dx_norm).astype(BF16)[None]

    half_order = reduce_order(*half_stages)
    blocks, order = [], []
    for i, masks in enumerate(half_order):
        for j, m in enumerate(masks):
            blocks.append((i, j))
            order.append(owner_half(m))
    second_stacks = cut_blocks(
        [grad_upkey, grad_upvalue, grad_out],
        [[(i, j, 0, 0) for i, j in blocks], [(i, j, 0, pair_width) for i, j in blocks],
         [(i, j, up_rows, 0) for i, j in blocks]],
        jnp.stack(order * 3),
        [(up_shard, pair_width), (up_shard, pair_width), (shard, width)],
        [(len(masks), up_rows + shard, width) for masks in half_order],
    )
    second_sum = plan.deal(reduce(plan, second_stacks, *half_stages), [(plan.top, core_bit)])
    grad_ups = second_sum[:up_rows].reshape(up_shard, 2 * pair_width)
    grad_w_out = second_sum[up_rows:]

    grad_query = contract_rows(normed_one, dqueries).astype(BF16)
    grad_latent = contract_rows(normed_one, dlatent).astype(BF16)
    gain_rows = jnp.concatenate([grad_gain_one.reshape(count, shard), grad_gain_two.reshape(count, shard)], 1)
    gain_rows = jnp.pad(gain_rows.astype(BF16)[:, None], ((0, 0), (0, INFO - 1), (0, span - 2 * shard)))
    gain_rows = gain_rows.reshape(count * INFO, span)
    query_blocks, latent_blocks, info_blocks, order = [], [], [], []
    for i, masks in enumerate(half_order):
        for j, m in enumerate(masks):
            for b in (0, 1):
                query_blocks.append((i, j, b * band, 0))
                latent_blocks.append((i, j, b * band, half))
                info_blocks.append((i, j, b * band + shard, 0))
                order.append(me ^ (m ^ b * core_bit))
    first_stacks = cut_blocks(
        [grad_query, grad_latent, gain_rows], [query_blocks, latent_blocks, info_blocks],
        jnp.stack(order * 3),
        [(shard, half), (shard, latent_half), (INFO, span)],
        [(len(masks), 2 * band, span) for masks in half_order],
    )
    first_sum = reduce(plan, first_stacks, *half_stages)
    own, got = first_sum[:band], plan.swap(first_sum[band:].astype(BF16), core_bit).astype(F32)
    low, high = jnp.where(core == 0, own, got), jnp.where(core == 0, got, own)
    grad_w_query = jnp.concatenate([low[:shard, :half], high[:shard, :half]], 1)
    grad_w_latent = jnp.concatenate([low[:shard, half:], high[:shard, half:]], 1)
    gain_sums = own[shard] + got[shard]

    return (
        output, grad_tokens, gain_sums[:shard], gain_sums[shard : 2 * shard],
        grad_w_query, grad_w_latent, grad_ups[:, :pair_width], grad_ups[:, pair_width:],
        grad_w_out, grad_w_gate, grad_w_up, grad_w_down,
    )


def solution(mesh):
    rows = P(("dp", "ctx"), None)
    vector = P(("dp", "ctx"))
    stretch = P("dp", "ctx", None)
    in_specs = (stretch, stretch, P("dp"), P(), P("dp", "ctx"), vector, vector) + (rows,) * 8
    out_specs = (stretch, stretch, vector, vector) + (rows,) * 8
    return jax.shard_map(
        functools.partial(per_device, Plan(mesh)), mesh=mesh, in_specs=in_specs, out_specs=out_specs,
        check_vma=False,
    )
```

time: 1470 us -> 438 us (0.30)
  waiting for transfers between devices: 997 us -> 161 us
  blocking collectives: 213 us -> 0 us
  starting transfers between devices: 1.21 us -> 103 us
  matrix products: 135 us -> 34.7 us
  Pallas kernels: 0 us -> 56.9 us
  loops' own time: 31.8 us -> 0 us
  other arithmetic: 19.5 us -> 41.6 us
  local copies, waits for them, and re-layouts: 51.3 us -> 35.2 us
    reduce_scatter x12 -> x0, waiting for transfers between devices: 629 us -> none  [the longest x1 66.4 us: per_device(): lax.psum_scatter(partial_sums[8].astype(jnp.bfloat16), 'ctx', scatter_dim...]
    unnamed x29 -> x0, waiting for transfers between devices: 196 us -> none
    all_gather x7 -> x0, waiting for transfers between devices: 172 us -> none  [the longest x1 64.4 us: per_device(): lax.all_gather(w_down, ('dp', 'ctx'), axis=0, tiled=True)]
    ppermute x0 -> x91, waiting for transfers between devices: none -> 161 us  [the longest x89 161 us: swap(): return lax.ppermute(value, AXES, [(n, n ^ mask) for n in range(self.count)])]
    all_gather x2 -> x0, blocking collectives: 132 us -> none  [the longest x1 68.7 us: per_device(): lax.all_gather(w_upkey, ('dp', 'ctx'), axis=0, tiled=True)]
    ppermute x0 -> x91, starting transfers between devices: none -> 103 us  [the longest x89 94.3 us: swap(): return lax.ppermute(value, AXES, [(n, n ^ mask) for n in range(self.count)])]
    dot_general x40 -> x6, matrix products: 97.6 us -> 11.3 us  [product(): return jnp.dot(left, right, preferred_element_type=F32)]
    unnamed x4 -> x0, blocking collectives: 80.9 us -> none
  transfers between devices with their start and end apart: 24 -> 91, of which waited for: 21 -> 42; matrix products, arithmetic and copies ran while one was open for 6% -> 22% of each run, Pallas kernels for 0% -> 12%
where the time goes in v1:
time: 438 us; the launch traced here: 437 us
  waiting for transfers between devices  161 us (37%)
  starting transfers between devices  103 us (24%)
  Pallas kernels  56.9 us (13%)
  other arithmetic  41.6 us (9%)
  local copies, waits for them, and re-layouts  35.2 us (8%)
  matrix products  34.7 us (8%)
  between operations  4.47 us (1%)
    ppermute x89, waiting for transfers between devices, swap(): return lax.ppermute(value, AXES, [(n, n ^ mask) for n in range(self.count)])  161 us
    ppermute x89, starting transfers between devices, swap(): return lax.ppermute(value, AXES, [(n, n ^ mask) for n in range(self.count)])  94.3 us
    pallas_call x1, Pallas kernels, attend_back(): pl.pallas_call(attend_back_kernel, grid=(seqs, pairs), in_specs=[pair, wi...  20.1 us
    dot_general x7, matrix products, contract_rows(): lax.dot_general(left, right, (((0,), (0,)), ((), ())), preferred_element_...  13.1 us
    pallas_call x1, Pallas kernels, attend(): pl.pallas_call(attend_kernel, grid=(seqs, pairs), in_specs=[pair, up, up,...  12.9 us
    pallas_call x4, Pallas kernels, cut_blocks(): pl.pallas_call(kernel, out_shape=[jax.ShapeDtypeStruct(shape, BF16) for s...  12 us
    pallas_call x4, Pallas kernels, place_blocks(): pl.pallas_call(kernel, out_shape=[jax.ShapeDtypeStruct((len(spots), rows,...  11.9 us
    dot_general x6, matrix products, product(): return jnp.dot(left, right, preferred_element_type=F32)  11.3 us
  transfers between devices with their start and end apart: 91, of which 42 were waited for; matrix products, arithmetic and copies ran while one was open for 22% of the time, Pallas kernels for 12%

profile of v1, /device:TPU:1, one launch (start us, length us, event | category | flops | bytes accessed | tf_op | source)
XLA Modules:
  0.0 436.9 jit_solution(4825538796403321611)
XLA Ops:
  4.7 4.5 %collective-permute-start.13 = (bf16[48,1024]{1,0:T(8,128)(2,1)S(1)}, bf16[48,1024]{1,0:T(8,128)(2,1)S(1)}, u32[]{:S(2)}, u32[]{:S(2)}) collective-permute-start(bf16[48,1024]{1,0:T(8,128)(2,1)S(1)} %pad_maximum_fusion.22), channel_id=1, source_target_pairs={{0,0},{1,1},{2,2},{3,3},{4,4},{5,5},{6,6},{7,7},{8,16},{9,17},{10,... | collective-permute-start | bytes 294920 | tf_op jit(solution)/shard_map/ppermute | solution.py:318
  12.5 2.4 collective-permute-start.3
  25.1 3.2 collective-permute-start.16
  30.9 3.3 collective-permute-done.14
  40.5 5.2 %collective-permute-done.18.refs_5_ = bf16[1,48,1024]{2,1,0:T(8,128)(2,1)S(1)} collective-permute-done((bf16[1,48,1024]{2,1,0:T(8,128)(2,1)S(1)}, bf16[1,48,1024]{2,1,0:T(8,128)(2,1)S(1)}, u32[]{:S(2)}, u32[]{:S(2)}) %collective-permute-start.18) | collective-permute-done | bytes 98336 | tf_op jit(solution)/shard_map/ppermute | solution.py:301
  47.8 2.8 collective-permute-done.19.refs_6_
  57.9 3.7 collective-permute-done.22.refs_9_
  63.1 2.8 collective-permute-done.21.refs_8_
  65.9 9.4 %collective-permute-done.24.refs_11_ = bf16[2,48,1024]{2,1,0:T(8,128)(2,1)} collective-permute-done((bf16[2,48,1024]{2,1,0:T(8,128)(2,1)}, bf16[2,48,1024]{2,1,0:T(8,128)(2,1)}, u32[]{:S(2)}, u32[]{:S(2)}) %collective-permute-start.24) | collective-permute-done | bytes 196640 | tf_op jit(solution)/shard_map/ppermute | solution.py:301
  75.3 8.1 %collective-permute-start.38 = (bf16[64,704]{1,0:T(8,128)(2,1)}, bf16[64,704]{1,0:T(8,128)(2,1)S(1)}, u32[]{:S(2)}, u32[]{:S(2)}) collective-permute-start(bf16[64,704]{1,0:T(8,128)(2,1)} %bitcast.329), channel_id=1, source_target_pairs={{0,24},{1,25},{2,26},{3,27},{4,28},{5,29},{6,30},{7,31},{8,16},{9,... | collective-permute-start | bytes 270344 | tf_op jit(solution)/shard_map/ppermute | solution.py:301
  83.4 3.2 collective-permute-start.36
  86.7 2.7 place_blocks.5
  90.3 2.9 place_blocks.4
  94.7 2.8 collective-permute-start.25
  98.7 5.0 %collective-permute-done.25 = bf16[2,128,256]{2,1,0:T(8,128)(2,1)S(1)} collective-permute-done((bf16[2,128,256]{2,1,0:T(8,128)(2,1)S(1)}, bf16[2,128,256]{2,1,0:T(8,128)(2,1)S(1)}, u32[]{:S(2)}, u32[]{:S(2)}) %collective-permute-start.25) | collective-permute-done | bytes 131104 | tf_op jit(solution)/shard_map/ppermute | solution.py:301
  104.9 3.3 collective-permute-done.27
  108.3 3.8 collective-permute-done.28
  112.1 4.0 collective-permute-done.29
  116.1 5.3 %collective-permute-done.30 = bf16[1,2,128,256]{3,2,1,0:T(8,128)(2,1)S(1)} collective-permute-done((bf16[1,2,128,256]{3,2,1,0:T(8,128)(2,1)S(1)}, bf16[1,2,128,256]{3,2,1,0:T(8,128)(2,1)S(1)}, u32[]{:S(2)}, u32[]{:S(2)}) %collective-permute-start.30) | collective-permute-done | bytes 131104 | tf_op jit(solution)/shard_map/ppermute | solution.py:301
  121.4 4.7 %collective-permute-done.31 = bf16[1,2,128,256]{3,2,1,0:T(8,128)(2,1)S(1)} collective-permute-done((bf16[1,2,128,256]{3,2,1,0:T(8,128)(2,1)S(1)}, bf16[1,2,128,256]{3,2,1,0:T(8,128)(2,1)S(1)}, u32[]{:S(2)}, u32[]{:S(2)}) %collective-permute-start.31) | collective-permute-done | bytes 131104 | tf_op jit(solution)/shard_map/ppermute | solution.py:301
  127.0 12.9 %attend.1 = (bf16[2,4,256,256]{3,2,1,0:T(8,128)(2,1)}, bf16[2,4,256,256]{3,2,1,0:T(8,128)(2,1)}, f32[2,4,256,1]{3,2,1,0:T(8,128)}, bf16[2,128,512]{2,1,0:T(8,128)(2,1)}) custom-call(bf16[2,128,512]{2,1,0:T(8,128)(2,1)} %bitcast.408, bf16[256,512]{1,0:T(8,128)(2,1)} %bitcast.403, bf16[256,512]{1,0:T(8,128)(2,1)} %bitcast.405, ...), custom_call_target="tpu_custom_call" | custom-call | flops 2147483648 | bytes 6291456 | tf_op jit(solution)/shard_map/attend/pallas_call | solution.py:241
  142.2 6.2 %collective-permute-start.32 = (f32[128,1024]{1,0:T(8,128)}, f32[128,1024]{1,0:T(8,128)}, u32[]{:S(2)}, u32[]{:S(2)}) collective-permute-start(f32[128,1024]{1,0:T(8,128)} %slice.359), channel_id=1, source_target_pairs={{0,8},{1,9},{2,10},{3,11},{4,12},{5,13},{6,14},{7,15},{8,0},{9,1},... | collective-permute-start | bytes 1572872 | tf_op jit(solution)/shard_map/ppermute | solution.py:301
  157.1 2.4 collective-permute-done.47.refs_2_
  160.8 9.8 %collective-permute-done.46 = bf16[88,1024]{1,0:T(8,128)(2,1)} collective-permute-done((bf16[88,1024]{1,0:T(8,128)(2,1)}, bf16[88,1024]{1,0:T(8,128)(2,1)}, u32[]{:S(2)}, u32[]{:S(2)}) %collective-permute-start.46) | collective-permute-done | bytes 180256 | tf_op jit(solution)/shard_map/ppermute | solution.py:301
  172.1 3.3 collective-permute-done.51.refs_6_
  175.4 3.5 collective-permute-done.39
  179.8 2.8 collective-permute-start.57
  182.6 9.2 %collective-permute-done.48.refs_3_ = bf16[1,88,1024]{2,1,0:T(8,128)(2,1)S(1)} collective-permute-done((bf16[1,88,1024]{2,1,0:T(8,128)(2,1)}, bf16[1,88,1024]{2,1,0:T(8,128)(2,1)S(1)}, u32[]{:S(2)}, u32[]{:S(2)}) %collective-permute-start.48) | collective-permute-done | bytes 180256 | tf_op jit(solution)/shard_map/ppermute | solution.py:301
  194.0 3.8 collective-permute-done.52.refs_7_
  202.7 2.6 place_blocks.7
  205.3 2.4 collective-permute-start.33
  207.9 2.6 fusion.25
  210.5 4.2 collective-permute-done.44.refs_6_
  214.7 8.4 %collective-permute-done.45.refs_7_ = bf16[1,256,704]{2,1,0:T(8,128)(2,1)} collective-permute-done((bf16[1,256,704]{2,1,0:T(8,128)(2,1)}, bf16[1,256,704]{2,1,0:T(8,128)(2,1)}, u32[]{:S(2)}, u32[]{:S(2)}) %collective-permute-start.45) | collective-permute-done | bytes 360480 | tf_op jit(solution)/shard_map/ppermute | solution.py:301
  223.1 3.7 place_blocks.6
  226.8 2.7 fusion.39
  229.6 3.5 multiply_convert_fusion.1
  233.0 3.5 convolution_convert_fusion.2
  236.5 2.6 cut_blocks.7
  240.5 2.4 fusion.49
  246.4 3.4 convolution_add_fusion
  249.9 3.1 convolution_convert_fusion.1
  253.0 2.6 copy.135
  255.5 3.8 cut_blocks.6
  261.6 2.3 copy.139
  266.5 2.9 collective-permute-start.58
  273.1 8.9 %collective-permute-done.89 = bf16[2,88,1024]{2,1,0:T(8,128)(2,1)S(1)} collective-permute-done((bf16[2,88,1024]{2,1,0:T(8,128)(2,1)S(1)}, bf16[2,88,1024]{2,1,0:T(8,128)(2,1)S(1)}, u32[]{:S(2)}, u32[]{:S(2)}) %collective-permute-start.89) | collective-permute-done | bytes 360480 | tf_op jit(solution)/shard_map/ppermute | solution.py:301
  288.0 2.3 copy.141
  291.5 3.5 collective-permute-done.80
  306.2 6.0 %collective-permute-start.60 = (bf16[128,1024]{1,0:T(8,128)(2,1)S(1)}, bf16[128,1024]{1,0:T(8,128)(2,1)S(1)}, u32[]{:S(2)}, u32[]{:S(2)}) collective-permute-start(bf16[128,1024]{1,0:T(8,128)(2,1)S(1)} %fusion.37), channel_id=1, source_target_pairs={{0,8},{1,9},{2,10},{3,11},{4,12},{5,13},{6,14},{7,15},{8,0},{9,1},... | collective-permute-start | bytes 786440 | tf_op jit(solution)/shard_map/ppermute | solution.py:301
  316.4 20.1 %attend_back.1 = (bf16[2,128,512]{2,1,0:T(8,128)(2,1)}, bf16[256,512]{1,0:T(8,128)(2,1)}, bf16[256,512]{1,0:T(8,128)(2,1)}, bf16[2,2,128,256]{3,2,1,0:T(8,128)(2...) custom-call(bf16[2,128,512]{2,1,0:T(8,128)(2,1)} %bitcast.409, ...), custom_call_target="tpu_custom_call" | custom-call | flops 5368709120 | bytes 8388608 | tf_op jit(solution)/shard_map/attend_back/pallas_call | solution.py:265
  339.6 2.7 cut_blocks.5
  345.8 4.6 %collective-permute-done.62 = bf16[2,2,128,256]{3,2,1,0:T(8,128)(2,1)S(1)} collective-permute-done((bf16[2,2,128,256]{3,2,1,0:T(8,128)(2,1)}, bf16[2,2,128,256]{3,2,1,0:T(8,128)(2,1)S(1)}, u32[]{:S(2)}, u32[]{:S(2)}) %collective-permute-start.62) | collective-permute-done | bytes 262176 | tf_op jit(solution)/shard_map/ppermute | solution.py:301
  352.6 2.9 collective-permute-done.86
  358.5 4.8 %collective-permute-done.63 = bf16[2,2,128,256]{3,2,1,0:T(8,128)(2,1)S(1)} collective-permute-done((bf16[2,2,128,256]{3,2,1,0:T(8,128)(2,1)S(1)}, bf16[2,2,128,256]{3,2,1,0:T(8,128)(2,1)S(1)}, u32[]{:S(2)}, u32[]{:S(2)}) %collective-permute-start.63) | collective-permute-done | bytes 262176 | tf_op jit(solution)/shard_map/ppermute | solution.py:301
  365.2 2.3 collective-permute-done.74
  368.6 3.1 collective-permute-done.64
  379.5 3.0 cut_blocks.4
  392.1 5.2 %collective-permute-done.77 = bf16[48,1024]{1,0:T(8,128)(2,1)} collective-permute-done((bf16[48,1024]{1,0:T(8,128)(2,1)}, bf16[48,1024]{1,0:T(8,128)(2,1)}, u32[]{:S(2)}, u32[]{:S(2)}) %collective-permute-start.77) | collective-permute-done | bytes 98336 | tf_op jit(solution)/shard_map/ppermute | solution.py:301
  398.4 4.5 %collective-permute-start.79 = (f32[48,1024]{1,0:T(8,128)S(1)}, f32[48,1024]{1,0:T(8,128)S(1)}, u32[]{:S(2)}, u32[]{:S(2)}) collective-permute-start(f32[48,1024]{1,0:T(8,128)S(1)} %fusion.24), channel_id=1, source_target_pairs={{0,0},{1,1},{2,2},{3,3},{4,4},{5,5},{6,6},{7,7},{8,16},{9,17},{10,... | collective-permute-start | bytes 589832 | tf_op jit(solution)/shard_map/ppermute | solution.py:318
  408.1 8.4 %collective-permute-done.66 = bf16[4,80,768]{2,1,0:T(8,128)(2,1)S(1)} collective-permute-done((bf16[4,80,768]{2,1,0:T(8,128)(2,1)}, bf16[4,80,768]{2,1,0:T(8,128)(2,1)S(1)}, u32[]{:S(2)}, u32[]{:S(2)}) %collective-permute-start.66) | collective-permute-done | bytes 491552 | tf_op jit(solution)/shard_map/ppermute | solution.py:301
  420.7 3.5 collective-permute-done.71
  424.2 5.5 %collective-permute-done.70 = bf16[80,768]{1,0:T(8,128)(2,1)S(1)} collective-permute-done((bf16[80,768]{1,0:T(8,128)(2,1)S(1)}, bf16[80,768]{1,0:T(8,128)(2,1)S(1)}, u32[]{:S(2)}, u32[]{:S(2)}) %collective-permute-start.70) | collective-permute-done | bytes 122912 | tf_op jit(solution)/shard_map/ppermute | solution.py:301
  432.0 2.9 fusion.18
  (464 shorter events, 145.0 us)
Async XLA Ops:
  4.7 15.7 %collective-permute-start.13 = (bf16[48,1024]{1,0:T(8,128)(2,1)S(1)}, bf16[48,1024]{1,0:T(8,128)(2,1)S(1)}, u32[]{:S(2)}, u32[]{:S(2)}) collective-permute-start(bf16[48,1024]{1,0:T(8,128)(2,1)S(1)} %pad_maximum_fusion.22), channel_id=1, source_target_pairs={{0,0},{1,1},{2,2},{3,3},{4,4},{5,5},{6,6},{7,7},{8,16},{9,17},{10,... | collective-permute-start | bytes 294920 | tf_op jit(solution)/shard_map/ppermute | solution.py:318
  9.2 29.6 %collective-permute-start = (bf16[128,1024]{1,0:T(8,128)(2,1)}, bf16[128,1024]{1,0:T(8,128)(2,1)S(1)}, u32[]{:S(2)}, u32[]{:S(2)}) collective-permute-start(bf16[128,1024]{1,0:T(8,128)(2,1)} %bitcast.350), channel_id=1, source_target_pairs={{0,8},{1,9},{2,10},{3,11},{4,12},{5,13},{6,14},{7,15},{8,0},{9,1},... | collective-permute-start | bytes 786440 | tf_op jit(solution)/shard_map/ppermute | solution.py:301
  12.5 11.3 %collective-permute-start.3 = (bf16[80,768]{1,0:T(8,128)(2,1)S(1)}, bf16[80,768]{1,0:T(8,128)(2,1)S(1)}, u32[]{:S(2)}, u32[]{:S(2)}) collective-permute-start(bf16[80,768]{1,0:T(8,128)(2,1)S(1)} %get-tuple-element.124), channel_id=1, source_target_pairs={{0,4},{1,5},{2,6},{3,7},{4,0},{5,1},{6,2},{7,3},{8,12},{9,13},{10,... | collective-permute-start | bytes 368648 | tf_op jit(solution)/shard_map/ppermute | solution.py:301
  14.9 10.2 %collective-permute-start.4 = (bf16[80,768]{1,0:T(8,128)(2,1)S(1)}, bf16[80,768]{1,0:T(8,128)(2,1)S(1)}, u32[]{:S(2)}, u32[]{:S(2)}) collective-permute-start(bf16[80,768]{1,0:T(8,128)(2,1)S(1)} %get-tuple-element.124), channel_id=1, source_target_pairs={{0,6},{1,7},{2,4},{3,5},{4,2},{5,3},{6,0},{7,1},{8,14},{9,15},{10,... | collective-permute-start | bytes 368648 | tf_op jit(solution)/shard_map/ppermute | solution.py:301
  20.1 9.0 %collective-permute-start.2 = (bf16[80,768]{1,0:T(8,128)(2,1)S(1)}, bf16[80,768]{1,0:T(8,128)(2,1)S(1)}, u32[]{:S(2)}, u32[]{:S(2)}) collective-permute-start(bf16[80,768]{1,0:T(8,128)(2,1)S(1)} %get-tuple-element.124), channel_id=1, source_target_pairs={{0,2},{1,3},{2,0},{3,1},{4,6},{5,7},{6,4},{7,5},{8,10},{9,11},{10,... | collective-permute-start | bytes 368648 | tf_op jit(solution)/shard_map/ppermute | solution.py:301
  20.4 10.1 %collective-permute-start.5 = (bf16[1,80,768]{2,1,0:T(8,128)(2,1)S(1)}, bf16[1,80,768]{2,1,0:T(8,128)(2,1)S(1)}, u32[]{:S(2)}, u32[]{:S(2)}) collective-permute-start(bf16[1,80,768]{2,1,0:T(8,128)(2,1)S(1)} %get-tuple-element.125.refs_0_), channel_id=1, source_target_pairs={{0,1},{1,0},{2,3},{3,2},{4,5},{5,4},{6,7},{7,6},{8,9},{9,8},{10,11... | collective-permute-start | bytes 368648 | tf_op jit(solution)/shard_map/ppermute | solution.py:301
  23.8 16.6 %collective-permute-start.17 = (bf16[1,48,1024]{2,1,0:T(8,128)(2,1)S(1)}, bf16[1,48,1024]{2,1,0:T(8,128)(2,1)S(1)}, u32[]{:S(2)}, u32[]{:S(2)}) collective-permute-start(bf16[1,48,1024]{2,1,0:T(8,128)(2,1)S(1)} %bitcast.374), channel_id=1, source_target_pairs={{0,1},{1,0},{2,3},{3,2},{4,5},{5,4},{6,7},{7,6},{8,9},{9,8},{10,11... | collective-permute-start | bytes 294920 | tf_op jit(solution)/shard_map/ppermute | solution.py:301
  25.1 11.2 %collective-permute-start.16 = (bf16[48,1024]{1,0:T(8,128)(2,1)S(1)}, bf16[48,1024]{1,0:T(8,128)(2,1)S(1)}, u32[]{:S(2)}, u32[]{:S(2)}) collective-permute-start(bf16[48,1024]{1,0:T(8,128)(2,1)S(1)} %collective-permute-done.13), channel_id=1, source_target_pairs={{0,6},{1,7},{2,4},{3,5},{4,2},{5,3},{6,0},{7,1},{8,14},{9,15},{10,... | collective-permute-start | bytes 294920 | tf_op jit(solution)/shard_map/ppermute | solution.py:301
  29.1 9.0 %collective-permute-start.15 = (bf16[48,1024]{1,0:T(8,128)(2,1)S(1)}, bf16[48,1024]{1,0:T(8,128)(2,1)S(1)}, u32[]{:S(2)}, u32[]{:S(2)}) collective-permute-start(bf16[48,1024]{1,0:T(8,128)(2,1)S(1)} %collective-permute-done.13), channel_id=1, source_target_pairs={{0,4},{1,5},{2,6},{3,7},{4,0},{5,1},{6,2},{7,3},{8,12},{9,13},{10,... | collective-permute-start | bytes 294920 | tf_op jit(solution)/shard_map/ppermute | solution.py:301
  34.2 17.1 %collective-permute-start.7 = (bf16[1,80,768]{2,1,0:T(8,128)(2,1)S(1)}, bf16[1,80,768]{2,1,0:T(8,128)(2,1)S(1)}, u32[]{:S(2)}, u32[]{:S(2)}) collective-permute-start(bf16[1,80,768]{2,1,0:T(8,128)(2,1)S(1)} %bitcast.364), channel_id=1, source_target_pairs={{0,1},{1,0},{2,3},{3,2},{4,5},{5,4},{6,7},{7,6},{8,9},{9,8},{10,11... | collective-permute-start | bytes 368648 | tf_op jit(solution)/shard_map/ppermute | solution.py:301
  36.3 16.7 %collective-permute-start.6 = (bf16[1,80,768]{2,1,0:T(8,128)(2,1)S(1)}, bf16[1,80,768]{2,1,0:T(8,128)(2,1)S(1)}, u32[]{:S(2)}, u32[]{:S(2)}) collective-permute-start(bf16[1,80,768]{2,1,0:T(8,128)(2,1)S(1)} %bitcast.372), channel_id=1, source_target_pairs={{0,1},{1,0},{2,3},{3,2},{4,5},{5,4},{6,7},{7,6},{8,9},{9,8},{10,11... | collective-permute-start | bytes 368648 | tf_op jit(solution)/shard_map/ppermute | solution.py:301
  38.1 15.1 %collective-permute-start.8 = (bf16[1,80,768]{2,1,0:T(8,128)(2,1)S(1)}, bf16[1,80,768]{2,1,0:T(8,128)(2,1)S(1)}, u32[]{:S(2)}, u32[]{:S(2)}) collective-permute-start(bf16[1,80,768]{2,1,0:T(8,128)(2,1)S(1)} %bitcast.368), channel_id=1, source_target_pairs={{0,1},{1,0},{2,3},{3,2},{4,5},{5,4},{6,7},{7,6},{8,9},{9,8},{10,11... | collective-permute-start | bytes 368648 | tf_op jit(solution)/shard_map/ppermute | solution.py:301
  47.8 9.9 %collective-permute-start.9 = (bf16[2,80,768]{2,1,0:T(8,128)(2,1)}, bf16[2,80,768]{2,1,0:T(8,128)(2,1)S(1)}, u32[]{:S(2)}, u32[]{:S(2)}) collective-permute-start(bf16[2,80,768]{2,1,0:T(8,128)(2,1)} %pad_maximum_fusion.10), channel_id=1, source_target_pairs={{0,16},{1,17},{2,18},{3,19},{4,20},{5,21},{6,22},{7,23},{8,24},{9,... | collective-permute-start | bytes 737288 | tf_op jit(solution)/shard_map/ppermute | solution.py:301
  50.6 11.3 %collective-permute-start.10 = (bf16[2,80,768]{2,1,0:T(8,128)(2,1)}, bf16[2,80,768]{2,1,0:T(8,128)(2,1)S(1)}, u32[]{:S(2)}, u32[]{:S(2)}) collective-permute-start(bf16[2,80,768]{2,1,0:T(8,128)(2,1)} %pad_maximum_fusion.11), channel_id=1, source_target_pairs={{0,16},{1,17},{2,18},{3,19},{4,20},{5,21},{6,22},{7,23},{8,24},{9,... | collective-permute-start | bytes 737288 | tf_op jit(solution)/shard_map/ppermute | solution.py:301
  51.4 10.3 %collective-permute-start.22 = (bf16[2,48,1024]{2,1,0:T(8,128)(2,1)}, bf16[2,48,1024]{2,1,0:T(8,128)(2,1)}, u32[]{:S(2)}, u32[]{:S(2)}) collective-permute-start(bf16[2,48,1024]{2,1,0:T(8,128)(2,1)} %pad_maximum_fusion.15), channel_id=1, source_target_pairs={{0,16},{1,17},{2,18},{3,19},{4,20},{5,21},{6,22},{7,23},{8,24},{9,... | collective-permute-start | bytes 589832 | tf_op jit(solution)/shard_map/ppermute | solution.py:301
  53.0 13.0 %collective-permute-start.21 = (bf16[2,48,1024]{2,1,0:T(8,128)(2,1)}, bf16[2,48,1024]{2,1,0:T(8,128)(2,1)}, u32[]{:S(2)}, u32[]{:S(2)}) collective-permute-start(bf16[2,48,1024]{2,1,0:T(8,128)(2,1)} %pad_maximum_fusion.14), channel_id=1, source_target_pairs={{0,16},{1,17},{2,18},{3,19},{4,20},{5,21},{6,22},{7,23},{8,24},{9,... | collective-permute-start | bytes 589832 | tf_op jit(solution)/shard_map/ppermute | solution.py:301
  54.9 34.6 %collective-permute-start.11 = (bf16[2,80,768]{2,1,0:T(8,128)(2,1)}, bf16[2,80,768]{2,1,0:T(8,128)(2,1)S(1)}, u32[]{:S(2)}, u32[]{:S(2)}) collective-permute-start(bf16[2,80,768]{2,1,0:T(8,128)(2,1)} %pad_maximum_fusion.12), channel_id=1, source_target_pairs={{0,16},{1,17},{2,18},{3,19},{4,20},{5,21},{6,22},{7,23},{8,24},{9,... | collective-permute-start | bytes 737288 | tf_op jit(solution)/shard_map/ppermute | solution.py:301
  57.8 17.5 %collective-permute-start.24 = (bf16[2,48,1024]{2,1,0:T(8,128)(2,1)}, bf16[2,48,1024]{2,1,0:T(8,128)(2,1)}, u32[]{:S(2)}, u32[]{:S(2)}) collective-permute-start(bf16[2,48,1024]{2,1,0:T(8,128)(2,1)} %pad_maximum_fusion.17), channel_id=1, source_target_pairs={{0,16},{1,17},{2,18},{3,19},{4,20},{5,21},{6,22},{7,23},{8,24},{9,... | collective-permute-start | bytes 589832 | tf_op jit(solution)/shard_map/ppermute | solution.py:301
  61.6 21.8 %collective-permute-start.23 = (bf16[2,48,1024]{2,1,0:T(8,128)(2,1)}, bf16[2,48,1024]{2,1,0:T(8,128)(2,1)}, u32[]{:S(2)}, u32[]{:S(2)}) collective-permute-start(bf16[2,48,1024]{2,1,0:T(8,128)(2,1)} %pad_maximum_fusion.16), channel_id=1, source_target_pairs={{0,16},{1,17},{2,18},{3,19},{4,20},{5,21},{6,22},{7,23},{8,24},{9,... | collective-permute-start | bytes 589832 | tf_op jit(solution)/shard_map/ppermute | solution.py:301
  61.9 27.6 %collective-permute-start.12 = (bf16[2,80,768]{2,1,0:T(8,128)(2,1)}, bf16[2,80,768]{2,1,0:T(8,128)(2,1)S(1)}, u32[]{:S(2)}, u32[]{:S(2)}) collective-permute-start(bf16[2,80,768]{2,1,0:T(8,128)(2,1)} %pad_maximum_fusion.13), channel_id=1, source_target_pairs={{0,16},{1,17},{2,18},{3,19},{4,20},{5,21},{6,22},{7,23},{8,24},{9,... | collective-permute-start | bytes 737288 | tf_op jit(solution)/shard_map/ppermute | solution.py:301
  65.9 88.5 %collective-permute-start.49 = (bf16[1,88,1024]{2,1,0:T(8,128)(2,1)}, bf16[1,88,1024]{2,1,0:T(8,128)(2,1)}, u32[]{:S(2)}, u32[]{:S(2)}) collective-permute-start(bf16[1,88,1024]{2,1,0:T(8,128)(2,1)} %bitcast.133.refs_0_), channel_id=1, source_target_pairs={{0,1},{1,0},{2,3},{3,2},{4,5},{5,4},{6,7},{7,6},{8,9},{9,8},{10,11... | collective-permute-start | bytes 540680 | tf_op jit(solution)/shard_map/ppermute | solution.py:301
  75.3 75.0 %collective-permute-start.38 = (bf16[64,704]{1,0:T(8,128)(2,1)}, bf16[64,704]{1,0:T(8,128)(2,1)S(1)}, u32[]{:S(2)}, u32[]{:S(2)}) collective-permute-start(bf16[64,704]{1,0:T(8,128)(2,1)} %bitcast.329), channel_id=1, source_target_pairs={{0,24},{1,25},{2,26},{3,27},{4,28},{5,29},{6,30},{7,31},{8,16},{9,... | collective-permute-start | bytes 270344 | tf_op jit(solution)/shard_map/ppermute | solution.py:301
  83.4 67.7 %collective-permute-start.36 = (bf16[64,704]{1,0:T(8,128)(2,1)}, bf16[64,704]{1,0:T(8,128)(2,1)S(1)}, u32[]{:S(2)}, u32[]{:S(2)}) collective-permute-start(bf16[64,704]{1,0:T(8,128)(2,1)} %bitcast.331), channel_id=1, source_target_pairs={{0,8},{1,9},{2,10},{3,11},{4,12},{5,13},{6,14},{7,15},{8,0},{9,1},... | collective-permute-start | bytes 270344 | tf_op jit(solution)/shard_map/ppermute | solution.py:301
  94.7 9.0 %collective-permute-start.25 = (bf16[2,128,256]{2,1,0:T(8,128)(2,1)S(1)}, bf16[2,128,256]{2,1,0:T(8,128)(2,1)S(1)}, u32[]{:S(2)}, u32[]{:S(2)}) collective-permute-start(bf16[2,128,256]{2,1,0:T(8,128)(2,1)S(1)} %bitcast.396), channel_id=1, source_target_pairs={{0,4},{1,5},{2,6},{3,7},{4,0},{5,1},{6,2},{7,3},{8,12},{9,13},{10,... | collective-permute-start | bytes 393224 | tf_op jit(solution)/shard_map/ppermute | solution.py:301
  103.7 48.2 %collective-permute-start.37 = (bf16[64,704]{1,0:T(8,128)(2,1)}, bf16[64,704]{1,0:T(8,128)(2,1)S(1)}, u32[]{:S(2)}, u32[]{:S(2)}) collective-permute-start(bf16[64,704]{1,0:T(8,128)(2,1)} %bitcast.330), channel_id=1, source_target_pairs={{0,16},{1,17},{2,18},{3,19},{4,20},{5,21},{6,22},{7,23},{8,24},{9,... | collective-permute-start | bytes 270344 | tf_op jit(solution)/shard_map/ppermute | solution.py:301
  142.2 13.1 %collective-permute-start.32 = (f32[128,1024]{1,0:T(8,128)}, f32[128,1024]{1,0:T(8,128)}, u32[]{:S(2)}, u32[]{:S(2)}) collective-permute-start(f32[128,1024]{1,0:T(8,128)} %slice.359), channel_id=1, source_target_pairs={{0,8},{1,9},{2,10},{3,11},{4,12},{5,13},{6,14},{7,15},{8,0},{9,1},... | collective-permute-start | bytes 1572872 | tf_op jit(solution)/shard_map/ppermute | solution.py:301
  150.3 9.2 %collective-permute-start.47 = (bf16[1,88,1024]{2,1,0:T(8,128)(2,1)}, bf16[1,88,1024]{2,1,0:T(8,128)(2,1)}, u32[]{:S(2)}, u32[]{:S(2)}) collective-permute-start(bf16[1,88,1024]{2,1,0:T(8,128)(2,1)} %bitcast.133.refs_0_), channel_id=1, source_target_pairs={{0,2},{1,3},{2,0},{3,1},{4,6},{5,7},{6,4},{7,5},{8,10},{9,11},{10,... | collective-permute-start | bytes 540680 | tf_op jit(solution)/shard_map/ppermute | solution.py:301
  151.2 19.4 %collective-permute-start.46 = (bf16[88,1024]{1,0:T(8,128)(2,1)}, bf16[88,1024]{1,0:T(8,128)(2,1)}, u32[]{:S(2)}, u32[]{:S(2)}) collective-permute-start(bf16[88,1024]{1,0:T(8,128)(2,1)} %param.29), channel_id=1, source_target_pairs={{0,4},{1,5},{2,6},{3,7},{4,0},{5,1},{6,2},{7,3},{8,12},{9,13},{10,... | collective-permute-start | bytes 540680 | tf_op jit(solution)/shard_map/ppermute | solution.py:301
  151.9 18.7 %collective-permute-start.56 = (bf16[128,1024]{1,0:T(8,128)(2,1)}, bf16[128,1024]{1,0:T(8,128)(2,1)}, u32[]{:S(2)}, u32[]{:S(2)}) collective-permute-start(bf16[128,1024]{1,0:T(8,128)(2,1)} %bitcast_convert_fusion), channel_id=1, source_target_pairs={{0,16},{1,17},{2,18},{3,19},{4,20},{5,21},{6,22},{7,23},{8,24},{9,... | collective-permute-start | bytes 786440 | tf_op jit(solution)/shard_map/ppermute | solution.py:301
  154.4 16.3 %collective-permute-start.55 = (bf16[128,1024]{1,0:T(8,128)(2,1)}, bf16[128,1024]{1,0:T(8,128)(2,1)S(1)}, u32[]{:S(2)}, u32[]{:S(2)}) collective-permute-start(bf16[128,1024]{1,0:T(8,128)(2,1)} %bitcast_convert_fusion), channel_id=1, source_target_pairs={{0,8},{1,9},{2,10},{3,11},{4,12},{5,13},{6,14},{7,15},{8,0},{9,1},... | collective-permute-start | bytes 786440 | tf_op jit(solution)/shard_map/ppermute | solution.py:301
  155.3 23.7 %collective-permute-start.39 = (bf16[256,704]{1,0:T(8,128)(2,1)}, bf16[256,704]{1,0:T(8,128)(2,1)S(1)}, u32[]{:S(2)}, u32[]{:S(2)}) collective-permute-start(bf16[256,704]{1,0:T(8,128)(2,1)} %get-tuple-element.114), channel_id=1, source_target_pairs={{0,4},{1,5},{2,6},{3,7},{4,0},{5,1},{6,2},{7,3},{8,12},{9,13},{10,... | collective-permute-start | bytes 1081352 | tf_op jit(solution)/shard_map/ppermute | solution.py:301
  159.5 33.0 %collective-permute-start.42 = (bf16[1,256,704]{2,1,0:T(8,128)(2,1)S(1)}, bf16[1,256,704]{2,1,0:T(8,128)(2,1)S(1)}, u32[]{:S(2)}, u32[]{:S(2)}) collective-permute-start(bf16[1,256,704]{2,1,0:T(8,128)(2,1)S(1)} %get-tuple-element.115.refs_0_), channel_id=1, source_target_pairs={{0,1},{1,0},{2,3},{3,2},{4,5},{5,4},{6,7},{7,6},{8,9},{9,8},{10,11... | collective-permute-start | bytes 1081352 | tf_op jit(solution)/shard_map/ppermute | solution.py:301
  170.6 22.5 %collective-permute-start.40 = (bf16[1,256,704]{2,1,0:T(8,128)(2,1)S(1)}, bf16[1,256,704]{2,1,0:T(8,128)(2,1)S(1)}, u32[]{:S(2)}, u32[]{:S(2)}) collective-permute-start(bf16[1,256,704]{2,1,0:T(8,128)(2,1)S(1)} %get-tuple-element.115.refs_0_), channel_id=1, source_target_pairs={{0,2},{1,3},{2,0},{3,1},{4,6},{5,7},{6,4},{7,5},{8,10},{9,11},{10,... | collective-permute-start | bytes 1081352 | tf_op jit(solution)/shard_map/ppermute | solution.py:301
  170.7 9.1 %collective-permute-start.50 = (bf16[1,88,1024]{2,1,0:T(8,128)(2,1)}, bf16[1,88,1024]{2,1,0:T(8,128)(2,1)S(1)}, u32[]{:S(2)}, u32[]{:S(2)}) collective-permute-start(bf16[1,88,1024]{2,1,0:T(8,128)(2,1)} %bitcast.134.refs_1_), channel_id=1, source_target_pairs={{0,1},{1,0},{2,3},{3,2},{4,5},{5,4},{6,7},{7,6},{8,9},{9,8},{10,11... | collective-permute-start | bytes 540680 | tf_op jit(solution)/shard_map/ppermute | solution.py:301
  175.4 16.4 %collective-permute-start.48 = (bf16[1,88,1024]{2,1,0:T(8,128)(2,1)}, bf16[1,88,1024]{2,1,0:T(8,128)(2,1)S(1)}, u32[]{:S(2)}, u32[]{:S(2)}) collective-permute-start(bf16[1,88,1024]{2,1,0:T(8,128)(2,1)} %bitcast.134.refs_1_), channel_id=1, source_target_pairs={{0,2},{1,3},{2,0},{3,1},{4,6},{5,7},{6,4},{7,5},{8,10},{9,11},{10,... | collective-permute-start | bytes 540680 | tf_op jit(solution)/shard_map/ppermute | solution.py:301
  178.9 21.4 %collective-permute-start.41 = (bf16[1,256,704]{2,1,0:T(8,128)(2,1)S(1)}, bf16[1,256,704]{2,1,0:T(8,128)(2,1)}, u32[]{:S(2)}, u32[]{:S(2)}) collective-permute-start(bf16[1,256,704]{2,1,0:T(8,128)(2,1)S(1)} %bitcast.387), channel_id=1, source_target_pairs={{0,2},{1,3},{2,0},{3,1},{4,6},{5,7},{6,4},{7,5},{8,10},{9,11},{10,... | collective-permute-start | bytes 1081352 | tf_op jit(solution)/shard_map/ppermute | solution.py:301
  179.8 25.5 %collective-permute-start.57 = (bf16[128,1024]{1,0:T(8,128)(2,1)}, bf16[128,1024]{1,0:T(8,128)(2,1)}, u32[]{:S(2)}, u32[]{:S(2)}) collective-permute-start(bf16[128,1024]{1,0:T(8,128)(2,1)} %collective-permute-done.56), channel_id=1, source_target_pairs={{0,8},{1,9},{2,10},{3,11},{4,12},{5,13},{6,14},{7,15},{8,0},{9,1},... | collective-permute-start | bytes 786440 | tf_op jit(solution)/shard_map/ppermute | solution.py:301
  191.8 16.0 %collective-permute-start.34 = (bf16[128,1024]{1,0:T(8,128)(2,1)}, bf16[128,1024]{1,0:T(8,128)(2,1)}, u32[]{:S(2)}, u32[]{:S(2)}) collective-permute-start(bf16[128,1024]{1,0:T(8,128)(2,1)} %multiply_convert_fusion.4), channel_id=1, source_target_pairs={{0,16},{1,17},{2,18},{3,19},{4,20},{5,21},{6,22},{7,23},{8,24},{9,... | collective-permute-start | bytes 786440 | tf_op jit(solution)/shard_map/ppermute | solution.py:301
  193.1 17.4 %collective-permute-start.43 = (bf16[1,256,704]{2,1,0:T(8,128)(2,1)S(1)}, bf16[1,256,704]{2,1,0:T(8,128)(2,1)S(1)}, u32[]{:S(2)}, u32[]{:S(2)}) collective-permute-start(bf16[1,256,704]{2,1,0:T(8,128)(2,1)S(1)} %bitcast.388), channel_id=1, source_target_pairs={{0,1},{1,0},{2,3},{3,2},{4,5},{5,4},{6,7},{7,6},{8,9},{9,8},{10,11... | collective-permute-start | bytes 1081352 | tf_op jit(solution)/shard_map/ppermute | solution.py:301
  197.8 16.9 %collective-permute-start.44 = (bf16[1,256,704]{2,1,0:T(8,128)(2,1)S(1)}, bf16[1,256,704]{2,1,0:T(8,128)(2,1)}, u32[]{:S(2)}, u32[]{:S(2)}) collective-permute-start(bf16[1,256,704]{2,1,0:T(8,128)(2,1)S(1)} %collective-permute-done.40.refs_2_), channel_id=1, source_target_pairs={{0,1},{1,0},{2,3},{3,2},{4,5},{5,4},{6,7},{7,6},{8,9},{9,8},{10,11... | collective-permute-start | bytes 1081352 | tf_op jit(solution)/shard_map/ppermute | solution.py:301
  200.3 22.7 %collective-permute-start.45 = (bf16[1,256,704]{2,1,0:T(8,128)(2,1)}, bf16[1,256,704]{2,1,0:T(8,128)(2,1)}, u32[]{:S(2)}, u32[]{:S(2)}) collective-permute-start(bf16[1,256,704]{2,1,0:T(8,128)(2,1)} %collective-permute-done.41.refs_3_), channel_id=1, source_target_pairs={{0,1},{1,0},{2,3},{3,2},{4,5},{5,4},{6,7},{7,6},{8,9},{9,8},{10,11... | collective-permute-start | bytes 1081352 | tf_op jit(solution)/shard_map/ppermute | solution.py:301
  205.3 21.4 %collective-permute-start.33 = (bf16[128,1024]{1,0:T(8,128)(2,1)}, bf16[128,1024]{1,0:T(8,128)(2,1)S(1)}, u32[]{:S(2)}, u32[]{:S(2)}) collective-permute-start(bf16[128,1024]{1,0:T(8,128)(2,1)} %multiply_convert_fusion.4), channel_id=1, source_target_pairs={{0,8},{1,9},{2,10},{3,11},{4,12},{5,13},{6,14},{7,15},{8,0},{9,1},... | collective-permute-start | bytes 786440 | tf_op jit(solution)/shard_map/ppermute | solution.py:301
  207.8 19.0 %collective-permute-start.35 = (bf16[128,1024]{1,0:T(8,128)(2,1)}, bf16[128,1024]{1,0:T(8,128)(2,1)S(1)}, u32[]{:S(2)}, u32[]{:S(2)}) collective-permute-start(bf16[128,1024]{1,0:T(8,128)(2,1)} %collective-permute-done.34), channel_id=1, source_target_pairs={{0,8},{1,9},{2,10},{3,11},{4,12},{5,13},{6,14},{7,15},{8,0},{9,1},... | collective-permute-start | bytes 786440 | tf_op jit(solution)/shard_map/ppermute | solution.py:301
  239.0 34.1 %collective-permute-start.87 = (bf16[2,88,1024]{2,1,0:T(8,128)(2,1)}, bf16[2,88,1024]{2,1,0:T(8,128)(2,1)}, u32[]{:S(2)}, u32[]{:S(2)}) collective-permute-start(bf16[2,88,1024]{2,1,0:T(8,128)(2,1)} %get-tuple-element.77), channel_id=1, source_target_pairs={{0,1},{1,0},{2,3},{3,2},{4,5},{5,4},{6,7},{7,6},{8,9},{9,8},{10,11... | collective-permute-start | bytes 1081352 | tf_op jit(solution)/shard_map/ppermute | solution.py:301
  239.6 30.8 %collective-permute-start.88 = (bf16[2,88,1024]{2,1,0:T(8,128)(2,1)}, bf16[2,88,1024]{2,1,0:T(8,128)(2,1)}, u32[]{:S(2)}, u32[]{:S(2)}) collective-permute-start(bf16[2,88,1024]{2,1,0:T(8,128)(2,1)} %get-tuple-element.79), channel_id=1, source_target_pairs={{0,1},{1,0},{2,3},{3,2},{4,5},{5,4},{6,7},{7,6},{8,9},{9,8},{10,11... | collective-permute-start | bytes 1081352 | tf_op jit(solution)/shard_map/ppermute | solution.py:301
  263.9 20.5 %collective-permute-start.81 = (bf16[2,256,704]{1,2,0:T(8,128)(2,1)}, bf16[2,256,704]{1,2,0:T(8,128)(2,1)}, u32[]{:S(2)}, u32[]{:S(2)}) collective-permute-start(bf16[2,256,704]{1,2,0:T(8,128)(2,1)} %copy.139), channel_id=1, source_target_pairs={{0,1},{1,0},{2,3},{3,2},{4,5},{5,4},{6,7},{7,6},{8,9},{9,8},{10,11... | collective-permute-start | bytes 2162696 | tf_op jit(solution)/shard_map/ppermute | solution.py:301
  264.5 30.5 %collective-permute-start.80 = (bf16[2,256,704]{1,2,0:T(8,128)(2,1)}, bf16[2,256,704]{1,2,0:T(8,128)(2,1)}, u32[]{:S(2)}, u32[]{:S(2)}) collective-permute-start(bf16[2,256,704]{1,2,0:T(8,128)(2,1)} %copy.137), channel_id=1, source_target_pairs={{0,1},{1,0},{2,3},{3,2},{4,5},{5,4},{6,7},{7,6},{8,9},{9,8},{10,11... | collective-permute-start | bytes 2162696 | tf_op jit(solution)/shard_map/ppermute | solution.py:301
  266.5 30.7 %collective-permute-start.58 = (f32[2,128,1024]{2,1,0:T(8,128)}, f32[2,128,1024]{2,1,0:T(8,128)}, u32[]{:S(2)}, u32[]{:S(2)}) collective-permute-start(f32[2,128,1024]{2,1,0:T(8,128)} %pad_maximum_fusion.3), channel_id=1, source_target_pairs={{0,8},{1,9},{2,10},{3,11},{4,12},{5,13},{6,14},{7,15},{8,0},{9,1},... | collective-permute-start | bytes 3145736 | tf_op jit(solution)/shard_map/ppermute | solution.py:301
  271.9 10.2 %collective-permute-start.89 = (bf16[2,88,1024]{2,1,0:T(8,128)(2,1)S(1)}, bf16[2,88,1024]{2,1,0:T(8,128)(2,1)S(1)}, u32[]{:S(2)}, u32[]{:S(2)}) collective-permute-start(bf16[2,88,1024]{2,1,0:T(8,128)(2,1)S(1)} %add_convert_fusion.7), channel_id=1, source_target_pairs={{0,2},{1,3},{2,0},{3,1},{4,6},{5,7},{6,4},{7,5},{8,10},{9,11},{10,... | collective-permute-start | bytes 1081352 | tf_op jit(solution)/shard_map/ppermute | solution.py:301
  273.1 27.8 %collective-permute-start.53 = (f32[2,128,1024]{2,1,0:T(8,128)}, f32[2,128,1024]{2,1,0:T(8,128)}, u32[]{:S(2)}, u32[]{:S(2)}) collective-permute-start(f32[2,128,1024]{2,1,0:T(8,128)} %pad_maximum_fusion.1), channel_id=1, source_target_pairs={{0,8},{1,9},{2,10},{3,11},{4,12},{5,13},{6,14},{7,15},{8,0},{9,1},... | collective-permute-start | bytes 3145736 | tf_op jit(solution)/shard_map/ppermute | solution.py:301
  284.0 15.2 %collective-permute-start.90 = (bf16[88,1024]{1,0:T(8,128)(2,1)}, bf16[88,1024]{1,0:T(8,128)(2,1)}, u32[]{:S(2)}, u32[]{:S(2)}) collective-permute-start(bf16[88,1024]{1,0:T(8,128)(2,1)} %slice_bitcast_fusion.11), channel_id=1, source_target_pairs={{0,4},{1,5},{2,6},{3,7},{4,0},{5,1},{6,2},{7,3},{8,12},{9,13},{10,... | collective-permute-start | bytes 540680 | tf_op jit(solution)/shard_map/ppermute | solution.py:301
  290.3 21.9 %collective-permute-start.82 = (bf16[2,256,704]{1,2,0:T(8,128)(2,1)}, bf16[2,256,704]{1,2,0:T(8,128)(2,1)}, u32[]{:S(2)}, u32[]{:S(2)}) collective-permute-start(bf16[2,256,704]{1,2,0:T(8,128)(2,1)} %copy.141), channel_id=1, source_target_pairs={{0,2},{1,3},{2,0},{3,1},{4,6},{5,7},{6,4},{7,5},{8,10},{9,11},{10,... | collective-permute-start | bytes 2162696 | tf_op jit(solution)/shard_map/ppermute | solution.py:301
  302.8 129.1 %collective-permute-start.54 = (bf16[128,1024]{1,0:T(8,128)(2,1)}, bf16[128,1024]{1,0:T(8,128)(2,1)}, u32[]{:S(2)}, u32[]{:S(2)}) collective-permute-start(bf16[128,1024]{1,0:T(8,128)(2,1)} %fusion.11), channel_id=1, source_target_pairs={{0,16},{1,17},{2,18},{3,19},{4,20},{5,21},{6,22},{7,23},{8,24},{9,... | collective-permute-start | bytes 786440 | tf_op jit(solution)/shard_map/ppermute | solution.py:301
  306.2 9.0 %collective-permute-start.60 = (bf16[128,1024]{1,0:T(8,128)(2,1)S(1)}, bf16[128,1024]{1,0:T(8,128)(2,1)S(1)}, u32[]{:S(2)}, u32[]{:S(2)}) collective-permute-start(bf16[128,1024]{1,0:T(8,128)(2,1)S(1)} %fusion.37), channel_id=1, source_target_pairs={{0,8},{1,9},{2,10},{3,11},{4,12},{5,13},{6,14},{7,15},{8,0},{9,1},... | collective-permute-start | bytes 786440 | tf_op jit(solution)/shard_map/ppermute | solution.py:301
  315.1 29.6 %collective-permute-start.83 = (bf16[256,704]{1,0:T(8,128)(2,1)S(1)}, bf16[256,704]{1,0:T(8,128)(2,1)S(1)}, u32[]{:S(2)}, u32[]{:S(2)}) collective-permute-start(bf16[256,704]{1,0:T(8,128)(2,1)S(1)} %slice_bitcast_fusion.8), channel_id=1, source_target_pairs={{0,4},{1,5},{2,6},{3,7},{4,0},{5,1},{6,2},{7,3},{8,12},{9,13},{10,... | collective-permute-start | bytes 1081352 | tf_op jit(solution)/shard_map/ppermute | solution.py:301
  336.5 22.0 %collective-permute-start.61 = (bf16[2,2,128,256]{3,2,1,0:T(8,128)(2,1)}, bf16[2,2,128,256]{3,2,1,0:T(8,128)(2,1)S(1)}, u32[]{:S(2)}, u32[]{:S(2)}) collective-permute-start(bf16[2,2,128,256]{3,2,1,0:T(8,128)(2,1)} %get-tuple-element.59), channel_id=1, source_target_pairs={{0,1},{1,0},{2,3},{3,2},{4,5},{5,4},{6,7},{7,6},{8,9},{9,8},{10,11... | collective-permute-start | bytes 786440 | tf_op jit(solution)/shard_map/ppermute | solution.py:301
  337.6 12.7 %collective-permute-start.62 = (bf16[2,2,128,256]{3,2,1,0:T(8,128)(2,1)}, bf16[2,2,128,256]{3,2,1,0:T(8,128)(2,1)S(1)}, u32[]{:S(2)}, u32[]{:S(2)}) collective-permute-start(bf16[2,2,128,256]{3,2,1,0:T(8,128)(2,1)} %get-tuple-element.61), channel_id=1, source_target_pairs={{0,1},{1,0},{2,3},{3,2},{4,5},{5,4},{6,7},{7,6},{8,9},{9,8},{10,11... | collective-permute-start | bytes 786440 | tf_op jit(solution)/shard_map/ppermute | solution.py:301
  342.3 34.0 %collective-permute-start.73 = (bf16[4,48,1024]{2,1,0:T(8,128)(2,1)}, bf16[4,48,1024]{2,1,0:T(8,128)(2,1)S(1)}, u32[]{:S(2)}, u32[]{:S(2)}) collective-permute-start(bf16[4,48,1024]{2,1,0:T(8,128)(2,1)} %get-tuple-element.69), channel_id=1, source_target_pairs={{0,16},{1,17},{2,18},{3,19},{4,20},{5,21},{6,22},{7,23},{8,24},{9,... | collective-permute-start | bytes 1179656 | tf_op jit(solution)/shard_map/ppermute | solution.py:301
  357.6 9.8 %collective-permute-start.74 = (bf16[4,48,1024]{2,1,0:T(8,128)(2,1)S(1)}, bf16[4,48,1024]{2,1,0:T(8,128)(2,1)S(1)}, u32[]{:S(2)}, u32[]{:S(2)}) collective-permute-start(bf16[4,48,1024]{2,1,0:T(8,128)(2,1)S(1)} %copy-done.67), channel_id=1, source_target_pairs={{0,16},{1,17},{2,18},{3,19},{4,20},{5,21},{6,22},{7,23},{8,24},{9,... | collective-permute-start | bytes 1179656 | tf_op jit(solution)/shard_map/ppermute | solution.py:301
  367.6 9.0 %collective-permute-start.75 = (bf16[4,48,1024]{2,1,0:T(8,128)(2,1)S(1)}, bf16[4,48,1024]{2,1,0:T(8,128)(2,1)S(1)}, u32[]{:S(2)}, u32[]{:S(2)}) collective-permute-start(bf16[4,48,1024]{2,1,0:T(8,128)(2,1)S(1)} %add_convert_fusion.5), channel_id=1, source_target_pairs={{0,1},{1,0},{2,3},{3,2},{4,5},{5,4},{6,7},{7,6},{8,9},{9,8},{10,11... | collective-permute-start | bytes 1179656 | tf_op jit(solution)/shard_map/ppermute | solution.py:301
  382.5 20.4 %collective-permute-start.67 = (bf16[4,80,768]{2,1,0:T(8,128)(2,1)}, bf16[4,80,768]{2,1,0:T(8,128)(2,1)}, u32[]{:S(2)}, u32[]{:S(2)}) collective-permute-start(bf16[4,80,768]{2,1,0:T(8,128)(2,1)} %get-tuple-element.65), channel_id=1, source_target_pairs={{0,16},{1,17},{2,18},{3,19},{4,20},{5,21},{6,22},{7,23},{8,24},{9,... | collective-permute-start | bytes 1474568 | tf_op jit(solution)/shard_map/ppermute | solution.py:301
  402.8 13.6 %collective-permute-start.66 = (bf16[4,80,768]{2,1,0:T(8,128)(2,1)}, bf16[4,80,768]{2,1,0:T(8,128)(2,1)S(1)}, u32[]{:S(2)}, u32[]{:S(2)}) collective-permute-start(bf16[4,80,768]{2,1,0:T(8,128)(2,1)} %get-tuple-element.63), channel_id=1, source_target_pairs={{0,16},{1,17},{2,18},{3,19},{4,20},{5,21},{6,22},{7,23},{8,24},{9,... | collective-permute-start | bytes 1474568 | tf_op jit(solution)/shard_map/ppermute | solution.py:301
  404.2 12.5 %collective-permute-start.68 = (bf16[4,80,768]{2,1,0:T(8,128)(2,1)S(1)}, bf16[4,80,768]{2,1,0:T(8,128)(2,1)S(1)}, u32[]{:S(2)}, u32[]{:S(2)}) collective-permute-start(bf16[4,80,768]{2,1,0:T(8,128)(2,1)S(1)} %add_convert_fusion.3), channel_id=1, source_target_pairs={{0,1},{1,0},{2,3},{3,2},{4,5},{5,4},{6,7},{7,6},{8,9},{9,8},{10,11... | collective-permute-start | bytes 1474568 | tf_op jit(solution)/shard_map/ppermute | solution.py:301
  418.8 10.9 %collective-permute-start.70 = (bf16[80,768]{1,0:T(8,128)(2,1)S(1)}, bf16[80,768]{1,0:T(8,128)(2,1)S(1)}, u32[]{:S(2)}, u32[]{:S(2)}) collective-permute-start(bf16[80,768]{1,0:T(8,128)(2,1)S(1)} %get-tuple-element.107), channel_id=1, source_target_pairs={{0,4},{1,5},{2,6},{3,7},{4,0},{5,1},{6,2},{7,3},{8,12},{9,13},{10,... | collective-permute-start | bytes 368648 | tf_op jit(solution)/shard_map/ppermute | solution.py:301
  (104 other events, 1685.3 us)

commit v2 on v1

--- a/solution.py
+++ b/solution.py
@@ -1,5 +1,6 @@
 import functools
 import itertools
+import math
 
 import jax
 import jax.numpy as jnp
@@ -53,82 +54,103 @@
     return [(key, [n for _, n in sorted(found)]) for key, found in groups.items()]
 
 
-def block_numbers(own):
-    return jnp.arange(own.shape[0], dtype=own.dtype)
-
-
 def permute_blocks(chosen, stack):
     out = product(chosen.astype(BF16), stack.reshape(stack.shape[0], -1)).astype(BF16)
     return out.reshape(-1, *stack.shape[1:])
 
 
-def place_blocks(pieces, blocks, order, shapes):
-    flat = [(o, *spot) for o, spots in enumerate(blocks) for spot in spots]
+def bands_of(widths):
+    return list(zip(widths, itertools.accumulate([0, *widths[:-1]])))
+
+
+def kernel_bytes(shapes):
+    return 4 * sum(math.prod(shape) for shape in shapes) + (4 << 20)
+
+
+def place_blocks(pieces, blocks, orders, shapes):
     if any(rows % 8 for rows, _ in shapes):
-        made, at = [], 0
-        for (rows, columns), spots in zip(shapes, blocks):
-            groups = groups_of(spots)
-            stack = jnp.concatenate([pieces[i][:, r : r + rows, k : k + columns] for (i, r, k), _ in groups])
-            own = order[jnp.asarray([at + n for _, ns in groups for n in ns])]
-            made.append(permute_blocks(own[None, :] == block_numbers(own)[:, None], stack).reshape(-1, columns))
-            at += len(spots)
+        made = []
+        for (rows, widths), bands, order in zip(shapes, blocks, orders):
+            parts = []
+            for (width, _), spots in zip(bands_of(widths), bands):
+                groups = groups_of(spots)
+                stack = jnp.concatenate([pieces[i][:, r : r + rows, k : k + width] for (i, r, k), _ in groups])
+                own = jnp.stack([order[n] for _, ns in groups for n in ns])
+                numbers = jnp.arange(len(spots), dtype=own.dtype)
+                parts.append(permute_blocks(own[None, :] == numbers[:, None], stack))
+            made.append(jnp.concatenate(parts, 2).reshape(-1, sum(widths)))
         return made
 
     def kernel(order_ref, *refs):
         sources, targets = refs[: len(pieces)], refs[len(pieces) :]
-        for n, (o, i, j, r, k) in enumerate(flat):
-            rows, columns = shapes[o]
-            targets[o][order_ref[n]] = sources[i][j, r : r + rows, k : k + columns]
-
+        first = 0
+        for target, (rows, widths), bands in zip(targets, shapes, blocks):
+            for (width, column), spots in zip(bands_of(widths), bands):
+                for n, (i, j, r, k) in enumerate(spots):
+                    target[order_ref[first + n], :, column : column + width] = sources[i][
+                        j, r : r + rows, k : k + width
+                    ]
+            first += len(bands[0])
+
+    out_shapes = [(len(bands[0]), rows, sum(widths)) for (rows, widths), bands in zip(shapes, blocks)]
     made = pl.pallas_call(
         kernel,
-        out_shape=[
-            jax.ShapeDtypeStruct((len(spots), rows, columns), BF16)
-            for (rows, columns), spots in zip(shapes, blocks)
-        ],
+        out_shape=[jax.ShapeDtypeStruct(shape, BF16) for shape in out_shapes],
         in_specs=[pl.BlockSpec(memory_space=pltpu.SMEM)]
         + [pl.BlockSpec(memory_space=pltpu.VMEM)] * len(pieces),
         out_specs=[pl.BlockSpec(memory_space=pltpu.VMEM)] * len(shapes),
-        compiler_params=pltpu.CompilerParams(vmem_limit_bytes=VMEM_BYTES),
+        compiler_params=pltpu.CompilerParams(
+            vmem_limit_bytes=kernel_bytes(out_shapes + [p.shape for p in pieces])
+        ),
         name="place_blocks",
-    )(order, *pieces)
+    )(jnp.stack([n for order in orders for n in order]), *pieces)
     return [whole.reshape(-1, whole.shape[-1]) for whole in made]
 
 
-def cut_blocks(matrices, blocks, order, shapes, piece_shapes):
-    flat = [(o, *spot) for o, spots in enumerate(blocks) for spot in spots]
+def cut_blocks(matrices, blocks, orders, shapes, piece_shapes, spare=()):
     if any(rows % 8 for rows, _ in shapes):
-        bands, at = [{} for _ in piece_shapes], 0
-        for (rows, columns), spots, matrix in zip(shapes, blocks, matrices):
-            grid = matrix.reshape(len(spots), rows, columns)
-            for (i, r, k), ns in groups_of(spots):
-                own = order[jnp.asarray([at + n for n in ns])]
-                chosen = own[:, None] == jnp.arange(len(spots), dtype=own.dtype)[None, :]
-                bands[i].setdefault(r, {})[k] = permute_blocks(chosen, grid)
-            at += len(spots)
+        bands_at = [{} for _ in piece_shapes]
+        for (rows, widths), bands, order, matrix in zip(shapes, blocks, orders, matrices):
+            grid = matrix.reshape(len(bands[0]), rows, -1)
+            for (width, column), spots in zip(bands_of(widths), bands):
+                for (i, r, k), ns in groups_of(spots):
+                    own = jnp.stack([order[n] for n in ns])
+                    chosen = own[:, None] == jnp.arange(len(spots), dtype=own.dtype)[None, :]
+                    bands_at[i].setdefault(r, {})[k] = permute_blocks(chosen, grid[:, :, column : column + width])
+        for i, r, rows, k, columns in spare:
+            bands_at[i].setdefault(r, {})[k] = jnp.zeros((piece_shapes[i][0], rows, columns), BF16)
         return [
             jnp.concatenate(
                 [jnp.concatenate([row[k] for k in sorted(row)], 2) for _, row in sorted(band.items())], 1
             )
-            for band in bands
+            for band in bands_at
         ]
 
     def kernel(order_ref, *refs):
         sources, targets = refs[: len(matrices)], refs[len(matrices) :]
-        for n, (o, i, j, r, k) in enumerate(flat):
-            rows, columns = shapes[o]
-            targets[i][j, r : r + rows, k : k + columns] = sources[o][order_ref[n]]
-
-    grids = [matrix.reshape(-1, rows, columns) for matrix, (rows, columns) in zip(matrices, shapes)]
+        for i, r, rows, k, columns in spare:
+            targets[i][:, r : r + rows, k : k + columns] = jnp.zeros((piece_shapes[i][0], rows, columns), BF16)
+        first = 0
+        for source, (rows, widths), bands in zip(sources, shapes, blocks):
+            for (width, column), spots in zip(bands_of(widths), bands):
+                for n, (i, j, r, k) in enumerate(spots):
+                    targets[i][j, r : r + rows, k : k + width] = source[
+                        order_ref[first + n], :, column : column + width
+                    ]
+            first += len(bands[0])
+
+    grids = [matrix.reshape(-1, rows, matrix.shape[-1]) for matrix, (rows, _) in zip(matrices, shapes)]
     return pl.pallas_call(
         kernel,
         out_shape=[jax.ShapeDtypeStruct(shape, BF16) for shape in piece_shapes],
         in_specs=[pl.BlockSpec(memory_space=pltpu.SMEM)]
         + [pl.BlockSpec(memory_space=pltpu.VMEM)] * len(matrices),
         out_specs=[pl.BlockSpec(memory_space=pltpu.VMEM)] * len(piece_shapes),
-        compiler_params=pltpu.CompilerParams(vmem_limit_bytes=VMEM_BYTES),
+        compiler_params=pltpu.CompilerParams(
+            vmem_limit_bytes=kernel_bytes(list(piece_shapes) + [g.shape for g in grids])
+        ),
         name="cut_blocks",
-    )(order, *grids)
+    )(jnp.stack([n for order in orders for n in order]), *grids)
 
 
 def pair_scores(query_latent, keys, query_pos, key_pos):
@@ -325,10 +347,10 @@
     return out
 
 
-def gather(plan, value, far, second, first, groups):
+def gather(plan, value, far, bits, groups):
     done = [([m], value[None] if m == 0 else plan.swap(value, m)[None]) for m in masks_of(far)]
-    for bit in (second, first):
-        size = -(-len(done) // groups)
+    for bit, count in zip(bits, groups):
+        size = -(-len(done) // count)
         sent = []
         for at in range(0, len(done), size):
             some = done[at : at + size]
@@ -344,24 +366,28 @@
     return [[m ^ one ^ two for m in base] for one in (0, first) for two in (0, second)]
 
 
+def reduce_far(plan, part, far):
+    total = part[0].astype(F32)
+    for n, mask in enumerate(masks_of(far)):
+        if n:
+            total = total + plan.swap(part[n].astype(BF16), mask).astype(F32)
+    return total
+
+
 def reduce(plan, stacks, far, second, first):
     keep0, keep1, send0, send1 = stacks
     got1 = plan.swap(send1, first)
     got0 = plan.swap(send0, first)
     part1 = (keep1.astype(F32) + got1.astype(F32)).astype(BF16)
     got = plan.swap(part1, second)
-    part = (keep0.astype(F32) + got0.astype(F32) + got.astype(F32)).astype(BF16)
-    total = part[0].astype(F32)
-    for n, mask in enumerate(masks_of(far)):
-        if n:
-            total = total + plan.swap(part[n], mask).astype(F32)
-    return total
+    return reduce_far(plan, (keep0.astype(F32) + got0.astype(F32) + got.astype(F32)).astype(BF16), far)
 
 
 def per_device(plan, tokens, cotangent, domain_ids, domain_weights, stretch_offsets, gain_attn, gain_ffn,
                w_query, w_latent, w_upkey, w_upvalue, w_out, w_gate, w_up, w_down):
     _, rows, width = tokens.shape
     me = lax.axis_index("dp") * plan.ctx + lax.axis_index("ctx")
+    here = lax.axis_index("ctx")
     core = (me // plan.core) % 2
     core_bit, cross_bit = plan.core, plan.cross
     count = plan.count
@@ -370,11 +396,13 @@
     down_shard = w_down.shape[0]
     half = w_query.shape[1] // 2
     latent_half = w_latent.shape[1] // 2
+    pair_width = w_upkey.shape[1]
     quarter = w_gate.shape[1] // 4
-    ctx_first, ctx_second, *ctx_far = plan.ctx_bits
+    y_bit, *z_bits = plan.ctx_bits
     x_bit = plan.half_bits[-1]
-    half_far = [b for b in plan.half_bits if b not in (x_bit, ctx_first)]
-    quarter_far = [b for b in plan.quarter_bits if b not in (ctx_first, ctx_second)]
+    half_far = [b for b in plan.half_bits if b not in (x_bit, y_bit)]
+    extra_bits = [b for b in plan.quarter_bits if b not in plan.ctx_bits]
+    half_stages = (half_far, y_bit, x_bit)
 
     def halves(value, size):
         low, high = value[:, :size], value[:, size:]
@@ -382,17 +410,18 @@
 
     query_own, query_other = halves(w_query, half)
     latent_own, latent_other = halves(w_latent, latent_half)
-    span = half + latent_half
     info = jnp.concatenate([gain_attn, gain_ffn, stretch_offsets[0].astype(BF16)])
-    info = jnp.pad(info[None], ((0, INFO - 1), (0, span - info.shape[0])))
-    mine = jnp.concatenate([jnp.concatenate([query_own, latent_own], 1), info])
-    other = jnp.concatenate([jnp.concatenate([query_other, latent_other], 1), info])
+    info = jnp.pad(info[None], ((0, INFO - 1), (0, latent_half - info.shape[0])))
     band = shard + INFO
-    first_message = jnp.concatenate([mine, plan.swap(other, core_bit)])
-    second_message = plan.deal(
-        jnp.concatenate([jnp.concatenate([w_upkey, w_upvalue], 1).reshape(-1, width), w_out]),
-        [(plan.top, core_bit)],
-    )
+    folds = half // latent_half
+    fold = lambda value: jnp.concatenate(jnp.split(value, folds, 1), 0)
+    unfold = lambda value: jnp.concatenate(jnp.split(value, folds, 0), 1)
+    got = plan.swap(jnp.concatenate([latent_other, info, fold(query_other)]), core_bit)
+    first_message = jnp.concatenate([latent_own, info, got[:band]])
+    dealt = plan.deal(
+        jnp.concatenate([jnp.concatenate([w_upkey, w_upvalue], 1), w_out]), [(plan.top, core_bit)]
+    )
+    second_message = jnp.concatenate([jnp.concatenate([query_own, unfold(got[band:])], 1), dealt])
     split_masks = masks_of(plan.split_bits)
     split = (me // core_bit) % 2 + 2 * ((me // cross_bit) % 2)
     columns = jnp.concatenate([w_gate, w_up]).reshape(2 * shard, 4, quarter).transpose(1, 0, 2)
@@ -400,82 +429,84 @@
     def quarter_of(mask_index):
         return lax.dynamic_index_in_dim(columns, split ^ mask_index, 0, keepdims=False)
 
+    down = plan.deal(w_down, [(plan.top, cross_bit), (plan.top // 2, core_bit)])
+    low_width = min(quarter // 128 * 128, width)
+    down_widths = [low_width, width - low_width]
+
+    def narrow(value, column, columns):
+        return jnp.pad(value[:, column : column + columns], ((0, 0), (0, quarter - columns)))
+
     third_message = jnp.concatenate(
-        [quarter_of(0)] + [plan.swap(quarter_of(n), m) for n, m in enumerate(split_masks) if n]
-    )
-    fourth_message = plan.deal(w_down, [(plan.top, cross_bit), (plan.top // 2, core_bit)])
+        [quarter_of(0)]
+        + [plan.swap(quarter_of(n), m) for n, m in enumerate(split_masks) if n]
+        + [narrow(down, column, columns) for columns, column in bands_of(down_widths)]
+    )
+    columns_rows = 8 * shard
+    third_rows = third_message.shape[0]
 
     tokens_two = jnp.concatenate([tokens[0], plan.swap(tokens[0], core_bit)])
     x_two = tokens_two.astype(F32)
 
-    half_stages = (half_far, ctx_first, x_bit)
-    quarter_stages = (quarter_far, ctx_second, ctx_first)
-    first_pieces = gather(plan, first_message, *half_stages, 4)
-    second_pieces = gather(plan, second_message, *half_stages, 4)
-    third_pieces = gather(plan, third_message, *quarter_stages, 4)
-    fourth_pieces = gather(plan, fourth_message, *quarter_stages, 4)
+    first_pieces = gather(plan, first_message, half_far, (y_bit, x_bit), (1, 1))
+    second_pieces = gather(plan, second_message, half_far, (y_bit, x_bit), (4, 2))
+    third_stack = jnp.concatenate([a for _, a in gather(plan, third_message, extra_bits, (), ())])
+    extra_masks = masks_of(extra_bits)
+    third_whole = lax.all_gather(third_stack, "ctx", axis=0, tiled=True)
+    third_spots = [(c * len(extra_masks) + e, (me - here + c) ^ m) for c in range(plan.ctx) for e, m in enumerate(extra_masks)]
 
     def spots(pieces):
         return [(i, j, m) for i, (masks, _) in enumerate(pieces) for j, m in enumerate(masks)]
 
-    query_blocks, latent_blocks, order = [], [], []
-    for i, j, m in spots(first_pieces):
-        for b in (0, 1):
-            query_blocks.append((i, j, b * band, 0))
-            latent_blocks.append((i, j, b * band, half))
-            order.append(me ^ (m ^ b * core_bit))
-    query_full, latent_full = place_blocks(
-        [a for _, a in first_pieces], [query_blocks, latent_blocks], jnp.stack(order + order),
-        [(shard, half), (shard, latent_half)],
-    )
-
-    def owner_half(m):
-        return plan.swap_bits(me ^ m, plan.top, core_bit) % (count // 2)
-
-    up_rows = 2 * up_shard * w_upkey.shape[1] // width
-    second_stacks = [a for _, a in second_pieces]
-    out_blocks = [(i, j, up_rows, 0) for i, j, m in spots(second_pieces)]
-    order_half = jnp.stack([owner_half(m) for _, _, m in spots(second_pieces)])
-    pair_width = w_upkey.shape[1]
-    upkey_blocks = [(i, j, 0, 0) for i, j, m in spots(second_pieces)]
-    upvalue_blocks = [(i, j, 0, pair_width) for i, j, m in spots(second_pieces)]
-    upkey_full, upvalue_full, out_full = place_blocks(
-        second_stacks, [upkey_blocks, upvalue_blocks, out_blocks],
-        jnp.concatenate([order_half] * 3),
-        [(up_shard, pair_width), (up_shard, pair_width), (shard, width)],
-    )
-
-    gate_blocks, up_blocks, order = [], [], []
-    for i, j, m in spots(third_pieces):
-        for n, s in enumerate(split_masks):
-            gate_blocks.append((i, j, n * 2 * shard, 0))
-            up_blocks.append((i, j, n * 2 * shard + shard, 0))
-            order.append(me ^ (m ^ s))
-    order_columns = jnp.stack(order + order)
-    gate_full, up_full = place_blocks(
-        [a for _, a in third_pieces], [gate_blocks, up_blocks], order_columns, [(shard, quarter)] * 2
-    )
-
-    def owner_quarter(m):
-        source = plan.swap_bits(me ^ m, plan.top // 2, core_bit)
+    def owner_half(number):
+        return plan.swap_bits(number, plan.top, core_bit) % (count // 2)
+
+    def owner_quarter(number):
+        source = plan.swap_bits(number, plan.top // 2, core_bit)
         return plan.swap_bits(source, plan.top, cross_bit) % (count // 4)
 
-    down_blocks = [(i, j, 0, 0) for i, j, m in spots(fourth_pieces)]
-    order_down = jnp.stack([owner_quarter(m) for _, _, m in spots(fourth_pieces)])
-    (down_full,) = place_blocks(
-        [a for _, a in fourth_pieces], [down_blocks], order_down, [(down_shard, width)]
-    )
-
+    found = spots(first_pieces)
+    (latent_full,) = place_blocks(
+        [a for _, a in first_pieces],
+        [[[(i, j, b * band, 0) for i, j, _ in found for b in (0, 1)]]],
+        [[me ^ (m ^ b * core_bit) for _, _, m in found for b in (0, 1)]],
+        [(shard, [latent_half])],
+    )
     rows_info = jnp.concatenate(
         [a[:, shard :: band, : 2 * shard + 1] for _, a in first_pieces]
     )
+
+    found = spots(second_pieces)
+    owners = [owner_half(me ^ m) for _, _, m in found]
+    query_full, upkey_full, upvalue_full, out_full = place_blocks(
+        [a for _, a in second_pieces],
+        [
+            [[(i, j, 0, b * half) for i, j, _ in found for b in (0, 1)]],
+            [[(i, j, shard, 0) for i, j, _ in found]],
+            [[(i, j, shard, pair_width) for i, j, _ in found]],
+            [[(i, j, shard + up_shard, 0) for i, j, _ in found]],
+        ],
+        [[me ^ (m ^ b * core_bit) for _, _, m in found for b in (0, 1)], owners, owners, owners],
+        [(shard, [half]), (up_shard, [pair_width]), (up_shard, [pair_width]), (shard, [width])],
+    )
+
+    column_order = [number ^ s for _, number in third_spots for s in split_masks]
+    down_order = [owner_quarter(number) for _, number in third_spots]
+    third_blocks = [
+        [[(0, j, n * 2 * shard, 0) for j, _ in third_spots for n in range(4)]],
+        [[(0, j, n * 2 * shard + shard, 0) for j, _ in third_spots for n in range(4)]],
+        [[(0, j, columns_rows + n * down_shard, 0) for j, _ in third_spots] for n in (0, 1)],
+    ]
+    third_orders = [column_order, column_order, down_order]
+    third_shapes = [(shard, [quarter]), (shard, [quarter]), (down_shard, down_widths)]
+    gate_full, up_full, down_full = place_blocks([third_whole], third_blocks, third_orders, third_shapes)
+
     masks_info = [m for _, _, m in spots(first_pieces)]
     number = jnp.stack([jnp.stack([me ^ m, me ^ m ^ core_bit]) for m in masks_info]).reshape(-1)
     chosen = (number[:, None] == jnp.arange(count)[None, :]).astype(BF16)
     gains = contract_rows(chosen, rows_info[..., : 2 * shard].reshape(count, 2 * shard))
     gain_one = gains[:, :shard].reshape(width)
     gain_two = gains[:, shard:].reshape(width)
-    ctx_masks = sum(reduce_order(ctx_far, ctx_second, ctx_first), [])
+    ctx_masks = [m ^ y for y in (0, y_bit) for m in masks_of(z_bits)]
     offsets = jnp.stack(
         [rows_info[masks_info.index(m), :, 2 * shard] for m in ctx_masks], 1
     ).astype(jnp.int32)
@@ -486,7 +517,7 @@
     normed_one = (x_two * inverse_rms(x_two) * gain_one).astype(BF16)
     latent = product(normed_one, latent_full).astype(BF16)
     latent_message = latent.reshape(2, rows, latent_half)
-    key_pieces = gather(plan, latent_message, ctx_far, ctx_second, ctx_first, 4)
+    key_pieces = gather(plan, latent_message, z_bits, (y_bit,), (4,))
     key_of = {m: a[j] for masks, a in key_pieces for j, m in enumerate(masks)}
     keys = jnp.concatenate([key_of[m] for m in ctx_masks], 1)
     queries = product(normed_one, query_full).astype(BF16).reshape(2, rows, half)
@@ -527,31 +558,18 @@
     grad_down = contract_rows(hidden, dy).astype(BF16)
     output = (middle + collect(product(hidden, down_full))).astype(BF16)[None]
 
-    quarter_order = reduce_order(*quarter_stages)
-    blocks, order = [], []
-    for i, masks in enumerate(quarter_order):
-        for j, m in enumerate(masks):
-            blocks.append((i, j, 0, 0))
-            order.append(owner_quarter(m))
-    down_stacks = cut_blocks(
-        [grad_down], [blocks], jnp.stack(order), [(down_shard, width)],
-        [(len(masks), down_shard, width) for masks in quarter_order],
-    )
-    down_sum = reduce(plan, down_stacks, *quarter_stages)
+    (third_grads,) = cut_blocks(
+        [grad_gate, grad_up, grad_down], third_blocks, third_orders, third_shapes,
+        [(len(third_spots), third_rows, quarter)],
+        [(0, columns_rows + n * down_shard, down_shard, w, quarter - w) for n, w in enumerate(down_widths) if w < quarter],
+    )
+    third_sum = reduce_far(
+        plan, lax.psum_scatter(third_grads, "ctx", scatter_dimension=0, tiled=True), extra_bits
+    )
+    down_sum = third_sum[columns_rows:].reshape(2, down_shard, quarter)
+    down_sum = jnp.concatenate([down_sum[n, :, :w] for n, w in enumerate(down_widths)], 1)
     grad_w_down = plan.deal(down_sum, [(plan.top // 2, core_bit), (plan.top, cross_bit)])
-
-    gate_blocks, up_blocks, order = [], [], []
-    for i, masks in enumerate(quarter_order):
-        for j, m in enumerate(masks):
-            for n, s in enumerate(split_masks):
-                gate_blocks.append((i, j, n * 2 * shard, 0))
-                up_blocks.append((i, j, n * 2 * shard + shard, 0))
-                order.append(me ^ (m ^ s))
-    column_stacks = cut_blocks(
-        [grad_gate, grad_up], [gate_blocks, up_blocks], jnp.stack(order + order), [(shard, quarter)] * 2,
-        [(len(masks), 8 * shard, quarter) for masks in quarter_order],
-    )
-    column_sum = reduce(plan, column_stacks, *quarter_stages).reshape(4, 2 * shard, quarter)
+    column_sum = third_sum[:columns_rows].reshape(4, 2 * shard, quarter)
     got = [column_sum[0]] + [
         plan.swap(column_sum[n].astype(BF16), m).astype(F32) for n, m in enumerate(split_masks) if n
     ]
@@ -567,10 +585,11 @@
     dm_two = jnp.concatenate([dm, plan.swap(dm, core_bit)])
     grad_out = contract_rows(values, dm_two).astype(BF16)
     dvalues = times_transposed(dm_two, out_full).astype(BF16).reshape(2, rows, half)
-    dqueries, grad_upkey, grad_upvalue, *dkeys = attend_back(
-        queries, query_latent, mixed, lse, dvalues, upkey_full, upvalue_full, keys, query_pos, key_pos, 4
-    )
-    dlatent = reduce(plan, dkeys, ctx_far, ctx_second, ctx_first).astype(BF16).reshape(2 * rows, latent_half)
+    dqueries, grad_upkey, grad_upvalue, keep, send = attend_back(
+        queries, query_latent, mixed, lse, dvalues, upkey_full, upvalue_full, keys, query_pos, key_pos, 2
+    )
+    dlatent = reduce_far(plan, keep.astype(F32) + plan.swap(send, y_bit).astype(F32), z_bits)
+    dlatent = dlatent.astype(BF16).reshape(2 * rows, latent_half)
     dqueries = dqueries.reshape(2 * rows, half)
     shares = times_transposed(dqueries, query_full) + times_transposed(dlatent, latent_full)
     dnormed_one = shares[:rows] + plan.swap(shares[rows:], core_bit)
@@ -578,52 +597,49 @@
     grad_tokens = (dmiddle + dx_norm).astype(BF16)[None]
 
     half_order = reduce_order(*half_stages)
-    blocks, order = [], []
-    for i, masks in enumerate(half_order):
-        for j, m in enumerate(masks):
-            blocks.append((i, j))
-            order.append(owner_half(m))
+    places = [(i, j, m) for i, masks in enumerate(half_order) for j, m in enumerate(masks)]
+    owners = [owner_half(me ^ m) for _, _, m in places]
+    grad_query = contract_rows(normed_one, dqueries).astype(BF16)
     second_stacks = cut_blocks(
-        [grad_upkey, grad_upvalue, grad_out],
-        [[(i, j, 0, 0) for i, j in blocks], [(i, j, 0, pair_width) for i, j in blocks],
-         [(i, j, up_rows, 0) for i, j in blocks]],
-        jnp.stack(order * 3),
-        [(up_shard, pair_width), (up_shard, pair_width), (shard, width)],
-        [(len(masks), up_rows + shard, width) for masks in half_order],
-    )
-    second_sum = plan.deal(reduce(plan, second_stacks, *half_stages), [(plan.top, core_bit)])
-    grad_ups = second_sum[:up_rows].reshape(up_shard, 2 * pair_width)
-    grad_w_out = second_sum[up_rows:]
-
-    grad_query = contract_rows(normed_one, dqueries).astype(BF16)
+        [grad_query, grad_upkey, grad_upvalue, grad_out],
+        [
+            [[(i, j, 0, b * half) for i, j, _ in places for b in (0, 1)]],
+            [[(i, j, shard, 0) for i, j, _ in places]],
+            [[(i, j, shard, pair_width) for i, j, _ in places]],
+            [[(i, j, shard + up_shard, 0) for i, j, _ in places]],
+        ],
+        [[me ^ (m ^ b * core_bit) for _, _, m in places for b in (0, 1)], owners, owners, owners],
+        [(shard, [half]), (up_shard, [pair_width]), (up_shard, [pair_width]), (shard, [width])],
+        [(len(masks),) + second_message.shape for masks in half_order],
+    )
+    second_sum = reduce(plan, second_stacks, *half_stages)
+    own, got = second_sum[:shard, :half], plan.swap(second_sum[:shard, half:].astype(BF16), core_bit).astype(F32)
+    grad_w_query = jnp.concatenate([jnp.where(core == 0, own, got), jnp.where(core == 0, got, own)], 1)
+    dealt = plan.deal(second_sum[shard:].astype(BF16), [(plan.top, core_bit)]).astype(F32)
+    grad_w_out = dealt[up_shard:]
+
     grad_latent = contract_rows(normed_one, dlatent).astype(BF16)
     gain_rows = jnp.concatenate([grad_gain_one.reshape(count, shard), grad_gain_two.reshape(count, shard)], 1)
-    gain_rows = jnp.pad(gain_rows.astype(BF16)[:, None], ((0, 0), (0, INFO - 1), (0, span - 2 * shard)))
-    gain_rows = gain_rows.reshape(count * INFO, span)
-    query_blocks, latent_blocks, info_blocks, order = [], [], [], []
-    for i, masks in enumerate(half_order):
-        for j, m in enumerate(masks):
-            for b in (0, 1):
-                query_blocks.append((i, j, b * band, 0))
-                latent_blocks.append((i, j, b * band, half))
-                info_blocks.append((i, j, b * band + shard, 0))
-                order.append(me ^ (m ^ b * core_bit))
+    gain_rows = jnp.pad(gain_rows.astype(BF16)[:, None], ((0, 0), (0, INFO - 1), (0, latent_half - 2 * shard)))
+    order = [me ^ (m ^ b * core_bit) for _, _, m in places for b in (0, 1)]
     first_stacks = cut_blocks(
-        [grad_query, grad_latent, gain_rows], [query_blocks, latent_blocks, info_blocks],
-        jnp.stack(order * 3),
-        [(shard, half), (shard, latent_half), (INFO, span)],
-        [(len(masks), 2 * band, span) for masks in half_order],
+        [grad_latent, gain_rows.reshape(count * INFO, latent_half)],
+        [
+            [[(i, j, b * band, 0) for i, j, _ in places for b in (0, 1)]],
+            [[(i, j, b * band + shard, 0) for i, j, _ in places for b in (0, 1)]],
+        ],
+        [order, order],
+        [(shard, [latent_half]), (INFO, [latent_half])],
+        [(len(masks), 2 * band, latent_half) for masks in half_order],
     )
     first_sum = reduce(plan, first_stacks, *half_stages)
     own, got = first_sum[:band], plan.swap(first_sum[band:].astype(BF16), core_bit).astype(F32)
-    low, high = jnp.where(core == 0, own, got), jnp.where(core == 0, got, own)
-    grad_w_query = jnp.concatenate([low[:shard, :half], high[:shard, :half]], 1)
-    grad_w_latent = jnp.concatenate([low[:shard, half:], high[:shard, half:]], 1)
+    grad_w_latent = jnp.concatenate([jnp.where(core == 0, own, got), jnp.where(core == 0, got, own)], 1)[:shard]
     gain_sums = own[shard] + got[shard]
 
     return (
         output, grad_tokens, gain_sums[:shard], gain_sums[shard : 2 * shard],
-        grad_w_query, grad_w_latent, grad_ups[:, :pair_width], grad_ups[:, pair_width:],
+        grad_w_query, grad_w_latent, dealt[:up_shard, :pair_width], dealt[:up_shard, pair_width:],
         grad_w_out, grad_w_gate, grad_w_up, grad_w_down,
     )
 

time: 438 us -> 317 us (0.72)
  waiting for transfers between devices: 161 us -> 99.2 us
  starting transfers between devices: 103 us -> 82.2 us
  Pallas kernels: 56.9 us -> 37.2 us
  between operations: 4.47 us -> 18.3 us
  other arithmetic: 41.6 us -> 28.5 us
  matrix products: 34.7 us -> 24 us
  local copies, waits for them, and re-layouts: 35.2 us -> 25.9 us
    ppermute x89 -> x60, waiting for transfers between devices: 161 us -> 99.2 us  [swap(): return lax.ppermute(value, AXES, [(n, n ^ mask) for n in range(self.count)])]
    ppermute x89 -> x60, starting transfers between devices: 94.3 us -> 75.1 us  [swap(): return lax.ppermute(value, AXES, [(n, n ^ mask) for n in range(self.count)])]
    pallas_call x4 -> x3, Pallas kernels: 12 us -> 2.25 us  [cut_blocks(): pl.pallas_call(kernel, out_shape=[jax.ShapeDtypeStruct(shape, BF16) for s...]
    pallas_call x4 -> x3, Pallas kernels: 11.9 us -> 2.17 us  [place_blocks(): pl.pallas_call(kernel, out_shape=[jax.ShapeDtypeStruct(shape, BF16) for s...]
    unnamed x176 -> x138, local copies, waits for them, and re-layouts: 4.42 us -> 12.3 us
    ppermute x3 -> x0, local copies, waits for them, and re-layouts: 5.03 us -> none  [swap(): return lax.ppermute(value, AXES, [(n, n ^ mask) for n in range(self.count)])]
    concatenate x8 -> x3, other arithmetic: 5.76 us -> 1.09 us  [gather(): jnp.concatenate([a for _, a in some])]
    pallas_call x2 -> x0, local copies, waits for them, and re-layouts: 4.55 us -> none  [cut_blocks(): pl.pallas_call(kernel, out_shape=[jax.ShapeDtypeStruct(shape, BF16) for s...]
  transfers between devices with their start and end apart: 91 -> 64, of which waited for: 42 -> 24; matrix products, arithmetic and copies ran while one was open for 22% -> 18% of each run, Pallas kernels for 12% -> 12%
where the time goes in v2:
time: 317 us; the launch traced here: 315 us
  waiting for transfers between devices  99.2 us (31%)
  starting transfers between devices  82.2 us (26%)
  Pallas kernels  37.2 us (12%)
  other arithmetic  28.5 us (9%)
  local copies, waits for them, and re-layouts  25.9 us (8%)
  matrix products  24 us (8%)
  between operations  18.3 us (6%)
    ppermute x60, waiting for transfers between devices, swap(): return lax.ppermute(value, AXES, [(n, n ^ mask) for n in range(self.count)])  99.2 us
    ppermute x60, starting transfers between devices, swap(): return lax.ppermute(value, AXES, [(n, n ^ mask) for n in range(self.count)])  75.1 us
    pallas_call x1, Pallas kernels, attend_back(): pl.pallas_call(attend_back_kernel, grid=(seqs, pairs), in_specs=[pair, wi...  20 us
    pallas_call x1, Pallas kernels, attend(): pl.pallas_call(attend_kernel, grid=(seqs, pairs), in_specs=[pair, up, up,...  12.8 us
    unnamed x138, local copies, waits for them, and re-layouts  12.3 us
    dot_general x7, matrix products, contract_rows(): lax.dot_general(left, right, (((0,), (0,)), ((), ())), preferred_element_...  9.53 us
    dot_general x6, matrix products, times_transposed(): lax.dot_general(left, right, (((1,), (1,)), ((), ())), preferred_element_...  7.49 us
    ppermute x2, starting transfers between devices, deal(): return lax.ppermute(value, AXES, table)  7.04 us
  transfers between devices with their start and end apart: 64, of which 24 were waited for; matrix products, arithmetic and copies ran while one was open for 18% of the time, Pallas kernels for 12%

profile of v2, /device:TPU:1, one launch (start us, length us, event | category | flops | bytes accessed | tf_op | source)
XLA Modules:
  0.0 315.2 jit_solution(2939176292759326489)
XLA Ops:
  8.2 4.5 %collective-permute-start.7 = (bf16[48,1024]{1,0:T(8,128)(2,1)S(1)}, bf16[48,1024]{1,0:T(8,128)(2,1)S(1)}, u32[]{:S(2)}, u32[]{:S(2)}) collective-permute-start(bf16[48,1024]{1,0:T(8,128)(2,1)S(1)} %pad_maximum_fusion.17), channel_id=1, source_target_pairs={{0,0},{1,1},{2,2},{3,3},{4,4},{5,5},{6,6},{7,7},{8,16},{9,17},{10,... | collective-permute-start | bytes 294920 | tf_op jit(solution)/shard_map/ppermute | solution.py:340
  21.4 1.7 collective-permute-start.30
  23.2 1.4 collective-permute-start.2
  24.6 2.4 collective-permute-start.3
  27.0 3.4 %collective-permute-start.4 = (bf16[80,256]{1,0:T(8,128)(2,1)S(1)}, bf16[80,256]{1,0:T(8,128)(2,1)S(1)}, u32[]{:S(2)}, u32[]{:S(2)}) collective-permute-start(bf16[80,256]{1,0:T(8,128)(2,1)S(1)} %get-tuple-element.115), channel_id=1, source_target_pairs={{0,6},{1,7},{2,4},{3,5},{4,2},{5,3},{6,0},{7,1},{8,14},{9,15},{10,... | collective-permute-start | bytes 122888 | tf_op jit(solution)/shard_map/ppermute | solution.py:323
  31.8 1.3 collective-permute-start.5
  33.5 3.5 %collective-permute-start.9 = (bf16[80,1024]{1,0:T(8,128)(2,1)S(1)}, bf16[80,1024]{1,0:T(8,128)(2,1)S(1)}, u32[]{:S(2)}, u32[]{:S(2)}) collective-permute-start(bf16[80,1024]{1,0:T(8,128)(2,1)S(1)} %get-tuple-element.105), channel_id=1, source_target_pairs={{0,4},{1,5},{2,6},{3,7},{4,0},{5,1},{6,2},{7,3},{8,12},{9,13},{10,... | collective-permute-start | bytes 491528 | tf_op jit(solution)/shard_map/ppermute | solution.py:323
  39.9 1.2 collective-permute-start.12
  41.1 2.4 collective-permute-done.9
  43.5 7.0 %collective-permute-done.10 = bf16[80,1024]{1,0:T(8,128)(2,1)S(1)} collective-permute-done((bf16[80,1024]{1,0:T(8,128)(2,1)S(1)}, bf16[80,1024]{1,0:T(8,128)(2,1)S(1)}, u32[]{:S(2)}, u32[]{:S(2)}) %collective-permute-start.10) | collective-permute-done | bytes 163872 | tf_op jit(solution)/shard_map/ppermute | solution.py:323
  54.0 10.4 %collective-permute-start.17 = (bf16[2,128,256]{2,1,0:T(8,128)(2,1)S(1)}, bf16[2,128,256]{2,1,0:T(8,128)(2,1)S(1)}, u32[]{:S(2)}, u32[]{:S(2)}) collective-permute-start(bf16[2,128,256]{2,1,0:T(8,128)(2,1)S(1)} %bitcast.429), channel_id=1, source_target_pairs={{0,2},{1,3},{2,0},{3,1},{4,6},{5,7},{6,4},{7,5},{8,10},{9,11},{10,... | collective-permute-start | bytes 393224 | tf_op jit(solution)/shard_map/ppermute | solution.py:323
  65.2 2.4 collective-permute-start.18
  67.5 1.5 collective-permute-start.19
  70.2 7.5 %collective-permute-done.18 = bf16[2,128,256]{2,1,0:T(8,128)(2,1)S(1)} collective-permute-done((bf16[2,128,256]{2,1,0:T(8,128)(2,1)S(1)}, bf16[2,128,256]{2,1,0:T(8,128)(2,1)S(1)}, u32[]{:S(2)}, u32[]{:S(2)}) %collective-permute-start.18) | collective-permute-done | bytes 131104 | tf_op jit(solution)/shard_map/ppermute | solution.py:323
  79.9 1.9 collective-permute-done.21
  81.8 2.7 collective-permute-done.22
  84.5 5.2 %collective-permute-done.23 = bf16[1,2,128,256]{3,2,1,0:T(8,128)(2,1)S(1)} collective-permute-done((bf16[1,2,128,256]{3,2,1,0:T(8,128)(2,1)S(1)}, bf16[1,2,128,256]{3,2,1,0:T(8,128)(2,1)S(1)}, u32[]{:S(2)}, u32[]{:S(2)}) %collective-permute-start.23) | collective-permute-done | bytes 131104 | tf_op jit(solution)/shard_map/ppermute | solution.py:323
  91.5 1.2 convolution_convert_fusion.7
  92.7 12.8 %attend.1 = (bf16[2,4,256,256]{3,2,1,0:T(8,128)(2,1)}, bf16[2,4,256,256]{3,2,1,0:T(8,128)(2,1)}, f32[2,4,256,1]{3,2,1,0:T(8,128)}, bf16[2,128,512]{2,1,0:T(8,128)(2,1)}) custom-call(bf16[2,128,512]{2,1,0:T(8,128)(2,1)} %bitcast.441, bf16[256,512]{1,0:T(8,128)(2,1)} %bitcast.409, bf16[256,512]{1,0:T(8,128)(2,1)} %bitcast.411, ...), custom_call_target="tpu_custom_call" | custom-call | flops 2147483648 | bytes 6291456 | tf_op jit(solution)/shard_map/attend/pallas_call | solution.py:263
  105.5 1.4 fusion.54
  106.9 11.0 %collective-permute-start.24 = (f32[128,1024]{1,0:T(8,128)S(1)}, f32[128,1024]{1,0:T(8,128)}, u32[]{:S(2)}, u32[]{:S(2)}) collective-permute-start(f32[128,1024]{1,0:T(8,128)S(1)} %slice.369), channel_id=1, source_target_pairs={{0,8},{1,9},{2,10},{3,11},{4,12},{5,13},{6,14},{7,15},{8,0},{9,1},... | collective-permute-start | bytes 1572872 | tf_op jit(solution)/shard_map/ppermute | solution.py:323
  119.6 1.3 multiply_reduce_fusion.6
  123.2 1.5 collective-permute-start.34
  125.6 3.9 %collective-permute-done.26 = bf16[128,1024]{1,0:T(8,128)(2,1)S(1)} collective-permute-done((bf16[128,1024]{1,0:T(8,128)(2,1)S(1)}, bf16[128,1024]{1,0:T(8,128)(2,1)S(1)}, u32[]{:S(2)}, u32[]{:S(2)}) %collective-permute-start.26) | collective-permute-done | bytes 262176 | tf_op jit(solution)/shard_map/ppermute | solution.py:323
  129.6 1.9 collective-permute-start.27
  131.6 3.5 %collective-permute-done.34 = bf16[128,1024]{1,0:T(8,128)(2,1)S(1)} collective-permute-done((bf16[128,1024]{1,0:T(8,128)(2,1)S(1)}, bf16[128,1024]{1,0:T(8,128)(2,1)S(1)}, u32[]{:S(2)}, u32[]{:S(2)}) %collective-permute-start.34) | collective-permute-done | bytes 262176 | tf_op jit(solution)/shard_map/ppermute | solution.py:323
  135.2 1.1 collective-permute-start.35
  136.3 2.5 copy-done.1
  142.7 3.2 %multiply_convert_fusion = (bf16[512,704]{0,1:T(8,128)(2,1)S(1)}, bf16[512,704]{0,1:T(8,128)(2,1)S(1)}, bf16[512,704]{0,1:T(8,128)(2,1)}) fusion(f32[512,704]{0,1:T(8,128)S(1)} %fusion.44, f32[512,704]{0,1:T(8,128)S(1)} %fusion.43, bf16[704,1024]{1,0:T(8,128)(2,1)S(1)} %bitcast.407, bf16[128,1024]{1,0:T(8,128)(2,1)S(1)} %collective-permute-done.35, ...), kind=kOutput, calls=%fused_computation.6 | convolution fusion | flops 747798528 | bytes 7536640 | tf_op jit(solution)/shard_map/dot_general | solution.py:35
  152.2 3.4 %convolution_convert_fusion = bf16[1024,704]{0,1:T(8,128)(2,1)} fusion(bf16[512,704]{0,1:T(8,128)(2,1)} %copy-done.33, bf16[128,1024]{1,0:T(8,128)(2,1)} %copy-done.54, bf16[128,1024]{1,0:T(8,128)(2,1)} %copy-done.49, bf16[128,1024]{1,0:T(8,128)(2,1)} %copy-done.51, bf16[128,1024]{1,0:T(8,128)(2,1)} %copy-done.37), kind=kOutput, calls=%fused_computation | convolution fusion | flops 743112704 | bytes 3211264 | tf_op jit(solution)/shard_map/dot_general | solution.py:31
  155.6 1.9 copy.124
  157.5 2.3 convolution_convert_fusion.2
  160.8 2.3 copy-done
  163.1 1.3 fusion.2
  166.1 6.2 %collective-permute-done.37 = bf16[128,1024]{1,0:T(8,128)(2,1)S(1)} collective-permute-done((bf16[128,1024]{1,0:T(8,128)(2,1)S(1)}, bf16[128,1024]{1,0:T(8,128)(2,1)S(1)}, u32[]{:S(2)}, u32[]{:S(2)}) %collective-permute-start.37) | collective-permute-done | bytes 262176 | tf_op jit(solution)/shard_map/ppermute | solution.py:323
  172.4 2.0 multiply_reduce_fusion.1
  176.9 2.1 fusion.55
  179.1 1.4 convolution_convert_fusion.6
  180.4 20.0 %attend_back.1 = (bf16[2,128,512]{2,1,0:T(8,128)(2,1)}, bf16[256,512]{1,0:T(8,128)(2,1)}, bf16[256,512]{1,0:T(8,128)(2,1)}, bf16[4,2,128,256]{3,2,1,0:T(8,128)(2,1)}, bf16[4,2,128,256]{3,2,1,0:T(8,128)(2,1)}) custom-call(bf16[2,128,512]{2,1,0:T(8,128)(2,1)} %bitcast.442, bf16[2,4,256,256]{3,2,1,0:T(8,128)(2,1)} %get-tuple-element.44.ql_ref, ...), custom_call_target="tpu_custom_call" | custom-call | flops 5368709120 | bytes 8388608 | tf_op jit(solution)/shard_map/attend_back/pallas_call | solution.py:287
  202.1 14.0 %collective-permute-done.39 = bf16[4,2,128,256]{3,2,1,0:T(8,128)(2,1)S(1)} collective-permute-done((bf16[4,2,128,256]{3,2,1,0:T(8,128)(2,1)}, bf16[4,2,128,256]{3,2,1,0:T(8,128)(2,1)S(1)}, u32[]{:S(2)}, u32[]{:S(2)}) %collective-permute-start.39) | collective-permute-done | bytes 524320 | tf_op jit(solution)/shard_map/ppermute | solution.py:323
  216.3 1.8 collective-permute-start.42
  218.1 2.2 collective-permute-start.41
  222.1 9.1 %collective-permute-done.41 = bf16[2,128,256]{2,1,0:T(8,128)(2,1)S(1)} collective-permute-done((bf16[2,128,256]{2,1,0:T(8,128)(2,1)S(1)}, bf16[2,128,256]{2,1,0:T(8,128)(2,1)S(1)}, u32[]{:S(2)}, u32[]{:S(2)}) %collective-permute-start.41) | collective-permute-done | bytes 131104 | tf_op jit(solution)/shard_map/ppermute | solution.py:323
  234.0 1.3 collective-permute-start.43
  237.1 1.5 collective-permute-start.51
  238.6 1.1 add_convert_fusion.1
  239.9 1.6 convolution_convert_fusion.5
  241.5 1.2 multiply_reduce_fusion.2
  244.4 1.5 collective-permute-start.44
  246.5 3.5 %fusion.14 = (bf16[1,128,1024]{2,1,0:T(8,128)(2,1)}, bf16[1,128,1024]{2,1,0:T(8,128)(2,1)}) fusion(f32[256,1024]{1,0:T(8,128)S(1)} %copy-done.20, f32[128]{0:T(128)S(1)} %fusion.33, f32[1024]{0:T(1024)S(1)} %mul.341, f32[128]{0:T(128)} %add_rsqrt_fusion.1, f32[128,1024]{1,0:T(8,128)} %collective-permute-done.43, f32[256,1024]{1,0:T(8,128)} %copy-done.21, ...), kind=kLoop, calls=%fused_computation.69 | loop fusion | flops 2490368 | bytes 4728836 | tf_op jit(solution)/shard_map/broadcast_in_dim | solution.py:597
  250.1 8.6 %collective-permute-done.51 = bf16[4,80,1024]{2,1,0:T(8,128)(2,1)} collective-permute-done((bf16[4,80,1024]{2,1,0:T(8,128)(2,1)S(1)}, bf16[4,80,1024]{2,1,0:T(8,128)(2,1)}, u32[]{:S(2)}, u32[]{:S(2)}) %collective-permute-start.51) | collective-permute-done | bytes 655392 | tf_op jit(solution)/shard_map/ppermute | solution.py:323
  258.7 4.1 %collective-permute-done.53 = bf16[4,80,1024]{2,1,0:T(8,128)(2,1)} collective-permute-done((bf16[4,80,1024]{2,1,0:T(8,128)(2,1)}, bf16[4,80,1024]{2,1,0:T(8,128)(2,1)}, u32[]{:S(2)}, u32[]{:S(2)}) %collective-permute-start.53) | collective-permute-done | bytes 655392 | tf_op jit(solution)/shard_map/ppermute | solution.py:323
  262.8 1.6 add_convert_fusion
  264.5 1.7 collective-permute-start.56
  266.2 2.0 collective-permute-start.54
  268.5 7.2 %collective-permute-done.56 = bf16[80,1024]{1,0:T(8,128)(2,1)S(1)} collective-permute-done((bf16[80,1024]{1,0:T(8,128)(2,1)S(1)}, bf16[80,1024]{1,0:T(8,128)(2,1)S(1)}, u32[]{:S(2)}, u32[]{:S(2)}) %collective-permute-start.56) | collective-permute-done | bytes 163872 | tf_op jit(solution)/shard_map/ppermute | solution.py:323
  275.6 8.1 %collective-permute-done.55 = bf16[80,1024]{1,0:T(8,128)(2,1)S(1)} collective-permute-done((bf16[80,1024]{1,0:T(8,128)(2,1)S(1)}, bf16[80,1024]{1,0:T(8,128)(2,1)S(1)}, u32[]{:S(2)}, u32[]{:S(2)}) %collective-permute-start.55) | collective-permute-done | bytes 163872 | tf_op jit(solution)/shard_map/ppermute | solution.py:323
  283.9 1.8 collective-permute-start.57
  285.6 2.6 collective-permute-start.58
  288.3 1.1 collective-permute-start.49
  289.5 2.5 collective-permute-start.47
  292.0 1.1 collective-permute-done.49
  299.8 2.4 collective-permute-start.61
  305.5 1.6 collective-permute-done.60
  (355 shorter events, 63.1 us)
Async XLA Ops:
  7.2 129.1 %all-gather.3.cloned.1.call-start = ((), (), s32[]{:S(2)}) async-start(), calls=%async_computation.2 | async-start | bytes 5971968 | tf_op jit(solution)/shard_map/all_gather | solution.py:454
  7.2 31.9 %collective-permute-start = (bf16[128,1024]{1,0:T(8,128)(2,1)}, bf16[128,1024]{1,0:T(8,128)(2,1)S(1)}, u32[]{:S(2)}, u32[]{:S(2)}) collective-permute-start(bf16[128,1024]{1,0:T(8,128)(2,1)} %bitcast.417), channel_id=1, source_target_pairs={{0,8},{1,9},{2,10},{3,11},{4,12},{5,13},{6,14},{7,15},{8,0},{9,1},... | collective-permute-start | bytes 786440 | tf_op jit(solution)/shard_map/ppermute | solution.py:323
  8.2 25.2 %collective-permute-start.7 = (bf16[48,1024]{1,0:T(8,128)(2,1)S(1)}, bf16[48,1024]{1,0:T(8,128)(2,1)S(1)}, u32[]{:S(2)}, u32[]{:S(2)}) collective-permute-start(bf16[48,1024]{1,0:T(8,128)(2,1)S(1)} %pad_maximum_fusion.17), channel_id=1, source_target_pairs={{0,0},{1,1},{2,2},{3,3},{4,4},{5,5},{6,6},{7,7},{8,16},{9,17},{10,... | collective-permute-start | bytes 294920 | tf_op jit(solution)/shard_map/ppermute | solution.py:340
  15.7 5.7 %collective-permute-start.1 = (bf16[104,256]{1,0:T(8,128)(2,1)S(1)}, bf16[104,256]{1,0:T(8,128)(2,1)S(1)}, u32[]{:S(2)}, u32[]{:S(2)}) collective-permute-start(bf16[104,256]{1,0:T(8,128)(2,1)S(1)} %pad_maximum_fusion.19), channel_id=1, source_target_pairs={{0,8},{1,9},{2,10},{3,11},{4,12},{5,13},{6,14},{7,15},{8,0},{9,1},... | collective-permute-start | bytes 159752 | tf_op jit(solution)/shard_map/ppermute | solution.py:323
  18.2 5.0 %collective-permute-start.28 = (bf16[64,704]{1,0:T(8,128)(2,1)S(1)}, bf16[64,704]{1,0:T(8,128)(2,1)S(1)}, u32[]{:S(2)}, u32[]{:S(2)}) collective-permute-start(bf16[64,704]{1,0:T(8,128)(2,1)S(1)} %bitcast.437), channel_id=1, source_target_pairs={{0,8},{1,9},{2,10},{3,11},{4,12},{5,13},{6,14},{7,15},{8,0},{9,1},... | collective-permute-start | bytes 270344 | tf_op jit(solution)/shard_map/ppermute | solution.py:323
  18.7 5.9 %collective-permute-start.29 = (bf16[64,704]{1,0:T(8,128)(2,1)S(1)}, bf16[64,704]{1,0:T(8,128)(2,1)S(1)}, u32[]{:S(2)}, u32[]{:S(2)}) collective-permute-start(bf16[64,704]{1,0:T(8,128)(2,1)S(1)} %bitcast.436), channel_id=1, source_target_pairs={{0,16},{1,17},{2,18},{3,19},{4,20},{5,21},{6,22},{7,23},{8,24},{9,... | collective-permute-start | bytes 270344 | tf_op jit(solution)/shard_map/ppermute | solution.py:323
  21.4 5.6 %collective-permute-start.30 = (bf16[64,704]{1,0:T(8,128)(2,1)S(1)}, bf16[64,704]{1,0:T(8,128)(2,1)S(1)}, u32[]{:S(2)}, u32[]{:S(2)}) collective-permute-start(bf16[64,704]{1,0:T(8,128)(2,1)S(1)} %bitcast.438), channel_id=1, source_target_pairs={{0,24},{1,25},{2,26},{3,27},{4,28},{5,29},{6,30},{7,31},{8,16},{9,... | collective-permute-start | bytes 270344 | tf_op jit(solution)/shard_map/ppermute | solution.py:323
  23.2 8.2 %collective-permute-start.2 = (bf16[80,256]{1,0:T(8,128)(2,1)S(1)}, bf16[80,256]{1,0:T(8,128)(2,1)S(1)}, u32[]{:S(2)}, u32[]{:S(2)}) collective-permute-start(bf16[80,256]{1,0:T(8,128)(2,1)S(1)} %get-tuple-element.115), channel_id=1, source_target_pairs={{0,2},{1,3},{2,0},{3,1},{4,6},{5,7},{6,4},{7,5},{8,10},{9,11},{10,... | collective-permute-start | bytes 122888 | tf_op jit(solution)/shard_map/ppermute | solution.py:323
  24.6 6.8 %collective-permute-start.3 = (bf16[80,256]{1,0:T(8,128)(2,1)S(1)}, bf16[80,256]{1,0:T(8,128)(2,1)S(1)}, u32[]{:S(2)}, u32[]{:S(2)}) collective-permute-start(bf16[80,256]{1,0:T(8,128)(2,1)S(1)} %get-tuple-element.115), channel_id=1, source_target_pairs={{0,4},{1,5},{2,6},{3,7},{4,0},{5,1},{6,2},{7,3},{8,12},{9,13},{10,... | collective-permute-start | bytes 122888 | tf_op jit(solution)/shard_map/ppermute | solution.py:323
  27.0 4.8 %collective-permute-start.4 = (bf16[80,256]{1,0:T(8,128)(2,1)S(1)}, bf16[80,256]{1,0:T(8,128)(2,1)S(1)}, u32[]{:S(2)}, u32[]{:S(2)}) collective-permute-start(bf16[80,256]{1,0:T(8,128)(2,1)S(1)} %get-tuple-element.115), channel_id=1, source_target_pairs={{0,6},{1,7},{2,4},{3,5},{4,2},{5,3},{6,0},{7,1},{8,14},{9,15},{10,... | collective-permute-start | bytes 122888 | tf_op jit(solution)/shard_map/ppermute | solution.py:323
  31.3 266.5 %reduce-scatter.2.cloned.1.call-start = ((), (), s32[]{:S(2)}) async-start(), calls=%async_computation.1 | async-start | bytes 5971968 | tf_op jit(solution)/shard_map/reduce_scatter | solution.py:567
  31.8 5.2 %collective-permute-start.5 = (bf16[4,80,256]{2,1,0:T(8,128)(2,1)S(1)}, bf16[4,80,256]{2,1,0:T(8,128)(2,1)S(1)}, u32[]{:S(2)}, u32[]{:S(2)}) collective-permute-start(bf16[4,80,256]{2,1,0:T(8,128)(2,1)S(1)} %pad_maximum_fusion.14), channel_id=1, source_target_pairs={{0,1},{1,0},{2,3},{3,2},{4,5},{5,4},{6,7},{7,6},{8,9},{9,8},{10,11... | collective-permute-start | bytes 491528 | tf_op jit(solution)/shard_map/ppermute | solution.py:323
  33.5 6.4 %collective-permute-start.8 = (bf16[80,1024]{1,0:T(8,128)(2,1)S(1)}, bf16[80,1024]{1,0:T(8,128)(2,1)S(1)}, u32[]{:S(2)}, u32[]{:S(2)}) collective-permute-start(bf16[80,1024]{1,0:T(8,128)(2,1)S(1)} %get-tuple-element.105), channel_id=1, source_target_pairs={{0,2},{1,3},{2,0},{3,1},{4,6},{5,7},{6,4},{7,5},{8,10},{9,11},{10,... | collective-permute-start | bytes 491528 | tf_op jit(solution)/shard_map/ppermute | solution.py:323
  33.5 10.0 %collective-permute-start.9 = (bf16[80,1024]{1,0:T(8,128)(2,1)S(1)}, bf16[80,1024]{1,0:T(8,128)(2,1)S(1)}, u32[]{:S(2)}, u32[]{:S(2)}) collective-permute-start(bf16[80,1024]{1,0:T(8,128)(2,1)S(1)} %get-tuple-element.105), channel_id=1, source_target_pairs={{0,4},{1,5},{2,6},{3,7},{4,0},{5,1},{6,2},{7,3},{8,12},{9,13},{10,... | collective-permute-start | bytes 491528 | tf_op jit(solution)/shard_map/ppermute | solution.py:323
  37.0 13.5 %collective-permute-start.10 = (bf16[80,1024]{1,0:T(8,128)(2,1)S(1)}, bf16[80,1024]{1,0:T(8,128)(2,1)S(1)}, u32[]{:S(2)}, u32[]{:S(2)}) collective-permute-start(bf16[80,1024]{1,0:T(8,128)(2,1)S(1)} %get-tuple-element.105), channel_id=1, source_target_pairs={{0,6},{1,7},{2,4},{3,5},{4,2},{5,3},{6,0},{7,1},{8,14},{9,15},{10,... | collective-permute-start | bytes 491528 | tf_op jit(solution)/shard_map/ppermute | solution.py:323
  37.1 17.0 %collective-permute-start.11 = (bf16[1,80,1024]{2,1,0:T(8,128)(2,1)S(1)}, bf16[1,80,1024]{2,1,0:T(8,128)(2,1)S(1)}, u32[]{:S(2)}, u32[]{:S(2)}) collective-permute-start(bf16[1,80,1024]{2,1,0:T(8,128)(2,1)S(1)} %get-tuple-element.106.refs_0_), channel_id=1, source_target_pairs={{0,1},{1,0},{2,3},{3,2},{4,5},{5,4},{6,7},{7,6},{8,9},{9,8},{10,11... | collective-permute-start | bytes 491528 | tf_op jit(solution)/shard_map/ppermute | solution.py:323
  39.1 12.6 %collective-permute-start.6 = (bf16[8,80,256]{2,1,0:T(8,128)(2,1)S(1)}, bf16[8,80,256]{2,1,0:T(8,128)(2,1)S(1)}, u32[]{:S(2)}, u32[]{:S(2)}) collective-permute-start(bf16[8,80,256]{2,1,0:T(8,128)(2,1)S(1)} %constant_dynamic-update-slice_fusion), channel_id=1, source_target_pairs={{0,16},{1,17},{2,18},{3,19},{4,20},{5,21},{6,22},{7,23},{8,24},{9,... | collective-permute-start | bytes 983048 | tf_op jit(solution)/shard_map/ppermute | solution.py:323
  39.9 24.5 %collective-permute-start.12 = (bf16[1,80,1024]{2,1,0:T(8,128)(2,1)S(1)}, bf16[1,80,1024]{2,1,0:T(8,128)(2,1)S(1)}, u32[]{:S(2)}, u32[]{:S(2)}) collective-permute-start(bf16[1,80,1024]{2,1,0:T(8,128)(2,1)S(1)} %bitcast.384), channel_id=1, source_target_pairs={{0,1},{1,0},{2,3},{3,2},{4,5},{5,4},{6,7},{7,6},{8,9},{9,8},{10,11... | collective-permute-start | bytes 491528 | tf_op jit(solution)/shard_map/ppermute | solution.py:323
  43.5 20.9 %collective-permute-start.13 = (bf16[1,80,1024]{2,1,0:T(8,128)(2,1)S(1)}, bf16[1,80,1024]{2,1,0:T(8,128)(2,1)S(1)}, u32[]{:S(2)}, u32[]{:S(2)}) collective-permute-start(bf16[1,80,1024]{2,1,0:T(8,128)(2,1)S(1)} %bitcast.387), channel_id=1, source_target_pairs={{0,1},{1,0},{2,3},{3,2},{4,5},{5,4},{6,7},{7,6},{8,9},{9,8},{10,11... | collective-permute-start | bytes 491528 | tf_op jit(solution)/shard_map/ppermute | solution.py:323
  50.5 13.9 %collective-permute-start.14 = (bf16[1,80,1024]{2,1,0:T(8,128)(2,1)S(1)}, bf16[1,80,1024]{2,1,0:T(8,128)(2,1)S(1)}, u32[]{:S(2)}, u32[]{:S(2)}) collective-permute-start(bf16[1,80,1024]{2,1,0:T(8,128)(2,1)S(1)} %bitcast.390), channel_id=1, source_target_pairs={{0,1},{1,0},{2,3},{3,2},{4,5},{5,4},{6,7},{7,6},{8,9},{9,8},{10,11... | collective-permute-start | bytes 491528 | tf_op jit(solution)/shard_map/ppermute | solution.py:323
  51.7 38.0 %collective-permute-start.15 = (bf16[4,80,1024]{2,1,0:T(8,128)(2,1)}, bf16[4,80,1024]{2,1,0:T(8,128)(2,1)S(1)}, u32[]{:S(2)}, u32[]{:S(2)}) collective-permute-start(bf16[4,80,1024]{2,1,0:T(8,128)(2,1)} %pad_maximum_fusion.5), channel_id=1, source_target_pairs={{0,16},{1,17},{2,18},{3,19},{4,20},{5,21},{6,22},{7,23},{8,24},{9,... | collective-permute-start | bytes 1966088 | tf_op jit(solution)/shard_map/ppermute | solution.py:323
  54.0 15.9 %collective-permute-start.17 = (bf16[2,128,256]{2,1,0:T(8,128)(2,1)S(1)}, bf16[2,128,256]{2,1,0:T(8,128)(2,1)S(1)}, u32[]{:S(2)}, u32[]{:S(2)}) collective-permute-start(bf16[2,128,256]{2,1,0:T(8,128)(2,1)S(1)} %bitcast.429), channel_id=1, source_target_pairs={{0,2},{1,3},{2,0},{3,1},{4,6},{5,7},{6,4},{7,5},{8,10},{9,11},{10,... | collective-permute-start | bytes 393224 | tf_op jit(solution)/shard_map/ppermute | solution.py:323
  64.5 25.2 %collective-permute-start.16 = (bf16[4,80,1024]{2,1,0:T(8,128)(2,1)S(1)}, bf16[4,80,1024]{2,1,0:T(8,128)(2,1)S(1)}, u32[]{:S(2)}, u32[]{:S(2)}) collective-permute-start(bf16[4,80,1024]{2,1,0:T(8,128)(2,1)S(1)} %pad_maximum_fusion.6), channel_id=1, source_target_pairs={{0,16},{1,17},{2,18},{3,19},{4,20},{5,21},{6,22},{7,23},{8,24},{9,... | collective-permute-start | bytes 1966088 | tf_op jit(solution)/shard_map/ppermute | solution.py:323
  65.2 12.5 %collective-permute-start.18 = (bf16[2,128,256]{2,1,0:T(8,128)(2,1)S(1)}, bf16[2,128,256]{2,1,0:T(8,128)(2,1)S(1)}, u32[]{:S(2)}, u32[]{:S(2)}) collective-permute-start(bf16[2,128,256]{2,1,0:T(8,128)(2,1)S(1)} %bitcast.430), channel_id=1, source_target_pairs={{0,4},{1,5},{2,6},{3,7},{4,0},{5,1},{6,2},{7,3},{8,12},{9,13},{10,... | collective-permute-start | bytes 393224 | tf_op jit(solution)/shard_map/ppermute | solution.py:323
  67.5 10.7 %collective-permute-start.19 = (bf16[2,128,256]{2,1,0:T(8,128)(2,1)S(1)}, bf16[2,128,256]{2,1,0:T(8,128)(2,1)S(1)}, u32[]{:S(2)}, u32[]{:S(2)}) collective-permute-start(bf16[2,128,256]{2,1,0:T(8,128)(2,1)S(1)} %bitcast.432), channel_id=1, source_target_pairs={{0,6},{1,7},{2,4},{3,5},{4,2},{5,3},{6,0},{7,1},{8,14},{9,15},{10,... | collective-permute-start | bytes 393224 | tf_op jit(solution)/shard_map/ppermute | solution.py:323
  69.9 9.3 %collective-permute-start.20 = (bf16[1,2,128,256]{3,2,1,0:T(8,128)(2,1)S(1)}, bf16[1,2,128,256]{3,2,1,0:T(8,128)(2,1)S(1)}, u32[]{:S(2)}, u32[]{:S(2)}) collective-permute-start(bf16[1,2,128,256]{3,2,1,0:T(8,128)(2,1)S(1)} %bitcast.433), channel_id=1, source_target_pairs={{0,1},{1,0},{2,3},{3,2},{4,5},{5,4},{6,7},{7,6},{8,9},{9,8},{10,11... | collective-permute-start | bytes 393224 | tf_op jit(solution)/shard_map/ppermute | solution.py:323
  77.7 4.1 %collective-permute-start.21 = (bf16[1,2,128,256]{3,2,1,0:T(8,128)(2,1)S(1)}, bf16[1,2,128,256]{3,2,1,0:T(8,128)(2,1)S(1)}, u32[]{:S(2)}, u32[]{:S(2)}) collective-permute-start(bf16[1,2,128,256]{3,2,1,0:T(8,128)(2,1)S(1)} %bitcast.428), channel_id=1, source_target_pairs={{0,1},{1,0},{2,3},{3,2},{4,5},{5,4},{6,7},{7,6},{8,9},{9,8},{10,11... | collective-permute-start | bytes 393224 | tf_op jit(solution)/shard_map/ppermute | solution.py:323
  78.3 6.2 %collective-permute-start.22 = (bf16[1,2,128,256]{3,2,1,0:T(8,128)(2,1)S(1)}, bf16[1,2,128,256]{3,2,1,0:T(8,128)(2,1)S(1)}, u32[]{:S(2)}, u32[]{:S(2)}) collective-permute-start(bf16[1,2,128,256]{3,2,1,0:T(8,128)(2,1)S(1)} %bitcast.435), channel_id=1, source_target_pairs={{0,1},{1,0},{2,3},{3,2},{4,5},{5,4},{6,7},{7,6},{8,9},{9,8},{10,11... | collective-permute-start | bytes 393224 | tf_op jit(solution)/shard_map/ppermute | solution.py:323
  79.3 10.4 %collective-permute-start.23 = (bf16[1,2,128,256]{3,2,1,0:T(8,128)(2,1)S(1)}, bf16[1,2,128,256]{3,2,1,0:T(8,128)(2,1)S(1)}, u32[]{:S(2)}, u32[]{:S(2)}) collective-permute-start(bf16[1,2,128,256]{3,2,1,0:T(8,128)(2,1)S(1)} %bitcast.434), channel_id=1, source_target_pairs={{0,1},{1,0},{2,3},{3,2},{4,5},{5,4},{6,7},{7,6},{8,9},{9,8},{10,11... | collective-permute-start | bytes 393224 | tf_op jit(solution)/shard_map/ppermute | solution.py:323
  106.9 12.7 %collective-permute-start.24 = (f32[128,1024]{1,0:T(8,128)S(1)}, f32[128,1024]{1,0:T(8,128)}, u32[]{:S(2)}, u32[]{:S(2)}) collective-permute-start(f32[128,1024]{1,0:T(8,128)S(1)} %slice.369), channel_id=1, source_target_pairs={{0,8},{1,9},{2,10},{3,11},{4,12},{5,13},{6,14},{7,15},{8,0},{9,1},... | collective-permute-start | bytes 1572872 | tf_op jit(solution)/shard_map/ppermute | solution.py:323
  121.9 7.7 %collective-permute-start.26 = (bf16[128,1024]{1,0:T(8,128)(2,1)S(1)}, bf16[128,1024]{1,0:T(8,128)(2,1)S(1)}, u32[]{:S(2)}, u32[]{:S(2)}) collective-permute-start(bf16[128,1024]{1,0:T(8,128)(2,1)S(1)} %multiply_convert_fusion.4), channel_id=1, source_target_pairs={{0,16},{1,17},{2,18},{3,19},{4,20},{5,21},{6,22},{7,23},{8,24},{9,... | collective-permute-start | bytes 786440 | tf_op jit(solution)/shard_map/ppermute | solution.py:323
  123.2 12.0 %collective-permute-start.34 = (bf16[128,1024]{1,0:T(8,128)(2,1)S(1)}, bf16[128,1024]{1,0:T(8,128)(2,1)S(1)}, u32[]{:S(2)}, u32[]{:S(2)}) collective-permute-start(bf16[128,1024]{1,0:T(8,128)(2,1)S(1)} %bitcast_convert_fusion), channel_id=1, source_target_pairs={{0,16},{1,17},{2,18},{3,19},{4,20},{5,21},{6,22},{7,23},{8,24},{9,... | collective-permute-start | bytes 786440 | tf_op jit(solution)/shard_map/ppermute | solution.py:323
  124.7 15.0 %collective-permute-start.25 = (bf16[128,1024]{1,0:T(8,128)(2,1)S(1)}, bf16[128,1024]{1,0:T(8,128)(2,1)S(1)}, u32[]{:S(2)}, u32[]{:S(2)}) collective-permute-start(bf16[128,1024]{1,0:T(8,128)(2,1)S(1)} %multiply_convert_fusion.4), channel_id=1, source_target_pairs={{0,8},{1,9},{2,10},{3,11},{4,12},{5,13},{6,14},{7,15},{8,0},{9,1},... | collective-permute-start | bytes 786440 | tf_op jit(solution)/shard_map/ppermute | solution.py:323
  129.6 10.1 %collective-permute-start.27 = (bf16[128,1024]{1,0:T(8,128)(2,1)S(1)}, bf16[128,1024]{1,0:T(8,128)(2,1)S(1)}, u32[]{:S(2)}, u32[]{:S(2)}) collective-permute-start(bf16[128,1024]{1,0:T(8,128)(2,1)S(1)} %collective-permute-done.26), channel_id=1, source_target_pairs={{0,8},{1,9},{2,10},{3,11},{4,12},{5,13},{6,14},{7,15},{8,0},{9,1},... | collective-permute-start | bytes 786440 | tf_op jit(solution)/shard_map/ppermute | solution.py:323
  131.5 10.5 %collective-permute-start.33 = (bf16[128,1024]{1,0:T(8,128)(2,1)S(1)}, bf16[128,1024]{1,0:T(8,128)(2,1)S(1)}, u32[]{:S(2)}, u32[]{:S(2)}) collective-permute-start(bf16[128,1024]{1,0:T(8,128)(2,1)S(1)} %bitcast_convert_fusion), channel_id=1, source_target_pairs={{0,8},{1,9},{2,10},{3,11},{4,12},{5,13},{6,14},{7,15},{8,0},{9,1},... | collective-permute-start | bytes 786440 | tf_op jit(solution)/shard_map/ppermute | solution.py:323
  135.2 6.8 %collective-permute-start.35 = (bf16[128,1024]{1,0:T(8,128)(2,1)S(1)}, bf16[128,1024]{1,0:T(8,128)(2,1)S(1)}, u32[]{:S(2)}, u32[]{:S(2)}) collective-permute-start(bf16[128,1024]{1,0:T(8,128)(2,1)S(1)} %collective-permute-done.34), channel_id=1, source_target_pairs={{0,8},{1,9},{2,10},{3,11},{4,12},{5,13},{6,14},{7,15},{8,0},{9,1},... | collective-permute-start | bytes 786440 | tf_op jit(solution)/shard_map/ppermute | solution.py:323
  149.8 13.4 %collective-permute-start.36 = (f32[2,128,1024]{2,1,0:T(8,128)}, f32[2,128,1024]{2,1,0:T(8,128)}, u32[]{:S(2)}, u32[]{:S(2)}) collective-permute-start(f32[2,128,1024]{2,1,0:T(8,128)} %pad_maximum_fusion.3), channel_id=1, source_target_pairs={{0,8},{1,9},{2,10},{3,11},{4,12},{5,13},{6,14},{7,15},{8,0},{9,1},... | collective-permute-start | bytes 3145736 | tf_op jit(solution)/shard_map/ppermute | solution.py:323
  164.5 7.9 %collective-permute-start.37 = (bf16[128,1024]{1,0:T(8,128)(2,1)S(1)}, bf16[128,1024]{1,0:T(8,128)(2,1)S(1)}, u32[]{:S(2)}, u32[]{:S(2)}) collective-permute-start(bf16[128,1024]{1,0:T(8,128)(2,1)S(1)} %fusion.2), channel_id=1, source_target_pairs={{0,16},{1,17},{2,18},{3,19},{4,20},{5,21},{6,22},{7,23},{8,24},{9,... | collective-permute-start | bytes 786440 | tf_op jit(solution)/shard_map/ppermute | solution.py:323
  175.9 3.1 collective-permute-start.38
  200.5 15.7 %collective-permute-start.39 = (bf16[4,2,128,256]{3,2,1,0:T(8,128)(2,1)}, bf16[4,2,128,256]{3,2,1,0:T(8,128)(2,1)S(1)}, u32[]{:S(2)}, u32[]{:S(2)}) collective-permute-start(bf16[4,2,128,256]{3,2,1,0:T(8,128)(2,1)} %get-tuple-element.49), channel_id=1, source_target_pairs={{0,1},{1,0},{2,3},{3,2},{4,5},{5,4},{6,7},{7,6},{8,9},{9,8},{10,11... | collective-permute-start | bytes 1572872 | tf_op jit(solution)/shard_map/ppermute | solution.py:323
  201.0 34.3 %collective-permute-start.31 = (f32[2,128,1024]{2,1,0:T(8,128)S(1)}, f32[2,128,1024]{2,1,0:T(8,128)S(1)}, u32[]{:S(2)}, u32[]{:S(2)}) collective-permute-start(f32[2,128,1024]{2,1,0:T(8,128)S(1)} %pad_maximum_fusion.1), channel_id=1, source_target_pairs={{0,8},{1,9},{2,10},{3,11},{4,12},{5,13},{6,14},{7,15},{8,0},{9,1},... | collective-permute-start | bytes 3145736 | tf_op jit(solution)/shard_map/ppermute | solution.py:323
  216.3 5.8 %collective-permute-start.42 = (bf16[2,128,256]{2,1,0:T(8,128)(2,1)S(1)}, bf16[2,128,256]{2,1,0:T(8,128)(2,1)S(1)}, u32[]{:S(2)}, u32[]{:S(2)}) collective-permute-start(bf16[2,128,256]{2,1,0:T(8,128)(2,1)S(1)} %get-tuple-element.94), channel_id=1, source_target_pairs={{0,6},{1,7},{2,4},{3,5},{4,2},{5,3},{6,0},{7,1},{8,14},{9,15},{10,... | collective-permute-start | bytes 393224 | tf_op jit(solution)/shard_map/ppermute | solution.py:323
  218.1 13.1 %collective-permute-start.41 = (bf16[2,128,256]{2,1,0:T(8,128)(2,1)S(1)}, bf16[2,128,256]{2,1,0:T(8,128)(2,1)S(1)}, u32[]{:S(2)}, u32[]{:S(2)}) collective-permute-start(bf16[2,128,256]{2,1,0:T(8,128)(2,1)S(1)} %get-tuple-element.95), channel_id=1, source_target_pairs={{0,4},{1,5},{2,6},{3,7},{4,0},{5,1},{6,2},{7,3},{8,12},{9,13},{10,... | collective-permute-start | bytes 393224 | tf_op jit(solution)/shard_map/ppermute | solution.py:323
  220.3 11.0 %collective-permute-start.40 = (bf16[2,128,256]{2,1,0:T(8,128)(2,1)S(1)}, bf16[2,128,256]{2,1,0:T(8,128)(2,1)S(1)}, u32[]{:S(2)}, u32[]{:S(2)}) collective-permute-start(bf16[2,128,256]{2,1,0:T(8,128)(2,1)S(1)} %get-tuple-element.93), channel_id=1, source_target_pairs={{0,2},{1,3},{2,0},{3,1},{4,6},{5,7},{6,4},{7,5},{8,10},{9,11},{10,... | collective-permute-start | bytes 393224 | tf_op jit(solution)/shard_map/ppermute | solution.py:323
  221.7 16.8 %collective-permute-start.52 = (bf16[4,80,1024]{2,1,0:T(8,128)(2,1)S(1)}, bf16[4,80,1024]{2,1,0:T(8,128)(2,1)S(1)}, u32[]{:S(2)}, u32[]{:S(2)}) collective-permute-start(bf16[4,80,1024]{2,1,0:T(8,128)(2,1)S(1)} %get-tuple-element.59), channel_id=1, source_target_pairs={{0,16},{1,17},{2,18},{3,19},{4,20},{5,21},{6,22},{7,23},{8,24},{9,... | collective-permute-start | bytes 1966088 | tf_op jit(solution)/shard_map/ppermute | solution.py:323
  234.0 7.5 %collective-permute-start.43 = (f32[128,1024]{1,0:T(8,128)}, f32[128,1024]{1,0:T(8,128)}, u32[]{:S(2)}, u32[]{:S(2)}) collective-permute-start(f32[128,1024]{1,0:T(8,128)} %slice.388), channel_id=1, source_target_pairs={{0,8},{1,9},{2,10},{3,11},{4,12},{5,13},{6,14},{7,15},{8,0},{9,1},... | collective-permute-start | bytes 1572872 | tf_op jit(solution)/shard_map/ppermute | solution.py:323
  236.4 10.1 %collective-permute-start.32 = (bf16[128,1024]{1,0:T(8,128)(2,1)}, bf16[128,1024]{1,0:T(8,128)(2,1)}, u32[]{:S(2)}, u32[]{:S(2)}) collective-permute-start(bf16[128,1024]{1,0:T(8,128)(2,1)} %fusion.6), channel_id=1, source_target_pairs={{0,16},{1,17},{2,18},{3,19},{4,20},{5,21},{6,22},{7,23},{8,24},{9,... | collective-permute-start | bytes 786440 | tf_op jit(solution)/shard_map/ppermute | solution.py:323
  237.1 21.6 %collective-permute-start.51 = (bf16[4,80,1024]{2,1,0:T(8,128)(2,1)S(1)}, bf16[4,80,1024]{2,1,0:T(8,128)(2,1)}, u32[]{:S(2)}, u32[]{:S(2)}) collective-permute-start(bf16[4,80,1024]{2,1,0:T(8,128)(2,1)S(1)} %get-tuple-element.57), channel_id=1, source_target_pairs={{0,16},{1,17},{2,18},{3,19},{4,20},{5,21},{6,22},{7,23},{8,24},{9,... | collective-permute-start | bytes 1966088 | tf_op jit(solution)/shard_map/ppermute | solution.py:323
  239.7 23.2 %collective-permute-start.53 = (bf16[4,80,1024]{2,1,0:T(8,128)(2,1)}, bf16[4,80,1024]{2,1,0:T(8,128)(2,1)}, u32[]{:S(2)}, u32[]{:S(2)}) collective-permute-start(bf16[4,80,1024]{2,1,0:T(8,128)(2,1)} %add_convert_fusion.1), channel_id=1, source_target_pairs={{0,1},{1,0},{2,3},{3,2},{4,5},{5,4},{6,7},{7,6},{8,9},{9,8},{10,11... | collective-permute-start | bytes 1966088 | tf_op jit(solution)/shard_map/ppermute | solution.py:323
  244.3 23.8 %collective-permute-start.45 = (bf16[4,80,256]{2,1,0:T(8,128)(2,1)S(1)}, bf16[4,80,256]{2,1,0:T(8,128)(2,1)S(1)}, u32[]{:S(2)}, u32[]{:S(2)}) collective-permute-start(bf16[4,80,256]{2,1,0:T(8,128)(2,1)S(1)} %get-tuple-element.53), channel_id=1, source_target_pairs={{0,16},{1,17},{2,18},{3,19},{4,20},{5,21},{6,22},{7,23},{8,24},{9,... | collective-permute-start | bytes 491528 | tf_op jit(solution)/shard_map/ppermute | solution.py:323
  244.4 43.8 %collective-permute-start.44 = (bf16[4,80,256]{2,1,0:T(8,128)(2,1)S(1)}, bf16[4,80,256]{2,1,0:T(8,128)(2,1)S(1)}, u32[]{:S(2)}, u32[]{:S(2)}) collective-permute-start(bf16[4,80,256]{2,1,0:T(8,128)(2,1)S(1)} %get-tuple-element.51), channel_id=1, source_target_pairs={{0,16},{1,17},{2,18},{3,19},{4,20},{5,21},{6,22},{7,23},{8,24},{9,... | collective-permute-start | bytes 491528 | tf_op jit(solution)/shard_map/ppermute | solution.py:323
  264.5 11.1 %collective-permute-start.56 = (bf16[80,1024]{1,0:T(8,128)(2,1)S(1)}, bf16[80,1024]{1,0:T(8,128)(2,1)S(1)}, u32[]{:S(2)}, u32[]{:S(2)}) collective-permute-start(bf16[80,1024]{1,0:T(8,128)(2,1)S(1)} %get-tuple-element.89), channel_id=1, source_target_pairs={{0,6},{1,7},{2,4},{3,5},{4,2},{5,3},{6,0},{7,1},{8,14},{9,15},{10,... | collective-permute-start | bytes 491528 | tf_op jit(solution)/shard_map/ppermute | solution.py:323
  266.2 17.6 %collective-permute-start.55 = (bf16[80,1024]{1,0:T(8,128)(2,1)S(1)}, bf16[80,1024]{1,0:T(8,128)(2,1)S(1)}, u32[]{:S(2)}, u32[]{:S(2)}) collective-permute-start(bf16[80,1024]{1,0:T(8,128)(2,1)S(1)} %get-tuple-element.90), channel_id=1, source_target_pairs={{0,4},{1,5},{2,6},{3,7},{4,0},{5,1},{6,2},{7,3},{8,12},{9,13},{10,... | collective-permute-start | bytes 491528 | tf_op jit(solution)/shard_map/ppermute | solution.py:323
  266.2 17.6 %collective-permute-start.54 = (bf16[80,1024]{1,0:T(8,128)(2,1)S(1)}, bf16[80,1024]{1,0:T(8,128)(2,1)S(1)}, u32[]{:S(2)}, u32[]{:S(2)}) collective-permute-start(bf16[80,1024]{1,0:T(8,128)(2,1)S(1)} %get-tuple-element.88), channel_id=1, source_target_pairs={{0,2},{1,3},{2,0},{3,1},{4,6},{5,7},{6,4},{7,5},{8,10},{9,11},{10,... | collective-permute-start | bytes 491528 | tf_op jit(solution)/shard_map/ppermute | solution.py:323
  268.2 20.1 %collective-permute-start.46 = (bf16[4,80,256]{2,1,0:T(8,128)(2,1)S(1)}, bf16[4,80,256]{2,1,0:T(8,128)(2,1)S(1)}, u32[]{:S(2)}, u32[]{:S(2)}) collective-permute-start(bf16[4,80,256]{2,1,0:T(8,128)(2,1)S(1)} %add_convert_fusion.4), channel_id=1, source_target_pairs={{0,1},{1,0},{2,3},{3,2},{4,5},{5,4},{6,7},{7,6},{8,9},{9,8},{10,11... | collective-permute-start | bytes 491528 | tf_op jit(solution)/shard_map/ppermute | solution.py:323
  283.9 8.1 %collective-permute-start.57 = (bf16[32,512]{1,0:T(8,128)(2,1)S(1)}, bf16[32,512]{1,0:T(8,128)(2,1)S(1)}, u32[]{:S(2)}, u32[]{:S(2)}) collective-permute-start(bf16[32,512]{1,0:T(8,128)(2,1)S(1)} %slice.403), channel_id=1, source_target_pairs={{0,8},{1,9},{2,10},{3,11},{4,12},{5,13},{6,14},{7,15},{8,0},{9,1},... | collective-permute-start | bytes 98312 | tf_op jit(solution)/shard_map/ppermute | solution.py:323
  285.6 10.8 %collective-permute-start.58 = (bf16[48,1024]{1,0:T(8,128)(2,1)S(1)}, bf16[48,1024]{1,0:T(8,128)(2,1)S(1)}, u32[]{:S(2)}, u32[]{:S(2)}) collective-permute-start(bf16[48,1024]{1,0:T(8,128)(2,1)S(1)} %slice.405), channel_id=1, source_target_pairs={{0,0},{1,1},{2,2},{3,3},{4,4},{5,5},{6,6},{7,7},{8,16},{9,17},{10,... | collective-permute-start | bytes 294920 | tf_op jit(solution)/shard_map/ppermute | solution.py:340
  288.3 4.8 %collective-permute-start.49 = (bf16[80,256]{1,0:T(8,128)(2,1)S(1)}, bf16[80,256]{1,0:T(8,128)(2,1)S(1)}, u32[]{:S(2)}, u32[]{:S(2)}) collective-permute-start(bf16[80,256]{1,0:T(8,128)(2,1)S(1)} %get-tuple-element.103), channel_id=1, source_target_pairs={{0,6},{1,7},{2,4},{3,5},{4,2},{5,3},{6,0},{7,1},{8,14},{9,15},{10,... | collective-permute-start | bytes 122888 | tf_op jit(solution)/shard_map/ppermute | solution.py:323
  289.5 4.5 %collective-permute-start.48 = (bf16[80,256]{1,0:T(8,128)(2,1)S(1)}, bf16[80,256]{1,0:T(8,128)(2,1)S(1)}, u32[]{:S(2)}, u32[]{:S(2)}) collective-permute-start(bf16[80,256]{1,0:T(8,128)(2,1)S(1)} %get-tuple-element.104), channel_id=1, source_target_pairs={{0,4},{1,5},{2,6},{3,7},{4,0},{5,1},{6,2},{7,3},{8,12},{9,13},{10,... | collective-permute-start | bytes 122888 | tf_op jit(solution)/shard_map/ppermute | solution.py:323
  289.5 4.5 %collective-permute-start.47 = (bf16[80,256]{1,0:T(8,128)(2,1)S(1)}, bf16[80,256]{1,0:T(8,128)(2,1)S(1)}, u32[]{:S(2)}, u32[]{:S(2)}) collective-permute-start(bf16[80,256]{1,0:T(8,128)(2,1)S(1)} %get-tuple-element.102), channel_id=1, source_target_pairs={{0,2},{1,3},{2,0},{3,1},{4,6},{5,7},{6,4},{7,5},{8,10},{9,11},{10,... | collective-permute-start | bytes 122888 | tf_op jit(solution)/shard_map/ppermute | solution.py:323
  294.0 1.3 collective-permute-start.50
  299.8 5.6 %collective-permute-start.61 = (bf16[64,704]{1,0:T(8,128)(2,1)S(1)}, bf16[64,704]{1,0:T(8,128)(2,1)S(1)}, u32[]{:S(2)}, u32[]{:S(2)}) collective-permute-start(bf16[64,704]{1,0:T(8,128)(2,1)S(1)} %get-tuple-element.86), channel_id=1, source_target_pairs={{0,24},{1,25},{2,26},{3,27},{4,28},{5,29},{6,30},{7,31},{8,16},{9,... | collective-permute-start | bytes 270344 | tf_op jit(solution)/shard_map/ppermute | solution.py:323
  302.2 4.8 %collective-permute-start.60 = (bf16[64,704]{1,0:T(8,128)(2,1)S(1)}, bf16[64,704]{1,0:T(8,128)(2,1)S(1)}, u32[]{:S(2)}, u32[]{:S(2)}) collective-permute-start(bf16[64,704]{1,0:T(8,128)(2,1)S(1)} %get-tuple-element.87), channel_id=1, source_target_pairs={{0,16},{1,17},{2,18},{3,19},{4,20},{5,21},{6,22},{7,23},{8,24},{9,... | collective-permute-start | bytes 270344 | tf_op jit(solution)/shard_map/ppermute | solution.py:323
  302.2 4.9 %collective-permute-start.59 = (bf16[64,704]{1,0:T(8,128)(2,1)S(1)}, bf16[64,704]{1,0:T(8,128)(2,1)S(1)}, u32[]{:S(2)}, u32[]{:S(2)}) collective-permute-start(bf16[64,704]{1,0:T(8,128)(2,1)S(1)} %get-tuple-element.85), channel_id=1, source_target_pairs={{0,8},{1,9},{2,10},{3,11},{4,12},{5,13},{6,14},{7,15},{8,0},{9,1},... | collective-permute-start | bytes 270344 | tf_op jit(solution)/shard_map/ppermute | solution.py:323
  (59 other events, 712.5 us)
Sparse Core Ops, SparseCore 0:
  31.4 104.6 all-gather.2
  163.3 117.9 reduce-scatter.1

commit v3 on v2

--- a/solution.py
+++ b/solution.py
@@ -9,7 +9,7 @@
 from jax.experimental.pallas import tpu as pltpu
 from jax.sharding import PartitionSpec as P
 
-HEADS = 16
+PAIRS_A_STEP = 2
 HEAD = 64
 LATENT = 256
 DOMAINS = 8
@@ -153,30 +153,41 @@
     )(jnp.stack([n for order in orders for n in order]), *grids)
 
 
-def pair_scores(query_latent, keys, query_pos, key_pos):
-    scores = times_transposed(query_latent, keys) * SCALE
-    both = jnp.concatenate([query_pos, query_pos], 0)
-    return jnp.where(both >= key_pos, scores, MASKED)
+def pair_scores(query_latent, keys, visible):
+    scores = times_transposed(query_latent * jnp.asarray(SCALE, BF16), keys)
+    return jnp.where(visible, scores, MASKED)
+
+
+def visible_keys(query_pos, key_pos):
+    return jnp.concatenate([query_pos, query_pos], 0) >= key_pos
+
+
+def pair_lanes(n):
+    return slice(2 * n * HEAD, 2 * (n + 1) * HEAD)
 
 
 def attend_kernel(q_ref, uk_ref, uv_ref, keys_ref, qpos_ref, kpos_ref, ql_ref, mixed_ref, lse_ref, values_ref):
-    q, uk, uv, keys = q_ref[0], uk_ref[...], uv_ref[...], keys_ref[0]
-    rows = q.shape[0]
-    ql = jnp.concatenate(
-        [times_transposed(q[:, k : k + HEAD], uk[:, k : k + HEAD]) for k in (0, HEAD)], 0
-    ).astype(BF16)
-    scores = pair_scores(ql, keys, qpos_ref[0], kpos_ref[0])
-    top = jnp.max(scores, -1, keepdims=True)
-    terms = jnp.exp(scores - top)
-    total = jnp.sum(terms, -1, keepdims=True)
-    probs = (terms * (1.0 / total)).astype(BF16)
-    mixed = product(probs, keys).astype(BF16)
-    ql_ref[0, 0] = ql
-    mixed_ref[0, 0] = mixed
-    lse_ref[0, 0] = top + jnp.log(total)
-    values_ref[0] = jnp.concatenate(
-        [product(mixed[:rows], uv[:, :HEAD]), product(mixed[rows:], uv[:, HEAD:])], 1
-    ).astype(BF16)
+    keys = keys_ref[0]
+    visible = visible_keys(qpos_ref[0], kpos_ref[0])
+    for n in range(ql_ref.shape[1]):
+        lanes = pair_lanes(n)
+        q, uk, uv = q_ref[0][:, lanes], uk_ref[:, lanes], uv_ref[:, lanes]
+        rows = q.shape[0]
+        ql = jnp.concatenate(
+            [times_transposed(q[:, k : k + HEAD], uk[:, k : k + HEAD]) for k in (0, HEAD)], 0
+        ).astype(BF16)
+        scores = pair_scores(ql, keys, visible)
+        top = jnp.max(scores, -1, keepdims=True)
+        terms = jnp.exp(scores - top)
+        total = jnp.sum(terms, -1, keepdims=True)
+        probs = (terms * (1.0 / total)).astype(BF16)
+        mixed = product(probs, keys).astype(BF16)
+        ql_ref[0, n] = ql
+        mixed_ref[0, n] = mixed
+        lse_ref[0, n] = top + jnp.log(total)
+        values_ref[0, :, lanes] = jnp.concatenate(
+            [product(mixed[:rows], uv[:, :HEAD]), product(mixed[rows:], uv[:, HEAD:])], 1
+        ).astype(BF16)
 
 
 def attend_back_kernel(
@@ -184,74 +195,73 @@
     dq_ref, guk_ref, guv_ref, *rest,
 ):
     dkeys_refs, (keys_acc, uk_acc, uv_acc) = rest[:-3], rest[-3:]
-    seq, pair = pl.program_id(0), pl.program_id(1)
-    q, ql, mixed, dval = q_ref[0], ql_ref[0, 0], mixed_ref[0, 0], dval_ref[0]
-    uk, uv, keys = uk_ref[...], uv_ref[...], keys_ref[0]
-    rows = q.shape[0]
+    seq, step = pl.program_id(0), pl.program_id(1)
+    keys = keys_ref[0]
+    visible = visible_keys(qpos_ref[0], kpos_ref[0])
     halves = (0, HEAD)
-    scores = pair_scores(ql, keys, qpos_ref[0], kpos_ref[0])
-    probs = jnp.exp(scores - lse_ref[0, 0])
-    dmixed = jnp.concatenate(
-        [times_transposed(dval[:, k : k + HEAD], uv[:, k : k + HEAD]) for k in halves], 0
-    ).astype(BF16)
-    dprobs = times_transposed(dmixed, keys)
-    dscores = probs * (dprobs - jnp.sum(probs * dprobs, -1, keepdims=True))
-    dscores = dscores.astype(BF16) * jnp.asarray(SCALE, BF16)
-    dql = product(dscores, keys).astype(BF16)
-    dkeys = contract_rows(dscores, ql) + contract_rows(probs.astype(BF16), dmixed)
-
-    @pl.when(pair == 0)
+    inside = ql_ref.shape[1]
+    dkeys = None
+    for n in range(inside):
+        lanes = pair_lanes(n)
+        q, dval, uk, uv = q_ref[0][:, lanes], dval_ref[0][:, lanes], uk_ref[:, lanes], uv_ref[:, lanes]
+        ql, mixed = ql_ref[0, n], mixed_ref[0, n]
+        rows = q.shape[0]
+        scores = pair_scores(ql, keys, visible)
+        probs = jnp.exp(scores - lse_ref[0, n])
+        dmixed = jnp.concatenate(
+            [times_transposed(dval[:, k : k + HEAD], uv[:, k : k + HEAD]) for k in halves], 0
+        ).astype(BF16)
+        dprobs = times_transposed(dmixed, keys)
+        dscores = probs * (dprobs - jnp.sum(probs * dprobs, -1, keepdims=True))
+        dscores = dscores.astype(BF16) * jnp.asarray(SCALE, BF16)
+        dql = product(dscores, keys).astype(BF16)
+        part = contract_rows(dscores, ql) + contract_rows(probs.astype(BF16), dmixed)
+        dkeys = part if dkeys is None else dkeys + part
+        guk = jnp.concatenate(
+            [contract_rows(dql[i * rows : (i + 1) * rows], q[:, k : k + HEAD]) for i, k in enumerate(halves)], 1
+        )
+        guv = jnp.concatenate(
+            [contract_rows(mixed[i * rows : (i + 1) * rows], dval[:, k : k + HEAD]) for i, k in enumerate(halves)], 1
+        )
+        pair = step * inside + n
+        uk_acc[pair] = jnp.where(seq == 0, guk, uk_acc[pair] + guk)
+        uv_acc[pair] = jnp.where(seq == 0, guv, uv_acc[pair] + guv)
+        dq_ref[0, :, lanes] = jnp.concatenate(
+            [product(dql[i * rows : (i + 1) * rows], uk[:, k : k + HEAD]) for i, k in enumerate(halves)], 1
+        ).astype(BF16)
+
+    @pl.when(step == 0)
     def _():
         keys_acc[...] = dkeys
 
-    @pl.when(pair > 0)
+    @pl.when(step > 0)
     def _():
         keys_acc[...] += dkeys
 
-    guk = jnp.concatenate(
-        [contract_rows(dql[n * rows : (n + 1) * rows], q[:, k : k + HEAD]) for n, k in enumerate(halves)], 1
-    )
-    guv = jnp.concatenate(
-        [contract_rows(mixed[n * rows : (n + 1) * rows], dval[:, k : k + HEAD]) for n, k in enumerate(halves)], 1
-    )
-
-    @pl.when(seq == 0)
-    def _():
-        uk_acc[pair] = guk
-        uv_acc[pair] = guv
-
-    @pl.when(seq > 0)
-    def _():
-        uk_acc[pair] += guk
-        uv_acc[pair] += guv
-
-    dq_ref[0] = jnp.concatenate(
-        [product(dql[n * rows : (n + 1) * rows], uk[:, k : k + HEAD]) for n, k in enumerate(halves)], 1
-    ).astype(BF16)
     last = pl.num_programs(1) - 1
 
-    @pl.when(pair == last)
+    @pl.when(step == last)
     def _():
         count = dkeys_refs[0].shape[0]
         for n, ref in enumerate(dkeys_refs):
             part = keys_acc[n * count * rows : (n + 1) * count * rows, :]
             ref[:, 0] = part.reshape(count, rows, LATENT).astype(BF16)
 
-    @pl.when((pair == last) & (seq == pl.num_programs(0) - 1))
+    @pl.when((step == last) & (seq == pl.num_programs(0) - 1))
     def _():
         for n in range(uk_acc.shape[0]):
-            guk_ref[:, 2 * n * HEAD : 2 * (n + 1) * HEAD] = uk_acc[n].astype(BF16)
-            guv_ref[:, 2 * n * HEAD : 2 * (n + 1) * HEAD] = uv_acc[n].astype(BF16)
+            guk_ref[:, pair_lanes(n)] = uk_acc[n].astype(BF16)
+            guv_ref[:, pair_lanes(n)] = uv_acc[n].astype(BF16)
 
 
 def attention_specs(length, rows):
-    pair = pl.BlockSpec((1, rows, 2 * HEAD), lambda s, p: (s, 0, p))
-    up = pl.BlockSpec((LATENT, 2 * HEAD), lambda s, p: (0, p))
+    pair = pl.BlockSpec((1, rows, 2 * PAIRS_A_STEP * HEAD), lambda s, p: (s, 0, p))
+    up = pl.BlockSpec((LATENT, 2 * PAIRS_A_STEP * HEAD), lambda s, p: (0, p))
     keys = pl.BlockSpec((1, length, LATENT), lambda s, p: (s, 0, 0))
     query_pos = pl.BlockSpec((1, rows, 1), lambda s, p: (s, 0, 0))
     key_pos = pl.BlockSpec((1, 1, length), lambda s, p: (s, 0, 0))
-    wide = pl.BlockSpec((1, 1, 2 * rows, LATENT), lambda s, p: (s, p, 0, 0))
-    thin = pl.BlockSpec((1, 1, 2 * rows, 1), lambda s, p: (s, p, 0, 0))
+    wide = pl.BlockSpec((1, PAIRS_A_STEP, 2 * rows, LATENT), lambda s, p: (s, p, 0, 0))
+    thin = pl.BlockSpec((1, PAIRS_A_STEP, 2 * rows, 1), lambda s, p: (s, p, 0, 0))
     return pair, up, keys, query_pos, key_pos, wide, thin
 
 
@@ -262,7 +272,7 @@
     flops = seqs * pairs * 2 * rows * length * LATENT * 4
     return pl.pallas_call(
         attend_kernel,
-        grid=(seqs, pairs),
+        grid=(seqs, pairs // PAIRS_A_STEP),
         in_specs=[pair, up, up, key, qpos, kpos],
         out_specs=[wide, wide, thin, pair],
         out_shape=[
@@ -286,7 +296,7 @@
     flops = seqs * pairs * 2 * rows * length * LATENT * 10
     return pl.pallas_call(
         attend_back_kernel,
-        grid=(seqs, pairs),
+        grid=(seqs, pairs // PAIRS_A_STEP),
         in_specs=[pair, wide, wide, thin, pair, up, up, key, qpos, kpos],
         out_specs=[pair, whole, whole]
         + [pl.BlockSpec((count, 1, rows, LATENT), lambda s, p: (0, s, 0, 0))] * parts,
@@ -304,6 +314,84 @@
     )(q, ql, mixed, lse, dval, uk, uv, keys, query_pos, key_pos)
 
 
+def row_tiles(total, size):
+    return [(at, min(size, total - at)) for at in range(0, total, size)]
+
+
+def feed_kernel(*refs):
+    rows_refs, dy_refs = refs[:4], refs[4:8]
+    gate_ref, up_ref, down_ref, hidden_ref, dgate_ref, dup_ref, keep_ref, send_ref = refs[8:]
+    rows = rows_refs[0].shape[0]
+    for pair in (0, 1):
+        left = jnp.concatenate([rows_refs[2 * pair][...], rows_refs[2 * pair + 1][...]])
+        dy = jnp.concatenate([dy_refs[2 * pair][...], dy_refs[2 * pair + 1][...]])
+        gate = product(left, gate_ref[...])
+        up = product(left, up_ref[...])
+        dhidden = times_transposed(dy, down_ref[...])
+        sigmoid = 1.0 / (1.0 + jnp.exp(-gate))
+        silu = gate * sigmoid
+        span = slice(2 * pair * rows, 2 * (pair + 1) * rows)
+        hidden_ref[span] = (silu * up).astype(BF16)
+        dgate = (dhidden * up * (sigmoid * (1.0 + gate * (1.0 - sigmoid)))).astype(BF16)
+        dup = (dhidden * silu).astype(BF16)
+        dgate_ref[span] = dgate
+        dup_ref[span] = dup
+        shares = times_transposed(dgate, gate_ref[...]) + times_transposed(dup, up_ref[...])
+        keep_ref[pair] = shares[:rows]
+        send_ref[pair] = shares[rows:]
+
+
+def feed_grads_kernel(*refs):
+    rows_refs, dy_refs = refs[:4], refs[4:8]
+    down_ref, hidden_ref, dgate_ref, dup_ref, ggate_ref, gup_ref, gdown_ref, keep_ref, send_ref = refs[8:]
+    rows = rows_refs[0].shape[0]
+    for at, size in row_tiles(rows_refs[0].shape[1], 256):
+        left = jnp.concatenate([ref[:, at : at + size] for ref in rows_refs])
+        ggate_ref[at : at + size] = contract_rows(left, dgate_ref[...]).astype(BF16)
+        gup_ref[at : at + size] = contract_rows(left, dup_ref[...]).astype(BF16)
+    dy = jnp.concatenate([ref[...] for ref in dy_refs])
+    for at, size in row_tiles(hidden_ref.shape[1], 256):
+        gdown_ref[at : at + size] = contract_rows(hidden_ref[:, at : at + size], dy).astype(BF16)
+    for pair in (0, 1):
+        shares = product(hidden_ref[2 * pair * rows : 2 * (pair + 1) * rows], down_ref[...])
+        keep_ref[pair] = shares[:rows]
+        send_ref[pair] = shares[rows:]
+
+
+def feed(normed, dy, gate_full, up_full, down_full):
+    rows, width = normed[0].shape
+    units = gate_full.shape[1]
+    low = jax.ShapeDtypeStruct((4 * rows, units), BF16)
+    share = jax.ShapeDtypeStruct((2, rows, width), F32)
+    flops = 2 * 4 * rows * width * units
+    return pl.pallas_call(
+        feed_kernel,
+        out_shape=[low, low, low, share, share],
+        in_specs=[pl.BlockSpec(memory_space=pltpu.VMEM)] * 11,
+        out_specs=[pl.BlockSpec(memory_space=pltpu.VMEM)] * 5,
+        compiler_params=pltpu.CompilerParams(vmem_limit_bytes=40 << 20),
+        cost_estimate=pl.CostEstimate(flops=5 * flops, bytes_accessed=11 << 20, transcendentals=4 * rows * units),
+        name="feed",
+    )(*normed, *dy, gate_full, up_full, down_full)
+
+
+def feed_grads(normed, dy, down_full, hidden, dgate, dup):
+    rows, width = normed[0].shape
+    units = hidden.shape[1]
+    share = jax.ShapeDtypeStruct((2, rows, width), F32)
+    flops = 2 * 4 * rows * width * units
+    return pl.pallas_call(
+        feed_grads_kernel,
+        out_shape=[jax.ShapeDtypeStruct((width, units), BF16)] * 2
+        + [jax.ShapeDtypeStruct((units, width), BF16), share, share],
+        in_specs=[pl.BlockSpec(memory_space=pltpu.VMEM)] * 12,
+        out_specs=[pl.BlockSpec(memory_space=pltpu.VMEM)] * 5,
+        compiler_params=pltpu.CompilerParams(vmem_limit_bytes=40 << 20),
+        cost_estimate=pl.CostEstimate(flops=4 * flops, bytes_accessed=14 << 20, transcendentals=0),
+        name="feed_grads",
+    )(*normed, *dy, down_full, hidden, dgate, dup)
+
+
 class Plan:
     def __init__(self, mesh):
         self.dp, self.ctx = mesh.shape["dp"], mesh.shape["ctx"]
@@ -374,13 +462,17 @@
     return total
 
 
-def reduce(plan, stacks, far, second, first):
+def reduce_near(plan, stacks, second, first):
     keep0, keep1, send0, send1 = stacks
     got1 = plan.swap(send1, first)
     got0 = plan.swap(send0, first)
     part1 = (keep1.astype(F32) + got1.astype(F32)).astype(BF16)
     got = plan.swap(part1, second)
-    return reduce_far(plan, (keep0.astype(F32) + got0.astype(F32) + got.astype(F32)).astype(BF16), far)
+    return (keep0.astype(F32) + got0.astype(F32) + got.astype(F32)).astype(BF16)
+
+
+def tie(*values):
+    return lax.optimization_barrier(values)
 
 
 def per_device(plan, tokens, cotangent, domain_ids, domain_weights, stretch_offsets, gain_attn, gain_ffn,
@@ -530,13 +622,12 @@
     def spread(value):
         near = plan.swap(value, core_bit)
         across = plan.swap(value, cross_bit)
-        return jnp.concatenate([value, near, across, plan.swap(across, core_bit)])
-
-    def collect(shares):
-        parts = shares.reshape(4, rows, width)
-        got = plan.swap(jnp.stack([parts[1], parts[3]]), core_bit)
-        across = plan.swap((parts[2] + got[1]).astype(BF16), cross_bit)
-        return parts[0] + got[0] + across.astype(F32)
+        return [value, near, across, plan.swap(across, core_bit)]
+
+    def collect(keep, send):
+        got = plan.swap(send, core_bit)
+        across = plan.swap((keep[1] + got[1]).astype(BF16), cross_bit)
+        return keep[0] + got[0] + across.astype(F32)
 
     match = domain_ids[:, None] == jnp.arange(DOMAINS, dtype=jnp.int32)[None, :]
     scale = jnp.sum(jnp.where(match, domain_weights[None, :], 0.0))
@@ -544,40 +635,17 @@
     dy = spread(dlayer.astype(BF16))
 
     normed_two = spread((middle * inverse_rms(middle) * gain_two).astype(BF16))
-    gate = product(normed_two, gate_full)
-    up = product(normed_two, up_full)
-    sigmoid = jax.nn.sigmoid(gate)
-    silu = gate * sigmoid
-    hidden = (silu * up).astype(BF16)
-    dhidden = times_transposed(dy, down_full)
-    dgate = (dhidden * up * (sigmoid * (1.0 + gate * (1.0 - sigmoid)))).astype(BF16)
-    dup = (dhidden * silu).astype(BF16)
-    dnormed_two = collect(times_transposed(dgate, gate_full) + times_transposed(dup, up_full))
-    grad_gate = contract_rows(normed_two, dgate).astype(BF16)
-    grad_up = contract_rows(normed_two, dup).astype(BF16)
-    grad_down = contract_rows(hidden, dy).astype(BF16)
-    output = (middle + collect(product(hidden, down_full))).astype(BF16)[None]
+    hidden, dgate, dup, keep, send = feed(normed_two, dy, gate_full, up_full, down_full)
+    dnormed_two = collect(keep, send)
+    grad_gate, grad_up, grad_down, keep, send = feed_grads(normed_two, dy, down_full, hidden, dgate, dup)
+    output = (middle + collect(keep, send)).astype(BF16)[None]
 
     (third_grads,) = cut_blocks(
         [grad_gate, grad_up, grad_down], third_blocks, third_orders, third_shapes,
         [(len(third_spots), third_rows, quarter)],
         [(0, columns_rows + n * down_shard, down_shard, w, quarter - w) for n, w in enumerate(down_widths) if w < quarter],
     )
-    third_sum = reduce_far(
-        plan, lax.psum_scatter(third_grads, "ctx", scatter_dimension=0, tiled=True), extra_bits
-    )
-    down_sum = third_sum[columns_rows:].reshape(2, down_shard, quarter)
-    down_sum = jnp.concatenate([down_sum[n, :, :w] for n, w in enumerate(down_widths)], 1)
-    grad_w_down = plan.deal(down_sum, [(plan.top // 2, core_bit), (plan.top, cross_bit)])
-    column_sum = third_sum[:columns_rows].reshape(4, 2 * shard, quarter)
-    got = [column_sum[0]] + [
-        plan.swap(column_sum[n].astype(BF16), m).astype(F32) for n, m in enumerate(split_masks) if n
-    ]
-    got = jnp.stack(got)
-    grad_columns = jnp.concatenate(
-        [lax.dynamic_index_in_dim(got, split ^ n, 0, keepdims=False) for n in range(4)], 1
-    )
-    grad_w_gate, grad_w_up = grad_columns[:shard], grad_columns[shard:]
+    third_sum = lax.psum_scatter(third_grads, "ctx", scatter_dimension=0, tiled=True)
 
     dmiddle_norm, grad_gain_two = norm_back(middle, gain_two, dnormed_two)
     dmiddle = dlayer + dmiddle_norm
@@ -612,12 +680,7 @@
         [(shard, [half]), (up_shard, [pair_width]), (up_shard, [pair_width]), (shard, [width])],
         [(len(masks),) + second_message.shape for masks in half_order],
     )
-    second_sum = reduce(plan, second_stacks, *half_stages)
-    own, got = second_sum[:shard, :half], plan.swap(second_sum[:shard, half:].astype(BF16), core_bit).astype(F32)
-    grad_w_query = jnp.concatenate([jnp.where(core == 0, own, got), jnp.where(core == 0, got, own)], 1)
-    dealt = plan.deal(second_sum[shard:].astype(BF16), [(plan.top, core_bit)]).astype(F32)
-    grad_w_out = dealt[up_shard:]
-
+    second_part = reduce_near(plan, second_stacks, y_bit, x_bit)
     grad_latent = contract_rows(normed_one, dlatent).astype(BF16)
     gain_rows = jnp.concatenate([grad_gain_one.reshape(count, shard), grad_gain_two.reshape(count, shard)], 1)
     gain_rows = jnp.pad(gain_rows.astype(BF16)[:, None], ((0, 0), (0, INFO - 1), (0, latent_half - 2 * shard)))
@@ -632,7 +695,26 @@
         [(shard, [latent_half]), (INFO, [latent_half])],
         [(len(masks), 2 * band, latent_half) for masks in half_order],
     )
-    first_sum = reduce(plan, first_stacks, *half_stages)
+    first_part = reduce_near(plan, first_stacks, y_bit, x_bit)
+    first_part, second_part, third_sum = tie(first_part, second_part, third_sum)
+    third_sum = reduce_far(plan, third_sum, extra_bits) if extra_bits else third_sum[0] if third_sum.ndim == 3 else third_sum
+    down_sum = third_sum[columns_rows:].reshape(2, down_shard, quarter)
+    down_sum = jnp.concatenate([down_sum[n, :, :w] for n, w in enumerate(down_widths)], 1)
+    grad_w_down = plan.deal(down_sum.astype(F32), [(plan.top // 2, core_bit), (plan.top, cross_bit)])
+    column_sum = third_sum[:columns_rows].reshape(4, 2 * shard, quarter)
+    got = jnp.stack(
+        [column_sum[0]] + [plan.swap(column_sum[n].astype(BF16), m).astype(third_sum.dtype) for n, m in enumerate(split_masks) if n]
+    )
+    grad_columns = jnp.concatenate(
+        [lax.dynamic_index_in_dim(got, split ^ n, 0, keepdims=False) for n in range(4)], 1
+    ).astype(F32)
+    grad_w_gate, grad_w_up = grad_columns[:shard], grad_columns[shard:]
+    first_sum = reduce_far(plan, first_part, half_far)
+    second_sum = reduce_far(plan, second_part, half_far)
+    own, got = second_sum[:shard, :half], plan.swap(second_sum[:shard, half:].astype(BF16), core_bit).astype(F32)
+    grad_w_query = jnp.concatenate([jnp.where(core == 0, own, got), jnp.where(core == 0, got, own)], 1)
+    dealt = plan.deal(second_sum[shard:].astype(BF16), [(plan.top, core_bit)]).astype(F32)
+    grad_w_out = dealt[up_shard:]
     own, got = first_sum[:band], plan.swap(first_sum[band:].astype(BF16), core_bit).astype(F32)
     grad_w_latent = jnp.concatenate([jnp.where(core == 0, own, got), jnp.where(core == 0, got, own)], 1)[:shard]
     gain_sums = own[shard] + got[shard]

time: 317 us -> 310 us (0.978)
  matrix products: 24 us -> 8.66 us
  starting transfers between devices: 82.2 us -> 88.9 us
  Pallas kernels: 37.2 us -> 42.1 us
  local copies, waits for them, and re-layouts: 25.9 us -> 30 us
  waiting for transfers between devices: 99.2 us -> 95.2 us
    ppermute x60, waiting for transfers between devices: 99.2 us -> 85.5 us  [swap(): return lax.ppermute(value, AXES, [(n, n ^ mask) for n in range(self.count)])]
    unnamed x138 -> x144, local copies, waits for them, and re-layouts: 12.3 us -> 20 us
    ppermute x60, starting transfers between devices: 75.1 us -> 82.1 us  [swap(): return lax.ppermute(value, AXES, [(n, n ^ mask) for n in range(self.count)])]
    dot_general x7 -> x4, matrix products: 9.53 us -> 2.69 us  [contract_rows(): lax.dot_general(left, right, (((0,), (0,)), ((), ())), preferred_element_...]
    reduce_scatter x1, waiting for transfers between devices: 0.01 us -> 5.69 us  [per_device(): lax.psum_scatter(third_grads, 'ctx', scatter_dimension=0, tiled=True)]
    dot_general x6 -> x3, matrix products: 7.49 us -> 2.05 us  [times_transposed(): lax.dot_general(left, right, (((1,), (1,)), ((), ())), preferred_element_...]
    pallas_call x2 -> x4, Pallas kernels: 32.8 us -> 36.8 us  [the longest x1 15.9 us: attend_back(): pl.pallas_call(attend_back_kernel, grid=(seqs, pairs // PAIRS_A_STEP), in...]
    convert_element_type x3 -> x0, local copies, waits for them, and re-layouts: 3.61 us -> none  [the longest x1 1.91 us: per_device(): grad_up = contract_rows(normed_two, dup).astype(BF16)]
  transfers between devices with their start and end apart: 64 -> 64, of which waited for: 24 -> 24; matrix products, arithmetic and copies ran while one was open for 18% -> 14% of each run, Pallas kernels for 12% -> 10%
where the time goes in v3:
time: 310 us; the launch traced here: 309 us
  waiting for transfers between devices  95.2 us (31%)
  starting transfers between devices  88.9 us (29%)
  Pallas kernels  42.1 us (14%)
  local copies, waits for them, and re-layouts  30 us (10%)
  other arithmetic  26.5 us (9%)
  between operations  18.1 us (6%)
  matrix products  8.66 us (3%)
    ppermute x60, waiting for transfers between devices, swap(): return lax.ppermute(value, AXES, [(n, n ^ mask) for n in range(self.count)])  85.5 us
    ppermute x60, starting transfers between devices, swap(): return lax.ppermute(value, AXES, [(n, n ^ mask) for n in range(self.count)])  82.1 us
    unnamed x144, local copies, waits for them, and re-layouts  20 us
    pallas_call x1, Pallas kernels, attend_back(): pl.pallas_call(attend_back_kernel, grid=(seqs, pairs // PAIRS_A_STEP), in...  15.9 us
    pallas_call x1, Pallas kernels, attend(): pl.pallas_call(attend_kernel, grid=(seqs, pairs // PAIRS_A_STEP), in_spec...  11.4 us
    ppermute x2, starting transfers between devices, deal(): return lax.ppermute(value, AXES, table)  6.74 us
  transfers between devices with their start and end apart: 64, of which 24 were waited for; matrix products, arithmetic and copies ran while one was open for 14% of the time, Pallas kernels for 10%

profile of v3, /device:TPU:1, one launch (start us, length us, event | category | flops | bytes accessed | tf_op | source)
XLA Modules:
  0.0 309.5 jit_solution(103488954240765911)
XLA Ops:
  8.2 4.5 %collective-permute-start.7 = (bf16[48,1024]{1,0:T(8,128)(2,1)S(1)}, bf16[48,1024]{1,0:T(8,128)(2,1)S(1)}, u32[]{:S(2)}, u32[]{:S(2)}) collective-permute-start(bf16[48,1024]{1,0:T(8,128)(2,1)S(1)} %pad_maximum_fusion.10), channel_id=1, source_target_pairs={{0,0},{1,1},{2,2},{3,3},{4,4},{5,5},{6,6},{7,7},{8,16},{9,17},{10,... | collective-permute-start | bytes 294920 | tf_op jit(solution)/shard_map/ppermute | solution.py:428
  21.4 1.7 collective-permute-start.33
  23.2 1.3 collective-permute-start.2
  24.5 2.4 collective-permute-start.3
  26.9 3.4 %collective-permute-start.4 = (bf16[80,256]{1,0:T(8,128)(2,1)S(1)}, bf16[80,256]{1,0:T(8,128)(2,1)S(1)}, u32[]{:S(2)}, u32[]{:S(2)}) collective-permute-start(bf16[80,256]{1,0:T(8,128)(2,1)S(1)} %get-tuple-element.135), channel_id=1, source_target_pairs={{0,6},{1,7},{2,4},{3,5},{4,2},{5,3},{6,0},{7,1},{8,14},{9,15},{10,... | collective-permute-start | bytes 122888 | tf_op jit(solution)/shard_map/ppermute | solution.py:411
  31.8 1.3 collective-permute-start.5
  33.5 3.5 %collective-permute-start.9 = (bf16[80,1024]{1,0:T(8,128)(2,1)S(1)}, bf16[80,1024]{1,0:T(8,128)(2,1)S(1)}, u32[]{:S(2)}, u32[]{:S(2)}) collective-permute-start(bf16[80,1024]{1,0:T(8,128)(2,1)S(1)} %get-tuple-element.125), channel_id=1, source_target_pairs={{0,4},{1,5},{2,6},{3,7},{4,0},{5,1},{6,2},{7,3},{8,12},{9,13},{10,... | collective-permute-start | bytes 491528 | tf_op jit(solution)/shard_map/ppermute | solution.py:411
  39.8 1.2 collective-permute-start.12
  41.1 2.2 collective-permute-done.9
  43.3 7.0 %collective-permute-done.10 = bf16[80,1024]{1,0:T(8,128)(2,1)S(1)} collective-permute-done((bf16[80,1024]{1,0:T(8,128)(2,1)S(1)}, bf16[80,1024]{1,0:T(8,128)(2,1)S(1)}, u32[]{:S(2)}, u32[]{:S(2)}) %collective-permute-start.10) | collective-permute-done | bytes 163872 | tf_op jit(solution)/shard_map/ppermute | solution.py:411
  52.6 1.3 convolution_convert_fusion.5
  53.9 10.1 %collective-permute-start.17 = (bf16[2,128,256]{2,1,0:T(8,128)(2,1)S(1)}, bf16[2,128,256]{2,1,0:T(8,128)(2,1)S(1)}, u32[]{:S(2)}, u32[]{:S(2)}) collective-permute-start(bf16[2,128,256]{2,1,0:T(8,128)(2,1)S(1)} %bitcast.385), channel_id=1, source_target_pairs={{0,2},{1,3},{2,0},{3,1},{4,6},{5,7},{6,4},{7,5},{8,10},{9,11},{10,... | collective-permute-start | bytes 393224 | tf_op jit(solution)/shard_map/ppermute | solution.py:411
  64.2 1.1 collective-permute-start.16
  65.3 2.2 collective-permute-start.18
  67.5 1.4 collective-permute-start.19
  68.9 1.4 collective-permute-done.17
  70.3 7.5 %collective-permute-done.18 = bf16[2,128,256]{2,1,0:T(8,128)(2,1)S(1)} collective-permute-done((bf16[2,128,256]{2,1,0:T(8,128)(2,1)S(1)}, bf16[2,128,256]{2,1,0:T(8,128)(2,1)S(1)}, u32[]{:S(2)}, u32[]{:S(2)}) %collective-permute-start.18) | collective-permute-done | bytes 131104 | tf_op jit(solution)/shard_map/ppermute | solution.py:411
  79.9 2.2 collective-permute-done.21
  82.1 3.2 %collective-permute-done.22 = bf16[1,2,128,256]{3,2,1,0:T(8,128)(2,1)S(1)} collective-permute-done((bf16[1,2,128,256]{3,2,1,0:T(8,128)(2,1)S(1)}, bf16[1,2,128,256]{3,2,1,0:T(8,128)(2,1)S(1)}, u32[]{:S(2)}, u32[]{:S(2)}) %collective-permute-start.22) | collective-permute-done | bytes 131104 | tf_op jit(solution)/shard_map/ppermute | solution.py:411
  85.4 5.0 %collective-permute-done.23 = bf16[1,2,128,256]{3,2,1,0:T(8,128)(2,1)S(1)} collective-permute-done((bf16[1,2,128,256]{3,2,1,0:T(8,128)(2,1)S(1)}, bf16[1,2,128,256]{3,2,1,0:T(8,128)(2,1)S(1)}, u32[]{:S(2)}, u32[]{:S(2)}) %collective-permute-start.23) | collective-permute-done | bytes 131104 | tf_op jit(solution)/shard_map/ppermute | solution.py:411
  93.0 1.2 convolution_convert_fusion.4
  94.2 11.4 %attend.1 = (bf16[2,4,256,256]{3,2,1,0:T(8,128)(2,1)}, bf16[2,4,256,256]{3,2,1,0:T(8,128)(2,1)}, f32[2,4,256,1]{3,2,1,0:T(8,128)}, bf16[2,128,512]{2,1,0:T(8,128)(2,1)}) custom-call(bf16[2,128,512]{2,1,0:T(8,128)(2,1)} %bitcast.400, bf16[256,512]{1,0:T(8,128)(2,1)} %bitcast.365, bf16[256,512]{1,0:T(8,128)(2,1)} %bitcast.367, ...), custom_call_target="tpu_custom_call" | custom-call | flops 2147483648 | bytes 6291456 | tf_op jit(solution)/shard_map/attend/pallas_call | solution.py:273
  105.7 1.4 fusion.49
  108.0 10.5 %collective-permute-start.24 = (f32[128,1024]{1,0:T(8,128)}, f32[128,1024]{1,0:T(8,128)}, u32[]{:S(2)}, u32[]{:S(2)}) collective-permute-start(f32[128,1024]{1,0:T(8,128)} %slice.327), channel_id=1, source_target_pairs={{0,8},{1,9},{2,10},{3,11},{4,12},{5,13},{6,14},{7,15},{8,0},{9,1},... | collective-permute-start | bytes 1572872 | tf_op jit(solution)/shard_map/ppermute | solution.py:411
  120.8 2.1 multiply_reduce_fusion.6
  123.8 1.5 collective-permute-start.26
  125.8 2.8 collective-permute-done.29.refs_6_
  129.7 4.6 %collective-permute-done.26.refs_2_ = bf16[128,1024]{1,0:T(8,128)(2,1)S(1)} collective-permute-done((bf16[128,1024]{1,0:T(8,128)(2,1)S(1)}, bf16[128,1024]{1,0:T(8,128)(2,1)S(1)}, u32[]{:S(2)}, u32[]{:S(2)}) %collective-permute-start.26) | collective-permute-done | bytes 262176 | tf_op jit(solution)/shard_map/ppermute | solution.py:411
  136.1 2.5 copy-done.1
  147.1 5.0 %feed.1 = (bf16[512,704]{1,0:T(8,128)(2,1)S(1)}, bf16[512,704]{1,0:T(8,128)(2,1)S(1)}, bf16[512,704]{1,0:T(8,128)(2,1)S(1)}, f32[2,128,1024]{2,1,0:T(8,128)S(1)}, f32[2,128,1024]{2,1,0:T(8,128)S(1)}) custom-call(bf16[128,1024]{1,0:T(8,128)(2,1)S(1)} %multiply_convert_fusion.1.refs_0_, bf16[128,1024]{1,0:T(8,128)(2,1)S(1)} %copy-done.22, ...), custom_call_target="tpu_custom_call" | custom-call | flops 3690987520 | bytes 11534336 | tf_op jit(solution)/shard_map/feed/pallas_call | solution.py:367
  153.1 4.4 %feed_grads.1 = (bf16[1024,704]{1,0:T(8,128)(2,1)S(1)}, bf16[1024,704]{1,0:T(8,128)(2,1)S(1)}, bf16[704,1024]{1,0:T(8,128)(2,1)S(1)}, f32[2,128,1024]{2,1,0:T(8,128)S(1)}, f32[2,128,1024]{2,1,0:T(8,128)}) custom-call(bf16[128,1024]{1,0:T(8,128)(2,1)S(1)} %multiply_convert_fusion.1.refs_0_, bf16[128,1024]{1,0:T(8,128)(2,1)S(1)} %copy-done.23, ...), custom_call_target="tpu_custom_call" | custom-call | flops 2952790016 | bytes 14680064 | tf_op jit(solution)/shard_map/feed_grads/pallas_call | solution.py:383
  158.5 2.4 copy-done
  161.9 2.5 collective-permute-done.36
  165.4 6.7 %collective-permute-done.37 = bf16[128,1024]{1,0:T(8,128)(2,1)S(1)} collective-permute-done((bf16[128,1024]{1,0:T(8,128)(2,1)S(1)}, bf16[128,1024]{1,0:T(8,128)(2,1)S(1)}, u32[]{:S(2)}, u32[]{:S(2)}) %collective-permute-start.37) | collective-permute-done | bytes 262176 | tf_op jit(solution)/shard_map/ppermute | solution.py:411
  174.3 1.2 collective-permute-start.38
  175.5 1.2 collective-permute-done.38
  176.7 1.2 convolution_convert_fusion.3
  177.9 15.9 %attend_back.1 = (bf16[2,128,512]{2,1,0:T(8,128)(2,1)}, bf16[256,512]{1,0:T(8,128)(2,1)}, bf16[256,512]{1,0:T(8,128)(2,1)}, bf16[4,2,128,256]{3,2,1,0:T(8,128)(2,1)}, bf16[4,2,128,256]{3,2,1,0:T(8,128)(2,1)}) custom-call(bf16[2,128,512]{2,1,0:T(8,128)(2,1)} %bitcast.401, bf16[2,4,256,256]{3,2,1,0:T(8,128)(2,1)} %get-tuple-element.64.ql_ref, ...), custom_call_target="tpu_custom_call" | custom-call | flops 5368709120 | bytes 8388608 | tf_op jit(solution)/shard_map/attend_back/pallas_call | solution.py:297
  195.1 1.5 convolution_convert_fusion.1
  196.6 10.8 %collective-permute-done.39 = bf16[4,2,128,256]{3,2,1,0:T(8,128)(2,1)S(1)} collective-permute-done((bf16[4,2,128,256]{3,2,1,0:T(8,128)(2,1)}, bf16[4,2,128,256]{3,2,1,0:T(8,128)(2,1)S(1)}, u32[]{:S(2)}, u32[]{:S(2)}) %collective-permute-start.39) | collective-permute-done | bytes 524320 | tf_op jit(solution)/shard_map/ppermute | solution.py:411
  208.2 1.2 fusion.36
  209.5 2.0 collective-permute-start.42
  211.5 1.6 collective-permute-start.40
  213.6 1.6 cut_blocks.4
  216.1 7.3 %collective-permute-done.41 = bf16[2,128,256]{2,1,0:T(8,128)(2,1)S(1)} collective-permute-done((bf16[2,128,256]{2,1,0:T(8,128)(2,1)S(1)}, bf16[2,128,256]{2,1,0:T(8,128)(2,1)S(1)}, u32[]{:S(2)}, u32[]{:S(2)}) %collective-permute-start.41) | collective-permute-done | bytes 131104 | tf_op jit(solution)/shard_map/ppermute | solution.py:411
  225.6 1.2 collective-permute-start.43
  228.6 1.2 collective-permute-start.35
  230.1 2.3 add_convert_fusion.1
  232.4 1.2 collective-permute-start.49
  234.1 1.3 multiply_reduce_fusion.2
  236.2 1.3 collective-permute-start.45
  237.8 3.8 %fusion.11 = (bf16[1,128,1024]{2,1,0:T(8,128)(2,1)}, bf16[1,128,1024]{2,1,0:T(8,128)(2,1)}) fusion(f32[256,1024]{1,0:T(8,128)} %copy-done.30, f32[128]{0:T(128)S(1)} %fusion.31, f32[1024]{0:T(1024)S(1)} %mul.320, f32[128]{0:T(128)S(1)} %add_rsqrt_fusion.1, f32[128,1024]{1,0:T(8,128)} %collective-permute-done.43, f32[256,1024]{1,0:T(8,128)} %copy-done.32, ...), kind=kLoop, calls=%fused_computation.49 | loop fusion | flops 2490368 | bytes 4728836 | tf_op jit(solution)/shard_map/broadcast_in_dim | solution.py:665
  241.6 13.2 %collective-permute-done.45 = bf16[4,80,256]{2,1,0:T(8,128)(2,1)S(1)} collective-permute-done((bf16[4,80,256]{2,1,0:T(8,128)(2,1)S(1)}, bf16[4,80,256]{2,1,0:T(8,128)(2,1)S(1)}, u32[]{:S(2)}, u32[]{:S(2)}) %collective-permute-start.45) | collective-permute-done | bytes 163872 | tf_op jit(solution)/shard_map/ppermute | solution.py:411
  255.7 1.7 add_convert_fusion
  258.3 1.2 collective-permute-done.46
  259.6 5.7 %reduce-scatter.2.cloned.1.call-done = bf16[1,432,704]{2,1,0:T(8,128)(2,1)} async-done(((bf16[8,432,704]{2,1,0:T(8,128)(2,1)}), bf16[1,432,704]{2,1,0:T(8,128)(2,1)}) %reduce-scatter.2.cloned.1.call-update) | async-done | bytes 608272 | tf_op jit(solution)/shard_map/reduce_scatter | solution.py:648
  267.3 2.4 collective-permute-start.52
  271.0 2.4 collective-permute-start.56
  273.4 3.5 %collective-permute-start.61 = (bf16[64,704]{1,0:T(8,128)(2,1)S(1)}, bf16[64,704]{1,0:T(8,128)(2,1)S(1)}, u32[]{:S(2)}, u32[]{:S(2)}) collective-permute-start(bf16[64,704]{1,0:T(8,128)(2,1)S(1)} %get-tuple-element.99), channel_id=1, source_target_pairs={{0,24},{1,25},{2,26},{3,27},{4,28},{5,29},{6,30},{7,31},{8,16},{9,... | collective-permute-start | bytes 270344 | tf_op jit(solution)/shard_map/ppermute | solution.py:411
  277.1 8.1 %collective-permute-start.53 = (bf16[40,256]{1,0:T(8,128)(2,1)S(1)}, bf16[40,256]{1,0:T(8,128)(2,1)S(1)}, u32[]{:S(2)}, u32[]{:S(2)}) collective-permute-start(bf16[40,256]{1,0:T(8,128)(2,1)S(1)} %slice.460), channel_id=1, source_target_pairs={{0,8},{1,9},{2,10},{3,11},{4,12},{5,13},{6,14},{7,15},{8,0},{9,1},... | collective-permute-start | bytes 61448 | tf_op jit(solution)/shard_map/ppermute | solution.py:411
  288.0 1.6 collective-permute-done.55
  289.6 3.8 %collective-permute-done.54 = bf16[80,1024]{1,0:T(8,128)(2,1)S(1)} collective-permute-done((bf16[80,1024]{1,0:T(8,128)(2,1)S(1)}, bf16[80,1024]{1,0:T(8,128)(2,1)S(1)}, u32[]{:S(2)}, u32[]{:S(2)}) %collective-permute-start.54) | collective-permute-done | bytes 163872 | tf_op jit(solution)/shard_map/ppermute | solution.py:411
  295.4 2.3 collective-permute-start.58
  298.4 3.0 collective-permute-done.58
  (344 shorter events, 61.7 us)
Async XLA Ops:
  7.2 128.9 %all-gather.3.cloned.1.call-start = ((), (), s32[]{:S(2)}) async-start(), calls=%async_computation.2 | async-start | bytes 5971968 | tf_op jit(solution)/shard_map/all_gather | solution.py:546
  7.2 31.9 %collective-permute-start = (bf16[128,1024]{1,0:T(8,128)(2,1)}, bf16[128,1024]{1,0:T(8,128)(2,1)S(1)}, u32[]{:S(2)}, u32[]{:S(2)}) collective-permute-start(bf16[128,1024]{1,0:T(8,128)(2,1)} %bitcast.371), channel_id=1, source_target_pairs={{0,8},{1,9},{2,10},{3,11},{4,12},{5,13},{6,14},{7,15},{8,0},{9,1},... | collective-permute-start | bytes 786440 | tf_op jit(solution)/shard_map/ppermute | solution.py:411
  8.2 25.2 %collective-permute-start.7 = (bf16[48,1024]{1,0:T(8,128)(2,1)S(1)}, bf16[48,1024]{1,0:T(8,128)(2,1)S(1)}, u32[]{:S(2)}, u32[]{:S(2)}) collective-permute-start(bf16[48,1024]{1,0:T(8,128)(2,1)S(1)} %pad_maximum_fusion.10), channel_id=1, source_target_pairs={{0,0},{1,1},{2,2},{3,3},{4,4},{5,5},{6,6},{7,7},{8,16},{9,17},{10,... | collective-permute-start | bytes 294920 | tf_op jit(solution)/shard_map/ppermute | solution.py:428
  15.7 5.7 %collective-permute-start.1 = (bf16[104,256]{1,0:T(8,128)(2,1)S(1)}, bf16[104,256]{1,0:T(8,128)(2,1)S(1)}, u32[]{:S(2)}, u32[]{:S(2)}) collective-permute-start(bf16[104,256]{1,0:T(8,128)(2,1)S(1)} %pad_maximum_fusion.12), channel_id=1, source_target_pairs={{0,8},{1,9},{2,10},{3,11},{4,12},{5,13},{6,14},{7,15},{8,0},{9,1},... | collective-permute-start | bytes 159752 | tf_op jit(solution)/shard_map/ppermute | solution.py:411
  18.2 5.0 %collective-permute-start.31 = (bf16[64,704]{1,0:T(8,128)(2,1)S(1)}, bf16[64,704]{1,0:T(8,128)(2,1)S(1)}, u32[]{:S(2)}, u32[]{:S(2)}) collective-permute-start(bf16[64,704]{1,0:T(8,128)(2,1)S(1)} %bitcast.396), channel_id=1, source_target_pairs={{0,8},{1,9},{2,10},{3,11},{4,12},{5,13},{6,14},{7,15},{8,0},{9,1},... | collective-permute-start | bytes 270344 | tf_op jit(solution)/shard_map/ppermute | solution.py:411
  18.7 5.8 %collective-permute-start.32 = (bf16[64,704]{1,0:T(8,128)(2,1)S(1)}, bf16[64,704]{1,0:T(8,128)(2,1)S(1)}, u32[]{:S(2)}, u32[]{:S(2)}) collective-permute-start(bf16[64,704]{1,0:T(8,128)(2,1)S(1)} %bitcast.395), channel_id=1, source_target_pairs={{0,16},{1,17},{2,18},{3,19},{4,20},{5,21},{6,22},{7,23},{8,24},{9,... | collective-permute-start | bytes 270344 | tf_op jit(solution)/shard_map/ppermute | solution.py:411
  21.4 5.5 %collective-permute-start.33 = (bf16[64,704]{1,0:T(8,128)(2,1)S(1)}, bf16[64,704]{1,0:T(8,128)(2,1)S(1)}, u32[]{:S(2)}, u32[]{:S(2)}) collective-permute-start(bf16[64,704]{1,0:T(8,128)(2,1)S(1)} %bitcast.397), channel_id=1, source_target_pairs={{0,24},{1,25},{2,26},{3,27},{4,28},{5,29},{6,30},{7,31},{8,16},{9,... | collective-permute-start | bytes 270344 | tf_op jit(solution)/shard_map/ppermute | solution.py:411
  23.2 8.2 %collective-permute-start.2 = (bf16[80,256]{1,0:T(8,128)(2,1)S(1)}, bf16[80,256]{1,0:T(8,128)(2,1)S(1)}, u32[]{:S(2)}, u32[]{:S(2)}) collective-permute-start(bf16[80,256]{1,0:T(8,128)(2,1)S(1)} %get-tuple-element.135), channel_id=1, source_target_pairs={{0,2},{1,3},{2,0},{3,1},{4,6},{5,7},{6,4},{7,5},{8,10},{9,11},{10,... | collective-permute-start | bytes 122888 | tf_op jit(solution)/shard_map/ppermute | solution.py:411
  24.5 7.0 %collective-permute-start.3 = (bf16[80,256]{1,0:T(8,128)(2,1)S(1)}, bf16[80,256]{1,0:T(8,128)(2,1)S(1)}, u32[]{:S(2)}, u32[]{:S(2)}) collective-permute-start(bf16[80,256]{1,0:T(8,128)(2,1)S(1)} %get-tuple-element.135), channel_id=1, source_target_pairs={{0,4},{1,5},{2,6},{3,7},{4,0},{5,1},{6,2},{7,3},{8,12},{9,13},{10,... | collective-permute-start | bytes 122888 | tf_op jit(solution)/shard_map/ppermute | solution.py:411
  26.9 4.9 %collective-permute-start.4 = (bf16[80,256]{1,0:T(8,128)(2,1)S(1)}, bf16[80,256]{1,0:T(8,128)(2,1)S(1)}, u32[]{:S(2)}, u32[]{:S(2)}) collective-permute-start(bf16[80,256]{1,0:T(8,128)(2,1)S(1)} %get-tuple-element.135), channel_id=1, source_target_pairs={{0,6},{1,7},{2,4},{3,5},{4,2},{5,3},{6,0},{7,1},{8,14},{9,15},{10,... | collective-permute-start | bytes 122888 | tf_op jit(solution)/shard_map/ppermute | solution.py:411
  31.4 233.9 %reduce-scatter.2.cloned.1.call-start = ((), (), s32[]{:S(2)}) async-start(), calls=%async_computation.1 | async-start | bytes 5971968 | tf_op jit(solution)/shard_map/reduce_scatter | solution.py:648
  31.8 5.2 %collective-permute-start.5 = (bf16[4,80,256]{2,1,0:T(8,128)(2,1)S(1)}, bf16[4,80,256]{2,1,0:T(8,128)(2,1)S(1)}, u32[]{:S(2)}, u32[]{:S(2)}) collective-permute-start(bf16[4,80,256]{2,1,0:T(8,128)(2,1)S(1)} %pad_maximum_fusion.7), channel_id=1, source_target_pairs={{0,1},{1,0},{2,3},{3,2},{4,5},{5,4},{6,7},{7,6},{8,9},{9,8},{10,11... | collective-permute-start | bytes 491528 | tf_op jit(solution)/shard_map/ppermute | solution.py:411
  33.5 6.4 %collective-permute-start.8 = (bf16[80,1024]{1,0:T(8,128)(2,1)S(1)}, bf16[80,1024]{1,0:T(8,128)(2,1)S(1)}, u32[]{:S(2)}, u32[]{:S(2)}) collective-permute-start(bf16[80,1024]{1,0:T(8,128)(2,1)S(1)} %get-tuple-element.125), channel_id=1, source_target_pairs={{0,2},{1,3},{2,0},{3,1},{4,6},{5,7},{6,4},{7,5},{8,10},{9,11},{10,... | collective-permute-start | bytes 491528 | tf_op jit(solution)/shard_map/ppermute | solution.py:411
  33.5 9.7 %collective-permute-start.9 = (bf16[80,1024]{1,0:T(8,128)(2,1)S(1)}, bf16[80,1024]{1,0:T(8,128)(2,1)S(1)}, u32[]{:S(2)}, u32[]{:S(2)}) collective-permute-start(bf16[80,1024]{1,0:T(8,128)(2,1)S(1)} %get-tuple-element.125), channel_id=1, source_target_pairs={{0,4},{1,5},{2,6},{3,7},{4,0},{5,1},{6,2},{7,3},{8,12},{9,13},{10,... | collective-permute-start | bytes 491528 | tf_op jit(solution)/shard_map/ppermute | solution.py:411
  37.0 13.3 %collective-permute-start.10 = (bf16[80,1024]{1,0:T(8,128)(2,1)S(1)}, bf16[80,1024]{1,0:T(8,128)(2,1)S(1)}, u32[]{:S(2)}, u32[]{:S(2)}) collective-permute-start(bf16[80,1024]{1,0:T(8,128)(2,1)S(1)} %get-tuple-element.125), channel_id=1, source_target_pairs={{0,6},{1,7},{2,4},{3,5},{4,2},{5,3},{6,0},{7,1},{8,14},{9,15},{10,... | collective-permute-start | bytes 491528 | tf_op jit(solution)/shard_map/ppermute | solution.py:411
  37.1 16.8 %collective-permute-start.11 = (bf16[1,80,1024]{2,1,0:T(8,128)(2,1)S(1)}, bf16[1,80,1024]{2,1,0:T(8,128)(2,1)S(1)}, u32[]{:S(2)}, u32[]{:S(2)}) collective-permute-start(bf16[1,80,1024]{2,1,0:T(8,128)(2,1)S(1)} %get-tuple-element.126.refs_0_), channel_id=1, source_target_pairs={{0,1},{1,0},{2,3},{3,2},{4,5},{5,4},{6,7},{7,6},{8,9},{9,8},{10,11... | collective-permute-start | bytes 491528 | tf_op jit(solution)/shard_map/ppermute | solution.py:411
  39.1 12.3 %collective-permute-start.6 = (bf16[8,80,256]{2,1,0:T(8,128)(2,1)S(1)}, bf16[8,80,256]{2,1,0:T(8,128)(2,1)S(1)}, u32[]{:S(2)}, u32[]{:S(2)}) collective-permute-start(bf16[8,80,256]{2,1,0:T(8,128)(2,1)S(1)} %constant_dynamic-update-slice_fusion), channel_id=1, source_target_pairs={{0,16},{1,17},{2,18},{3,19},{4,20},{5,21},{6,22},{7,23},{8,24},{9,... | collective-permute-start | bytes 983048 | tf_op jit(solution)/shard_map/ppermute | solution.py:411
  39.8 24.2 %collective-permute-start.12 = (bf16[1,80,1024]{2,1,0:T(8,128)(2,1)S(1)}, bf16[1,80,1024]{2,1,0:T(8,128)(2,1)S(1)}, u32[]{:S(2)}, u32[]{:S(2)}) collective-permute-start(bf16[1,80,1024]{2,1,0:T(8,128)(2,1)S(1)} %bitcast.340), channel_id=1, source_target_pairs={{0,1},{1,0},{2,3},{3,2},{4,5},{5,4},{6,7},{7,6},{8,9},{9,8},{10,11... | collective-permute-start | bytes 491528 | tf_op jit(solution)/shard_map/ppermute | solution.py:411
  43.3 20.8 %collective-permute-start.13 = (bf16[1,80,1024]{2,1,0:T(8,128)(2,1)S(1)}, bf16[1,80,1024]{2,1,0:T(8,128)(2,1)S(1)}, u32[]{:S(2)}, u32[]{:S(2)}) collective-permute-start(bf16[1,80,1024]{2,1,0:T(8,128)(2,1)S(1)} %bitcast.343), channel_id=1, source_target_pairs={{0,1},{1,0},{2,3},{3,2},{4,5},{5,4},{6,7},{7,6},{8,9},{9,8},{10,11... | collective-permute-start | bytes 491528 | tf_op jit(solution)/shard_map/ppermute | solution.py:411
  50.3 13.8 %collective-permute-start.14 = (bf16[1,80,1024]{2,1,0:T(8,128)(2,1)S(1)}, bf16[1,80,1024]{2,1,0:T(8,128)(2,1)S(1)}, u32[]{:S(2)}, u32[]{:S(2)}) collective-permute-start(bf16[1,80,1024]{2,1,0:T(8,128)(2,1)S(1)} %bitcast.346), channel_id=1, source_target_pairs={{0,1},{1,0},{2,3},{3,2},{4,5},{5,4},{6,7},{7,6},{8,9},{9,8},{10,11... | collective-permute-start | bytes 491528 | tf_op jit(solution)/shard_map/ppermute | solution.py:411
  51.4 38.9 %collective-permute-start.15 = (bf16[4,80,1024]{2,1,0:T(8,128)(2,1)}, bf16[4,80,1024]{2,1,0:T(8,128)(2,1)S(1)}, u32[]{:S(2)}, u32[]{:S(2)}) collective-permute-start(bf16[4,80,1024]{2,1,0:T(8,128)(2,1)} %pad_maximum_fusion), channel_id=1, source_target_pairs={{0,16},{1,17},{2,18},{3,19},{4,20},{5,21},{6,22},{7,23},{8,24},{9,... | collective-permute-start | bytes 1966088 | tf_op jit(solution)/shard_map/ppermute | solution.py:411
  53.9 16.4 %collective-permute-start.17 = (bf16[2,128,256]{2,1,0:T(8,128)(2,1)S(1)}, bf16[2,128,256]{2,1,0:T(8,128)(2,1)S(1)}, u32[]{:S(2)}, u32[]{:S(2)}) collective-permute-start(bf16[2,128,256]{2,1,0:T(8,128)(2,1)S(1)} %bitcast.385), channel_id=1, source_target_pairs={{0,2},{1,3},{2,0},{3,1},{4,6},{5,7},{6,4},{7,5},{8,10},{9,11},{10,... | collective-permute-start | bytes 393224 | tf_op jit(solution)/shard_map/ppermute | solution.py:411
  64.2 27.2 %collective-permute-start.16 = (bf16[4,80,1024]{2,1,0:T(8,128)(2,1)S(1)}, bf16[4,80,1024]{2,1,0:T(8,128)(2,1)S(1)}, u32[]{:S(2)}, u32[]{:S(2)}) collective-permute-start(bf16[4,80,1024]{2,1,0:T(8,128)(2,1)S(1)} %pad_maximum_fusion.1), channel_id=1, source_target_pairs={{0,16},{1,17},{2,18},{3,19},{4,20},{5,21},{6,22},{7,23},{8,24},{9,... | collective-permute-start | bytes 1966088 | tf_op jit(solution)/shard_map/ppermute | solution.py:411
  65.3 12.5 %collective-permute-start.18 = (bf16[2,128,256]{2,1,0:T(8,128)(2,1)S(1)}, bf16[2,128,256]{2,1,0:T(8,128)(2,1)S(1)}, u32[]{:S(2)}, u32[]{:S(2)}) collective-permute-start(bf16[2,128,256]{2,1,0:T(8,128)(2,1)S(1)} %bitcast.386), channel_id=1, source_target_pairs={{0,4},{1,5},{2,6},{3,7},{4,0},{5,1},{6,2},{7,3},{8,12},{9,13},{10,... | collective-permute-start | bytes 393224 | tf_op jit(solution)/shard_map/ppermute | solution.py:411
  67.5 10.8 %collective-permute-start.19 = (bf16[2,128,256]{2,1,0:T(8,128)(2,1)S(1)}, bf16[2,128,256]{2,1,0:T(8,128)(2,1)S(1)}, u32[]{:S(2)}, u32[]{:S(2)}) collective-permute-start(bf16[2,128,256]{2,1,0:T(8,128)(2,1)S(1)} %bitcast.388), channel_id=1, source_target_pairs={{0,6},{1,7},{2,4},{3,5},{4,2},{5,3},{6,0},{7,1},{8,14},{9,15},{10,... | collective-permute-start | bytes 393224 | tf_op jit(solution)/shard_map/ppermute | solution.py:411
  70.3 9.1 %collective-permute-start.20 = (bf16[1,2,128,256]{3,2,1,0:T(8,128)(2,1)S(1)}, bf16[1,2,128,256]{3,2,1,0:T(8,128)(2,1)S(1)}, u32[]{:S(2)}, u32[]{:S(2)}) collective-permute-start(bf16[1,2,128,256]{3,2,1,0:T(8,128)(2,1)S(1)} %bitcast.389), channel_id=1, source_target_pairs={{0,1},{1,0},{2,3},{3,2},{4,5},{5,4},{6,7},{7,6},{8,9},{9,8},{10,11... | collective-permute-start | bytes 393224 | tf_op jit(solution)/shard_map/ppermute | solution.py:411
  77.8 4.3 %collective-permute-start.21 = (bf16[1,2,128,256]{3,2,1,0:T(8,128)(2,1)S(1)}, bf16[1,2,128,256]{3,2,1,0:T(8,128)(2,1)S(1)}, u32[]{:S(2)}, u32[]{:S(2)}) collective-permute-start(bf16[1,2,128,256]{3,2,1,0:T(8,128)(2,1)S(1)} %bitcast.384), channel_id=1, source_target_pairs={{0,1},{1,0},{2,3},{3,2},{4,5},{5,4},{6,7},{7,6},{8,9},{9,8},{10,11... | collective-permute-start | bytes 393224 | tf_op jit(solution)/shard_map/ppermute | solution.py:411
  78.3 7.1 %collective-permute-start.22 = (bf16[1,2,128,256]{3,2,1,0:T(8,128)(2,1)S(1)}, bf16[1,2,128,256]{3,2,1,0:T(8,128)(2,1)S(1)}, u32[]{:S(2)}, u32[]{:S(2)}) collective-permute-start(bf16[1,2,128,256]{3,2,1,0:T(8,128)(2,1)S(1)} %bitcast.391), channel_id=1, source_target_pairs={{0,1},{1,0},{2,3},{3,2},{4,5},{5,4},{6,7},{7,6},{8,9},{9,8},{10,11... | collective-permute-start | bytes 393224 | tf_op jit(solution)/shard_map/ppermute | solution.py:411
  79.4 10.9 %collective-permute-start.23 = (bf16[1,2,128,256]{3,2,1,0:T(8,128)(2,1)S(1)}, bf16[1,2,128,256]{3,2,1,0:T(8,128)(2,1)S(1)}, u32[]{:S(2)}, u32[]{:S(2)}) collective-permute-start(bf16[1,2,128,256]{3,2,1,0:T(8,128)(2,1)S(1)} %bitcast.390), channel_id=1, source_target_pairs={{0,1},{1,0},{2,3},{3,2},{4,5},{5,4},{6,7},{7,6},{8,9},{9,8},{10,11... | collective-permute-start | bytes 393224 | tf_op jit(solution)/shard_map/ppermute | solution.py:411
  108.0 12.8 %collective-permute-start.24 = (f32[128,1024]{1,0:T(8,128)}, f32[128,1024]{1,0:T(8,128)}, u32[]{:S(2)}, u32[]{:S(2)}) collective-permute-start(f32[128,1024]{1,0:T(8,128)} %slice.327), channel_id=1, source_target_pairs={{0,8},{1,9},{2,10},{3,11},{4,12},{5,13},{6,14},{7,15},{8,0},{9,1},... | collective-permute-start | bytes 1572872 | tf_op jit(solution)/shard_map/ppermute | solution.py:411
  120.5 8.1 %collective-permute-start.29 = (bf16[128,1024]{1,0:T(8,128)(2,1)S(1)}, bf16[128,1024]{1,0:T(8,128)(2,1)S(1)}, u32[]{:S(2)}, u32[]{:S(2)}) collective-permute-start(bf16[128,1024]{1,0:T(8,128)(2,1)S(1)} %bitcast_convert_fusion.refs_4_), channel_id=1, source_target_pairs={{0,16},{1,17},{2,18},{3,19},{4,20},{5,21},{6,22},{7,23},{8,24},{9,... | collective-permute-start | bytes 786440 | tf_op jit(solution)/shard_map/ppermute | solution.py:411
  123.8 10.5 %collective-permute-start.26 = (bf16[128,1024]{1,0:T(8,128)(2,1)S(1)}, bf16[128,1024]{1,0:T(8,128)(2,1)S(1)}, u32[]{:S(2)}, u32[]{:S(2)}) collective-permute-start(bf16[128,1024]{1,0:T(8,128)(2,1)S(1)} %multiply_convert_fusion.1.refs_0_), channel_id=1, source_target_pairs={{0,16},{1,17},{2,18},{3,19},{4,20},{5,21},{6,22},{7,23},{8,24},{9,... | collective-permute-start | bytes 786440 | tf_op jit(solution)/shard_map/ppermute | solution.py:411
  125.3 14.2 %collective-permute-start.28 = (bf16[128,1024]{1,0:T(8,128)(2,1)S(1)}, bf16[128,1024]{1,0:T(8,128)(2,1)S(1)}, u32[]{:S(2)}, u32[]{:S(2)}) collective-permute-start(bf16[128,1024]{1,0:T(8,128)(2,1)S(1)} %bitcast_convert_fusion.refs_4_), channel_id=1, source_target_pairs={{0,8},{1,9},{2,10},{3,11},{4,12},{5,13},{6,14},{7,15},{8,0},{9,1},... | collective-permute-start | bytes 786440 | tf_op jit(solution)/shard_map/ppermute | solution.py:411
  128.6 11.6 %collective-permute-start.30 = (bf16[128,1024]{1,0:T(8,128)(2,1)S(1)}, bf16[128,1024]{1,0:T(8,128)(2,1)S(1)}, u32[]{:S(2)}, u32[]{:S(2)}) collective-permute-start(bf16[128,1024]{1,0:T(8,128)(2,1)S(1)} %collective-permute-done.29.refs_6_), channel_id=1, source_target_pairs={{0,8},{1,9},{2,10},{3,11},{4,12},{5,13},{6,14},{7,15},{8,0},{9,1},... | collective-permute-start | bytes 786440 | tf_op jit(solution)/shard_map/ppermute | solution.py:411
  129.7 11.2 %collective-permute-start.25 = (bf16[128,1024]{1,0:T(8,128)(2,1)S(1)}, bf16[128,1024]{1,0:T(8,128)(2,1)S(1)}, u32[]{:S(2)}, u32[]{:S(2)}) collective-permute-start(bf16[128,1024]{1,0:T(8,128)(2,1)S(1)} %multiply_convert_fusion.1.refs_0_), channel_id=1, source_target_pairs={{0,8},{1,9},{2,10},{3,11},{4,12},{5,13},{6,14},{7,15},{8,0},{9,1},... | collective-permute-start | bytes 786440 | tf_op jit(solution)/shard_map/ppermute | solution.py:411
  134.2 7.4 %collective-permute-start.27 = (bf16[128,1024]{1,0:T(8,128)(2,1)S(1)}, bf16[128,1024]{1,0:T(8,128)(2,1)S(1)}, u32[]{:S(2)}, u32[]{:S(2)}) collective-permute-start(bf16[128,1024]{1,0:T(8,128)(2,1)S(1)} %collective-permute-done.26.refs_2_), channel_id=1, source_target_pairs={{0,8},{1,9},{2,10},{3,11},{4,12},{5,13},{6,14},{7,15},{8,0},{9,1},... | collective-permute-start | bytes 786440 | tf_op jit(solution)/shard_map/ppermute | solution.py:411
  160.9 3.5 %collective-permute-start.36 = (f32[2,128,1024]{2,1,0:T(8,128)}, f32[2,128,1024]{2,1,0:T(8,128)S(1)}, u32[]{:S(2)}, u32[]{:S(2)}) collective-permute-start(f32[2,128,1024]{2,1,0:T(8,128)} %copy-done.8), channel_id=1, source_target_pairs={{0,8},{1,9},{2,10},{3,11},{4,12},{5,13},{6,14},{7,15},{8,0},{9,1},... | collective-permute-start | bytes 3145736 | tf_op jit(solution)/shard_map/ppermute | solution.py:411
  164.5 7.7 %collective-permute-start.37 = (bf16[128,1024]{1,0:T(8,128)(2,1)S(1)}, bf16[128,1024]{1,0:T(8,128)(2,1)S(1)}, u32[]{:S(2)}, u32[]{:S(2)}) collective-permute-start(bf16[128,1024]{1,0:T(8,128)(2,1)S(1)} %fusion.14), channel_id=1, source_target_pairs={{0,16},{1,17},{2,18},{3,19},{4,20},{5,21},{6,22},{7,23},{8,24},{9,... | collective-permute-start | bytes 786440 | tf_op jit(solution)/shard_map/ppermute | solution.py:411
  174.3 2.3 collective-permute-start.38
  193.9 13.5 %collective-permute-start.39 = (bf16[4,2,128,256]{3,2,1,0:T(8,128)(2,1)}, bf16[4,2,128,256]{3,2,1,0:T(8,128)(2,1)S(1)}, u32[]{:S(2)}, u32[]{:S(2)}) collective-permute-start(bf16[4,2,128,256]{3,2,1,0:T(8,128)(2,1)} %get-tuple-element.69), channel_id=1, source_target_pairs={{0,1},{1,0},{2,3},{3,2},{4,5},{5,4},{6,7},{7,6},{8,9},{9,8},{10,11... | collective-permute-start | bytes 1572872 | tf_op jit(solution)/shard_map/ppermute | solution.py:411
  194.4 32.4 %collective-permute-start.34 = (f32[2,128,1024]{2,1,0:T(8,128)}, f32[2,128,1024]{2,1,0:T(8,128)S(1)}, u32[]{:S(2)}, u32[]{:S(2)}) collective-permute-start(f32[2,128,1024]{2,1,0:T(8,128)} %get-tuple-element.61), channel_id=1, source_target_pairs={{0,8},{1,9},{2,10},{3,11},{4,12},{5,13},{6,14},{7,15},{8,0},{9,1},... | collective-permute-start | bytes 3145736 | tf_op jit(solution)/shard_map/ppermute | solution.py:411
  209.5 6.6 %collective-permute-start.42 = (bf16[2,128,256]{2,1,0:T(8,128)(2,1)S(1)}, bf16[2,128,256]{2,1,0:T(8,128)(2,1)S(1)}, u32[]{:S(2)}, u32[]{:S(2)}) collective-permute-start(bf16[2,128,256]{2,1,0:T(8,128)(2,1)S(1)} %get-tuple-element.108), channel_id=1, source_target_pairs={{0,6},{1,7},{2,4},{3,5},{4,2},{5,3},{6,0},{7,1},{8,14},{9,15},{10,... | collective-permute-start | bytes 393224 | tf_op jit(solution)/shard_map/ppermute | solution.py:411
  211.5 11.9 %collective-permute-start.41 = (bf16[2,128,256]{2,1,0:T(8,128)(2,1)S(1)}, bf16[2,128,256]{2,1,0:T(8,128)(2,1)S(1)}, u32[]{:S(2)}, u32[]{:S(2)}) collective-permute-start(bf16[2,128,256]{2,1,0:T(8,128)(2,1)S(1)} %get-tuple-element.109), channel_id=1, source_target_pairs={{0,4},{1,5},{2,6},{3,7},{4,0},{5,1},{6,2},{7,3},{8,12},{9,13},{10,... | collective-permute-start | bytes 393224 | tf_op jit(solution)/shard_map/ppermute | solution.py:411
  211.5 11.9 %collective-permute-start.40 = (bf16[2,128,256]{2,1,0:T(8,128)(2,1)S(1)}, bf16[2,128,256]{2,1,0:T(8,128)(2,1)S(1)}, u32[]{:S(2)}, u32[]{:S(2)}) collective-permute-start(bf16[2,128,256]{2,1,0:T(8,128)(2,1)S(1)} %get-tuple-element.107), channel_id=1, source_target_pairs={{0,2},{1,3},{2,0},{3,1},{4,6},{5,7},{6,4},{7,5},{8,10},{9,11},{10,... | collective-permute-start | bytes 393224 | tf_op jit(solution)/shard_map/ppermute | solution.py:411
  215.2 14.9 %collective-permute-start.48 = (bf16[4,80,1024]{2,1,0:T(8,128)(2,1)}, bf16[4,80,1024]{2,1,0:T(8,128)(2,1)}, u32[]{:S(2)}, u32[]{:S(2)}) collective-permute-start(bf16[4,80,1024]{2,1,0:T(8,128)(2,1)} %get-tuple-element.79), channel_id=1, source_target_pairs={{0,16},{1,17},{2,18},{3,19},{4,20},{5,21},{6,22},{7,23},{8,24},{9,... | collective-permute-start | bytes 1966088 | tf_op jit(solution)/shard_map/ppermute | solution.py:411
  225.6 8.5 %collective-permute-start.43 = (f32[128,1024]{1,0:T(8,128)}, f32[128,1024]{1,0:T(8,128)}, u32[]{:S(2)}, u32[]{:S(2)}) collective-permute-start(f32[128,1024]{1,0:T(8,128)} %slice.338), channel_id=1, source_target_pairs={{0,8},{1,9},{2,10},{3,11},{4,12},{5,13},{6,14},{7,15},{8,0},{9,1},... | collective-permute-start | bytes 1572872 | tf_op jit(solution)/shard_map/ppermute | solution.py:411
  228.6 9.2 %collective-permute-start.35 = (bf16[128,1024]{1,0:T(8,128)(2,1)}, bf16[128,1024]{1,0:T(8,128)(2,1)}, u32[]{:S(2)}, u32[]{:S(2)}) collective-permute-start(bf16[128,1024]{1,0:T(8,128)(2,1)} %fusion.13), channel_id=1, source_target_pairs={{0,16},{1,17},{2,18},{3,19},{4,20},{5,21},{6,22},{7,23},{8,24},{9,... | collective-permute-start | bytes 786440 | tf_op jit(solution)/shard_map/ppermute | solution.py:411
  229.8 25.8 %collective-permute-start.47 = (bf16[4,80,1024]{2,1,0:T(8,128)(2,1)}, bf16[4,80,1024]{2,1,0:T(8,128)(2,1)}, u32[]{:S(2)}, u32[]{:S(2)}) collective-permute-start(bf16[4,80,1024]{2,1,0:T(8,128)(2,1)} %copy-done.9), channel_id=1, source_target_pairs={{0,16},{1,17},{2,18},{3,19},{4,20},{5,21},{6,22},{7,23},{8,24},{9,... | collective-permute-start | bytes 1966088 | tf_op jit(solution)/shard_map/ppermute | solution.py:411
  232.4 23.3 %collective-permute-start.49 = (bf16[4,80,1024]{2,1,0:T(8,128)(2,1)}, bf16[4,80,1024]{2,1,0:T(8,128)(2,1)}, u32[]{:S(2)}, u32[]{:S(2)}) collective-permute-start(bf16[4,80,1024]{2,1,0:T(8,128)(2,1)} %add_convert_fusion.1), channel_id=1, source_target_pairs={{0,1},{1,0},{2,3},{3,2},{4,5},{5,4},{6,7},{7,6},{8,9},{9,8},{10,11... | collective-permute-start | bytes 1966088 | tf_op jit(solution)/shard_map/ppermute | solution.py:411
  236.2 18.6 %collective-permute-start.45 = (bf16[4,80,256]{2,1,0:T(8,128)(2,1)S(1)}, bf16[4,80,256]{2,1,0:T(8,128)(2,1)S(1)}, u32[]{:S(2)}, u32[]{:S(2)}) collective-permute-start(bf16[4,80,256]{2,1,0:T(8,128)(2,1)S(1)} %get-tuple-element.73), channel_id=1, source_target_pairs={{0,16},{1,17},{2,18},{3,19},{4,20},{5,21},{6,22},{7,23},{8,24},{9,... | collective-permute-start | bytes 491528 | tf_op jit(solution)/shard_map/ppermute | solution.py:411
  237.5 20.8 %collective-permute-start.44 = (bf16[4,80,256]{2,1,0:T(8,128)(2,1)S(1)}, bf16[4,80,256]{2,1,0:T(8,128)(2,1)S(1)}, u32[]{:S(2)}, u32[]{:S(2)}) collective-permute-start(bf16[4,80,256]{2,1,0:T(8,128)(2,1)S(1)} %get-tuple-element.71), channel_id=1, source_target_pairs={{0,16},{1,17},{2,18},{3,19},{4,20},{5,21},{6,22},{7,23},{8,24},{9,... | collective-permute-start | bytes 491528 | tf_op jit(solution)/shard_map/ppermute | solution.py:411
  254.9 4.6 %collective-permute-start.46 = (bf16[4,80,256]{2,1,0:T(8,128)(2,1)S(1)}, bf16[4,80,256]{2,1,0:T(8,128)(2,1)S(1)}, u32[]{:S(2)}, u32[]{:S(2)}) collective-permute-start(bf16[4,80,256]{2,1,0:T(8,128)(2,1)S(1)} %add_convert_fusion.4), channel_id=1, source_target_pairs={{0,1},{1,0},{2,3},{3,2},{4,5},{5,4},{6,7},{7,6},{8,9},{9,8},{10,11... | collective-permute-start | bytes 491528 | tf_op jit(solution)/shard_map/ppermute | solution.py:411
  267.3 6.1 %collective-permute-start.52 = (bf16[80,256]{1,0:T(8,128)(2,1)S(1)}, bf16[80,256]{1,0:T(8,128)(2,1)S(1)}, u32[]{:S(2)}, u32[]{:S(2)}) collective-permute-start(bf16[80,256]{1,0:T(8,128)(2,1)S(1)} %get-tuple-element.123), channel_id=1, source_target_pairs={{0,6},{1,7},{2,4},{3,5},{4,2},{5,3},{6,0},{7,1},{8,14},{9,15},{10,... | collective-permute-start | bytes 122888 | tf_op jit(solution)/shard_map/ppermute | solution.py:411
  269.7 7.2 %collective-permute-start.51 = (bf16[80,256]{1,0:T(8,128)(2,1)S(1)}, bf16[80,256]{1,0:T(8,128)(2,1)S(1)}, u32[]{:S(2)}, u32[]{:S(2)}) collective-permute-start(bf16[80,256]{1,0:T(8,128)(2,1)S(1)} %get-tuple-element.124), channel_id=1, source_target_pairs={{0,4},{1,5},{2,6},{3,7},{4,0},{5,1},{6,2},{7,3},{8,12},{9,13},{10,... | collective-permute-start | bytes 122888 | tf_op jit(solution)/shard_map/ppermute | solution.py:411
  269.9 7.2 %collective-permute-start.50 = (bf16[80,256]{1,0:T(8,128)(2,1)S(1)}, bf16[80,256]{1,0:T(8,128)(2,1)S(1)}, u32[]{:S(2)}, u32[]{:S(2)}) collective-permute-start(bf16[80,256]{1,0:T(8,128)(2,1)S(1)} %get-tuple-element.122), channel_id=1, source_target_pairs={{0,2},{1,3},{2,0},{3,1},{4,6},{5,7},{6,4},{7,5},{8,10},{9,11},{10,... | collective-permute-start | bytes 122888 | tf_op jit(solution)/shard_map/ppermute | solution.py:411
  271.0 17.0 %collective-permute-start.56 = (bf16[80,1024]{1,0:T(8,128)(2,1)S(1)}, bf16[80,1024]{1,0:T(8,128)(2,1)S(1)}, u32[]{:S(2)}, u32[]{:S(2)}) collective-permute-start(bf16[80,1024]{1,0:T(8,128)(2,1)S(1)} %get-tuple-element.103), channel_id=1, source_target_pairs={{0,6},{1,7},{2,4},{3,5},{4,2},{5,3},{6,0},{7,1},{8,14},{9,15},{10,... | collective-permute-start | bytes 491528 | tf_op jit(solution)/shard_map/ppermute | solution.py:411
  273.4 16.2 %collective-permute-start.55 = (bf16[80,1024]{1,0:T(8,128)(2,1)S(1)}, bf16[80,1024]{1,0:T(8,128)(2,1)S(1)}, u32[]{:S(2)}, u32[]{:S(2)}) collective-permute-start(bf16[80,1024]{1,0:T(8,128)(2,1)S(1)} %get-tuple-element.104), channel_id=1, source_target_pairs={{0,4},{1,5},{2,6},{3,7},{4,0},{5,1},{6,2},{7,3},{8,12},{9,13},{10,... | collective-permute-start | bytes 491528 | tf_op jit(solution)/shard_map/ppermute | solution.py:411
  273.4 14.3 %collective-permute-start.61 = (bf16[64,704]{1,0:T(8,128)(2,1)S(1)}, bf16[64,704]{1,0:T(8,128)(2,1)S(1)}, u32[]{:S(2)}, u32[]{:S(2)}) collective-permute-start(bf16[64,704]{1,0:T(8,128)(2,1)S(1)} %get-tuple-element.99), channel_id=1, source_target_pairs={{0,24},{1,25},{2,26},{3,27},{4,28},{5,29},{6,30},{7,31},{8,16},{9,... | collective-permute-start | bytes 270344 | tf_op jit(solution)/shard_map/ppermute | solution.py:411
  276.9 10.8 %collective-permute-start.60 = (bf16[64,704]{1,0:T(8,128)(2,1)S(1)}, bf16[64,704]{1,0:T(8,128)(2,1)S(1)}, u32[]{:S(2)}, u32[]{:S(2)}) collective-permute-start(bf16[64,704]{1,0:T(8,128)(2,1)S(1)} %get-tuple-element.100), channel_id=1, source_target_pairs={{0,16},{1,17},{2,18},{3,19},{4,20},{5,21},{6,22},{7,23},{8,24},{9,... | collective-permute-start | bytes 270344 | tf_op jit(solution)/shard_map/ppermute | solution.py:411
  277.1 9.0 %collective-permute-start.53 = (bf16[40,256]{1,0:T(8,128)(2,1)S(1)}, bf16[40,256]{1,0:T(8,128)(2,1)S(1)}, u32[]{:S(2)}, u32[]{:S(2)}) collective-permute-start(bf16[40,256]{1,0:T(8,128)(2,1)S(1)} %slice.460), channel_id=1, source_target_pairs={{0,8},{1,9},{2,10},{3,11},{4,12},{5,13},{6,14},{7,15},{8,0},{9,1},... | collective-permute-start | bytes 61448 | tf_op jit(solution)/shard_map/ppermute | solution.py:411
  286.1 1.6 collective-permute-start.59
  287.7 5.6 %collective-permute-start.54 = (bf16[80,1024]{1,0:T(8,128)(2,1)S(1)}, bf16[80,1024]{1,0:T(8,128)(2,1)S(1)}, u32[]{:S(2)}, u32[]{:S(2)}) collective-permute-start(bf16[80,1024]{1,0:T(8,128)(2,1)S(1)} %get-tuple-element.102), channel_id=1, source_target_pairs={{0,2},{1,3},{2,0},{3,1},{4,6},{5,7},{6,4},{7,5},{8,10},{9,11},{10,... | collective-permute-start | bytes 491528 | tf_op jit(solution)/shard_map/ppermute | solution.py:411
  293.5 4.2 %collective-permute-start.57 = (bf16[32,512]{1,0:T(8,128)(2,1)S(1)}, bf16[32,512]{1,0:T(8,128)(2,1)S(1)}, u32[]{:S(2)}, u32[]{:S(2)}) collective-permute-start(bf16[32,512]{1,0:T(8,128)(2,1)S(1)} %slice.345), channel_id=1, source_target_pairs={{0,8},{1,9},{2,10},{3,11},{4,12},{5,13},{6,14},{7,15},{8,0},{9,1},... | collective-permute-start | bytes 98312 | tf_op jit(solution)/shard_map/ppermute | solution.py:411
  295.4 5.9 %collective-permute-start.58 = (bf16[48,1024]{1,0:T(8,128)(2,1)S(1)}, bf16[48,1024]{1,0:T(8,128)(2,1)S(1)}, u32[]{:S(2)}, u32[]{:S(2)}) collective-permute-start(bf16[48,1024]{1,0:T(8,128)(2,1)S(1)} %slice.347), channel_id=1, source_target_pairs={{0,0},{1,1},{2,2},{3,3},{4,4},{5,5},{6,6},{7,7},{8,16},{9,17},{10,... | collective-permute-start | bytes 294920 | tf_op jit(solution)/shard_map/ppermute | solution.py:428
  (62 other events, 403.7 us)
Sparse Core Ops, SparseCore 0:
  31.5 104.5 all-gather.2
  161.0 104.2 reduce-scatter.1

commit v4 on v3

--- a/solution.py
+++ b/solution.py
@@ -318,13 +318,27 @@
     return [(at, min(size, total - at)) for at in range(0, total, size)]
 
 
+def fetch_rows(sources, buffer, sem):
+    rows = sources[0].shape[0]
+    copies = [
+        pltpu.make_async_copy(source, buffer.at[pl.ds(n * rows, rows), :], sem.at[n])
+        for n, source in enumerate(sources)
+    ]
+    for copy in copies:
+        copy.start()
+    return copies
+
+
 def feed_kernel(*refs):
-    rows_refs, dy_refs = refs[:4], refs[4:8]
-    gate_ref, up_ref, down_ref, hidden_ref, dgate_ref, dup_ref, keep_ref, send_ref = refs[8:]
-    rows = rows_refs[0].shape[0]
+    sources = refs[:8]
+    gate_ref, up_ref, down_ref, hidden_ref, dgate_ref, dup_ref, keep_ref, send_ref, buffer, sem = refs[8:]
+    rows = sources[0].shape[0]
+    copies = fetch_rows(sources, buffer, sem)
     for pair in (0, 1):
-        left = jnp.concatenate([rows_refs[2 * pair][...], rows_refs[2 * pair + 1][...]])
-        dy = jnp.concatenate([dy_refs[2 * pair][...], dy_refs[2 * pair + 1][...]])
+        for n in (2 * pair, 2 * pair + 1, 2 * pair + 4, 2 * pair + 5):
+            copies[n].wait()
+        left = buffer[2 * pair * rows : 2 * (pair + 1) * rows]
+        dy = buffer[(2 * pair + 4) * rows : (2 * pair + 6) * rows]
         gate = product(left, gate_ref[...])
         up = product(left, up_ref[...])
         dhidden = times_transposed(dy, down_ref[...])
@@ -342,14 +356,16 @@
 
 
 def feed_grads_kernel(*refs):
-    rows_refs, dy_refs = refs[:4], refs[4:8]
-    down_ref, hidden_ref, dgate_ref, dup_ref, ggate_ref, gup_ref, gdown_ref, keep_ref, send_ref = refs[8:]
-    rows = rows_refs[0].shape[0]
-    for at, size in row_tiles(rows_refs[0].shape[1], 256):
-        left = jnp.concatenate([ref[:, at : at + size] for ref in rows_refs])
+    sources = refs[:8]
+    down_ref, hidden_ref, dgate_ref, dup_ref, ggate_ref, gup_ref, gdown_ref, keep_ref, send_ref, buffer, sem = refs[8:]
+    rows = sources[0].shape[0]
+    for copy in fetch_rows(sources, buffer, sem):
+        copy.wait()
+    for at, size in row_tiles(buffer.shape[1], 256):
+        left = buffer[: 4 * rows, at : at + size]
         ggate_ref[at : at + size] = contract_rows(left, dgate_ref[...]).astype(BF16)
         gup_ref[at : at + size] = contract_rows(left, dup_ref[...]).astype(BF16)
-    dy = jnp.concatenate([ref[...] for ref in dy_refs])
+    dy = buffer[4 * rows :]
     for at, size in row_tiles(hidden_ref.shape[1], 256):
         gdown_ref[at : at + size] = contract_rows(hidden_ref[:, at : at + size], dy).astype(BF16)
     for pair in (0, 1):
@@ -367,8 +383,9 @@
     return pl.pallas_call(
         feed_kernel,
         out_shape=[low, low, low, share, share],
-        in_specs=[pl.BlockSpec(memory_space=pltpu.VMEM)] * 11,
+        in_specs=[pl.BlockSpec(memory_space=pl.ANY)] * 8 + [pl.BlockSpec(memory_space=pltpu.VMEM)] * 3,
         out_specs=[pl.BlockSpec(memory_space=pltpu.VMEM)] * 5,
+        scratch_shapes=[pltpu.VMEM((8 * rows, width), BF16), pltpu.SemaphoreType.DMA((8,))],
         compiler_params=pltpu.CompilerParams(vmem_limit_bytes=40 << 20),
         cost_estimate=pl.CostEstimate(flops=5 * flops, bytes_accessed=11 << 20, transcendentals=4 * rows * units),
         name="feed",
@@ -384,8 +401,9 @@
         feed_grads_kernel,
         out_shape=[jax.ShapeDtypeStruct((width, units), BF16)] * 2
         + [jax.ShapeDtypeStruct((units, width), BF16), share, share],
-        in_specs=[pl.BlockSpec(memory_space=pltpu.VMEM)] * 12,
+        in_specs=[pl.BlockSpec(memory_space=pl.ANY)] * 8 + [pl.BlockSpec(memory_space=pltpu.VMEM)] * 4,
         out_specs=[pl.BlockSpec(memory_space=pltpu.VMEM)] * 5,
+        scratch_shapes=[pltpu.VMEM((8 * rows, width), BF16), pltpu.SemaphoreType.DMA((8,))],
         compiler_params=pltpu.CompilerParams(vmem_limit_bytes=40 << 20),
         cost_estimate=pl.CostEstimate(flops=4 * flops, bytes_accessed=14 << 20, transcendentals=0),
         name="feed_grads",
@@ -540,7 +558,7 @@
     x_two = tokens_two.astype(F32)
 
     first_pieces = gather(plan, first_message, half_far, (y_bit, x_bit), (1, 1))
-    second_pieces = gather(plan, second_message, half_far, (y_bit, x_bit), (4, 2))
+    second_pieces = gather(plan, second_message, half_far, (y_bit, x_bit), (4, 1))
     third_stack = jnp.concatenate([a for _, a in gather(plan, third_message, extra_bits, (), ())])
     extra_masks = masks_of(extra_bits)
     third_whole = lax.all_gather(third_stack, "ctx", axis=0, tiled=True)

time: 310 us -> 311 us (level)
    unnamed x144 -> x154, local copies, waits for them, and re-layouts: 20 us -> 22.8 us
    ppermute x60 -> x59, starting transfers between devices: 82.1 us -> 80.1 us  [swap(): return lax.ppermute(value, AXES, [(n, n ^ mask) for n in range(self.count)])]
    ppermute x60 -> x59, waiting for transfers between devices: 85.5 us -> 84.4 us  [swap(): return lax.ppermute(value, AXES, [(n, n ^ mask) for n in range(self.count)])]
  transfers between devices with their start and end apart: 64 -> 63, of which waited for: 24 -> 24; matrix products, arithmetic and copies ran while one was open for 14% -> 14% of each run, Pallas kernels for 10% -> 10%
where the time goes in v4:
time: 311 us
  waiting for transfers between devices  94.7 us (30%)
  starting transfers between devices  87.7 us (28%)
  Pallas kernels  43.4 us (14%)
  local copies, waits for them, and re-layouts  32.9 us (11%)
  other arithmetic  25.8 us (8%)
  between operations  18.1 us (6%)
  matrix products  7.99 us (3%)
    ppermute x59, waiting for transfers between devices, swap(): return lax.ppermute(value, AXES, [(n, n ^ mask) for n in range(self.count)])  84.4 us
    ppermute x59, starting transfers between devices, swap(): return lax.ppermute(value, AXES, [(n, n ^ mask) for n in range(self.count)])  80.1 us
    unnamed x154, local copies, waits for them, and re-layouts  22.8 us
    pallas_call x1, Pallas kernels, attend_back(): pl.pallas_call(attend_back_kernel, grid=(seqs, pairs // PAIRS_A_STEP), in...  15.7 us
    pallas_call x1, Pallas kernels, attend(): pl.pallas_call(attend_kernel, grid=(seqs, pairs // PAIRS_A_STEP), in_spec...  11.4 us
    ppermute x2, starting transfers between devices, deal(): return lax.ppermute(value, AXES, table)  7.35 us
  transfers between devices with their start and end apart: 63, of which 24 were waited for; matrix products, arithmetic and copies ran while one was open for 14% of the time, Pallas kernels for 10%

profile of v4, /device:TPU:1, one launch (start us, length us, event | category | flops | bytes accessed | tf_op | source)
XLA Modules:
  0.0 310.6 jit_solution(9276742095643057121)
XLA Ops:
  8.2 4.5 %collective-permute-start.7 = (bf16[48,1024]{1,0:T(8,128)(2,1)S(1)}, bf16[48,1024]{1,0:T(8,128)(2,1)S(1)}, u32[]{:S(2)}, u32[]{:S(2)}) collective-permute-start(bf16[48,1024]{1,0:T(8,128)(2,1)S(1)} %pad_maximum_fusion.8), channel_id=1, source_target_pairs={{0,0},{1,1},{2,2},{3,3},{4,4},{5,5},{6,6},{7,7},{8,16},{9,17},{10,... | collective-permute-start | bytes 294920 | tf_op jit(solution)/shard_map/ppermute | solution.py:446
  21.4 1.7 collective-permute-start.32
  23.2 1.4 collective-permute-start.2
  24.6 2.4 collective-permute-start.3
  27.0 3.4 %collective-permute-start.4 = (bf16[80,256]{1,0:T(8,128)(2,1)S(1)}, bf16[80,256]{1,0:T(8,128)(2,1)S(1)}, u32[]{:S(2)}, u32[]{:S(2)}) collective-permute-start(bf16[80,256]{1,0:T(8,128)(2,1)S(1)} %get-tuple-element.135), channel_id=1, source_target_pairs={{0,6},{1,7},{2,4},{3,5},{4,2},{5,3},{6,0},{7,1},{8,14},{9,15},{10,... | collective-permute-start | bytes 122888 | tf_op jit(solution)/shard_map/ppermute | solution.py:429
  31.9 1.2 collective-permute-start.5
  33.5 3.5 %collective-permute-start.9 = (bf16[80,1024]{1,0:T(8,128)(2,1)S(1)}, bf16[80,1024]{1,0:T(8,128)(2,1)S(1)}, u32[]{:S(2)}, u32[]{:S(2)}) collective-permute-start(bf16[80,1024]{1,0:T(8,128)(2,1)S(1)} %get-tuple-element.125), channel_id=1, source_target_pairs={{0,4},{1,5},{2,6},{3,7},{4,0},{5,1},{6,2},{7,3},{8,12},{9,13},{10,... | collective-permute-start | bytes 491528 | tf_op jit(solution)/shard_map/ppermute | solution.py:429
  41.2 1.2 collective-permute-start.12
  43.3 7.0 %collective-permute-done.10 = bf16[80,1024]{1,0:T(8,128)(2,1)S(1)} collective-permute-done((bf16[80,1024]{1,0:T(8,128)(2,1)S(1)}, bf16[80,1024]{1,0:T(8,128)(2,1)S(1)}, u32[]{:S(2)}, u32[]{:S(2)}) %collective-permute-start.10) | collective-permute-done | bytes 163872 | tf_op jit(solution)/shard_map/ppermute | solution.py:429
  53.9 2.2 collective-permute-done.13.refs_6_
  58.3 7.5 %collective-permute-start.16 = (bf16[2,128,256]{2,1,0:T(8,128)(2,1)S(1)}, bf16[2,128,256]{2,1,0:T(8,128)(2,1)S(1)}, u32[]{:S(2)}, u32[]{:S(2)}) collective-permute-start(bf16[2,128,256]{2,1,0:T(8,128)(2,1)S(1)} %bitcast.388), channel_id=1, source_target_pairs={{0,2},{1,3},{2,0},{3,1},{4,6},{5,7},{6,4},{7,5},{8,10},{9,11},{10,... | collective-permute-start | bytes 393224 | tf_op jit(solution)/shard_map/ppermute | solution.py:429
  65.7 2.1 collective-permute-start.17
  70.1 1.3 collective-permute-start.19
  72.3 5.7 %collective-permute-done.17 = bf16[2,128,256]{2,1,0:T(8,128)(2,1)S(1)} collective-permute-done((bf16[2,128,256]{2,1,0:T(8,128)(2,1)S(1)}, bf16[2,128,256]{2,1,0:T(8,128)(2,1)S(1)}, u32[]{:S(2)}, u32[]{:S(2)}) %collective-permute-start.17) | collective-permute-done | bytes 131104 | tf_op jit(solution)/shard_map/ppermute | solution.py:429
  78.0 1.5 collective-permute-start.22
  79.5 2.2 collective-permute-done.21
  81.8 3.7 %collective-permute-done.22 = bf16[1,2,128,256]{3,2,1,0:T(8,128)(2,1)S(1)} collective-permute-done((bf16[1,2,128,256]{3,2,1,0:T(8,128)(2,1)S(1)}, bf16[1,2,128,256]{3,2,1,0:T(8,128)(2,1)S(1)}, u32[]{:S(2)}, u32[]{:S(2)}) %collective-permute-start.22) | collective-permute-done | bytes 131104 | tf_op jit(solution)/shard_map/ppermute | solution.py:429
  85.5 4.0 %collective-permute-done.15.refs_8_ = bf16[8,80,1024]{2,1,0:T(8,128)(2,1)S(1)} collective-permute-done((bf16[8,80,1024]{2,1,0:T(8,128)(2,1)S(1)}, bf16[8,80,1024]{2,1,0:T(8,128)(2,1)S(1)}, u32[]{:S(2)}, u32[]{:S(2)}) %collective-permute-start.15) | collective-permute-done | bytes 1310752 | tf_op jit(solution)/shard_map/ppermute | solution.py:429
  90.3 1.5 convolution_convert_fusion.4
  91.8 11.4 %attend.1 = (bf16[2,4,256,256]{3,2,1,0:T(8,128)(2,1)}, bf16[2,4,256,256]{3,2,1,0:T(8,128)(2,1)}, f32[2,4,256,1]{3,2,1,0:T(8,128)}, bf16[2,128,512]{2,1,0:T(8,128)(2,1)}) custom-call(bf16[2,128,512]{2,1,0:T(8,128)(2,1)} %bitcast.401, bf16[256,512]{1,0:T(8,128)(2,1)} %bitcast.366, bf16[256,512]{1,0:T(8,128)(2,1)} %bitcast.368, ...), custom_call_target="tpu_custom_call" | custom-call | flops 2147483648 | bytes 6291456 | tf_op jit(solution)/shard_map/attend/pallas_call | solution.py:273
  103.3 1.4 fusion.49
  105.5 10.7 %collective-permute-start.23 = (f32[128,1024]{1,0:T(8,128)}, f32[128,1024]{1,0:T(8,128)}, u32[]{:S(2)}, u32[]{:S(2)}) collective-permute-start(f32[128,1024]{1,0:T(8,128)} %slice.327), channel_id=1, source_target_pairs={{0,8},{1,9},{2,10},{3,11},{4,12},{5,13},{6,14},{7,15},{8,0},{9,1},... | collective-permute-start | bytes 1572872 | tf_op jit(solution)/shard_map/ppermute | solution.py:429
  119.4 2.1 multiply_reduce_fusion.6
  123.4 2.8 collective-permute-done.28.refs_6_
  127.3 4.6 %collective-permute-done.25.refs_2_ = bf16[128,1024]{1,0:T(8,128)(2,1)S(1)} collective-permute-done((bf16[128,1024]{1,0:T(8,128)(2,1)S(1)}, bf16[128,1024]{1,0:T(8,128)(2,1)S(1)}, u32[]{:S(2)}, u32[]{:S(2)}) %collective-permute-start.25) | collective-permute-done | bytes 262176 | tf_op jit(solution)/shard_map/ppermute | solution.py:429
  132.7 2.0 all-gather.3.cloned.1.call-done
  134.7 2.5 copy-done.1
  145.7 6.2 %feed.1 = (bf16[512,704]{1,0:T(8,128)(2,1)S(1)}, bf16[512,704]{1,0:T(8,128)(2,1)S(1)}, bf16[512,704]{1,0:T(8,128)(2,1)S(1)}, f32[2,128,1024]{2,1,0:T(8,128)S(1)}, f32[2,128,1024]{2,1,0:T(8,128)S(1)}) custom-call(bf16[128,1024]{1,0:T(8,128)(2,1)S(1)} %multiply_convert_fusion.1.refs_0_, bf16[128,1024]{1,0:T(8,128)(2,1)S(1)} %copy-done.22, ...), custom_call_target="tpu_custom_call" | custom-call | flops 3690987520 | bytes 11534336 | tf_op jit(solution)/shard_map/feed/pallas_call | solution.py:383
  152.8 4.9 %feed_grads.1 = (bf16[1024,704]{1,0:T(8,128)(2,1)S(1)}, bf16[1024,704]{1,0:T(8,128)(2,1)S(1)}, bf16[704,1024]{1,0:T(8,128)(2,1)S(1)}, f32[2,128,1024]{2,1,0:T(8,128)S(1)}, f32[2,128,1024]{2,1,0:T(8,128)}) custom-call(bf16[128,1024]{1,0:T(8,128)(2,1)S(1)} %multiply_convert_fusion.1.refs_0_, bf16[128,1024]{1,0:T(8,128)(2,1)S(1)} %copy-done.23, ...), custom_call_target="tpu_custom_call" | custom-call | flops 2952790016 | bytes 14680064 | tf_op jit(solution)/shard_map/feed_grads/pallas_call | solution.py:400
  158.6 2.4 copy-done
  162.0 2.5 collective-permute-done.35
  165.6 6.7 %collective-permute-done.36 = bf16[128,1024]{1,0:T(8,128)(2,1)S(1)} collective-permute-done((bf16[128,1024]{1,0:T(8,128)(2,1)S(1)}, bf16[128,1024]{1,0:T(8,128)(2,1)S(1)}, u32[]{:S(2)}, u32[]{:S(2)}) %collective-permute-start.36) | collective-permute-done | bytes 262176 | tf_op jit(solution)/shard_map/ppermute | solution.py:429
  174.4 1.2 collective-permute-start.37
  175.5 1.2 collective-permute-done.37
  176.7 1.2 convolution_convert_fusion.3
  177.9 15.7 %attend_back.1 = (bf16[2,128,512]{2,1,0:T(8,128)(2,1)}, bf16[256,512]{1,0:T(8,128)(2,1)}, bf16[256,512]{1,0:T(8,128)(2,1)}, bf16[4,2,128,256]{3,2,1,0:T(8,128)(2,1)}, bf16[4,2,128,256]{3,2,1,0:T(8,128)(2,1)}) custom-call(bf16[2,128,512]{2,1,0:T(8,128)(2,1)} %bitcast.402, bf16[2,4,256,256]{3,2,1,0:T(8,128)(2,1)} %get-tuple-element.64.ql_ref, ...), custom_call_target="tpu_custom_call" | custom-call | flops 5368709120 | bytes 8388608 | tf_op jit(solution)/shard_map/attend_back/pallas_call | solution.py:297
  195.7 1.5 convolution_convert_fusion.1
  197.2 11.2 %collective-permute-done.38 = bf16[4,2,128,256]{3,2,1,0:T(8,128)(2,1)S(1)} collective-permute-done((bf16[4,2,128,256]{3,2,1,0:T(8,128)(2,1)}, bf16[4,2,128,256]{3,2,1,0:T(8,128)(2,1)S(1)}, u32[]{:S(2)}, u32[]{:S(2)}) %collective-permute-start.38) | collective-permute-done | bytes 524320 | tf_op jit(solution)/shard_map/ppermute | solution.py:429
  209.3 1.2 fusion.36
  210.5 1.6 collective-permute-start.41
  213.0 1.2 collective-permute-start.39
  214.7 1.6 cut_blocks.4
  216.2 1.1 collective-permute-start.47
  217.4 7.2 %collective-permute-done.40 = bf16[2,128,256]{2,1,0:T(8,128)(2,1)S(1)} collective-permute-done((bf16[2,128,256]{2,1,0:T(8,128)(2,1)S(1)}, bf16[2,128,256]{2,1,0:T(8,128)(2,1)S(1)}, u32[]{:S(2)}, u32[]{:S(2)}) %collective-permute-start.40) | collective-permute-done | bytes 131104 | tf_op jit(solution)/shard_map/ppermute | solution.py:429
  226.7 1.4 collective-permute-start.42
  229.8 1.1 collective-permute-start.34
  231.4 2.3 add_convert_fusion.1
  233.7 1.1 collective-permute-start.48
  235.3 1.3 multiply_reduce_fusion.2
  237.4 1.3 collective-permute-start.44
  239.0 3.8 %fusion.11 = (bf16[1,128,1024]{2,1,0:T(8,128)(2,1)}, bf16[1,128,1024]{2,1,0:T(8,128)(2,1)}) fusion(f32[256,1024]{1,0:T(8,128)} %copy-done.30, f32[128]{0:T(128)S(1)} %fusion.31, f32[1024]{0:T(1024)S(1)} %mul.320, f32[128]{0:T(128)S(1)} %add_rsqrt_fusion.1, f32[128,1024]{1,0:T(8,128)} %collective-permute-done.42, f32[256,1024]{1,0:T(8,128)} %copy-done.32, ...), kind=kLoop, calls=%fused_computation.47 | loop fusion | flops 2490368 | bytes 4728836 | tf_op jit(solution)/shard_map/broadcast_in_dim | solution.py:683
  242.7 13.4 %collective-permute-done.44 = bf16[4,80,256]{2,1,0:T(8,128)(2,1)S(1)} collective-permute-done((bf16[4,80,256]{2,1,0:T(8,128)(2,1)S(1)}, bf16[4,80,256]{2,1,0:T(8,128)(2,1)S(1)}, u32[]{:S(2)}, u32[]{:S(2)}) %collective-permute-start.44) | collective-permute-done | bytes 163872 | tf_op jit(solution)/shard_map/ppermute | solution.py:429
  256.9 1.7 add_convert_fusion
  259.6 1.3 collective-permute-done.45
  261.0 5.9 %reduce-scatter.2.cloned.1.call-done = bf16[1,432,704]{2,1,0:T(8,128)(2,1)} async-done(((bf16[8,432,704]{2,1,0:T(8,128)(2,1)}), bf16[1,432,704]{2,1,0:T(8,128)(2,1)}) %reduce-scatter.2.cloned.1.call-update) | async-done | bytes 608272 | tf_op jit(solution)/shard_map/reduce_scatter | solution.py:666
  269.0 2.5 collective-permute-start.51
  272.6 2.5 collective-permute-start.55
  275.2 3.1 %collective-permute-start.60 = (bf16[64,704]{1,0:T(8,128)(2,1)S(1)}, bf16[64,704]{1,0:T(8,128)(2,1)S(1)}, u32[]{:S(2)}, u32[]{:S(2)}) collective-permute-start(bf16[64,704]{1,0:T(8,128)(2,1)S(1)} %get-tuple-element.99), channel_id=1, source_target_pairs={{0,24},{1,25},{2,26},{3,27},{4,28},{5,29},{6,30},{7,31},{8,16},{9,... | collective-permute-start | bytes 270344 | tf_op jit(solution)/shard_map/ppermute | solution.py:429
  278.3 1.3 collective-permute-start.59
  279.6 6.1 %collective-permute-start.52 = (bf16[40,256]{1,0:T(8,128)(2,1)S(1)}, bf16[40,256]{1,0:T(8,128)(2,1)S(1)}, u32[]{:S(2)}, u32[]{:S(2)}) collective-permute-start(bf16[40,256]{1,0:T(8,128)(2,1)S(1)} %slice.460), channel_id=1, source_target_pairs={{0,8},{1,9},{2,10},{3,11},{4,12},{5,13},{6,14},{7,15},{8,0},{9,1},... | collective-permute-start | bytes 61448 | tf_op jit(solution)/shard_map/ppermute | solution.py:429
  288.5 2.4 collective-permute-done.54
  290.8 4.2 %collective-permute-done.53 = bf16[80,1024]{1,0:T(8,128)(2,1)S(1)} collective-permute-done((bf16[80,1024]{1,0:T(8,128)(2,1)S(1)}, bf16[80,1024]{1,0:T(8,128)(2,1)S(1)}, u32[]{:S(2)}, u32[]{:S(2)}) %collective-permute-start.53) | collective-permute-done | bytes 163872 | tf_op jit(solution)/shard_map/ppermute | solution.py:429
  296.5 2.9 collective-permute-start.57
  300.1 2.3 collective-permute-done.57
  (352 shorter events, 66.8 us)
Async XLA Ops:
  7.2 127.5 %all-gather.3.cloned.1.call-start = ((), (), s32[]{:S(2)}) async-start(), calls=%async_computation.2 | async-start | bytes 5971968 | tf_op jit(solution)/shard_map/all_gather | solution.py:564
  7.2 33.2 %collective-permute-start = (bf16[128,1024]{1,0:T(8,128)(2,1)}, bf16[128,1024]{1,0:T(8,128)(2,1)S(1)}, u32[]{:S(2)}, u32[]{:S(2)}) collective-permute-start(bf16[128,1024]{1,0:T(8,128)(2,1)} %bitcast.372), channel_id=1, source_target_pairs={{0,8},{1,9},{2,10},{3,11},{4,12},{5,13},{6,14},{7,15},{8,0},{9,1},... | collective-permute-start | bytes 786440 | tf_op jit(solution)/shard_map/ppermute | solution.py:429
  8.2 25.2 %collective-permute-start.7 = (bf16[48,1024]{1,0:T(8,128)(2,1)S(1)}, bf16[48,1024]{1,0:T(8,128)(2,1)S(1)}, u32[]{:S(2)}, u32[]{:S(2)}) collective-permute-start(bf16[48,1024]{1,0:T(8,128)(2,1)S(1)} %pad_maximum_fusion.8), channel_id=1, source_target_pairs={{0,0},{1,1},{2,2},{3,3},{4,4},{5,5},{6,6},{7,7},{8,16},{9,17},{10,... | collective-permute-start | bytes 294920 | tf_op jit(solution)/shard_map/ppermute | solution.py:446
  15.7 5.7 %collective-permute-start.1 = (bf16[104,256]{1,0:T(8,128)(2,1)S(1)}, bf16[104,256]{1,0:T(8,128)(2,1)S(1)}, u32[]{:S(2)}, u32[]{:S(2)}) collective-permute-start(bf16[104,256]{1,0:T(8,128)(2,1)S(1)} %pad_maximum_fusion.10), channel_id=1, source_target_pairs={{0,8},{1,9},{2,10},{3,11},{4,12},{5,13},{6,14},{7,15},{8,0},{9,1},... | collective-permute-start | bytes 159752 | tf_op jit(solution)/shard_map/ppermute | solution.py:429
  18.2 5.1 %collective-permute-start.30 = (bf16[64,704]{1,0:T(8,128)(2,1)S(1)}, bf16[64,704]{1,0:T(8,128)(2,1)S(1)}, u32[]{:S(2)}, u32[]{:S(2)}) collective-permute-start(bf16[64,704]{1,0:T(8,128)(2,1)S(1)} %bitcast.397), channel_id=1, source_target_pairs={{0,8},{1,9},{2,10},{3,11},{4,12},{5,13},{6,14},{7,15},{8,0},{9,1},... | collective-permute-start | bytes 270344 | tf_op jit(solution)/shard_map/ppermute | solution.py:429
  18.7 5.9 %collective-permute-start.31 = (bf16[64,704]{1,0:T(8,128)(2,1)S(1)}, bf16[64,704]{1,0:T(8,128)(2,1)S(1)}, u32[]{:S(2)}, u32[]{:S(2)}) collective-permute-start(bf16[64,704]{1,0:T(8,128)(2,1)S(1)} %bitcast.396), channel_id=1, source_target_pairs={{0,16},{1,17},{2,18},{3,19},{4,20},{5,21},{6,22},{7,23},{8,24},{9,... | collective-permute-start | bytes 270344 | tf_op jit(solution)/shard_map/ppermute | solution.py:429
  21.4 5.6 %collective-permute-start.32 = (bf16[64,704]{1,0:T(8,128)(2,1)S(1)}, bf16[64,704]{1,0:T(8,128)(2,1)S(1)}, u32[]{:S(2)}, u32[]{:S(2)}) collective-permute-start(bf16[64,704]{1,0:T(8,128)(2,1)S(1)} %bitcast.398), channel_id=1, source_target_pairs={{0,24},{1,25},{2,26},{3,27},{4,28},{5,29},{6,30},{7,31},{8,16},{9,... | collective-permute-start | bytes 270344 | tf_op jit(solution)/shard_map/ppermute | solution.py:429
  23.2 8.3 %collective-permute-start.2 = (bf16[80,256]{1,0:T(8,128)(2,1)S(1)}, bf16[80,256]{1,0:T(8,128)(2,1)S(1)}, u32[]{:S(2)}, u32[]{:S(2)}) collective-permute-start(bf16[80,256]{1,0:T(8,128)(2,1)S(1)} %get-tuple-element.135), channel_id=1, source_target_pairs={{0,2},{1,3},{2,0},{3,1},{4,6},{5,7},{6,4},{7,5},{8,10},{9,11},{10,... | collective-permute-start | bytes 122888 | tf_op jit(solution)/shard_map/ppermute | solution.py:429
  24.6 7.0 %collective-permute-start.3 = (bf16[80,256]{1,0:T(8,128)(2,1)S(1)}, bf16[80,256]{1,0:T(8,128)(2,1)S(1)}, u32[]{:S(2)}, u32[]{:S(2)}) collective-permute-start(bf16[80,256]{1,0:T(8,128)(2,1)S(1)} %get-tuple-element.135), channel_id=1, source_target_pairs={{0,4},{1,5},{2,6},{3,7},{4,0},{5,1},{6,2},{7,3},{8,12},{9,13},{10,... | collective-permute-start | bytes 122888 | tf_op jit(solution)/shard_map/ppermute | solution.py:429
  27.0 4.8 %collective-permute-start.4 = (bf16[80,256]{1,0:T(8,128)(2,1)S(1)}, bf16[80,256]{1,0:T(8,128)(2,1)S(1)}, u32[]{:S(2)}, u32[]{:S(2)}) collective-permute-start(bf16[80,256]{1,0:T(8,128)(2,1)S(1)} %get-tuple-element.135), channel_id=1, source_target_pairs={{0,6},{1,7},{2,4},{3,5},{4,2},{5,3},{6,0},{7,1},{8,14},{9,15},{10,... | collective-permute-start | bytes 122888 | tf_op jit(solution)/shard_map/ppermute | solution.py:429
  31.3 235.6 %reduce-scatter.2.cloned.1.call-start = ((), (), s32[]{:S(2)}) async-start(), calls=%async_computation.1 | async-start | bytes 5971968 | tf_op jit(solution)/shard_map/reduce_scatter | solution.py:666
  31.9 5.8 %collective-permute-start.5 = (bf16[4,80,256]{2,1,0:T(8,128)(2,1)S(1)}, bf16[4,80,256]{2,1,0:T(8,128)(2,1)S(1)}, u32[]{:S(2)}, u32[]{:S(2)}) collective-permute-start(bf16[4,80,256]{2,1,0:T(8,128)(2,1)S(1)} %pad_maximum_fusion.5), channel_id=1, source_target_pairs={{0,1},{1,0},{2,3},{3,2},{4,5},{5,4},{6,7},{7,6},{8,9},{9,8},{10,11... | collective-permute-start | bytes 491528 | tf_op jit(solution)/shard_map/ppermute | solution.py:429
  33.4 7.8 %collective-permute-start.8 = (bf16[80,1024]{1,0:T(8,128)(2,1)S(1)}, bf16[80,1024]{1,0:T(8,128)(2,1)S(1)}, u32[]{:S(2)}, u32[]{:S(2)}) collective-permute-start(bf16[80,1024]{1,0:T(8,128)(2,1)S(1)} %get-tuple-element.125), channel_id=1, source_target_pairs={{0,2},{1,3},{2,0},{3,1},{4,6},{5,7},{6,4},{7,5},{8,10},{9,11},{10,... | collective-permute-start | bytes 491528 | tf_op jit(solution)/shard_map/ppermute | solution.py:429
  33.5 9.8 %collective-permute-start.9 = (bf16[80,1024]{1,0:T(8,128)(2,1)S(1)}, bf16[80,1024]{1,0:T(8,128)(2,1)S(1)}, u32[]{:S(2)}, u32[]{:S(2)}) collective-permute-start(bf16[80,1024]{1,0:T(8,128)(2,1)S(1)} %get-tuple-element.125), channel_id=1, source_target_pairs={{0,4},{1,5},{2,6},{3,7},{4,0},{5,1},{6,2},{7,3},{8,12},{9,13},{10,... | collective-permute-start | bytes 491528 | tf_op jit(solution)/shard_map/ppermute | solution.py:429
  37.0 13.4 %collective-permute-start.10 = (bf16[80,1024]{1,0:T(8,128)(2,1)S(1)}, bf16[80,1024]{1,0:T(8,128)(2,1)S(1)}, u32[]{:S(2)}, u32[]{:S(2)}) collective-permute-start(bf16[80,1024]{1,0:T(8,128)(2,1)S(1)} %get-tuple-element.125), channel_id=1, source_target_pairs={{0,6},{1,7},{2,4},{3,5},{4,2},{5,3},{6,0},{7,1},{8,14},{9,15},{10,... | collective-permute-start | bytes 491528 | tf_op jit(solution)/shard_map/ppermute | solution.py:429
  37.7 14.9 %collective-permute-start.11 = (bf16[1,80,1024]{2,1,0:T(8,128)(2,1)S(1)}, bf16[1,80,1024]{2,1,0:T(8,128)(2,1)S(1)}, u32[]{:S(2)}, u32[]{:S(2)}) collective-permute-start(bf16[1,80,1024]{2,1,0:T(8,128)(2,1)S(1)} %get-tuple-element.126.refs_0_), channel_id=1, source_target_pairs={{0,1},{1,0},{2,3},{3,2},{4,5},{5,4},{6,7},{7,6},{8,9},{9,8},{10,11... | collective-permute-start | bytes 491528 | tf_op jit(solution)/shard_map/ppermute | solution.py:429
  40.4 49.8 %copy-start.42 = (bf16[128,1024]{1,0:T(8,128)(2,1)}, bf16[128,1024]{1,0:T(8,128)(2,1)S(1)}, u32[]{:S(2)}) copy-start(bf16[128,1024]{1,0:T(8,128)(2,1)S(1)} %collective-permute-done) | copy-start | bytes 786436
  40.5 16.4 %collective-permute-start.6 = (bf16[8,80,256]{2,1,0:T(8,128)(2,1)}, bf16[8,80,256]{2,1,0:T(8,128)(2,1)S(1)}, u32[]{:S(2)}, u32[]{:S(2)}) collective-permute-start(bf16[8,80,256]{2,1,0:T(8,128)(2,1)} %copy-done.55), channel_id=1, source_target_pairs={{0,16},{1,17},{2,18},{3,19},{4,20},{5,21},{6,22},{7,23},{8,24},{9,... | collective-permute-start | bytes 983048 | tf_op jit(solution)/shard_map/ppermute | solution.py:429
  41.2 12.1 %collective-permute-start.12 = (bf16[1,80,1024]{2,1,0:T(8,128)(2,1)S(1)}, bf16[1,80,1024]{2,1,0:T(8,128)(2,1)S(1)}, u32[]{:S(2)}, u32[]{:S(2)}) collective-permute-start(bf16[1,80,1024]{2,1,0:T(8,128)(2,1)S(1)} %bitcast.344), channel_id=1, source_target_pairs={{0,1},{1,0},{2,3},{3,2},{4,5},{5,4},{6,7},{7,6},{8,9},{9,8},{10,11... | collective-permute-start | bytes 491528 | tf_op jit(solution)/shard_map/ppermute | solution.py:429
  43.3 12.8 %collective-permute-start.13 = (bf16[1,80,1024]{2,1,0:T(8,128)(2,1)S(1)}, bf16[1,80,1024]{2,1,0:T(8,128)(2,1)S(1)}, u32[]{:S(2)}, u32[]{:S(2)}) collective-permute-start(bf16[1,80,1024]{2,1,0:T(8,128)(2,1)S(1)} %bitcast.346), channel_id=1, source_target_pairs={{0,1},{1,0},{2,3},{3,2},{4,5},{5,4},{6,7},{7,6},{8,9},{9,8},{10,11... | collective-permute-start | bytes 491528 | tf_op jit(solution)/shard_map/ppermute | solution.py:429
  50.3 18.6 %collective-permute-start.14 = (bf16[1,80,1024]{2,1,0:T(8,128)(2,1)S(1)}, bf16[1,80,1024]{2,1,0:T(8,128)(2,1)S(1)}, u32[]{:S(2)}, u32[]{:S(2)}) collective-permute-start(bf16[1,80,1024]{2,1,0:T(8,128)(2,1)S(1)} %bitcast.348), channel_id=1, source_target_pairs={{0,1},{1,0},{2,3},{3,2},{4,5},{5,4},{6,7},{7,6},{8,9},{9,8},{10,11... | collective-permute-start | bytes 491528 | tf_op jit(solution)/shard_map/ppermute | solution.py:429
  58.3 13.1 %collective-permute-start.16 = (bf16[2,128,256]{2,1,0:T(8,128)(2,1)S(1)}, bf16[2,128,256]{2,1,0:T(8,128)(2,1)S(1)}, u32[]{:S(2)}, u32[]{:S(2)}) collective-permute-start(bf16[2,128,256]{2,1,0:T(8,128)(2,1)S(1)} %bitcast.388), channel_id=1, source_target_pairs={{0,2},{1,3},{2,0},{3,1},{4,6},{5,7},{6,4},{7,5},{8,10},{9,11},{10,... | collective-permute-start | bytes 393224 | tf_op jit(solution)/shard_map/ppermute | solution.py:429
  65.7 12.2 %collective-permute-start.17 = (bf16[2,128,256]{2,1,0:T(8,128)(2,1)S(1)}, bf16[2,128,256]{2,1,0:T(8,128)(2,1)S(1)}, u32[]{:S(2)}, u32[]{:S(2)}) collective-permute-start(bf16[2,128,256]{2,1,0:T(8,128)(2,1)S(1)} %bitcast.389), channel_id=1, source_target_pairs={{0,4},{1,5},{2,6},{3,7},{4,0},{5,1},{6,2},{7,3},{8,12},{9,13},{10,... | collective-permute-start | bytes 393224 | tf_op jit(solution)/shard_map/ppermute | solution.py:429
  67.8 10.2 %collective-permute-start.18 = (bf16[2,128,256]{2,1,0:T(8,128)(2,1)S(1)}, bf16[2,128,256]{2,1,0:T(8,128)(2,1)S(1)}, u32[]{:S(2)}, u32[]{:S(2)}) collective-permute-start(bf16[2,128,256]{2,1,0:T(8,128)(2,1)S(1)} %bitcast.390), channel_id=1, source_target_pairs={{0,6},{1,7},{2,4},{3,5},{4,2},{5,3},{6,0},{7,1},{8,14},{9,15},{10,... | collective-permute-start | bytes 393224 | tf_op jit(solution)/shard_map/ppermute | solution.py:429
  68.9 20.6 %collective-permute-start.15 = (bf16[8,80,1024]{2,1,0:T(8,128)(2,1)S(1)}, bf16[8,80,1024]{2,1,0:T(8,128)(2,1)S(1)}, u32[]{:S(2)}, u32[]{:S(2)}) collective-permute-start(bf16[8,80,1024]{2,1,0:T(8,128)(2,1)S(1)} %constant_dynamic-update-slice_fusion.11), channel_id=1, source_target_pairs={{0,16},{1,17},{2,18},{3,19},{4,20},{5,21},{6,22},{7,23},{8,24},{9,... | collective-permute-start | bytes 3932168 | tf_op jit(solution)/shard_map/ppermute | solution.py:429
  70.1 9.4 %collective-permute-start.19 = (bf16[1,2,128,256]{3,2,1,0:T(8,128)(2,1)S(1)}, bf16[1,2,128,256]{3,2,1,0:T(8,128)(2,1)S(1)}, u32[]{:S(2)}, u32[]{:S(2)}) collective-permute-start(bf16[1,2,128,256]{3,2,1,0:T(8,128)(2,1)S(1)} %bitcast.392), channel_id=1, source_target_pairs={{0,1},{1,0},{2,3},{3,2},{4,5},{5,4},{6,7},{7,6},{8,9},{9,8},{10,11... | collective-permute-start | bytes 393224 | tf_op jit(solution)/shard_map/ppermute | solution.py:429
  71.4 8.2 %collective-permute-start.20 = (bf16[1,2,128,256]{3,2,1,0:T(8,128)(2,1)S(1)}, bf16[1,2,128,256]{3,2,1,0:T(8,128)(2,1)S(1)}, u32[]{:S(2)}, u32[]{:S(2)}) collective-permute-start(bf16[1,2,128,256]{3,2,1,0:T(8,128)(2,1)S(1)} %bitcast.387), channel_id=1, source_target_pairs={{0,1},{1,0},{2,3},{3,2},{4,5},{5,4},{6,7},{7,6},{8,9},{9,8},{10,11... | collective-permute-start | bytes 393224 | tf_op jit(solution)/shard_map/ppermute | solution.py:429
  78.0 3.8 %collective-permute-start.21 = (bf16[1,2,128,256]{3,2,1,0:T(8,128)(2,1)S(1)}, bf16[1,2,128,256]{3,2,1,0:T(8,128)(2,1)S(1)}, u32[]{:S(2)}, u32[]{:S(2)}) collective-permute-start(bf16[1,2,128,256]{3,2,1,0:T(8,128)(2,1)S(1)} %bitcast.386), channel_id=1, source_target_pairs={{0,1},{1,0},{2,3},{3,2},{4,5},{5,4},{6,7},{7,6},{8,9},{9,8},{10,11... | collective-permute-start | bytes 393224 | tf_op jit(solution)/shard_map/ppermute | solution.py:429
  78.0 7.5 %collective-permute-start.22 = (bf16[1,2,128,256]{3,2,1,0:T(8,128)(2,1)S(1)}, bf16[1,2,128,256]{3,2,1,0:T(8,128)(2,1)S(1)}, u32[]{:S(2)}, u32[]{:S(2)}) collective-permute-start(bf16[1,2,128,256]{3,2,1,0:T(8,128)(2,1)S(1)} %bitcast.385), channel_id=1, source_target_pairs={{0,1},{1,0},{2,3},{3,2},{4,5},{5,4},{6,7},{7,6},{8,9},{9,8},{10,11... | collective-permute-start | bytes 393224 | tf_op jit(solution)/shard_map/ppermute | solution.py:429
  105.5 13.8 %collective-permute-start.23 = (f32[128,1024]{1,0:T(8,128)}, f32[128,1024]{1,0:T(8,128)}, u32[]{:S(2)}, u32[]{:S(2)}) collective-permute-start(f32[128,1024]{1,0:T(8,128)} %slice.327), channel_id=1, source_target_pairs={{0,8},{1,9},{2,10},{3,11},{4,12},{5,13},{6,14},{7,15},{8,0},{9,1},... | collective-permute-start | bytes 1572872 | tf_op jit(solution)/shard_map/ppermute | solution.py:429
  118.1 8.1 %collective-permute-start.28 = (bf16[128,1024]{1,0:T(8,128)(2,1)S(1)}, bf16[128,1024]{1,0:T(8,128)(2,1)S(1)}, u32[]{:S(2)}, u32[]{:S(2)}) collective-permute-start(bf16[128,1024]{1,0:T(8,128)(2,1)S(1)} %bitcast_convert_fusion.refs_4_), channel_id=1, source_target_pairs={{0,16},{1,17},{2,18},{3,19},{4,20},{5,21},{6,22},{7,23},{8,24},{9,... | collective-permute-start | bytes 786440 | tf_op jit(solution)/shard_map/ppermute | solution.py:429
  122.4 9.4 %collective-permute-start.25 = (bf16[128,1024]{1,0:T(8,128)(2,1)S(1)}, bf16[128,1024]{1,0:T(8,128)(2,1)S(1)}, u32[]{:S(2)}, u32[]{:S(2)}) collective-permute-start(bf16[128,1024]{1,0:T(8,128)(2,1)S(1)} %multiply_convert_fusion.1.refs_0_), channel_id=1, source_target_pairs={{0,16},{1,17},{2,18},{3,19},{4,20},{5,21},{6,22},{7,23},{8,24},{9,... | collective-permute-start | bytes 786440 | tf_op jit(solution)/shard_map/ppermute | solution.py:429
  122.9 15.2 %collective-permute-start.27 = (bf16[128,1024]{1,0:T(8,128)(2,1)S(1)}, bf16[128,1024]{1,0:T(8,128)(2,1)S(1)}, u32[]{:S(2)}, u32[]{:S(2)}) collective-permute-start(bf16[128,1024]{1,0:T(8,128)(2,1)S(1)} %bitcast_convert_fusion.refs_4_), channel_id=1, source_target_pairs={{0,8},{1,9},{2,10},{3,11},{4,12},{5,13},{6,14},{7,15},{8,0},{9,1},... | collective-permute-start | bytes 786440 | tf_op jit(solution)/shard_map/ppermute | solution.py:429
  126.2 12.6 %collective-permute-start.29 = (bf16[128,1024]{1,0:T(8,128)(2,1)S(1)}, bf16[128,1024]{1,0:T(8,128)(2,1)S(1)}, u32[]{:S(2)}, u32[]{:S(2)}) collective-permute-start(bf16[128,1024]{1,0:T(8,128)(2,1)S(1)} %collective-permute-done.28.refs_6_), channel_id=1, source_target_pairs={{0,8},{1,9},{2,10},{3,11},{4,12},{5,13},{6,14},{7,15},{8,0},{9,1},... | collective-permute-start | bytes 786440 | tf_op jit(solution)/shard_map/ppermute | solution.py:429
  127.3 12.2 %collective-permute-start.24 = (bf16[128,1024]{1,0:T(8,128)(2,1)S(1)}, bf16[128,1024]{1,0:T(8,128)(2,1)S(1)}, u32[]{:S(2)}, u32[]{:S(2)}) collective-permute-start(bf16[128,1024]{1,0:T(8,128)(2,1)S(1)} %multiply_convert_fusion.1.refs_0_), channel_id=1, source_target_pairs={{0,8},{1,9},{2,10},{3,11},{4,12},{5,13},{6,14},{7,15},{8,0},{9,1},... | collective-permute-start | bytes 786440 | tf_op jit(solution)/shard_map/ppermute | solution.py:429
  131.8 8.4 %collective-permute-start.26 = (bf16[128,1024]{1,0:T(8,128)(2,1)S(1)}, bf16[128,1024]{1,0:T(8,128)(2,1)S(1)}, u32[]{:S(2)}, u32[]{:S(2)}) collective-permute-start(bf16[128,1024]{1,0:T(8,128)(2,1)S(1)} %collective-permute-done.25.refs_2_), channel_id=1, source_target_pairs={{0,8},{1,9},{2,10},{3,11},{4,12},{5,13},{6,14},{7,15},{8,0},{9,1},... | collective-permute-start | bytes 786440 | tf_op jit(solution)/shard_map/ppermute | solution.py:429
  161.1 3.5 %collective-permute-start.35 = (f32[2,128,1024]{2,1,0:T(8,128)}, f32[2,128,1024]{2,1,0:T(8,128)S(1)}, u32[]{:S(2)}, u32[]{:S(2)}) collective-permute-start(f32[2,128,1024]{2,1,0:T(8,128)} %copy-done.8), channel_id=1, source_target_pairs={{0,8},{1,9},{2,10},{3,11},{4,12},{5,13},{6,14},{7,15},{8,0},{9,1},... | collective-permute-start | bytes 3145736 | tf_op jit(solution)/shard_map/ppermute | solution.py:429
  164.6 7.7 %collective-permute-start.36 = (bf16[128,1024]{1,0:T(8,128)(2,1)S(1)}, bf16[128,1024]{1,0:T(8,128)(2,1)S(1)}, u32[]{:S(2)}, u32[]{:S(2)}) collective-permute-start(bf16[128,1024]{1,0:T(8,128)(2,1)S(1)} %fusion.14), channel_id=1, source_target_pairs={{0,16},{1,17},{2,18},{3,19},{4,20},{5,21},{6,22},{7,23},{8,24},{9,... | collective-permute-start | bytes 786440 | tf_op jit(solution)/shard_map/ppermute | solution.py:429
  174.4 2.3 collective-permute-start.37
  193.7 14.8 %collective-permute-start.38 = (bf16[4,2,128,256]{3,2,1,0:T(8,128)(2,1)}, bf16[4,2,128,256]{3,2,1,0:T(8,128)(2,1)S(1)}, u32[]{:S(2)}, u32[]{:S(2)}) collective-permute-start(bf16[4,2,128,256]{3,2,1,0:T(8,128)(2,1)} %get-tuple-element.69), channel_id=1, source_target_pairs={{0,1},{1,0},{2,3},{3,2},{4,5},{5,4},{6,7},{7,6},{8,9},{9,8},{10,11... | collective-permute-start | bytes 1572872 | tf_op jit(solution)/shard_map/ppermute | solution.py:429
  195.0 33.1 %collective-permute-start.33 = (f32[2,128,1024]{2,1,0:T(8,128)}, f32[2,128,1024]{2,1,0:T(8,128)S(1)}, u32[]{:S(2)}, u32[]{:S(2)}) collective-permute-start(f32[2,128,1024]{2,1,0:T(8,128)} %get-tuple-element.61), channel_id=1, source_target_pairs={{0,8},{1,9},{2,10},{3,11},{4,12},{5,13},{6,14},{7,15},{8,0},{9,1},... | collective-permute-start | bytes 3145736 | tf_op jit(solution)/shard_map/ppermute | solution.py:429
  210.5 6.8 %collective-permute-start.41 = (bf16[2,128,256]{2,1,0:T(8,128)(2,1)S(1)}, bf16[2,128,256]{2,1,0:T(8,128)(2,1)S(1)}, u32[]{:S(2)}, u32[]{:S(2)}) collective-permute-start(bf16[2,128,256]{2,1,0:T(8,128)(2,1)S(1)} %get-tuple-element.108), channel_id=1, source_target_pairs={{0,6},{1,7},{2,4},{3,5},{4,2},{5,3},{6,0},{7,1},{8,14},{9,15},{10,... | collective-permute-start | bytes 393224 | tf_op jit(solution)/shard_map/ppermute | solution.py:429
  212.2 12.3 %collective-permute-start.40 = (bf16[2,128,256]{2,1,0:T(8,128)(2,1)S(1)}, bf16[2,128,256]{2,1,0:T(8,128)(2,1)S(1)}, u32[]{:S(2)}, u32[]{:S(2)}) collective-permute-start(bf16[2,128,256]{2,1,0:T(8,128)(2,1)S(1)} %get-tuple-element.109), channel_id=1, source_target_pairs={{0,4},{1,5},{2,6},{3,7},{4,0},{5,1},{6,2},{7,3},{8,12},{9,13},{10,... | collective-permute-start | bytes 393224 | tf_op jit(solution)/shard_map/ppermute | solution.py:429
  213.0 11.6 %collective-permute-start.39 = (bf16[2,128,256]{2,1,0:T(8,128)(2,1)S(1)}, bf16[2,128,256]{2,1,0:T(8,128)(2,1)S(1)}, u32[]{:S(2)}, u32[]{:S(2)}) collective-permute-start(bf16[2,128,256]{2,1,0:T(8,128)(2,1)S(1)} %get-tuple-element.107), channel_id=1, source_target_pairs={{0,2},{1,3},{2,0},{3,1},{4,6},{5,7},{6,4},{7,5},{8,10},{9,11},{10,... | collective-permute-start | bytes 393224 | tf_op jit(solution)/shard_map/ppermute | solution.py:429
  216.2 15.1 %collective-permute-start.47 = (bf16[4,80,1024]{2,1,0:T(8,128)(2,1)}, bf16[4,80,1024]{2,1,0:T(8,128)(2,1)}, u32[]{:S(2)}, u32[]{:S(2)}) collective-permute-start(bf16[4,80,1024]{2,1,0:T(8,128)(2,1)} %get-tuple-element.79), channel_id=1, source_target_pairs={{0,16},{1,17},{2,18},{3,19},{4,20},{5,21},{6,22},{7,23},{8,24},{9,... | collective-permute-start | bytes 1966088 | tf_op jit(solution)/shard_map/ppermute | solution.py:429
  226.7 8.6 %collective-permute-start.42 = (f32[128,1024]{1,0:T(8,128)}, f32[128,1024]{1,0:T(8,128)}, u32[]{:S(2)}, u32[]{:S(2)}) collective-permute-start(f32[128,1024]{1,0:T(8,128)} %slice.338), channel_id=1, source_target_pairs={{0,8},{1,9},{2,10},{3,11},{4,12},{5,13},{6,14},{7,15},{8,0},{9,1},... | collective-permute-start | bytes 1572872 | tf_op jit(solution)/shard_map/ppermute | solution.py:429
  229.8 9.1 %collective-permute-start.34 = (bf16[128,1024]{1,0:T(8,128)(2,1)}, bf16[128,1024]{1,0:T(8,128)(2,1)}, u32[]{:S(2)}, u32[]{:S(2)}) collective-permute-start(bf16[128,1024]{1,0:T(8,128)(2,1)} %fusion.13), channel_id=1, source_target_pairs={{0,16},{1,17},{2,18},{3,19},{4,20},{5,21},{6,22},{7,23},{8,24},{9,... | collective-permute-start | bytes 786440 | tf_op jit(solution)/shard_map/ppermute | solution.py:429
  231.0 25.8 %collective-permute-start.46 = (bf16[4,80,1024]{2,1,0:T(8,128)(2,1)}, bf16[4,80,1024]{2,1,0:T(8,128)(2,1)}, u32[]{:S(2)}, u32[]{:S(2)}) collective-permute-start(bf16[4,80,1024]{2,1,0:T(8,128)(2,1)} %copy-done.9), channel_id=1, source_target_pairs={{0,16},{1,17},{2,18},{3,19},{4,20},{5,21},{6,22},{7,23},{8,24},{9,... | collective-permute-start | bytes 1966088 | tf_op jit(solution)/shard_map/ppermute | solution.py:429
  233.7 23.2 %collective-permute-start.48 = (bf16[4,80,1024]{2,1,0:T(8,128)(2,1)}, bf16[4,80,1024]{2,1,0:T(8,128)(2,1)}, u32[]{:S(2)}, u32[]{:S(2)}) collective-permute-start(bf16[4,80,1024]{2,1,0:T(8,128)(2,1)} %add_convert_fusion.1), channel_id=1, source_target_pairs={{0,1},{1,0},{2,3},{3,2},{4,5},{5,4},{6,7},{7,6},{8,9},{9,8},{10,11... | collective-permute-start | bytes 1966088 | tf_op jit(solution)/shard_map/ppermute | solution.py:429
  237.4 18.7 %collective-permute-start.44 = (bf16[4,80,256]{2,1,0:T(8,128)(2,1)S(1)}, bf16[4,80,256]{2,1,0:T(8,128)(2,1)S(1)}, u32[]{:S(2)}, u32[]{:S(2)}) collective-permute-start(bf16[4,80,256]{2,1,0:T(8,128)(2,1)S(1)} %get-tuple-element.73), channel_id=1, source_target_pairs={{0,16},{1,17},{2,18},{3,19},{4,20},{5,21},{6,22},{7,23},{8,24},{9,... | collective-permute-start | bytes 491528 | tf_op jit(solution)/shard_map/ppermute | solution.py:429
  238.7 20.9 %collective-permute-start.43 = (bf16[4,80,256]{2,1,0:T(8,128)(2,1)S(1)}, bf16[4,80,256]{2,1,0:T(8,128)(2,1)S(1)}, u32[]{:S(2)}, u32[]{:S(2)}) collective-permute-start(bf16[4,80,256]{2,1,0:T(8,128)(2,1)S(1)} %get-tuple-element.71), channel_id=1, source_target_pairs={{0,16},{1,17},{2,18},{3,19},{4,20},{5,21},{6,22},{7,23},{8,24},{9,... | collective-permute-start | bytes 491528 | tf_op jit(solution)/shard_map/ppermute | solution.py:429
  256.1 4.8 %collective-permute-start.45 = (bf16[4,80,256]{2,1,0:T(8,128)(2,1)S(1)}, bf16[4,80,256]{2,1,0:T(8,128)(2,1)S(1)}, u32[]{:S(2)}, u32[]{:S(2)}) collective-permute-start(bf16[4,80,256]{2,1,0:T(8,128)(2,1)S(1)} %add_convert_fusion.4), channel_id=1, source_target_pairs={{0,1},{1,0},{2,3},{3,2},{4,5},{5,4},{6,7},{7,6},{8,9},{9,8},{10,11... | collective-permute-start | bytes 491528 | tf_op jit(solution)/shard_map/ppermute | solution.py:429
  269.0 6.2 %collective-permute-start.51 = (bf16[80,256]{1,0:T(8,128)(2,1)S(1)}, bf16[80,256]{1,0:T(8,128)(2,1)S(1)}, u32[]{:S(2)}, u32[]{:S(2)}) collective-permute-start(bf16[80,256]{1,0:T(8,128)(2,1)S(1)} %get-tuple-element.123), channel_id=1, source_target_pairs={{0,6},{1,7},{2,4},{3,5},{4,2},{5,3},{6,0},{7,1},{8,14},{9,15},{10,... | collective-permute-start | bytes 122888 | tf_op jit(solution)/shard_map/ppermute | solution.py:429
  271.5 6.8 %collective-permute-start.50 = (bf16[80,256]{1,0:T(8,128)(2,1)S(1)}, bf16[80,256]{1,0:T(8,128)(2,1)S(1)}, u32[]{:S(2)}, u32[]{:S(2)}) collective-permute-start(bf16[80,256]{1,0:T(8,128)(2,1)S(1)} %get-tuple-element.124), channel_id=1, source_target_pairs={{0,4},{1,5},{2,6},{3,7},{4,0},{5,1},{6,2},{7,3},{8,12},{9,13},{10,... | collective-permute-start | bytes 122888 | tf_op jit(solution)/shard_map/ppermute | solution.py:429
  272.3 7.3 %collective-permute-start.49 = (bf16[80,256]{1,0:T(8,128)(2,1)S(1)}, bf16[80,256]{1,0:T(8,128)(2,1)S(1)}, u32[]{:S(2)}, u32[]{:S(2)}) collective-permute-start(bf16[80,256]{1,0:T(8,128)(2,1)S(1)} %get-tuple-element.122), channel_id=1, source_target_pairs={{0,2},{1,3},{2,0},{3,1},{4,6},{5,7},{6,4},{7,5},{8,10},{9,11},{10,... | collective-permute-start | bytes 122888 | tf_op jit(solution)/shard_map/ppermute | solution.py:429
  272.6 15.8 %collective-permute-start.55 = (bf16[80,1024]{1,0:T(8,128)(2,1)S(1)}, bf16[80,1024]{1,0:T(8,128)(2,1)S(1)}, u32[]{:S(2)}, u32[]{:S(2)}) collective-permute-start(bf16[80,1024]{1,0:T(8,128)(2,1)S(1)} %get-tuple-element.103), channel_id=1, source_target_pairs={{0,6},{1,7},{2,4},{3,5},{4,2},{5,3},{6,0},{7,1},{8,14},{9,15},{10,... | collective-permute-start | bytes 491528 | tf_op jit(solution)/shard_map/ppermute | solution.py:429
  275.1 15.7 %collective-permute-start.54 = (bf16[80,1024]{1,0:T(8,128)(2,1)S(1)}, bf16[80,1024]{1,0:T(8,128)(2,1)S(1)}, u32[]{:S(2)}, u32[]{:S(2)}) collective-permute-start(bf16[80,1024]{1,0:T(8,128)(2,1)S(1)} %get-tuple-element.104), channel_id=1, source_target_pairs={{0,4},{1,5},{2,6},{3,7},{4,0},{5,1},{6,2},{7,3},{8,12},{9,13},{10,... | collective-permute-start | bytes 491528 | tf_op jit(solution)/shard_map/ppermute | solution.py:429
  275.2 13.0 %collective-permute-start.60 = (bf16[64,704]{1,0:T(8,128)(2,1)S(1)}, bf16[64,704]{1,0:T(8,128)(2,1)S(1)}, u32[]{:S(2)}, u32[]{:S(2)}) collective-permute-start(bf16[64,704]{1,0:T(8,128)(2,1)S(1)} %get-tuple-element.99), channel_id=1, source_target_pairs={{0,24},{1,25},{2,26},{3,27},{4,28},{5,29},{6,30},{7,31},{8,16},{9,... | collective-permute-start | bytes 270344 | tf_op jit(solution)/shard_map/ppermute | solution.py:429
  278.3 9.8 %collective-permute-start.59 = (bf16[64,704]{1,0:T(8,128)(2,1)S(1)}, bf16[64,704]{1,0:T(8,128)(2,1)S(1)}, u32[]{:S(2)}, u32[]{:S(2)}) collective-permute-start(bf16[64,704]{1,0:T(8,128)(2,1)S(1)} %get-tuple-element.100), channel_id=1, source_target_pairs={{0,16},{1,17},{2,18},{3,19},{4,20},{5,21},{6,22},{7,23},{8,24},{9,... | collective-permute-start | bytes 270344 | tf_op jit(solution)/shard_map/ppermute | solution.py:429
  279.6 6.9 %collective-permute-start.52 = (bf16[40,256]{1,0:T(8,128)(2,1)S(1)}, bf16[40,256]{1,0:T(8,128)(2,1)S(1)}, u32[]{:S(2)}, u32[]{:S(2)}) collective-permute-start(bf16[40,256]{1,0:T(8,128)(2,1)S(1)} %slice.460), channel_id=1, source_target_pairs={{0,8},{1,9},{2,10},{3,11},{4,12},{5,13},{6,14},{7,15},{8,0},{9,1},... | collective-permute-start | bytes 61448 | tf_op jit(solution)/shard_map/ppermute | solution.py:429
  286.5 1.6 collective-permute-start.58
  288.1 6.8 %collective-permute-start.53 = (bf16[80,1024]{1,0:T(8,128)(2,1)S(1)}, bf16[80,1024]{1,0:T(8,128)(2,1)S(1)}, u32[]{:S(2)}, u32[]{:S(2)}) collective-permute-start(bf16[80,1024]{1,0:T(8,128)(2,1)S(1)} %get-tuple-element.102), channel_id=1, source_target_pairs={{0,2},{1,3},{2,0},{3,1},{4,6},{5,7},{6,4},{7,5},{8,10},{9,11},{10,... | collective-permute-start | bytes 491528 | tf_op jit(solution)/shard_map/ppermute | solution.py:429
  295.1 4.3 %collective-permute-start.56 = (bf16[32,512]{1,0:T(8,128)(2,1)S(1)}, bf16[32,512]{1,0:T(8,128)(2,1)S(1)}, u32[]{:S(2)}, u32[]{:S(2)}) collective-permute-start(bf16[32,512]{1,0:T(8,128)(2,1)S(1)} %slice.345), channel_id=1, source_target_pairs={{0,8},{1,9},{2,10},{3,11},{4,12},{5,13},{6,14},{7,15},{8,0},{9,1},... | collective-permute-start | bytes 98312 | tf_op jit(solution)/shard_map/ppermute | solution.py:429
  296.5 5.9 %collective-permute-start.57 = (bf16[48,1024]{1,0:T(8,128)(2,1)S(1)}, bf16[48,1024]{1,0:T(8,128)(2,1)S(1)}, u32[]{:S(2)}, u32[]{:S(2)}) collective-permute-start(bf16[48,1024]{1,0:T(8,128)(2,1)S(1)} %slice.347), channel_id=1, source_target_pairs={{0,0},{1,1},{2,2},{3,3},{4,4},{5,5},{6,6},{7,7},{8,16},{9,17},{10,... | collective-permute-start | bytes 294920 | tf_op jit(solution)/shard_map/ppermute | solution.py:446
  (63 other events, 408.9 us)
Sparse Core Ops, SparseCore 0:
  31.4 103.2 all-gather.2
  161.2 105.6 reduce-scatter.1

commit v5 on v3

--- a/solution.py
+++ b/solution.py
@@ -540,7 +540,7 @@
     x_two = tokens_two.astype(F32)
 
     first_pieces = gather(plan, first_message, half_far, (y_bit, x_bit), (1, 1))
-    second_pieces = gather(plan, second_message, half_far, (y_bit, x_bit), (4, 2))
+    second_pieces = gather(plan, second_message, half_far, (y_bit, x_bit), (4, 1))
     third_stack = jnp.concatenate([a for _, a in gather(plan, third_message, extra_bits, (), ())])
     extra_masks = masks_of(extra_bits)
     third_whole = lax.all_gather(third_stack, "ctx", axis=0, tiled=True)

time: 310 us -> 308 us (level)
  starting transfers between devices: 88.9 us -> 83.7 us
    ppermute x60 -> x59, starting transfers between devices: 82.1 us -> 75.7 us  [swap(): return lax.ppermute(value, AXES, [(n, n ^ mask) for n in range(self.count)])]
    unnamed x144 -> x154, local copies, waits for them, and re-layouts: 20 us -> 22.8 us
    ppermute x60 -> x59, waiting for transfers between devices: 85.5 us -> 86.3 us  [swap(): return lax.ppermute(value, AXES, [(n, n ^ mask) for n in range(self.count)])]
  transfers between devices with their start and end apart: 64 -> 63, of which waited for: 24 -> 23; matrix products, arithmetic and copies ran while one was open for 14% -> 15% of each run, Pallas kernels for 10% -> 10%
where the time goes in v5:
time: 308 us; the launch traced here: 306 us
  waiting for transfers between devices  95.7 us (31%)
  starting transfers between devices  83.7 us (27%)
  Pallas kernels  42 us (14%)
  local copies, waits for them, and re-layouts  32.9 us (11%)
  other arithmetic  25.8 us (8%)
  between operations  18.1 us (6%)
  matrix products  7.99 us (3%)
    ppermute x59, waiting for transfers between devices, swap(): return lax.ppermute(value, AXES, [(n, n ^ mask) for n in range(self.count)])  86.3 us
    ppermute x59, starting transfers between devices, swap(): return lax.ppermute(value, AXES, [(n, n ^ mask) for n in range(self.count)])  75.7 us
    unnamed x154, local copies, waits for them, and re-layouts  22.8 us
    pallas_call x1, Pallas kernels, attend_back(): pl.pallas_call(attend_back_kernel, grid=(seqs, pairs // PAIRS_A_STEP), in...  15.9 us
    pallas_call x1, Pallas kernels, attend(): pl.pallas_call(attend_kernel, grid=(seqs, pairs // PAIRS_A_STEP), in_spec...  11.4 us
    ppermute x2, starting transfers between devices, deal(): return lax.ppermute(value, AXES, table)  7.96 us
  transfers between devices with their start and end apart: 63, of which 23 were waited for; matrix products, arithmetic and copies ran while one was open for 15% of the time, Pallas kernels for 10%

profile of v5, /device:TPU:1, one launch (start us, length us, event | category | flops | bytes accessed | tf_op | source)
XLA Modules:
  0.0 306.2 jit_solution(10510802658901205514)
XLA Ops:
  8.2 4.5 %collective-permute-start.7 = (bf16[48,1024]{1,0:T(8,128)(2,1)S(1)}, bf16[48,1024]{1,0:T(8,128)(2,1)S(1)}, u32[]{:S(2)}, u32[]{:S(2)}) collective-permute-start(bf16[48,1024]{1,0:T(8,128)(2,1)S(1)} %pad_maximum_fusion.8), channel_id=1, source_target_pairs={{0,0},{1,1},{2,2},{3,3},{4,4},{5,5},{6,6},{7,7},{8,16},{9,17},{10,... | collective-permute-start | bytes 294920 | tf_op jit(solution)/shard_map/ppermute | solution.py:428
  21.4 1.7 collective-permute-start.32
  23.2 1.4 collective-permute-start.2
  24.6 2.4 collective-permute-start.3
  27.0 3.4 %collective-permute-start.4 = (bf16[80,256]{1,0:T(8,128)(2,1)S(1)}, bf16[80,256]{1,0:T(8,128)(2,1)S(1)}, u32[]{:S(2)}, u32[]{:S(2)}) collective-permute-start(bf16[80,256]{1,0:T(8,128)(2,1)S(1)} %get-tuple-element.135), channel_id=1, source_target_pairs={{0,6},{1,7},{2,4},{3,5},{4,2},{5,3},{6,0},{7,1},{8,14},{9,15},{10,... | collective-permute-start | bytes 122888 | tf_op jit(solution)/shard_map/ppermute | solution.py:411
  31.9 1.2 collective-permute-start.5
  33.5 3.5 %collective-permute-start.9 = (bf16[80,1024]{1,0:T(8,128)(2,1)S(1)}, bf16[80,1024]{1,0:T(8,128)(2,1)S(1)}, u32[]{:S(2)}, u32[]{:S(2)}) collective-permute-start(bf16[80,1024]{1,0:T(8,128)(2,1)S(1)} %get-tuple-element.125), channel_id=1, source_target_pairs={{0,4},{1,5},{2,6},{3,7},{4,0},{5,1},{6,2},{7,3},{8,12},{9,13},{10,... | collective-permute-start | bytes 491528 | tf_op jit(solution)/shard_map/ppermute | solution.py:411
  41.2 1.2 collective-permute-start.12
  43.3 7.0 %collective-permute-done.10 = bf16[80,1024]{1,0:T(8,128)(2,1)S(1)} collective-permute-done((bf16[80,1024]{1,0:T(8,128)(2,1)S(1)}, bf16[80,1024]{1,0:T(8,128)(2,1)S(1)}, u32[]{:S(2)}, u32[]{:S(2)}) %collective-permute-start.10) | collective-permute-done | bytes 163872 | tf_op jit(solution)/shard_map/ppermute | solution.py:411
  53.9 2.2 collective-permute-done.13.refs_6_
  58.3 7.5 %collective-permute-start.16 = (bf16[2,128,256]{2,1,0:T(8,128)(2,1)S(1)}, bf16[2,128,256]{2,1,0:T(8,128)(2,1)S(1)}, u32[]{:S(2)}, u32[]{:S(2)}) collective-permute-start(bf16[2,128,256]{2,1,0:T(8,128)(2,1)S(1)} %bitcast.388), channel_id=1, source_target_pairs={{0,2},{1,3},{2,0},{3,1},{4,6},{5,7},{6,4},{7,5},{8,10},{9,11},{10,... | collective-permute-start | bytes 393224 | tf_op jit(solution)/shard_map/ppermute | solution.py:411
  65.7 2.1 collective-permute-start.17
  67.8 1.1 collective-permute-start.18
  68.9 1.1 collective-permute-start.15
  70.1 1.3 collective-permute-start.19
  72.3 5.7 %collective-permute-done.17 = bf16[2,128,256]{2,1,0:T(8,128)(2,1)S(1)} collective-permute-done((bf16[2,128,256]{2,1,0:T(8,128)(2,1)S(1)}, bf16[2,128,256]{2,1,0:T(8,128)(2,1)S(1)}, u32[]{:S(2)}, u32[]{:S(2)}) %collective-permute-start.17) | collective-permute-done | bytes 131104 | tf_op jit(solution)/shard_map/ppermute | solution.py:411
  78.0 1.5 collective-permute-start.22
  79.5 2.2 collective-permute-done.21
  81.8 3.7 %collective-permute-done.22 = bf16[1,2,128,256]{3,2,1,0:T(8,128)(2,1)S(1)} collective-permute-done((bf16[1,2,128,256]{3,2,1,0:T(8,128)(2,1)S(1)}, bf16[1,2,128,256]{3,2,1,0:T(8,128)(2,1)S(1)}, u32[]{:S(2)}, u32[]{:S(2)}) %collective-permute-start.22) | collective-permute-done | bytes 131104 | tf_op jit(solution)/shard_map/ppermute | solution.py:411
  85.5 4.0 %collective-permute-done.15.refs_8_ = bf16[8,80,1024]{2,1,0:T(8,128)(2,1)S(1)} collective-permute-done((bf16[8,80,1024]{2,1,0:T(8,128)(2,1)S(1)}, bf16[8,80,1024]{2,1,0:T(8,128)(2,1)S(1)}, u32[]{:S(2)}, u32[]{:S(2)}) %collective-permute-start.15) | collective-permute-done | bytes 1310752 | tf_op jit(solution)/shard_map/ppermute | solution.py:411
  90.3 1.5 convolution_convert_fusion.4
  91.8 11.4 %attend.1 = (bf16[2,4,256,256]{3,2,1,0:T(8,128)(2,1)}, bf16[2,4,256,256]{3,2,1,0:T(8,128)(2,1)}, f32[2,4,256,1]{3,2,1,0:T(8,128)}, bf16[2,128,512]{2,1,0:T(8,128)(2,1)}) custom-call(bf16[2,128,512]{2,1,0:T(8,128)(2,1)} %bitcast.401, bf16[256,512]{1,0:T(8,128)(2,1)} %bitcast.366, bf16[256,512]{1,0:T(8,128)(2,1)} %bitcast.368, ...), custom_call_target="tpu_custom_call" | custom-call | flops 2147483648 | bytes 6291456 | tf_op jit(solution)/shard_map/attend/pallas_call | solution.py:273
  103.3 1.4 fusion.49
  105.6 10.7 %collective-permute-start.23 = (f32[128,1024]{1,0:T(8,128)}, f32[128,1024]{1,0:T(8,128)}, u32[]{:S(2)}, u32[]{:S(2)}) collective-permute-start(f32[128,1024]{1,0:T(8,128)} %slice.327), channel_id=1, source_target_pairs={{0,8},{1,9},{2,10},{3,11},{4,12},{5,13},{6,14},{7,15},{8,0},{9,1},... | collective-permute-start | bytes 1572872 | tf_op jit(solution)/shard_map/ppermute | solution.py:411
  119.4 2.1 multiply_reduce_fusion.6
  123.4 2.8 collective-permute-done.28.refs_6_
  127.3 4.6 %collective-permute-done.25.refs_2_ = bf16[128,1024]{1,0:T(8,128)(2,1)S(1)} collective-permute-done((bf16[128,1024]{1,0:T(8,128)(2,1)S(1)}, bf16[128,1024]{1,0:T(8,128)(2,1)S(1)}, u32[]{:S(2)}, u32[]{:S(2)}) %collective-permute-start.25) | collective-permute-done | bytes 262176 | tf_op jit(solution)/shard_map/ppermute | solution.py:411
  132.7 2.0 all-gather.3.cloned.1.call-done
  134.7 2.5 copy-done.1
  145.7 5.0 %feed.1 = (bf16[512,704]{1,0:T(8,128)(2,1)S(1)}, bf16[512,704]{1,0:T(8,128)(2,1)S(1)}, bf16[512,704]{1,0:T(8,128)(2,1)S(1)}, f32[2,128,1024]{2,1,0:T(8,128)S(1)}, f32[2,128,1024]{2,1,0:T(8,128)S(1)}) custom-call(bf16[128,1024]{1,0:T(8,128)(2,1)S(1)} %multiply_convert_fusion.1.refs_0_, bf16[128,1024]{1,0:T(8,128)(2,1)S(1)} %copy-done.22, ...), custom_call_target="tpu_custom_call" | custom-call | flops 3690987520 | bytes 11534336 | tf_op jit(solution)/shard_map/feed/pallas_call | solution.py:367
  151.7 4.4 %feed_grads.1 = (bf16[1024,704]{1,0:T(8,128)(2,1)S(1)}, bf16[1024,704]{1,0:T(8,128)(2,1)S(1)}, bf16[704,1024]{1,0:T(8,128)(2,1)S(1)}, f32[2,128,1024]{2,1,0:T(8,128)S(1)}, f32[2,128,1024]{2,1,0:T(8,128)}) custom-call(bf16[128,1024]{1,0:T(8,128)(2,1)S(1)} %multiply_convert_fusion.1.refs_0_, bf16[128,1024]{1,0:T(8,128)(2,1)S(1)} %copy-done.23, ...), custom_call_target="tpu_custom_call" | custom-call | flops 2952790016 | bytes 14680064 | tf_op jit(solution)/shard_map/feed_grads/pallas_call | solution.py:383
  157.1 2.4 copy-done
  160.5 2.5 collective-permute-done.35
  164.0 6.7 %collective-permute-done.36 = bf16[128,1024]{1,0:T(8,128)(2,1)S(1)} collective-permute-done((bf16[128,1024]{1,0:T(8,128)(2,1)S(1)}, bf16[128,1024]{1,0:T(8,128)(2,1)S(1)}, u32[]{:S(2)}, u32[]{:S(2)}) %collective-permute-start.36) | collective-permute-done | bytes 262176 | tf_op jit(solution)/shard_map/ppermute | solution.py:411
  172.8 1.2 collective-permute-start.37
  173.9 1.2 collective-permute-done.37
  175.1 1.2 convolution_convert_fusion.3
  176.4 15.9 %attend_back.1 = (bf16[2,128,512]{2,1,0:T(8,128)(2,1)}, bf16[256,512]{1,0:T(8,128)(2,1)}, bf16[256,512]{1,0:T(8,128)(2,1)}, bf16[4,2,128,256]{3,2,1,0:T(8,128)(2,1)}, bf16[4,2,128,256]{3,2,1,0:T(8,128)(2,1)}) custom-call(bf16[2,128,512]{2,1,0:T(8,128)(2,1)} %bitcast.402, bf16[2,4,256,256]{3,2,1,0:T(8,128)(2,1)} %get-tuple-element.64.ql_ref, ...), custom_call_target="tpu_custom_call" | custom-call | flops 5368709120 | bytes 8388608 | tf_op jit(solution)/shard_map/attend_back/pallas_call | solution.py:297
  192.3 1.1 collective-permute-start.38
  194.3 1.5 convolution_convert_fusion.1
  195.8 11.0 %collective-permute-done.38 = bf16[4,2,128,256]{3,2,1,0:T(8,128)(2,1)S(1)} collective-permute-done((bf16[4,2,128,256]{3,2,1,0:T(8,128)(2,1)}, bf16[4,2,128,256]{3,2,1,0:T(8,128)(2,1)S(1)}, u32[]{:S(2)}, u32[]{:S(2)}) %collective-permute-start.38) | collective-permute-done | bytes 524320 | tf_op jit(solution)/shard_map/ppermute | solution.py:411
  207.6 1.2 fusion.36
  208.9 1.7 collective-permute-start.41
  213.0 1.6 cut_blocks.4
  214.6 1.3 collective-permute-start.47
  215.9 7.3 %collective-permute-done.40 = bf16[2,128,256]{2,1,0:T(8,128)(2,1)S(1)} collective-permute-done((bf16[2,128,256]{2,1,0:T(8,128)(2,1)S(1)}, bf16[2,128,256]{2,1,0:T(8,128)(2,1)S(1)}, u32[]{:S(2)}, u32[]{:S(2)}) %collective-permute-start.40) | collective-permute-done | bytes 131104 | tf_op jit(solution)/shard_map/ppermute | solution.py:411
  225.4 1.3 collective-permute-start.42
  229.9 2.3 add_convert_fusion.1
  233.7 1.3 multiply_reduce_fusion.2
  235.8 1.3 collective-permute-start.44
  237.4 3.8 %fusion.11 = (bf16[1,128,1024]{2,1,0:T(8,128)(2,1)}, bf16[1,128,1024]{2,1,0:T(8,128)(2,1)}) fusion(f32[256,1024]{1,0:T(8,128)} %copy-done.30, f32[128]{0:T(128)S(1)} %fusion.31, f32[1024]{0:T(1024)S(1)} %mul.320, f32[128]{0:T(128)S(1)} %add_rsqrt_fusion.1, f32[128,1024]{1,0:T(8,128)} %collective-permute-done.42, f32[256,1024]{1,0:T(8,128)} %copy-done.32, ...), kind=kLoop, calls=%fused_computation.47 | loop fusion | flops 2490368 | bytes 4728836 | tf_op jit(solution)/shard_map/broadcast_in_dim | solution.py:665
  241.1 13.5 %collective-permute-done.44 = bf16[4,80,256]{2,1,0:T(8,128)(2,1)S(1)} collective-permute-done((bf16[4,80,256]{2,1,0:T(8,128)(2,1)S(1)}, bf16[4,80,256]{2,1,0:T(8,128)(2,1)S(1)}, u32[]{:S(2)}, u32[]{:S(2)}) %collective-permute-start.44) | collective-permute-done | bytes 163872 | tf_op jit(solution)/shard_map/ppermute | solution.py:411
  255.3 1.7 add_convert_fusion
  257.0 1.1 collective-permute-done.43
  258.1 1.7 collective-permute-done.45
  259.9 5.6 %reduce-scatter.2.cloned.1.call-done = bf16[1,432,704]{2,1,0:T(8,128)(2,1)} async-done(((bf16[8,432,704]{2,1,0:T(8,128)(2,1)}), bf16[1,432,704]{2,1,0:T(8,128)(2,1)}) %reduce-scatter.2.cloned.1.call-update) | async-done | bytes 608272 | tf_op jit(solution)/shard_map/reduce_scatter | solution.py:648
  267.6 2.5 collective-permute-start.51
  271.3 2.5 collective-permute-start.55
  273.8 2.9 collective-permute-start.60
  276.7 1.5 collective-permute-start.59
  282.0 7.4 %collective-permute-done.54 = bf16[80,1024]{1,0:T(8,128)(2,1)S(1)} collective-permute-done((bf16[80,1024]{1,0:T(8,128)(2,1)S(1)}, bf16[80,1024]{1,0:T(8,128)(2,1)S(1)}, u32[]{:S(2)}, u32[]{:S(2)}) %collective-permute-start.54) | collective-permute-done | bytes 163872 | tf_op jit(solution)/shard_map/ppermute | solution.py:411
  289.5 1.7 collective-permute-start.56
  292.2 3.5 %collective-permute-start.57 = (bf16[48,1024]{1,0:T(8,128)(2,1)S(1)}, bf16[48,1024]{1,0:T(8,128)(2,1)S(1)}, u32[]{:S(2)}, u32[]{:S(2)}) collective-permute-start(bf16[48,1024]{1,0:T(8,128)(2,1)S(1)} %slice.347), channel_id=1, source_target_pairs={{0,0},{1,1},{2,2},{3,3},{4,4},{5,5},{6,6},{7,7},{8,16},{9,17},{10,... | collective-permute-start | bytes 294920 | tf_op jit(solution)/shard_map/ppermute | solution.py:428
  296.4 1.7 collective-permute-done.57
  (352 shorter events, 66.0 us)
Async XLA Ops:
  7.2 127.5 %all-gather.3.cloned.1.call-start = ((), (), s32[]{:S(2)}) async-start(), calls=%async_computation.2 | async-start | bytes 5971968 | tf_op jit(solution)/shard_map/all_gather | solution.py:546
  7.2 33.2 %collective-permute-start = (bf16[128,1024]{1,0:T(8,128)(2,1)}, bf16[128,1024]{1,0:T(8,128)(2,1)S(1)}, u32[]{:S(2)}, u32[]{:S(2)}) collective-permute-start(bf16[128,1024]{1,0:T(8,128)(2,1)} %bitcast.372), channel_id=1, source_target_pairs={{0,8},{1,9},{2,10},{3,11},{4,12},{5,13},{6,14},{7,15},{8,0},{9,1},... | collective-permute-start | bytes 786440 | tf_op jit(solution)/shard_map/ppermute | solution.py:411
  8.2 25.2 %collective-permute-start.7 = (bf16[48,1024]{1,0:T(8,128)(2,1)S(1)}, bf16[48,1024]{1,0:T(8,128)(2,1)S(1)}, u32[]{:S(2)}, u32[]{:S(2)}) collective-permute-start(bf16[48,1024]{1,0:T(8,128)(2,1)S(1)} %pad_maximum_fusion.8), channel_id=1, source_target_pairs={{0,0},{1,1},{2,2},{3,3},{4,4},{5,5},{6,6},{7,7},{8,16},{9,17},{10,... | collective-permute-start | bytes 294920 | tf_op jit(solution)/shard_map/ppermute | solution.py:428
  15.7 5.7 %collective-permute-start.1 = (bf16[104,256]{1,0:T(8,128)(2,1)S(1)}, bf16[104,256]{1,0:T(8,128)(2,1)S(1)}, u32[]{:S(2)}, u32[]{:S(2)}) collective-permute-start(bf16[104,256]{1,0:T(8,128)(2,1)S(1)} %pad_maximum_fusion.10), channel_id=1, source_target_pairs={{0,8},{1,9},{2,10},{3,11},{4,12},{5,13},{6,14},{7,15},{8,0},{9,1},... | collective-permute-start | bytes 159752 | tf_op jit(solution)/shard_map/ppermute | solution.py:411
  18.2 5.1 %collective-permute-start.30 = (bf16[64,704]{1,0:T(8,128)(2,1)S(1)}, bf16[64,704]{1,0:T(8,128)(2,1)S(1)}, u32[]{:S(2)}, u32[]{:S(2)}) collective-permute-start(bf16[64,704]{1,0:T(8,128)(2,1)S(1)} %bitcast.397), channel_id=1, source_target_pairs={{0,8},{1,9},{2,10},{3,11},{4,12},{5,13},{6,14},{7,15},{8,0},{9,1},... | collective-permute-start | bytes 270344 | tf_op jit(solution)/shard_map/ppermute | solution.py:411
  18.7 5.9 %collective-permute-start.31 = (bf16[64,704]{1,0:T(8,128)(2,1)S(1)}, bf16[64,704]{1,0:T(8,128)(2,1)S(1)}, u32[]{:S(2)}, u32[]{:S(2)}) collective-permute-start(bf16[64,704]{1,0:T(8,128)(2,1)S(1)} %bitcast.396), channel_id=1, source_target_pairs={{0,16},{1,17},{2,18},{3,19},{4,20},{5,21},{6,22},{7,23},{8,24},{9,... | collective-permute-start | bytes 270344 | tf_op jit(solution)/shard_map/ppermute | solution.py:411
  21.4 5.6 %collective-permute-start.32 = (bf16[64,704]{1,0:T(8,128)(2,1)S(1)}, bf16[64,704]{1,0:T(8,128)(2,1)S(1)}, u32[]{:S(2)}, u32[]{:S(2)}) collective-permute-start(bf16[64,704]{1,0:T(8,128)(2,1)S(1)} %bitcast.398), channel_id=1, source_target_pairs={{0,24},{1,25},{2,26},{3,27},{4,28},{5,29},{6,30},{7,31},{8,16},{9,... | collective-permute-start | bytes 270344 | tf_op jit(solution)/shard_map/ppermute | solution.py:411
  23.2 8.1 %collective-permute-start.2 = (bf16[80,256]{1,0:T(8,128)(2,1)S(1)}, bf16[80,256]{1,0:T(8,128)(2,1)S(1)}, u32[]{:S(2)}, u32[]{:S(2)}) collective-permute-start(bf16[80,256]{1,0:T(8,128)(2,1)S(1)} %get-tuple-element.135), channel_id=1, source_target_pairs={{0,2},{1,3},{2,0},{3,1},{4,6},{5,7},{6,4},{7,5},{8,10},{9,11},{10,... | collective-permute-start | bytes 122888 | tf_op jit(solution)/shard_map/ppermute | solution.py:411
  24.6 6.8 %collective-permute-start.3 = (bf16[80,256]{1,0:T(8,128)(2,1)S(1)}, bf16[80,256]{1,0:T(8,128)(2,1)S(1)}, u32[]{:S(2)}, u32[]{:S(2)}) collective-permute-start(bf16[80,256]{1,0:T(8,128)(2,1)S(1)} %get-tuple-element.135), channel_id=1, source_target_pairs={{0,4},{1,5},{2,6},{3,7},{4,0},{5,1},{6,2},{7,3},{8,12},{9,13},{10,... | collective-permute-start | bytes 122888 | tf_op jit(solution)/shard_map/ppermute | solution.py:411
  27.0 4.8 %collective-permute-start.4 = (bf16[80,256]{1,0:T(8,128)(2,1)S(1)}, bf16[80,256]{1,0:T(8,128)(2,1)S(1)}, u32[]{:S(2)}, u32[]{:S(2)}) collective-permute-start(bf16[80,256]{1,0:T(8,128)(2,1)S(1)} %get-tuple-element.135), channel_id=1, source_target_pairs={{0,6},{1,7},{2,4},{3,5},{4,2},{5,3},{6,0},{7,1},{8,14},{9,15},{10,... | collective-permute-start | bytes 122888 | tf_op jit(solution)/shard_map/ppermute | solution.py:411
  31.3 234.2 %reduce-scatter.2.cloned.1.call-start = ((), (), s32[]{:S(2)}) async-start(), calls=%async_computation.1 | async-start | bytes 5971968 | tf_op jit(solution)/shard_map/reduce_scatter | solution.py:648
  31.9 5.8 %collective-permute-start.5 = (bf16[4,80,256]{2,1,0:T(8,128)(2,1)S(1)}, bf16[4,80,256]{2,1,0:T(8,128)(2,1)S(1)}, u32[]{:S(2)}, u32[]{:S(2)}) collective-permute-start(bf16[4,80,256]{2,1,0:T(8,128)(2,1)S(1)} %pad_maximum_fusion.5), channel_id=1, source_target_pairs={{0,1},{1,0},{2,3},{3,2},{4,5},{5,4},{6,7},{7,6},{8,9},{9,8},{10,11... | collective-permute-start | bytes 491528 | tf_op jit(solution)/shard_map/ppermute | solution.py:411
  33.4 7.8 %collective-permute-start.8 = (bf16[80,1024]{1,0:T(8,128)(2,1)S(1)}, bf16[80,1024]{1,0:T(8,128)(2,1)S(1)}, u32[]{:S(2)}, u32[]{:S(2)}) collective-permute-start(bf16[80,1024]{1,0:T(8,128)(2,1)S(1)} %get-tuple-element.125), channel_id=1, source_target_pairs={{0,2},{1,3},{2,0},{3,1},{4,6},{5,7},{6,4},{7,5},{8,10},{9,11},{10,... | collective-permute-start | bytes 491528 | tf_op jit(solution)/shard_map/ppermute | solution.py:411
  33.5 9.8 %collective-permute-start.9 = (bf16[80,1024]{1,0:T(8,128)(2,1)S(1)}, bf16[80,1024]{1,0:T(8,128)(2,1)S(1)}, u32[]{:S(2)}, u32[]{:S(2)}) collective-permute-start(bf16[80,1024]{1,0:T(8,128)(2,1)S(1)} %get-tuple-element.125), channel_id=1, source_target_pairs={{0,4},{1,5},{2,6},{3,7},{4,0},{5,1},{6,2},{7,3},{8,12},{9,13},{10,... | collective-permute-start | bytes 491528 | tf_op jit(solution)/shard_map/ppermute | solution.py:411
  37.0 13.4 %collective-permute-start.10 = (bf16[80,1024]{1,0:T(8,128)(2,1)S(1)}, bf16[80,1024]{1,0:T(8,128)(2,1)S(1)}, u32[]{:S(2)}, u32[]{:S(2)}) collective-permute-start(bf16[80,1024]{1,0:T(8,128)(2,1)S(1)} %get-tuple-element.125), channel_id=1, source_target_pairs={{0,6},{1,7},{2,4},{3,5},{4,2},{5,3},{6,0},{7,1},{8,14},{9,15},{10,... | collective-permute-start | bytes 491528 | tf_op jit(solution)/shard_map/ppermute | solution.py:411
  37.7 14.9 %collective-permute-start.11 = (bf16[1,80,1024]{2,1,0:T(8,128)(2,1)S(1)}, bf16[1,80,1024]{2,1,0:T(8,128)(2,1)S(1)}, u32[]{:S(2)}, u32[]{:S(2)}) collective-permute-start(bf16[1,80,1024]{2,1,0:T(8,128)(2,1)S(1)} %get-tuple-element.126.refs_0_), channel_id=1, source_target_pairs={{0,1},{1,0},{2,3},{3,2},{4,5},{5,4},{6,7},{7,6},{8,9},{9,8},{10,11... | collective-permute-start | bytes 491528 | tf_op jit(solution)/shard_map/ppermute | solution.py:411
  40.4 49.8 %copy-start.42 = (bf16[128,1024]{1,0:T(8,128)(2,1)}, bf16[128,1024]{1,0:T(8,128)(2,1)S(1)}, u32[]{:S(2)}) copy-start(bf16[128,1024]{1,0:T(8,128)(2,1)S(1)} %collective-permute-done) | copy-start | bytes 786436
  40.5 16.4 %collective-permute-start.6 = (bf16[8,80,256]{2,1,0:T(8,128)(2,1)}, bf16[8,80,256]{2,1,0:T(8,128)(2,1)S(1)}, u32[]{:S(2)}, u32[]{:S(2)}) collective-permute-start(bf16[8,80,256]{2,1,0:T(8,128)(2,1)} %copy-done.55), channel_id=1, source_target_pairs={{0,16},{1,17},{2,18},{3,19},{4,20},{5,21},{6,22},{7,23},{8,24},{9,... | collective-permute-start | bytes 983048 | tf_op jit(solution)/shard_map/ppermute | solution.py:411
  41.2 12.1 %collective-permute-start.12 = (bf16[1,80,1024]{2,1,0:T(8,128)(2,1)S(1)}, bf16[1,80,1024]{2,1,0:T(8,128)(2,1)S(1)}, u32[]{:S(2)}, u32[]{:S(2)}) collective-permute-start(bf16[1,80,1024]{2,1,0:T(8,128)(2,1)S(1)} %bitcast.344), channel_id=1, source_target_pairs={{0,1},{1,0},{2,3},{3,2},{4,5},{5,4},{6,7},{7,6},{8,9},{9,8},{10,11... | collective-permute-start | bytes 491528 | tf_op jit(solution)/shard_map/ppermute | solution.py:411
  43.3 12.8 %collective-permute-start.13 = (bf16[1,80,1024]{2,1,0:T(8,128)(2,1)S(1)}, bf16[1,80,1024]{2,1,0:T(8,128)(2,1)S(1)}, u32[]{:S(2)}, u32[]{:S(2)}) collective-permute-start(bf16[1,80,1024]{2,1,0:T(8,128)(2,1)S(1)} %bitcast.346), channel_id=1, source_target_pairs={{0,1},{1,0},{2,3},{3,2},{4,5},{5,4},{6,7},{7,6},{8,9},{9,8},{10,11... | collective-permute-start | bytes 491528 | tf_op jit(solution)/shard_map/ppermute | solution.py:411
  50.3 18.6 %collective-permute-start.14 = (bf16[1,80,1024]{2,1,0:T(8,128)(2,1)S(1)}, bf16[1,80,1024]{2,1,0:T(8,128)(2,1)S(1)}, u32[]{:S(2)}, u32[]{:S(2)}) collective-permute-start(bf16[1,80,1024]{2,1,0:T(8,128)(2,1)S(1)} %bitcast.348), channel_id=1, source_target_pairs={{0,1},{1,0},{2,3},{3,2},{4,5},{5,4},{6,7},{7,6},{8,9},{9,8},{10,11... | collective-permute-start | bytes 491528 | tf_op jit(solution)/shard_map/ppermute | solution.py:411
  58.3 13.1 %collective-permute-start.16 = (bf16[2,128,256]{2,1,0:T(8,128)(2,1)S(1)}, bf16[2,128,256]{2,1,0:T(8,128)(2,1)S(1)}, u32[]{:S(2)}, u32[]{:S(2)}) collective-permute-start(bf16[2,128,256]{2,1,0:T(8,128)(2,1)S(1)} %bitcast.388), channel_id=1, source_target_pairs={{0,2},{1,3},{2,0},{3,1},{4,6},{5,7},{6,4},{7,5},{8,10},{9,11},{10,... | collective-permute-start | bytes 393224 | tf_op jit(solution)/shard_map/ppermute | solution.py:411
  65.7 12.2 %collective-permute-start.17 = (bf16[2,128,256]{2,1,0:T(8,128)(2,1)S(1)}, bf16[2,128,256]{2,1,0:T(8,128)(2,1)S(1)}, u32[]{:S(2)}, u32[]{:S(2)}) collective-permute-start(bf16[2,128,256]{2,1,0:T(8,128)(2,1)S(1)} %bitcast.389), channel_id=1, source_target_pairs={{0,4},{1,5},{2,6},{3,7},{4,0},{5,1},{6,2},{7,3},{8,12},{9,13},{10,... | collective-permute-start | bytes 393224 | tf_op jit(solution)/shard_map/ppermute | solution.py:411
  67.8 10.2 %collective-permute-start.18 = (bf16[2,128,256]{2,1,0:T(8,128)(2,1)S(1)}, bf16[2,128,256]{2,1,0:T(8,128)(2,1)S(1)}, u32[]{:S(2)}, u32[]{:S(2)}) collective-permute-start(bf16[2,128,256]{2,1,0:T(8,128)(2,1)S(1)} %bitcast.390), channel_id=1, source_target_pairs={{0,6},{1,7},{2,4},{3,5},{4,2},{5,3},{6,0},{7,1},{8,14},{9,15},{10,... | collective-permute-start | bytes 393224 | tf_op jit(solution)/shard_map/ppermute | solution.py:411
  68.9 20.6 %collective-permute-start.15 = (bf16[8,80,1024]{2,1,0:T(8,128)(2,1)S(1)}, bf16[8,80,1024]{2,1,0:T(8,128)(2,1)S(1)}, u32[]{:S(2)}, u32[]{:S(2)}) collective-permute-start(bf16[8,80,1024]{2,1,0:T(8,128)(2,1)S(1)} %constant_dynamic-update-slice_fusion.11), channel_id=1, source_target_pairs={{0,16},{1,17},{2,18},{3,19},{4,20},{5,21},{6,22},{7,23},{8,24},{9,... | collective-permute-start | bytes 3932168 | tf_op jit(solution)/shard_map/ppermute | solution.py:411
  70.1 9.4 %collective-permute-start.19 = (bf16[1,2,128,256]{3,2,1,0:T(8,128)(2,1)S(1)}, bf16[1,2,128,256]{3,2,1,0:T(8,128)(2,1)S(1)}, u32[]{:S(2)}, u32[]{:S(2)}) collective-permute-start(bf16[1,2,128,256]{3,2,1,0:T(8,128)(2,1)S(1)} %bitcast.392), channel_id=1, source_target_pairs={{0,1},{1,0},{2,3},{3,2},{4,5},{5,4},{6,7},{7,6},{8,9},{9,8},{10,11... | collective-permute-start | bytes 393224 | tf_op jit(solution)/shard_map/ppermute | solution.py:411
  71.4 8.2 %collective-permute-start.20 = (bf16[1,2,128,256]{3,2,1,0:T(8,128)(2,1)S(1)}, bf16[1,2,128,256]{3,2,1,0:T(8,128)(2,1)S(1)}, u32[]{:S(2)}, u32[]{:S(2)}) collective-permute-start(bf16[1,2,128,256]{3,2,1,0:T(8,128)(2,1)S(1)} %bitcast.387), channel_id=1, source_target_pairs={{0,1},{1,0},{2,3},{3,2},{4,5},{5,4},{6,7},{7,6},{8,9},{9,8},{10,11... | collective-permute-start | bytes 393224 | tf_op jit(solution)/shard_map/ppermute | solution.py:411
  78.0 3.8 %collective-permute-start.21 = (bf16[1,2,128,256]{3,2,1,0:T(8,128)(2,1)S(1)}, bf16[1,2,128,256]{3,2,1,0:T(8,128)(2,1)S(1)}, u32[]{:S(2)}, u32[]{:S(2)}) collective-permute-start(bf16[1,2,128,256]{3,2,1,0:T(8,128)(2,1)S(1)} %bitcast.386), channel_id=1, source_target_pairs={{0,1},{1,0},{2,3},{3,2},{4,5},{5,4},{6,7},{7,6},{8,9},{9,8},{10,11... | collective-permute-start | bytes 393224 | tf_op jit(solution)/shard_map/ppermute | solution.py:411
  78.0 7.5 %collective-permute-start.22 = (bf16[1,2,128,256]{3,2,1,0:T(8,128)(2,1)S(1)}, bf16[1,2,128,256]{3,2,1,0:T(8,128)(2,1)S(1)}, u32[]{:S(2)}, u32[]{:S(2)}) collective-permute-start(bf16[1,2,128,256]{3,2,1,0:T(8,128)(2,1)S(1)} %bitcast.385), channel_id=1, source_target_pairs={{0,1},{1,0},{2,3},{3,2},{4,5},{5,4},{6,7},{7,6},{8,9},{9,8},{10,11... | collective-permute-start | bytes 393224 | tf_op jit(solution)/shard_map/ppermute | solution.py:411
  105.6 13.8 %collective-permute-start.23 = (f32[128,1024]{1,0:T(8,128)}, f32[128,1024]{1,0:T(8,128)}, u32[]{:S(2)}, u32[]{:S(2)}) collective-permute-start(f32[128,1024]{1,0:T(8,128)} %slice.327), channel_id=1, source_target_pairs={{0,8},{1,9},{2,10},{3,11},{4,12},{5,13},{6,14},{7,15},{8,0},{9,1},... | collective-permute-start | bytes 1572872 | tf_op jit(solution)/shard_map/ppermute | solution.py:411
  118.1 8.1 %collective-permute-start.28 = (bf16[128,1024]{1,0:T(8,128)(2,1)S(1)}, bf16[128,1024]{1,0:T(8,128)(2,1)S(1)}, u32[]{:S(2)}, u32[]{:S(2)}) collective-permute-start(bf16[128,1024]{1,0:T(8,128)(2,1)S(1)} %bitcast_convert_fusion.refs_4_), channel_id=1, source_target_pairs={{0,16},{1,17},{2,18},{3,19},{4,20},{5,21},{6,22},{7,23},{8,24},{9,... | collective-permute-start | bytes 786440 | tf_op jit(solution)/shard_map/ppermute | solution.py:411
  122.4 9.4 %collective-permute-start.25 = (bf16[128,1024]{1,0:T(8,128)(2,1)S(1)}, bf16[128,1024]{1,0:T(8,128)(2,1)S(1)}, u32[]{:S(2)}, u32[]{:S(2)}) collective-permute-start(bf16[128,1024]{1,0:T(8,128)(2,1)S(1)} %multiply_convert_fusion.1.refs_0_), channel_id=1, source_target_pairs={{0,16},{1,17},{2,18},{3,19},{4,20},{5,21},{6,22},{7,23},{8,24},{9,... | collective-permute-start | bytes 786440 | tf_op jit(solution)/shard_map/ppermute | solution.py:411
  122.9 15.2 %collective-permute-start.27 = (bf16[128,1024]{1,0:T(8,128)(2,1)S(1)}, bf16[128,1024]{1,0:T(8,128)(2,1)S(1)}, u32[]{:S(2)}, u32[]{:S(2)}) collective-permute-start(bf16[128,1024]{1,0:T(8,128)(2,1)S(1)} %bitcast_convert_fusion.refs_4_), channel_id=1, source_target_pairs={{0,8},{1,9},{2,10},{3,11},{4,12},{5,13},{6,14},{7,15},{8,0},{9,1},... | collective-permute-start | bytes 786440 | tf_op jit(solution)/shard_map/ppermute | solution.py:411
  126.2 12.6 %collective-permute-start.29 = (bf16[128,1024]{1,0:T(8,128)(2,1)S(1)}, bf16[128,1024]{1,0:T(8,128)(2,1)S(1)}, u32[]{:S(2)}, u32[]{:S(2)}) collective-permute-start(bf16[128,1024]{1,0:T(8,128)(2,1)S(1)} %collective-permute-done.28.refs_6_), channel_id=1, source_target_pairs={{0,8},{1,9},{2,10},{3,11},{4,12},{5,13},{6,14},{7,15},{8,0},{9,1},... | collective-permute-start | bytes 786440 | tf_op jit(solution)/shard_map/ppermute | solution.py:411
  127.3 12.2 %collective-permute-start.24 = (bf16[128,1024]{1,0:T(8,128)(2,1)S(1)}, bf16[128,1024]{1,0:T(8,128)(2,1)S(1)}, u32[]{:S(2)}, u32[]{:S(2)}) collective-permute-start(bf16[128,1024]{1,0:T(8,128)(2,1)S(1)} %multiply_convert_fusion.1.refs_0_), channel_id=1, source_target_pairs={{0,8},{1,9},{2,10},{3,11},{4,12},{5,13},{6,14},{7,15},{8,0},{9,1},... | collective-permute-start | bytes 786440 | tf_op jit(solution)/shard_map/ppermute | solution.py:411
  131.8 8.4 %collective-permute-start.26 = (bf16[128,1024]{1,0:T(8,128)(2,1)S(1)}, bf16[128,1024]{1,0:T(8,128)(2,1)S(1)}, u32[]{:S(2)}, u32[]{:S(2)}) collective-permute-start(bf16[128,1024]{1,0:T(8,128)(2,1)S(1)} %collective-permute-done.25.refs_2_), channel_id=1, source_target_pairs={{0,8},{1,9},{2,10},{3,11},{4,12},{5,13},{6,14},{7,15},{8,0},{9,1},... | collective-permute-start | bytes 786440 | tf_op jit(solution)/shard_map/ppermute | solution.py:411
  159.5 3.5 %collective-permute-start.35 = (f32[2,128,1024]{2,1,0:T(8,128)}, f32[2,128,1024]{2,1,0:T(8,128)S(1)}, u32[]{:S(2)}, u32[]{:S(2)}) collective-permute-start(f32[2,128,1024]{2,1,0:T(8,128)} %copy-done.8), channel_id=1, source_target_pairs={{0,8},{1,9},{2,10},{3,11},{4,12},{5,13},{6,14},{7,15},{8,0},{9,1},... | collective-permute-start | bytes 3145736 | tf_op jit(solution)/shard_map/ppermute | solution.py:411
  163.0 7.7 %collective-permute-start.36 = (bf16[128,1024]{1,0:T(8,128)(2,1)S(1)}, bf16[128,1024]{1,0:T(8,128)(2,1)S(1)}, u32[]{:S(2)}, u32[]{:S(2)}) collective-permute-start(bf16[128,1024]{1,0:T(8,128)(2,1)S(1)} %fusion.14), channel_id=1, source_target_pairs={{0,16},{1,17},{2,18},{3,19},{4,20},{5,21},{6,22},{7,23},{8,24},{9,... | collective-permute-start | bytes 786440 | tf_op jit(solution)/shard_map/ppermute | solution.py:411
  172.8 2.3 collective-permute-start.37
  192.3 14.5 %collective-permute-start.38 = (bf16[4,2,128,256]{3,2,1,0:T(8,128)(2,1)}, bf16[4,2,128,256]{3,2,1,0:T(8,128)(2,1)S(1)}, u32[]{:S(2)}, u32[]{:S(2)}) collective-permute-start(bf16[4,2,128,256]{3,2,1,0:T(8,128)(2,1)} %get-tuple-element.69), channel_id=1, source_target_pairs={{0,1},{1,0},{2,3},{3,2},{4,5},{5,4},{6,7},{7,6},{8,9},{9,8},{10,11... | collective-permute-start | bytes 1572872 | tf_op jit(solution)/shard_map/ppermute | solution.py:411
  193.6 33.1 %collective-permute-start.33 = (f32[2,128,1024]{2,1,0:T(8,128)}, f32[2,128,1024]{2,1,0:T(8,128)S(1)}, u32[]{:S(2)}, u32[]{:S(2)}) collective-permute-start(f32[2,128,1024]{2,1,0:T(8,128)} %get-tuple-element.61), channel_id=1, source_target_pairs={{0,8},{1,9},{2,10},{3,11},{4,12},{5,13},{6,14},{7,15},{8,0},{9,1},... | collective-permute-start | bytes 3145736 | tf_op jit(solution)/shard_map/ppermute | solution.py:411
  208.9 7.0 %collective-permute-start.41 = (bf16[2,128,256]{2,1,0:T(8,128)(2,1)S(1)}, bf16[2,128,256]{2,1,0:T(8,128)(2,1)S(1)}, u32[]{:S(2)}, u32[]{:S(2)}) collective-permute-start(bf16[2,128,256]{2,1,0:T(8,128)(2,1)S(1)} %get-tuple-element.108), channel_id=1, source_target_pairs={{0,6},{1,7},{2,4},{3,5},{4,2},{5,3},{6,0},{7,1},{8,14},{9,15},{10,... | collective-permute-start | bytes 393224 | tf_op jit(solution)/shard_map/ppermute | solution.py:411
  210.6 12.6 %collective-permute-start.40 = (bf16[2,128,256]{2,1,0:T(8,128)(2,1)S(1)}, bf16[2,128,256]{2,1,0:T(8,128)(2,1)S(1)}, u32[]{:S(2)}, u32[]{:S(2)}) collective-permute-start(bf16[2,128,256]{2,1,0:T(8,128)(2,1)S(1)} %get-tuple-element.109), channel_id=1, source_target_pairs={{0,4},{1,5},{2,6},{3,7},{4,0},{5,1},{6,2},{7,3},{8,12},{9,13},{10,... | collective-permute-start | bytes 393224 | tf_op jit(solution)/shard_map/ppermute | solution.py:411
  211.6 11.6 %collective-permute-start.39 = (bf16[2,128,256]{2,1,0:T(8,128)(2,1)S(1)}, bf16[2,128,256]{2,1,0:T(8,128)(2,1)S(1)}, u32[]{:S(2)}, u32[]{:S(2)}) collective-permute-start(bf16[2,128,256]{2,1,0:T(8,128)(2,1)S(1)} %get-tuple-element.107), channel_id=1, source_target_pairs={{0,2},{1,3},{2,0},{3,1},{4,6},{5,7},{6,4},{7,5},{8,10},{9,11},{10,... | collective-permute-start | bytes 393224 | tf_op jit(solution)/shard_map/ppermute | solution.py:411
  214.6 15.3 %collective-permute-start.47 = (bf16[4,80,1024]{2,1,0:T(8,128)(2,1)}, bf16[4,80,1024]{2,1,0:T(8,128)(2,1)}, u32[]{:S(2)}, u32[]{:S(2)}) collective-permute-start(bf16[4,80,1024]{2,1,0:T(8,128)(2,1)} %get-tuple-element.79), channel_id=1, source_target_pairs={{0,16},{1,17},{2,18},{3,19},{4,20},{5,21},{6,22},{7,23},{8,24},{9,... | collective-permute-start | bytes 1966088 | tf_op jit(solution)/shard_map/ppermute | solution.py:411
  225.4 8.3 %collective-permute-start.42 = (f32[128,1024]{1,0:T(8,128)}, f32[128,1024]{1,0:T(8,128)}, u32[]{:S(2)}, u32[]{:S(2)}) collective-permute-start(f32[128,1024]{1,0:T(8,128)} %slice.338), channel_id=1, source_target_pairs={{0,8},{1,9},{2,10},{3,11},{4,12},{5,13},{6,14},{7,15},{8,0},{9,1},... | collective-permute-start | bytes 1572872 | tf_op jit(solution)/shard_map/ppermute | solution.py:411
  228.4 9.0 %collective-permute-start.34 = (bf16[128,1024]{1,0:T(8,128)(2,1)}, bf16[128,1024]{1,0:T(8,128)(2,1)}, u32[]{:S(2)}, u32[]{:S(2)}) collective-permute-start(bf16[128,1024]{1,0:T(8,128)(2,1)} %fusion.13), channel_id=1, source_target_pairs={{0,16},{1,17},{2,18},{3,19},{4,20},{5,21},{6,22},{7,23},{8,24},{9,... | collective-permute-start | bytes 786440 | tf_op jit(solution)/shard_map/ppermute | solution.py:411
  229.5 25.8 %collective-permute-start.46 = (bf16[4,80,1024]{2,1,0:T(8,128)(2,1)}, bf16[4,80,1024]{2,1,0:T(8,128)(2,1)}, u32[]{:S(2)}, u32[]{:S(2)}) collective-permute-start(bf16[4,80,1024]{2,1,0:T(8,128)(2,1)} %copy-done.9), channel_id=1, source_target_pairs={{0,16},{1,17},{2,18},{3,19},{4,20},{5,21},{6,22},{7,23},{8,24},{9,... | collective-permute-start | bytes 1966088 | tf_op jit(solution)/shard_map/ppermute | solution.py:411
  232.2 23.1 %collective-permute-start.48 = (bf16[4,80,1024]{2,1,0:T(8,128)(2,1)}, bf16[4,80,1024]{2,1,0:T(8,128)(2,1)}, u32[]{:S(2)}, u32[]{:S(2)}) collective-permute-start(bf16[4,80,1024]{2,1,0:T(8,128)(2,1)} %add_convert_fusion.1), channel_id=1, source_target_pairs={{0,1},{1,0},{2,3},{3,2},{4,5},{5,4},{6,7},{7,6},{8,9},{9,8},{10,11... | collective-permute-start | bytes 1966088 | tf_op jit(solution)/shard_map/ppermute | solution.py:411
  235.8 18.8 %collective-permute-start.44 = (bf16[4,80,256]{2,1,0:T(8,128)(2,1)S(1)}, bf16[4,80,256]{2,1,0:T(8,128)(2,1)S(1)}, u32[]{:S(2)}, u32[]{:S(2)}) collective-permute-start(bf16[4,80,256]{2,1,0:T(8,128)(2,1)S(1)} %get-tuple-element.73), channel_id=1, source_target_pairs={{0,16},{1,17},{2,18},{3,19},{4,20},{5,21},{6,22},{7,23},{8,24},{9,... | collective-permute-start | bytes 491528 | tf_op jit(solution)/shard_map/ppermute | solution.py:411
  237.1 21.0 %collective-permute-start.43 = (bf16[4,80,256]{2,1,0:T(8,128)(2,1)S(1)}, bf16[4,80,256]{2,1,0:T(8,128)(2,1)S(1)}, u32[]{:S(2)}, u32[]{:S(2)}) collective-permute-start(bf16[4,80,256]{2,1,0:T(8,128)(2,1)S(1)} %get-tuple-element.71), channel_id=1, source_target_pairs={{0,16},{1,17},{2,18},{3,19},{4,20},{5,21},{6,22},{7,23},{8,24},{9,... | collective-permute-start | bytes 491528 | tf_op jit(solution)/shard_map/ppermute | solution.py:411
  254.7 5.2 %collective-permute-start.45 = (bf16[4,80,256]{2,1,0:T(8,128)(2,1)S(1)}, bf16[4,80,256]{2,1,0:T(8,128)(2,1)S(1)}, u32[]{:S(2)}, u32[]{:S(2)}) collective-permute-start(bf16[4,80,256]{2,1,0:T(8,128)(2,1)S(1)} %add_convert_fusion.4), channel_id=1, source_target_pairs={{0,1},{1,0},{2,3},{3,2},{4,5},{5,4},{6,7},{7,6},{8,9},{9,8},{10,11... | collective-permute-start | bytes 491528 | tf_op jit(solution)/shard_map/ppermute | solution.py:411
  267.6 6.2 %collective-permute-start.51 = (bf16[80,256]{1,0:T(8,128)(2,1)S(1)}, bf16[80,256]{1,0:T(8,128)(2,1)S(1)}, u32[]{:S(2)}, u32[]{:S(2)}) collective-permute-start(bf16[80,256]{1,0:T(8,128)(2,1)S(1)} %get-tuple-element.123), channel_id=1, source_target_pairs={{0,6},{1,7},{2,4},{3,5},{4,2},{5,3},{6,0},{7,1},{8,14},{9,15},{10,... | collective-permute-start | bytes 122888 | tf_op jit(solution)/shard_map/ppermute | solution.py:411
  270.1 6.6 %collective-permute-start.50 = (bf16[80,256]{1,0:T(8,128)(2,1)S(1)}, bf16[80,256]{1,0:T(8,128)(2,1)S(1)}, u32[]{:S(2)}, u32[]{:S(2)}) collective-permute-start(bf16[80,256]{1,0:T(8,128)(2,1)S(1)} %get-tuple-element.124), channel_id=1, source_target_pairs={{0,4},{1,5},{2,6},{3,7},{4,0},{5,1},{6,2},{7,3},{8,12},{9,13},{10,... | collective-permute-start | bytes 122888 | tf_op jit(solution)/shard_map/ppermute | solution.py:411
  271.0 7.3 %collective-permute-start.49 = (bf16[80,256]{1,0:T(8,128)(2,1)S(1)}, bf16[80,256]{1,0:T(8,128)(2,1)S(1)}, u32[]{:S(2)}, u32[]{:S(2)}) collective-permute-start(bf16[80,256]{1,0:T(8,128)(2,1)S(1)} %get-tuple-element.122), channel_id=1, source_target_pairs={{0,2},{1,3},{2,0},{3,1},{4,6},{5,7},{6,4},{7,5},{8,10},{9,11},{10,... | collective-permute-start | bytes 122888 | tf_op jit(solution)/shard_map/ppermute | solution.py:411
  271.3 10.7 %collective-permute-start.55 = (bf16[80,1024]{1,0:T(8,128)(2,1)S(1)}, bf16[80,1024]{1,0:T(8,128)(2,1)S(1)}, u32[]{:S(2)}, u32[]{:S(2)}) collective-permute-start(bf16[80,1024]{1,0:T(8,128)(2,1)S(1)} %get-tuple-element.103), channel_id=1, source_target_pairs={{0,6},{1,7},{2,4},{3,5},{4,2},{5,3},{6,0},{7,1},{8,14},{9,15},{10,... | collective-permute-start | bytes 491528 | tf_op jit(solution)/shard_map/ppermute | solution.py:411
  273.8 15.6 %collective-permute-start.54 = (bf16[80,1024]{1,0:T(8,128)(2,1)S(1)}, bf16[80,1024]{1,0:T(8,128)(2,1)S(1)}, u32[]{:S(2)}, u32[]{:S(2)}) collective-permute-start(bf16[80,1024]{1,0:T(8,128)(2,1)S(1)} %get-tuple-element.104), channel_id=1, source_target_pairs={{0,4},{1,5},{2,6},{3,7},{4,0},{5,1},{6,2},{7,3},{8,12},{9,13},{10,... | collective-permute-start | bytes 491528 | tf_op jit(solution)/shard_map/ppermute | solution.py:411
  273.8 7.1 %collective-permute-start.60 = (bf16[64,704]{1,0:T(8,128)(2,1)S(1)}, bf16[64,704]{1,0:T(8,128)(2,1)S(1)}, u32[]{:S(2)}, u32[]{:S(2)}) collective-permute-start(bf16[64,704]{1,0:T(8,128)(2,1)S(1)} %get-tuple-element.99), channel_id=1, source_target_pairs={{0,24},{1,25},{2,26},{3,27},{4,28},{5,29},{6,30},{7,31},{8,16},{9,... | collective-permute-start | bytes 270344 | tf_op jit(solution)/shard_map/ppermute | solution.py:411
  276.7 5.0 %collective-permute-start.59 = (bf16[64,704]{1,0:T(8,128)(2,1)S(1)}, bf16[64,704]{1,0:T(8,128)(2,1)S(1)}, u32[]{:S(2)}, u32[]{:S(2)}) collective-permute-start(bf16[64,704]{1,0:T(8,128)(2,1)S(1)} %get-tuple-element.100), channel_id=1, source_target_pairs={{0,16},{1,17},{2,18},{3,19},{4,20},{5,21},{6,22},{7,23},{8,24},{9,... | collective-permute-start | bytes 270344 | tf_op jit(solution)/shard_map/ppermute | solution.py:411
  278.3 1.3 collective-permute-start.52
  279.5 2.1 collective-permute-start.58
  281.0 8.5 %collective-permute-start.53 = (bf16[80,1024]{1,0:T(8,128)(2,1)S(1)}, bf16[80,1024]{1,0:T(8,128)(2,1)S(1)}, u32[]{:S(2)}, u32[]{:S(2)}) collective-permute-start(bf16[80,1024]{1,0:T(8,128)(2,1)S(1)} %get-tuple-element.102), channel_id=1, source_target_pairs={{0,2},{1,3},{2,0},{3,1},{4,6},{5,7},{6,4},{7,5},{8,10},{9,11},{10,... | collective-permute-start | bytes 491528 | tf_op jit(solution)/shard_map/ppermute | solution.py:411
  289.5 6.1 %collective-permute-start.56 = (bf16[32,512]{1,0:T(8,128)(2,1)S(1)}, bf16[32,512]{1,0:T(8,128)(2,1)S(1)}, u32[]{:S(2)}, u32[]{:S(2)}) collective-permute-start(bf16[32,512]{1,0:T(8,128)(2,1)S(1)} %slice.345), channel_id=1, source_target_pairs={{0,8},{1,9},{2,10},{3,11},{4,12},{5,13},{6,14},{7,15},{8,0},{9,1},... | collective-permute-start | bytes 98312 | tf_op jit(solution)/shard_map/ppermute | solution.py:411
  292.2 5.9 %collective-permute-start.57 = (bf16[48,1024]{1,0:T(8,128)(2,1)S(1)}, bf16[48,1024]{1,0:T(8,128)(2,1)S(1)}, u32[]{:S(2)}, u32[]{:S(2)}) collective-permute-start(bf16[48,1024]{1,0:T(8,128)(2,1)S(1)} %slice.347), channel_id=1, source_target_pairs={{0,0},{1,1},{2,2},{3,3},{4,4},{5,5},{6,6},{7,7},{8,16},{9,17},{10,... | collective-permute-start | bytes 294920 | tf_op jit(solution)/shard_map/ppermute | solution.py:428
  (63 other events, 404.1 us)
Sparse Core Ops, SparseCore 0:
  31.4 103.2 all-gather.2
  159.6 105.8 reduce-scatter.1
